TPU v7x, 32 devices: a whole 2x2x4 slice. The times are simulated.
32 devices in a mesh: ka: 8 (over z, x), band: 4 (over y, core).
Axes of the slice: x: 2, y: 2, z: 4, core: 2. Of those that a mesh axis runs over, the one named last changes fastest.
Arguments:
- occupied: bfloat16 [16, 8, 4096], P('ka'), may hold values from -6 to 6
- virtual: bfloat16 [16, 128, 4096], P('ka', 'band'), may hold values from -6 to 6
- occ_energy: float32 [16, 8], P('ka'), may hold values from -2 to -0.5
- virt_energy: float32 [16, 128], P(None, 'band'), may hold values from 0.5 to 2
- partner: int32 [2, 16], replicated, may hold values from 0 to 15, as said below
- coulomb: float32 [2, 512], replicated, may hold values from 0.5 to 2
- basis: bfloat16 [512, 4096], replicated, may hold values from -0.09375 to 0.09375
Outputs:
- occ_update: bfloat16 [16, 8, 4096], P('ka', None, 'band')
- virt_update: bfloat16 [16, 128, 4096], P('ka', 'band')
Inputs may be any that keep to these rules, and one draw needn't show every extreme that they name: Each row pairs the 16 k-points: partner[q, partner[q, k]] == k and partner[q, k] != k.
All inputs are finite; a program needn't handle non-finite values.
Results may differ from a plain program's by a relative error of at most 0.012.
Values may be sent and summed in bfloat16 or wider, within the bound.
No kernel may reach another device: no remote copies, remote signals or barrier semaphores. Data moves between devices by JAX's collectives and lax.ppermute only.
A program may use at most 64 MiB of HBM per device.

v0:
```python
import math

import jax
import jax.numpy as jnp
from jax import lax
from jax.sharding import PartitionSpec as P

FREQUENCY = 2.5
BROADENING = 0.4


def response(energy_gaps):
    shifted = FREQUENCY - energy_gaps
    return shifted / (shifted * shifted + BROADENING * BROADENING)


def contract_grid(left, right):
    return lax.dot_general(
        left, right, (((1,), (1,)), ((), ())), preferred_element_type=jnp.float32
    )


def contract_rows(left, right):
    return lax.dot_general(
        left, right, (((0,), (0,)), ((), ())), preferred_element_type=jnp.float32
    )


def shards(occupied, virtual, occ_energy, virt_energy, partner, coulomb, basis):
    local_k, occ_count, grid_count = occupied.shape
    group_count = virtual.shape[1]
    aux_count = basis.shape[0]
    transfers = partner.shape[0]
    ka_size = lax.axis_size("ka")
    band_size = lax.axis_size("band")
    total_k = local_k * ka_size
    virt_count = group_count * band_size
    slice_width = group_count * grid_count // ka_size
    gram_scale = 1.0 / math.sqrt(total_k * occ_count * virt_count * aux_count)
    occ_scale = 1.0 / math.sqrt(transfers * virt_count)
    own_k = lax.axis_index("ka") * local_k + jnp.arange(local_k, dtype=jnp.int32)

    def regroup(slices):
        picked = jnp.stack(
            [jnp.take(slices, partner[transfer], axis=0) for transfer in range(transfers)]
        )
        return lax.all_to_all(picked, "ka", split_axis=1, concat_axis=2, tiled=True)

    routed = regroup(
        lax.all_to_all(
            virtual.reshape(local_k, ka_size, slice_width),
            "ka",
            split_axis=1,
            concat_axis=0,
            tiled=True,
        )
    )
    partner_virt = routed.reshape(transfers, local_k, group_count, grid_count)
    partner_energy = jnp.take(virt_energy, jnp.take(partner, own_k, axis=1), axis=0)
    occ_total = jnp.zeros((local_k, occ_count, grid_count), jnp.float32)
    virt_terms = []
    for transfer in range(transfers):
        pair_rows = (occupied[:, :, None, :] * partner_virt[transfer][:, None, :, :]).reshape(
            -1, grid_count
        )
        project_coeffs = contract_grid(pair_rows, basis).astype(jnp.bfloat16)
        energy_gaps = partner_energy[transfer][:, None, :] - occ_energy[:, :, None]
        weights = response(energy_gaps).reshape(-1, 1)
        weighted = (project_coeffs.astype(jnp.float32) * weights).astype(jnp.bfloat16)
        gram_block = contract_rows(weighted, project_coeffs)
        coul_rows = coulomb[transfer : transfer + 1]
        totals = lax.psum(gram_block[None], ("ka", "band"))
        screen_block = (coul_rows[:, :, None] * totals * coul_rows[:, None, :] * gram_scale).astype(
            jnp.bfloat16
        )[0]
        screened = jnp.dot(project_coeffs, screen_block, preferred_element_type=jnp.float32).astype(
            jnp.bfloat16
        )
        grid_field = jnp.dot(screened, basis, preferred_element_type=jnp.float32).astype(
            jnp.bfloat16
        )
        grid_field = grid_field.reshape(local_k, occ_count, group_count, grid_count).astype(
            jnp.float32
        )
        occ_term = jnp.sum(
            grid_field * partner_virt[transfer][:, None, :, :].astype(jnp.float32), axis=2
        )
        virt_term = jnp.sum(
            grid_field * occupied[:, :, None, :].astype(jnp.float32), axis=1
        ).astype(jnp.bfloat16)
        occ_term, virt_term = (occ_term, virt_term)
        occ_total = occ_total + occ_term
        virt_terms.append(virt_term)
    stacked = jnp.stack(virt_terms).reshape(transfers, local_k, ka_size, slice_width)
    slices = lax.all_to_all(stacked, "ka", split_axis=2, concat_axis=1, tiled=True)
    returned = jnp.take(slices[0], partner[0], axis=0).astype(jnp.float32)
    transfer = 1
    returned = returned + jnp.take(slices[transfer], partner[transfer], axis=0).astype(jnp.float32)
    home_rows = lax.all_to_all(
        returned.astype(jnp.bfloat16), "ka", split_axis=0, concat_axis=1, tiled=True
    )
    virt_update = home_rows.reshape(local_k, group_count, grid_count)
    occ_share = lax.psum_scatter(
        occ_total.astype(jnp.bfloat16), "band", scatter_dimension=2, tiled=True
    ).astype(jnp.float32)
    return ((occ_share * occ_scale).astype(jnp.bfloat16), virt_update)


def solution(mesh):
    in_specs = (
        P("ka", None, None),
        P("ka", "band", None),
        P("ka", None),
        P(None, "band"),
        P(),
        P(),
        P(),
    )
    out_specs = (P("ka", None, "band"), P("ka", "band", None))
    return jax.shard_map(shards, mesh=mesh, in_specs=in_specs, out_specs=out_specs, check_vma=False)
```

profile of v0, /device:TPU:0, one launch (start us, length us, event | category | flops | bytes accessed | tf_op | source)
XLA Modules:
  0.0 310.9 jit_solution(7381379015960021521)
XLA Ops:
  7.2 1.5 reshape.231
  8.6 1.3 copy.50
  10.0 7.3 %all-to-all-start = ((bf16[2,8,16384]{2,0,1:T(2,128)(2,1)}), bf16[2,8,16384]{2,0,1:T(2,128)(2,1)S(1)}, u32[]{:S(2)}, u32[]{:S(2)}) async-start(bf16[2,8,16384]{2,0,1:T(2,128)(2,1)} %copy.50), calls=%async_computation | async-start | bytes 1048576 | tf_op jit(solution)/shard_map/all_to_all | solution.py:50
  18.1 13.7 %all-to-all-done = bf16[2,8,16384]{2,0,1:T(2,128)(2,1)S(1)} async-done(((bf16[2,8,16384]{2,0,1:T(2,128)(2,1)}), bf16[2,8,16384]{2,0,1:T(2,128)(2,1)S(1)}, u32[]{:S(2)}, u32[]{:S(2)}) %all-to-all-start) | async-done | bytes 524320 | tf_op jit(solution)/shard_map/all_to_all | solution.py:50
  34.0 2.0 copy.51
  36.1 3.6 %all-to-all-start.1 = ((bf16[2,16,1,16384]{3,0,2,1:T(2,128)(2,1)}), bf16[2,16,1,16384]{3,0,2,1:T(2,128)(2,1)S(1)}, u32[]{:S(2)}, u32[]{:S(2)}) async-start(bf16[2,16,1,16384]{3,0,2,1:T(2,128)(2,1)} %copy.51), calls=%async_computation.1 | async-start | bytes 2097152 | tf_op jit(solution)/shard_map/all_to_all | solution.py:47
  41.7 24.0 %all-to-all-done.1 = bf16[2,16,1,16384]{3,0,2,1:T(2,128)(2,1)S(1)} async-done(((bf16[2,16,1,16384]{3,0,2,1:T(2,128)(2,1)}), bf16[2,16,1,16384]{3,0,2,1:T(2,128)(2,1)S(1)}, u32[]{:S(2)}, u32[]{:S(2)}) %all-to-all-start.1) | async-done | bytes 1048608 | tf_op jit(solution)/shard_map/all_to_all | solution.py:47
  65.7 1.7 fusion.32
  70.1 1.4 copy-done.1
  71.6 2.4 convolution_convert_fusion.3
  73.9 2.4 convolution_convert_fusion.5
  76.3 1.6 convolution_bitcast_fusion
  77.9 1.6 convolution_bitcast_fusion.1
  80.7 132.6 %all-reduce.3.cloned.1.call-done = (f32[1,512,512]{2,1,0:T(8,128)}, f32[1,512,512]{2,1,0:T(8,128)}) async-done(((f32[1,512,512]{2,1,0:T(8,128)}, f32[1,512,512]{2,1,0:T(8,128)}), (f32[1,512,512]{2,1,0:T(8,128)}, f32[1,512,512]{2,1,0:T(8,128)})) %all-reduce.3.cloned.1.call-update) | async-done | bytes 2097168 | tf_op jit(solution)/shard_map/psum | solution.py:72
  213.3 7.6 %fusion.2 = (f32[2,8,4096]{2,1,0:T(8,128)S(1)}, bf16[512,4096]{1,0:T(8,128)(2,1)}) fusion(f32[2,32,4096]{2,1,0:T(8,128)} %convert_element_type.132, bf16[512,4096]{1,0:T(8,128)(2,1)} %param.15, bf16[512,512]{1,0:T(8,128)(2,1)S(1)} %convolution_convert_fusion.3, f32[1,512,512]{2,1,0:T(8,128)} %get-tuple-element.6, f32[512]{0:T(512)S(1)} %bitcast.114), kind=kOutput, calls=%fused_computation.12 | convolution fusion | flops 2425552896 | bytes 11274240 | tf_op jit(solution)/shard_map/dot_general | solution.py:79
  220.9 7.6 %fusion = (f32[2,8,4096]{2,1,0:T(8,128)S(1)}, bf16[512,4096]{1,0:T(8,128)(2,1)}) fusion(f32[2,32,4096]{2,1,0:T(8,128)S(1)} %convert_element_type.123, bf16[512,4096]{1,0:T(8,128)(2,1)} %param.15, bf16[512,512]{1,0:T(8,128)(2,1)S(1)} %convolution_convert_fusion.5, f32[1,512,512]{2,1,0:T(8,128)} %get-tuple-element.5, f32[512]{0:T(512)S(1)} %bitcast.113), kind=kOutput, calls=%fused_computation.10 | convolution fusion | flops 2425552896 | bytes 11274240 | tf_op jit(solution)/shard_map/dot_general | solution.py:79
  228.5 4.6 %fusion.1 = (bf16[2,32,4096]{2,1,0:T(8,128)(2,1)S(1)}, bf16[2,32,4096]{2,1,0:T(8,128)(2,1)S(1)}) fusion(bf16[2,8,32,4096]{3,2,1,0:T(8,128)(2,1)} %bitcast.106, f32[2,8,4096]{2,1,0:T(8,128)S(1)} %convert_element_type.136, bf16[2,8,32,4096]{3,2,1,0:T(8,128)(2,1)} %bitcast.105), kind=kLoop, calls=%fused_computation.11 | loop fusion | flops 12058624 | bytes 9699328 | tf_op jit(solution)/shard_map/reduce_sum | solution.py:88
  235.2 28.1 %all_to_all.63 = bf16[2,2,8,16384]{3,1,0,2:T(2,128)(2,1)S(1)} all-to-all(bf16[2,2,8,16384]{3,1,0,2:T(2,128)(2,1)S(1)} %copy.57), channel_id=1, replica_groups=mesh['ka'=8,'band'=4] {'ka'}, dimensions={2} | all-to-all | bytes 2097152 | tf_op jit(solution)/shard_map/all_to_all | solution.py:95
  268.0 1.1 reshape.317
  269.2 3.6 %all-to-all-start.3 = ((bf16[8,2,16384]{2,1,0:T(2,128)(2,1)}), bf16[8,2,16384]{2,1,0:T(2,128)(2,1)S(1)}, u32[]{:S(2)}, u32[]{:S(2)}) async-start(bf16[8,2,16384]{2,1,0:T(2,128)(2,1)} %reshape.317), calls=%async_computation.4 | async-start | bytes 1048576 | tf_op jit(solution)/shard_map/all_to_all | solution.py:99
  273.5 23.5 %reduce-scatter.2.cloned.1.call-done = bf16[2,8,1024]{2,1,0:T(8,128)(2,1)} async-done(((bf16[2,8,4096]{2,1,0:T(8,128)(2,1)}), bf16[2,8,1024]{2,1,0:T(8,128)(2,1)}) %reduce-scatter.2.cloned.1.call-update) | async-done | bytes 32784 | tf_op jit(solution)/shard_map/reduce_scatter | solution.py:103
  297.0 1.4 multiply_convert_fusion.6
  298.9 3.3 %reduce = bf16[16,16384]{1,0:T(8,128)(2,1)S(1)} reduce(bf16[16,1,16384]{2,1,0:T(2,128)(2,1)S(1)} %reshape.318, bf16[]{:T(256)} %constant.60), dimensions={1}, to_apply=%all_to_all.56.reduce_sub_computation | reduce | bytes 1048578 | tf_op jit(solution)/shard_map/all_to_all | solution.py:99
  302.9 1.2 reshape.232
  (68 shorter events, 17.5 us)
Async XLA Ops:
  7.2 33.6 %copy-start = (f32[16,32]{1,0:T(8,128)S(1)}, f32[16,32]{1,0:T(8,128)}, u32[]{:S(2)}) copy-start(f32[16,32]{1,0:T(8,128)} %param.12) | copy-start | bytes 6148
  10.0 21.8 %all-to-all-start = ((bf16[2,8,16384]{2,0,1:T(2,128)(2,1)}), bf16[2,8,16384]{2,0,1:T(2,128)(2,1)S(1)}, u32[]{:S(2)}, u32[]{:S(2)}) async-start(bf16[2,8,16384]{2,0,1:T(2,128)(2,1)} %copy.50), calls=%async_computation | async-start | bytes 1048576 | tf_op jit(solution)/shard_map/all_to_all | solution.py:50
  33.7 6.0 %copy-start.3 = (s32[2,16]{1,0:T(2,128)S(1)}, s32[2,16]{1,0:T(2,128)}, u32[]{:S(2)}) copy-start(s32[2,16]{1,0:T(2,128)} %param.13) | copy-start | bytes 388
  33.7 7.7 %copy-start.5 = (f32[2,8]{1,0:T(2,128)S(1)}, f32[2,8]{1,0:T(2,128)}, u32[]{:S(2)}) copy-start(f32[2,8]{1,0:T(2,128)} %param.11) | copy-start | bytes 196
  36.1 29.6 %all-to-all-start.1 = ((bf16[2,16,1,16384]{3,0,2,1:T(2,128)(2,1)}), bf16[2,16,1,16384]{3,0,2,1:T(2,128)(2,1)S(1)}, u32[]{:S(2)}, u32[]{:S(2)}) async-start(bf16[2,16,1,16384]{3,0,2,1:T(2,128)(2,1)} %copy.51), calls=%async_computation.1 | async-start | bytes 2097152 | tf_op jit(solution)/shard_map/all_to_all | solution.py:47
  39.7 173.6 %all-reduce.3.cloned.1.call-start = ((), (), s32[]{:S(2)}) async-start(), calls=%async_computation.6 | async-start | bytes 4194304 | tf_op jit(solution)/shard_map/psum | solution.py:72
  65.7 3.7 %copy-start.2 = (bf16[2,8,4096]{2,1,0:T(8,128)(2,1)S(1)}, bf16[2,8,4096]{2,1,0:T(8,128)(2,1)}, u32[]{:S(2)}) copy-start(bf16[2,8,4096]{2,1,0:T(8,128)(2,1)} %param.9) | copy-start | bytes 393220
  69.4 2.2 copy-start.1
  76.3 3.2 %copy-start.4 = (f32[2,512]{1,0:T(2,128)S(1)}, f32[2,512]{1,0:T(2,128)}, u32[]{:S(2)}) copy-start(f32[2,512]{1,0:T(2,128)} %param.14) | copy-start | bytes 12292
  269.2 29.2 %all-to-all-start.3 = ((bf16[8,2,16384]{2,1,0:T(2,128)(2,1)}), bf16[8,2,16384]{2,1,0:T(2,128)(2,1)S(1)}, u32[]{:S(2)}, u32[]{:S(2)}) async-start(bf16[8,2,16384]{2,1,0:T(2,128)(2,1)} %reshape.317), calls=%async_computation.4 | async-start | bytes 1048576 | tf_op jit(solution)/shard_map/all_to_all | solution.py:99
  272.8 24.2 %reduce-scatter.2.cloned.1.call-start = ((), (), s32[]{:S(2)}) async-start(), calls=%async_computation.5 | async-start | bytes 163840 | tf_op jit(solution)/shard_map/reduce_scatter | solution.py:103
Sparse Core Ops, SparseCore 0:
  79.6 133.6 all-reduce.2
  276.0 20.9 reduce-scatter.1
where the time goes:
time: 311 us
  waiting for transfers between devices  194 us (62%)
  blocking collectives  28.1 us (9%)
  matrix products  23 us (7%)
  local copies, waits for them, and re-layouts  22.5 us (7%)
  starting transfers between devices  14.6 us (5%)
  other arithmetic  14.6 us (5%)
  between operations  14.3 us (5%)
    psum x1, waiting for transfers between devices, shards(): totals = lax.psum(gram_block[None], ('ka', 'band'))  133 us
    all_to_all x1, blocking collectives, shards(): lax.all_to_all(stacked, 'ka', split_axis=2, concat_axis=1, tiled=True)  28.1 us
    all_to_all x1, waiting for transfers between devices, regroup(): return lax.all_to_all(picked, 'ka', split_axis=1, concat_axis=2, tiled=True)  24 us
    reduce_scatter x1, waiting for transfers between devices, shards(): lax.psum_scatter(occ_total.astype(jnp.bfloat16), 'band', scatter_dimensio...  23.5 us
    dot_general x2, matrix products, shards(): jnp.dot(screened, basis, preferred_element_type=jnp.float32)  15.2 us
    all_to_all x1, waiting for transfers between devices, shards(): lax.all_to_all(virtual.reshape(local_k, ka_size, slice_width), 'ka', spli...  13.7 us
    all_to_all x1, starting transfers between devices, shards(): lax.all_to_all(virtual.reshape(local_k, ka_size, slice_width), 'ka', spli...  7.28 us
  transfers between devices with their start and end apart: 5, of which 4 were waited for; matrix products, arithmetic and copies ran while one was open for 2% of the time, Pallas kernels for 0%

commit v1 on v0

v1 whole, which is shorter than its diff:
```python
import math

import jax
import jax.numpy as jnp
from jax import lax
from jax.sharding import PartitionSpec as P

FREQUENCY = 2.5
BROADENING = 0.4
LANES = 128
BF16 = jnp.bfloat16
F32 = jnp.float32


def response(energy_gaps):
    shifted = FREQUENCY - energy_gaps
    return shifted / (shifted * shifted + BROADENING * BROADENING)


def pick(stack, index):
    return lax.dynamic_index_in_dim(stack, index, 0, keepdims=False)


class Hypercube:
    def __init__(self):
        self.ka = lax.axis_size("ka")
        self.band = lax.axis_size("band")
        self.count = self.ka * self.band
        assert self.band == 4 and self.ka >= 2 and self.ka & (self.ka - 1) == 0
        self.index = lax.axis_index("ka") * self.band + lax.axis_index("band")
        self.core, self.y, self.x = 1, 2, 4
        rest = [bit for bit in (1 << n for n in range(3, 31)) if bit < self.count]
        self.groups = [rest[n : n + 2] for n in range(0, len(rest), 2)]

    def bit(self, mask):
        return (self.index // mask) % 2

    def swap(self, value, mask):
        return lax.ppermute(
            value, ("ka", "band"), [(device, device ^ mask) for device in range(self.count)]
        )


def masks_of(bits):
    return [sum(bit for n, bit in enumerate(bits) if (d >> n) & 1) for d in range(1, 1 << len(bits))]


def sum_scatter(cube, parts, bits):
    me = sum(cube.bit(bit) << n for n, bit in enumerate(bits))
    total = pick(parts, me).astype(F32)
    arrived = [
        cube.swap(pick(parts, jnp.bitwise_xor(me, d + 1)), mask)
        for d, mask in enumerate(masks_of(bits))
    ]
    for term in arrived:
        total = total + term.astype(F32)
    return total


def gather_differences(cube, value, bits):
    return jnp.stack([value] + [cube.swap(value, mask) for mask in masks_of(bits)])


def gather_parts(cube, value, bits):
    me = sum(cube.bit(bit) << n for n, bit in enumerate(bits))
    differences = gather_differences(cube, value, bits)
    return jnp.stack(
        [pick(differences, jnp.bitwise_xor(me, d)) for d in range(1 << len(bits))]
    )


def blocks_of(aux_count):
    count = aux_count // LANES
    return [(row, column) for row in range(count) for column in range(row, count)]


def pack_upper(gram):
    return jnp.stack(
        [
            gram[row * LANES : (row + 1) * LANES, column * LANES : (column + 1) * LANES]
            for row, column in blocks_of(gram.shape[0])
        ]
    )


def unpack_upper(packed, aux_count):
    count = aux_count // LANES
    where = {pair: n for n, pair in enumerate(blocks_of(aux_count))}
    return jnp.concatenate(
        [
            jnp.concatenate(
                [
                    packed[where[row, column]]
                    if row <= column
                    else packed[where[column, row]].T
                    for column in range(count)
                ],
                axis=1,
            )
            for row in range(count)
        ],
        axis=0,
    )


def split_float(value):
    high = lax.reduce_precision(value, 8, 7)
    middle = lax.reduce_precision(value - high, 8, 7)
    low = value - high - middle
    return high.astype(BF16), middle.astype(BF16), low.astype(BF16)


def fetch_partners(cube, occupied, occ_energy, partner):
    local_k, occ_count, grid_count = occupied.shape
    transfers = partner.shape[0]
    width = grid_count // cube.band
    ka = lax.axis_index("ka")
    quarter = lax.dynamic_slice_in_dim(occupied, lax.axis_index("band") * width, width, axis=2)
    pieces = jnp.stack(split_float(occ_energy), axis=2)
    payload = jnp.concatenate(
        [quarter, jnp.pad(pieces, ((0, 0), (0, 0), (0, LANES - pieces.shape[2])))], axis=2
    )
    gathered = payload[None]
    for bits in cube.groups:
        gathered = gather_differences(cube, gathered, bits).reshape((-1,) + payload.shape)
    gathered = gathered.reshape((-1,) + payload.shape[1:])
    side, upper = ka % 2, ka // 2

    def wanted(target_side):
        target = (upper * 2 + target_side) * local_k
        sources = lax.dynamic_slice_in_dim(partner, target, local_k, axis=1)
        devices = sources // local_k
        slots = jnp.bitwise_xor(devices // 2, upper) * local_k + sources % local_k
        rows = [
            pick(gathered, slots[transfer, k])
            for transfer in range(transfers)
            for k in range(local_k)
        ]
        return jnp.stack(rows), devices % 2

    mine, sides = wanted(side)
    theirs, _ = wanted(1 - side)
    received = cube.swap(theirs, cube.x)
    chosen = jnp.where((sides == side).reshape(-1, 1, 1), mine, received)
    energy = chosen[:, :, width : width + 3].astype(F32)
    energy = (energy[:, :, 0] + energy[:, :, 1]) + energy[:, :, 2]
    part = chosen[:, :, :width]
    for mask in (cube.core, cube.y):
        other = cube.swap(part, mask)
        first = cube.bit(mask) == 0
        part = jnp.concatenate(
            [jnp.where(first, part, other), jnp.where(first, other, part)], axis=2
        )
    shape = (transfers, local_k, occ_count)
    return part.reshape(shape + (grid_count,)), energy.reshape(shape)


def reduce_screen(cube, packed, coulomb, scale):
    transfers, aux_count = coulomb.shape
    core = cube.bit(cube.core)
    own = sum_scatter(cube, packed, [cube.core]).astype(BF16)
    rows = own.shape[0] * LANES
    piece = sum_scatter(cube, own.reshape(4, rows // 4, LANES), [cube.y, cube.x])
    for bits in cube.groups:
        piece = piece.astype(BF16)
        arrived = [cube.swap(piece, mask) for mask in masks_of(bits)]
        piece = piece.astype(F32)
        for term in arrived:
            piece = piece + term.astype(F32)
    factors = pick(coulomb, core)
    scales = pack_upper(factors[:, None] * factors[None, :] * scale).reshape(4, rows // 4, LANES)
    me = cube.bit(cube.y) + 2 * cube.bit(cube.x)
    piece = (piece * pick(scales, me)).astype(BF16)
    own = gather_parts(cube, piece, [cube.y, cube.x])
    both = gather_parts(cube, own, [cube.core])
    return both.reshape(packed.shape)


def return_occupied(cube, terms, partner):
    transfers, local_k, occ_count, grid_count = terms.shape
    ka = lax.axis_index("ka")
    part = terms.reshape(transfers * local_k, occ_count, grid_count).astype(BF16)
    for mask in (cube.y, cube.core):
        width = part.shape[2] // 2
        bit = cube.bit(mask)
        keep = lax.dynamic_slice_in_dim(part, bit * width, width, axis=2)
        give = lax.dynamic_slice_in_dim(part, (1 - bit) * width, width, axis=2)
        part = (keep.astype(F32) + cube.swap(give, mask).astype(F32)).astype(BF16)
    side, upper = ka % 2, ka // 2
    received = cube.swap(part, cube.x)
    both = jnp.stack([part, received]).reshape((2 * transfers * local_k,) + part.shape[1:])
    devices = jnp.stack([ka, jnp.bitwise_xor(ka, 1)])
    own_k = devices[:, None] * local_k + jnp.arange(local_k, dtype=jnp.int32)[None]
    targets = jnp.take(partner, own_k, axis=1).transpose(1, 0, 2).reshape(-1)

    def placed(uppers):
        wanted_k = ((uppers * 2 + side) * local_k)[:, None] + jnp.arange(local_k, dtype=jnp.int32)
        hits = targets[None, None, :] == wanted_k[:, :, None]
        return jnp.sum(
            jnp.where(hits[:, :, :, None, None], both[None, None].astype(F32), 0.0), axis=2
        )

    spans = 1
    for bits in cube.groups:
        spans *= 1 << len(bits)
    differences = jnp.arange(spans, dtype=jnp.int32)
    value = placed(jnp.bitwise_xor(differences, upper))
    for bits in reversed(cube.groups):
        size = 1 << len(bits)
        value = value.reshape((size, -1) + value.shape[1:])
        total = value[0]
        arrived = [
            cube.swap(value[d + 1].astype(BF16), mask) for d, mask in enumerate(masks_of(bits))
        ]
        for term in arrived:
            total = total + term.astype(F32)
        value = total
    return value[0]


def contract_grid(left, right):
    return lax.dot_general(left, right, (((1,), (1,)), ((), ())), preferred_element_type=F32)


def contract_rows(left, right):
    return lax.dot_general(left, right, (((0,), (0,)), ((), ())), preferred_element_type=F32)


def shards(occupied, virtual, occ_energy, virt_energy, partner, coulomb, basis):
    local_k, occ_count, grid_count = occupied.shape
    group_count = virtual.shape[1]
    aux_count = basis.shape[0]
    transfers = partner.shape[0]
    cube = Hypercube()
    total_k = local_k * cube.ka
    virt_count = group_count * cube.band
    gram_scale = 1.0 / math.sqrt(total_k * occ_count * virt_count * aux_count)
    occ_scale = 1.0 / math.sqrt(transfers * virt_count)
    ka = lax.axis_index("ka")

    partner_occ, partner_energy = fetch_partners(cube, occupied, occ_energy, partner)
    own_energy = lax.dynamic_slice_in_dim(virt_energy, ka * local_k, local_k, axis=0)
    coeffs, grams = [], []
    for transfer in range(transfers):
        pair_rows = partner_occ[transfer][:, :, None, :] * virtual[:, None, :, :]
        pair_coeffs = contract_grid(pair_rows.reshape(-1, grid_count), basis).astype(BF16)
        gaps = own_energy[:, None, :] - partner_energy[transfer][:, :, None]
        weights = response(gaps).reshape(-1, 1)
        weighted = (pair_coeffs.astype(F32) * weights).astype(BF16)
        grams.append(pack_upper(contract_rows(weighted, pair_coeffs)).astype(BF16))
        coeffs.append(pair_coeffs)
    screens = reduce_screen(cube, jnp.stack(grams), coulomb, gram_scale)
    virt_total = jnp.zeros((local_k, group_count, grid_count), F32)
    occ_terms = []
    for transfer in range(transfers):
        screen = unpack_upper(screens[transfer], aux_count)
        screened = jnp.dot(coeffs[transfer], screen, preferred_element_type=F32).astype(BF16)
        field = jnp.dot(screened, basis, preferred_element_type=F32).astype(BF16)
        field = field.reshape(local_k, occ_count, group_count, grid_count).astype(F32)
        occ_terms.append(jnp.sum(field * virtual[:, None].astype(F32), axis=2))
        virt_term = jnp.sum(field * partner_occ[transfer][:, :, None, :].astype(F32), axis=1)
        virt_total = virt_total + virt_term.astype(BF16).astype(F32)
    occ_total = return_occupied(cube, jnp.stack(occ_terms), partner)
    return ((occ_total * occ_scale).astype(BF16), virt_total.astype(BF16))


def solution(mesh):
    in_specs = (
        P("ka", None, None),
        P("ka", "band", None),
        P("ka", None),
        P(None, "band"),
        P(),
        P(),
        P(),
    )
    out_specs = (P("ka", None, "band"), P("ka", "band", None))
    return jax.shard_map(shards, mesh=mesh, in_specs=in_specs, out_specs=out_specs, check_vma=False)
```

time: 311 us -> 125 us (0.40)
  waiting for transfers between devices: 194 us -> 34 us
  blocking collectives: 28.1 us -> 0 us
  starting transfers between devices: 14.6 us -> 26 us
  local copies, waits for them, and re-layouts: 22.5 us -> 13.4 us
    psum x1 -> x0, waiting for transfers between devices: 133 us -> none  [shards(): totals = lax.psum(gram_block[None], ('ka', 'band'))]
    all_to_all x3 -> x0, waiting for transfers between devices: 37.6 us -> none  [the longest x1 24 us: regroup(): return lax.all_to_all(picked, 'ka', split_axis=1, concat_axis=2, tiled=True)]
    ppermute x0 -> x23, waiting for transfers between devices: none -> 34 us  [swap(): lax.ppermute(value, ('ka', 'band'), [(device, device ^ mask) for device i...]
    all_to_all x1 -> x0, blocking collectives: 28.1 us -> none  [shards(): lax.all_to_all(stacked, 'ka', split_axis=2, concat_axis=1, tiled=True)]
    ppermute x0 -> x23, starting transfers between devices: none -> 26 us  [swap(): lax.ppermute(value, ('ka', 'band'), [(device, device ^ mask) for device i...]
    reduce_scatter x1 -> x0, waiting for transfers between devices: 23.5 us -> none  [shards(): lax.psum_scatter(occ_total.astype(jnp.bfloat16), 'band', scatter_dimensio...]
    all_to_all x3 -> x0, starting transfers between devices: 14.5 us -> none  [the longest x1 7.28 us: shards(): lax.all_to_all(virtual.reshape(local_k, ka_size, slice_width), 'ka', spli...]
    unnamed x15 -> x47, local copies, waits for them, and re-layouts: 3.21 us -> 8.34 us
  transfers between devices with their start and end apart: 5 -> 23, of which waited for: 4 -> 16; matrix products, arithmetic and copies ran while one was open for 2% -> 13% of each run, Pallas kernels for 0% -> 0%
where the time goes in v1:
time: 125 us; the launch traced here: 124 us
  waiting for transfers between devices  34 us (27%)
  starting transfers between devices  26 us (21%)
  matrix products  20.6 us (16%)
  between operations  16.4 us (13%)
  local copies, waits for them, and re-layouts  13.4 us (11%)
  other arithmetic  13.4 us (11%)
    ppermute x23, waiting for transfers between devices, swap(): lax.ppermute(value, ('ka', 'band'), [(device, device ^ mask) for device i...  34 us
    ppermute x23, starting transfers between devices, swap(): lax.ppermute(value, ('ka', 'band'), [(device, device ^ mask) for device i...  26 us
    dot_general x2, matrix products, shards(): field = jnp.dot(screened, basis, preferred_element_type=F32).astype(BF16)  14.8 us
    unnamed x47, local copies, waits for them, and re-layouts  8.34 us
    dot_general x2, matrix products, contract_grid(): lax.dot_general(left, right, (((1,), (1,)), ((), ())), preferred_element_...  4.71 us
    reduce_sum x2, other arithmetic, shards(): jnp.sum(field * partner_occ[transfer][:, :, None, :].astype(F32), axis=1)  3.91 us
  transfers between devices with their start and end apart: 23, of which 16 were waited for; matrix products, arithmetic and copies ran while one was open for 13% of the time, Pallas kernels for 0%

profile of v1, /device:TPU:0, one launch (start us, length us, event | category | flops | bytes accessed | tf_op | source)
XLA Modules:
  0.0 124.0 jit_solution(15407194070739448382)
XLA Ops:
  1.6 5.1 %collective-permute-start.2 = (bf16[1,2,8,1152]{3,2,1,0:T(8,128)(2,1)S(1)}, bf16[1,2,8,1152]{3,2,1,0:T(8,128)(2,1)S(1)}, u32[]{:S(2)}, u32[]{:S(2)}) collective-permute-start(bf16[1,2,8,1152]{3,2,1,0:T(8,128)(2,1)S(1)} %get-tuple-element.71), channel_id=1, source_target_pairs={{0,24},{1,25},{2,26},{3,27},{4,28},{5,29},{6,30},{7,31},{8,16},{9,... | collective-permute-start | bytes 110600 | tf_op jit(solution)/shard_map/ppermute | solution.py:39
  32.3 1.7 %collective-permute-start.3 = (bf16[4,8,1152]{2,1,0:T(8,128)(2,1)S(1)}, bf16[4,8,1152]{2,1,0:T(8,128)(2,1)S(1)}, u32[]{:S(2)}, u32[]{:S(2)}) collective-permute-start(bf16[4,8,1152]{2,1,0:T(8,128)(2,1)S(1)} %pad_maximum_fusion.9), channel_id=1, source_target_pairs={{0,4},{1,5},{2,6},{3,7},{4,0},{5,1},{6,2},{7,3},{8,12},{9,13},{10,... | collective-permute-start | bytes 221192 | tf_op jit(solution)/shard_map/ppermute | solution.py:39
  34.1 2.6 %collective-permute-done.3 = bf16[4,8,1152]{2,1,0:T(8,128)(2,1)S(1)} collective-permute-done((bf16[4,8,1152]{2,1,0:T(8,128)(2,1)S(1)}, bf16[4,8,1152]{2,1,0:T(8,128)(2,1)S(1)}, u32[]{:S(2)}, u32[]{:S(2)}) %collective-permute-start.3) | collective-permute-done | bytes 73760 | tf_op jit(solution)/shard_map/ppermute | solution.py:39
  38.5 1.7 %collective-permute-start.5 = (bf16[4,8,2048]{2,1,0:T(8,128)(2,1)S(1)}, bf16[4,8,2048]{2,1,0:T(8,128)(2,1)S(1)}, u32[]{:S(2)}, u32[]{:S(2)}) collective-permute-start(bf16[4,8,2048]{2,1,0:T(8,128)(2,1)S(1)} %pad_maximum_fusion.5), channel_id=1, source_target_pairs={{0,2},{1,3},{2,0},{3,1},{4,6},{5,7},{6,4},{7,5},{8,10},{9,11},{10,... | collective-permute-start | bytes 393224 | tf_op jit(solution)/shard_map/ppermute | solution.py:39
  40.2 3.9 %collective-permute-done.5 = bf16[4,8,2048]{2,1,0:T(8,128)(2,1)S(1)} collective-permute-done((bf16[4,8,2048]{2,1,0:T(8,128)(2,1)S(1)}, bf16[4,8,2048]{2,1,0:T(8,128)(2,1)S(1)}, u32[]{:S(2)}, u32[]{:S(2)}) %collective-permute-start.5) | collective-permute-done | bytes 131104 | tf_op jit(solution)/shard_map/ppermute | solution.py:39
  46.4 2.4 %convolution_convert_fusion.5 = bf16[512,512]{1,0:T(8,128)(2,1)S(1)} fusion(bf16[512,4096]{1,0:T(8,128)(2,1)S(1)} %bitcast.282, bf16[512,4096]{1,0:T(8,128)(2,1)S(1)} %copy-done.2), kind=kOutput, calls=%fused_computation.17 | convolution fusion | flops 2147745792 | bytes 8912896 | tf_op jit(solution)/shard_map/dot_general | solution.py:222
  48.8 2.4 %convolution_convert_fusion.7 = bf16[512,512]{1,0:T(8,128)(2,1)S(1)} fusion(bf16[512,4096]{1,0:T(8,128)(2,1)S(1)} %bitcast.281, bf16[512,4096]{1,0:T(8,128)(2,1)S(1)} %copy-done.2), kind=kOutput, calls=%fused_computation.19 | convolution fusion | flops 2147745792 | bytes 8912896 | tf_op jit(solution)/shard_map/dot_general | solution.py:222
  56.7 1.7 %collective-permute-start.7 = (bf16[320,128]{1,0:T(8,128)(2,1)S(1)}, bf16[320,128]{1,0:T(8,128)(2,1)S(1)}, u32[]{:S(2)}, u32[]{:S(2)}) collective-permute-start(bf16[320,128]{1,0:T(8,128)(2,1)S(1)} %get-tuple-element.50), channel_id=1, source_target_pairs={{0,2},{1,3},{2,0},{3,1},{4,6},{5,7},{6,4},{7,5},{8,10},{9,11},{10,... | collective-permute-start | bytes 245768 | tf_op jit(solution)/shard_map/ppermute | solution.py:39
  58.4 1.4 %collective-permute-start.9 = (bf16[320,128]{1,0:T(8,128)(2,1)S(1)}, bf16[320,128]{1,0:T(8,128)(2,1)S(1)}, u32[]{:S(2)}, u32[]{:S(2)}) collective-permute-start(bf16[320,128]{1,0:T(8,128)(2,1)S(1)} %get-tuple-element.51), channel_id=1, source_target_pairs={{0,6},{1,7},{2,4},{3,5},{4,2},{5,3},{6,0},{7,1},{8,14},{9,15},{10,... | collective-permute-start | bytes 245768 | tf_op jit(solution)/shard_map/ppermute | solution.py:39
  60.5 1.5 %collective-permute-done.7 = bf16[320,128]{1,0:T(8,128)(2,1)S(1)} collective-permute-done((bf16[320,128]{1,0:T(8,128)(2,1)S(1)}, bf16[320,128]{1,0:T(8,128)(2,1)S(1)}, u32[]{:S(2)}, u32[]{:S(2)}) %collective-permute-start.7) | collective-permute-done | bytes 81952 | tf_op jit(solution)/shard_map/ppermute | solution.py:39
  62.0 2.6 %collective-permute-done.9 = bf16[320,128]{1,0:T(8,128)(2,1)S(1)} collective-permute-done((bf16[320,128]{1,0:T(8,128)(2,1)S(1)}, bf16[320,128]{1,0:T(8,128)(2,1)S(1)}, u32[]{:S(2)}, u32[]{:S(2)}) %collective-permute-start.9) | collective-permute-done | bytes 81952 | tf_op jit(solution)/shard_map/ppermute | solution.py:39
  64.6 3.7 %collective-permute-start.12 = (bf16[320,128]{1,0:T(8,128)(2,1)S(1)}, bf16[320,128]{1,0:T(8,128)(2,1)S(1)}, u32[]{:S(2)}, u32[]{:S(2)}) collective-permute-start(bf16[320,128]{1,0:T(8,128)(2,1)S(1)} %fusion.115), channel_id=1, source_target_pairs={{0,24},{1,25},{2,26},{3,27},{4,28},{5,29},{6,30},{7,31},{8,16},{9,... | collective-permute-start | bytes 245768 | tf_op jit(solution)/shard_map/ppermute | solution.py:39
  69.7 1.6 %collective-permute-done.12 = bf16[320,128]{1,0:T(8,128)(2,1)S(1)} collective-permute-done((bf16[320,128]{1,0:T(8,128)(2,1)S(1)}, bf16[320,128]{1,0:T(8,128)(2,1)S(1)}, u32[]{:S(2)}, u32[]{:S(2)}) %collective-permute-start.12) | collective-permute-done | bytes 81952 | tf_op jit(solution)/shard_map/ppermute | solution.py:39
  71.3 3.3 %collective-permute-done.11 = bf16[320,128]{1,0:T(8,128)(2,1)S(1)} collective-permute-done((bf16[320,128]{1,0:T(8,128)(2,1)S(1)}, bf16[320,128]{1,0:T(8,128)(2,1)S(1)}, u32[]{:S(2)}, u32[]{:S(2)}) %collective-permute-start.11) | collective-permute-done | bytes 81952 | tf_op jit(solution)/shard_map/ppermute | solution.py:39
  75.6 1.9 %collective-permute-start.15 = (bf16[320,128]{1,0:T(8,128)(2,1)S(1)}, bf16[320,128]{1,0:T(8,128)(2,1)S(1)}, u32[]{:S(2)}, u32[]{:S(2)}) collective-permute-start(bf16[320,128]{1,0:T(8,128)(2,1)S(1)} %fusion.116), channel_id=1, source_target_pairs={{0,6},{1,7},{2,4},{3,5},{4,2},{5,3},{6,0},{7,1},{8,14},{9,15},{10,... | collective-permute-start | bytes 245768 | tf_op jit(solution)/shard_map/ppermute | solution.py:39
  79.3 1.9 %collective-permute-done.15 = bf16[320,128]{1,0:T(8,128)(2,1)S(1)} collective-permute-done((bf16[320,128]{1,0:T(8,128)(2,1)S(1)}, bf16[320,128]{1,0:T(8,128)(2,1)S(1)}, u32[]{:S(2)}, u32[]{:S(2)}) %collective-permute-start.15) | collective-permute-done | bytes 81952 | tf_op jit(solution)/shard_map/ppermute | solution.py:39
  83.4 1.5 %collective-permute-done.16 = bf16[4,320,128]{2,1,0:T(8,128)(2,1)S(1)} collective-permute-done((bf16[4,320,128]{2,1,0:T(8,128)(2,1)S(1)}, bf16[4,320,128]{2,1,0:T(8,128)(2,1)S(1)}, u32[]{:S(2)}, u32[]{:S(2)}) %collective-permute-start.16) | collective-permute-done | bytes 327712 | tf_op jit(solution)/shard_map/ppermute | solution.py:39
  87.1 7.1 %convolution_convert_fusion = bf16[512,4096]{1,0:T(8,128)(2,1)} fusion(bf16[512,4096]{1,0:T(8,128)(2,1)} %param.13, bf16[512,512]{1,0:T(8,128)(2,1)} %copy-done.5, bf16[128,128]{1,0:T(8,128)(2,1)S(1)} %get-tuple-element.25, bf16[128,128]{1,0:T(8,128)(2,1)S(1)} %copy.129, bf16[128,128]{1,0:T(8,128)(2,1)S(1)} %bitcast.302, bf16[128,128]{1,0:T(8,128)(2,1)S(1)} %copy.128, ...), kind=kOutput, calls=%fused_computation.9 | convolution fusion | flops 2425094144 | bytes 9437184 | tf_op jit(solution)/shard_map/dot_general | solution.py:258
  94.2 7.7 %fusion = (bf16[2,8,4096]{2,1,0:T(8,128)(2,1)S(1)}, bf16[2,8,4096]{2,1,0:T(8,128)(2,1)S(1)}, bf16[512,4096]{1,0:T(8,128)(2,1)}) fusion(f32[2,32,4096]{2,1,0:T(8,128)S(1)} %convert_element_type.231, bf16[512,4096]{1,0:T(8,128)(2,1)} %convolution_convert_fusion, bf16[512,4096]{1,0:T(8,128)(2,1)} %param.13, bf16[512,512]{1,0:T(8,128)(2,1)S(1)} %convolution_convert_fusion.7, ...), kind=kOutput, calls=%fused_computation.5 | convolution fusion | flops 2437545984 | bytes 14942208 | tf_op jit(solution)/shard_map/dot_general | solution.py:258
  102.6 5.0 %collective-permute-done.17 = bf16[4,8,2048]{2,1,0:T(8,128)(2,1)S(1)} collective-permute-done((bf16[4,8,2048]{2,1,0:T(8,128)(2,1)S(1)}, bf16[4,8,2048]{2,1,0:T(8,128)(2,1)S(1)}, u32[]{:S(2)}, u32[]{:S(2)}) %collective-permute-start.17) | collective-permute-done | bytes 131104 | tf_op jit(solution)/shard_map/ppermute | solution.py:39
  107.7 3.0 %fusion.3 = bf16[2,32,4096]{2,1,0:T(8,128)(2,1)S(1)} fusion(bf16[2,8,32,4096]{3,2,1,0:T(8,128)(2,1)} %bitcast.279, f32[2,8,4096]{2,1,0:T(8,128)S(1)} %get-tuple-element.8), kind=kLoop, calls=%fused_computation.8 | loop fusion | flops 6029312 | bytes 4980736 | tf_op jit(solution)/shard_map/reduce_sum | solution.py:261
  112.7 2.7 %collective-permute-done.19 = bf16[4,8,1024]{2,1,0:T(8,128)(2,1)S(1)} collective-permute-done((bf16[4,8,1024]{2,1,0:T(8,128)(2,1)S(1)}, bf16[4,8,1024]{2,1,0:T(8,128)(2,1)S(1)}, u32[]{:S(2)}, u32[]{:S(2)}) %collective-permute-start.19) | collective-permute-done | bytes 65568 | tf_op jit(solution)/shard_map/ppermute | solution.py:39
  116.7 1.9 %collective-permute-start.22 = (bf16[1,2,8,1024]{3,2,1,0:T(8,128)(2,1)S(1)}, bf16[1,2,8,1024]{3,2,1,0:T(8,128)(2,1)S(1)}, u32[]{:S(2)}, u32[]{:S(2)}) collective-permute-start(bf16[1,2,8,1024]{3,2,1,0:T(8,128)(2,1)S(1)} %get-tuple-element.68), channel_id=1, source_target_pairs={{0,24},{1,25},{2,26},{3,27},{4,28},{5,29},{6,30},{7,31},{8,16},{9,... | collective-permute-start | bytes 98312 | tf_op jit(solution)/shard_map/ppermute | solution.py:39
  120.2 2.2 %collective-permute-done.22 = bf16[1,2,8,1024]{3,2,1,0:T(8,128)(2,1)S(1)} collective-permute-done((bf16[1,2,8,1024]{3,2,1,0:T(8,128)(2,1)S(1)}, bf16[1,2,8,1024]{3,2,1,0:T(8,128)(2,1)S(1)}, u32[]{:S(2)}, u32[]{:S(2)}) %collective-permute-start.22) | collective-permute-done | bytes 32800 | tf_op jit(solution)/shard_map/ppermute | solution.py:39
  (156 shorter events, 37.0 us)
Async XLA Ops:
  0.6 43.5 %copy-start.3 = (bf16[2,32,4096]{2,1,0:T(8,128)(2,1)S(1)}, bf16[2,32,4096]{2,1,0:T(8,128)(2,1)}, u32[]{:S(2)}) copy-start(bf16[2,32,4096]{2,1,0:T(8,128)(2,1)} %param.8) | copy-start | bytes 1572868
  1.6 30.6 %collective-permute-start.2 = (bf16[1,2,8,1152]{3,2,1,0:T(8,128)(2,1)S(1)}, bf16[1,2,8,1152]{3,2,1,0:T(8,128)(2,1)S(1)}, u32[]{:S(2)}, u32[]{:S(2)}) collective-permute-start(bf16[1,2,8,1152]{3,2,1,0:T(8,128)(2,1)S(1)} %get-tuple-element.71), channel_id=1, source_target_pairs={{0,24},{1,25},{2,26},{3,27},{4,28},{5,29},{6,30},{7,31},{8,16},{9,... | collective-permute-start | bytes 110600 | tf_op jit(solution)/shard_map/ppermute | solution.py:39
  6.7 25.5 %collective-permute-start.1 = (bf16[1,2,8,1152]{3,2,1,0:T(8,128)(2,1)S(1)}, bf16[1,2,8,1152]{3,2,1,0:T(8,128)(2,1)S(1)}, u32[]{:S(2)}, u32[]{:S(2)}) collective-permute-start(bf16[1,2,8,1152]{3,2,1,0:T(8,128)(2,1)S(1)} %get-tuple-element.71), channel_id=1, source_target_pairs={{0,16},{1,17},{2,18},{3,19},{4,20},{5,21},{6,22},{7,23},{8,24},{9,... | collective-permute-start | bytes 110600 | tf_op jit(solution)/shard_map/ppermute | solution.py:39
  6.7 25.5 %collective-permute-start = (bf16[1,2,8,1152]{3,2,1,0:T(8,128)(2,1)S(1)}, bf16[1,2,8,1152]{3,2,1,0:T(8,128)(2,1)S(1)}, u32[]{:S(2)}, u32[]{:S(2)}) collective-permute-start(bf16[1,2,8,1152]{3,2,1,0:T(8,128)(2,1)S(1)} %get-tuple-element.71), channel_id=1, source_target_pairs={{0,8},{1,9},{2,10},{3,11},{4,12},{5,13},{6,14},{7,15},{8,0},{9,1},... | collective-permute-start | bytes 110600 | tf_op jit(solution)/shard_map/ppermute | solution.py:39
  32.3 4.4 %collective-permute-start.3 = (bf16[4,8,1152]{2,1,0:T(8,128)(2,1)S(1)}, bf16[4,8,1152]{2,1,0:T(8,128)(2,1)S(1)}, u32[]{:S(2)}, u32[]{:S(2)}) collective-permute-start(bf16[4,8,1152]{2,1,0:T(8,128)(2,1)S(1)} %pad_maximum_fusion.9), channel_id=1, source_target_pairs={{0,4},{1,5},{2,6},{3,7},{4,0},{5,1},{6,2},{7,3},{8,12},{9,13},{10,... | collective-permute-start | bytes 221192 | tf_op jit(solution)/shard_map/ppermute | solution.py:39
  37.2 1.3 %collective-permute-start.4 = (bf16[4,8,1024]{2,1,0:T(8,128)(2,1)S(1)}, bf16[4,8,1024]{2,1,0:T(8,128)(2,1)S(1)}, u32[]{:S(2)}, u32[]{:S(2)}) collective-permute-start(bf16[4,8,1024]{2,1,0:T(8,128)(2,1)S(1)} %slice.343), channel_id=1, source_target_pairs={{0,1},{1,0},{2,3},{3,2},{4,5},{5,4},{6,7},{7,6},{8,9},{9,8},{10,11... | collective-permute-start | bytes 196616 | tf_op jit(solution)/shard_map/ppermute | solution.py:39
  38.5 5.6 %collective-permute-start.5 = (bf16[4,8,2048]{2,1,0:T(8,128)(2,1)S(1)}, bf16[4,8,2048]{2,1,0:T(8,128)(2,1)S(1)}, u32[]{:S(2)}, u32[]{:S(2)}) collective-permute-start(bf16[4,8,2048]{2,1,0:T(8,128)(2,1)S(1)} %pad_maximum_fusion.5), channel_id=1, source_target_pairs={{0,2},{1,3},{2,0},{3,1},{4,6},{5,7},{6,4},{7,5},{8,10},{9,11},{10,... | collective-permute-start | bytes 393224 | tf_op jit(solution)/shard_map/ppermute | solution.py:39
  53.5 2.0 %collective-permute-start.6 = (bf16[10,128,128]{2,1,0:T(8,128)(2,1)}, bf16[10,128,128]{2,1,0:T(8,128)(2,1)}, u32[]{:S(2)}, u32[]{:S(2)}) collective-permute-start(bf16[10,128,128]{2,1,0:T(8,128)(2,1)} %fusion.110), channel_id=1, source_target_pairs={{0,1},{1,0},{2,3},{3,2},{4,5},{5,4},{6,7},{7,6},{8,9},{9,8},{10,11... | collective-permute-start | bytes 983048 | tf_op jit(solution)/shard_map/ppermute | solution.py:39
  56.7 5.3 %collective-permute-start.7 = (bf16[320,128]{1,0:T(8,128)(2,1)S(1)}, bf16[320,128]{1,0:T(8,128)(2,1)S(1)}, u32[]{:S(2)}, u32[]{:S(2)}) collective-permute-start(bf16[320,128]{1,0:T(8,128)(2,1)S(1)} %get-tuple-element.50), channel_id=1, source_target_pairs={{0,2},{1,3},{2,0},{3,1},{4,6},{5,7},{6,4},{7,5},{8,10},{9,11},{10,... | collective-permute-start | bytes 245768 | tf_op jit(solution)/shard_map/ppermute | solution.py:39
  58.4 6.1 %collective-permute-start.9 = (bf16[320,128]{1,0:T(8,128)(2,1)S(1)}, bf16[320,128]{1,0:T(8,128)(2,1)S(1)}, u32[]{:S(2)}, u32[]{:S(2)}) collective-permute-start(bf16[320,128]{1,0:T(8,128)(2,1)S(1)} %get-tuple-element.51), channel_id=1, source_target_pairs={{0,6},{1,7},{2,4},{3,5},{4,2},{5,3},{6,0},{7,1},{8,14},{9,15},{10,... | collective-permute-start | bytes 245768 | tf_op jit(solution)/shard_map/ppermute | solution.py:39
  59.9 4.7 %collective-permute-start.8 = (bf16[320,128]{1,0:T(8,128)(2,1)S(1)}, bf16[320,128]{1,0:T(8,128)(2,1)S(1)}, u32[]{:S(2)}, u32[]{:S(2)}) collective-permute-start(bf16[320,128]{1,0:T(8,128)(2,1)S(1)} %get-tuple-element.52), channel_id=1, source_target_pairs={{0,4},{1,5},{2,6},{3,7},{4,0},{5,1},{6,2},{7,3},{8,12},{9,13},{10,... | collective-permute-start | bytes 245768 | tf_op jit(solution)/shard_map/ppermute | solution.py:39
  64.6 6.7 %collective-permute-start.12 = (bf16[320,128]{1,0:T(8,128)(2,1)S(1)}, bf16[320,128]{1,0:T(8,128)(2,1)S(1)}, u32[]{:S(2)}, u32[]{:S(2)}) collective-permute-start(bf16[320,128]{1,0:T(8,128)(2,1)S(1)} %fusion.115), channel_id=1, source_target_pairs={{0,24},{1,25},{2,26},{3,27},{4,28},{5,29},{6,30},{7,31},{8,16},{9,... | collective-permute-start | bytes 245768 | tf_op jit(solution)/shard_map/ppermute | solution.py:39
  68.3 6.3 %collective-permute-start.11 = (bf16[320,128]{1,0:T(8,128)(2,1)S(1)}, bf16[320,128]{1,0:T(8,128)(2,1)S(1)}, u32[]{:S(2)}, u32[]{:S(2)}) collective-permute-start(bf16[320,128]{1,0:T(8,128)(2,1)S(1)} %fusion.115), channel_id=1, source_target_pairs={{0,16},{1,17},{2,18},{3,19},{4,20},{5,21},{6,22},{7,23},{8,24},{9,... | collective-permute-start | bytes 245768 | tf_op jit(solution)/shard_map/ppermute | solution.py:39
  68.3 6.3 %collective-permute-start.10 = (bf16[320,128]{1,0:T(8,128)(2,1)S(1)}, bf16[320,128]{1,0:T(8,128)(2,1)S(1)}, u32[]{:S(2)}, u32[]{:S(2)}) collective-permute-start(bf16[320,128]{1,0:T(8,128)(2,1)S(1)} %fusion.115), channel_id=1, source_target_pairs={{0,8},{1,9},{2,10},{3,11},{4,12},{5,13},{6,14},{7,15},{8,0},{9,1},... | collective-permute-start | bytes 245768 | tf_op jit(solution)/shard_map/ppermute | solution.py:39
  75.6 5.6 %collective-permute-start.15 = (bf16[320,128]{1,0:T(8,128)(2,1)S(1)}, bf16[320,128]{1,0:T(8,128)(2,1)S(1)}, u32[]{:S(2)}, u32[]{:S(2)}) collective-permute-start(bf16[320,128]{1,0:T(8,128)(2,1)S(1)} %fusion.116), channel_id=1, source_target_pairs={{0,6},{1,7},{2,4},{3,5},{4,2},{5,3},{6,0},{7,1},{8,14},{9,15},{10,... | collective-permute-start | bytes 245768 | tf_op jit(solution)/shard_map/ppermute | solution.py:39
  77.5 4.5 %collective-permute-start.14 = (bf16[320,128]{1,0:T(8,128)(2,1)S(1)}, bf16[320,128]{1,0:T(8,128)(2,1)S(1)}, u32[]{:S(2)}, u32[]{:S(2)}) collective-permute-start(bf16[320,128]{1,0:T(8,128)(2,1)S(1)} %fusion.116), channel_id=1, source_target_pairs={{0,4},{1,5},{2,6},{3,7},{4,0},{5,1},{6,2},{7,3},{8,12},{9,13},{10,... | collective-permute-start | bytes 245768 | tf_op jit(solution)/shard_map/ppermute | solution.py:39
  78.6 4.4 %collective-permute-start.13 = (bf16[320,128]{1,0:T(8,128)(2,1)S(1)}, bf16[320,128]{1,0:T(8,128)(2,1)S(1)}, u32[]{:S(2)}, u32[]{:S(2)}) collective-permute-start(bf16[320,128]{1,0:T(8,128)(2,1)S(1)} %fusion.116), channel_id=1, source_target_pairs={{0,2},{1,3},{2,0},{3,1},{4,6},{5,7},{6,4},{7,5},{8,10},{9,11},{10,... | collective-permute-start | bytes 245768 | tf_op jit(solution)/shard_map/ppermute | solution.py:39
  83.2 1.7 %collective-permute-start.16 = (bf16[4,320,128]{2,1,0:T(8,128)(2,1)S(1)}, bf16[4,320,128]{2,1,0:T(8,128)(2,1)S(1)}, u32[]{:S(2)}, u32[]{:S(2)}) collective-permute-start(bf16[4,320,128]{2,1,0:T(8,128)(2,1)S(1)} %get-tuple-element.44), channel_id=1, source_target_pairs={{0,1},{1,0},{2,3},{3,2},{4,5},{5,4},{6,7},{7,6},{8,9},{9,8},{10,11... | collective-permute-start | bytes 983048 | tf_op jit(solution)/shard_map/ppermute | solution.py:39
  102.0 5.6 %collective-permute-start.17 = (bf16[4,8,2048]{2,1,0:T(8,128)(2,1)S(1)}, bf16[4,8,2048]{2,1,0:T(8,128)(2,1)S(1)}, u32[]{:S(2)}, u32[]{:S(2)}) collective-permute-start(bf16[4,8,2048]{2,1,0:T(8,128)(2,1)S(1)} %constant_dynamic-slice_fusion.1), channel_id=1, source_target_pairs={{0,2},{1,3},{2,0},{3,1},{4,6},{5,7},{6,4},{7,5},{8,10},{9,11},{10,... | collective-permute-start | bytes 393224 | tf_op jit(solution)/shard_map/ppermute | solution.py:39
  107.7 3.1 %collective-permute-start.18 = (bf16[4,8,1024]{2,1,0:T(8,128)(2,1)S(1)}, bf16[4,8,1024]{2,1,0:T(8,128)(2,1)S(1)}, u32[]{:S(2)}, u32[]{:S(2)}) collective-permute-start(bf16[4,8,1024]{2,1,0:T(8,128)(2,1)S(1)} %constant_dynamic-slice_fusion), channel_id=1, source_target_pairs={{0,1},{1,0},{2,3},{3,2},{4,5},{5,4},{6,7},{7,6},{8,9},{9,8},{10,11... | collective-permute-start | bytes 196616 | tf_op jit(solution)/shard_map/ppermute | solution.py:39
  110.8 4.6 %collective-permute-start.19 = (bf16[4,8,1024]{2,1,0:T(8,128)(2,1)S(1)}, bf16[4,8,1024]{2,1,0:T(8,128)(2,1)S(1)}, u32[]{:S(2)}, u32[]{:S(2)}) collective-permute-start(bf16[4,8,1024]{2,1,0:T(8,128)(2,1)S(1)} %add_convert_fusion.2), channel_id=1, source_target_pairs={{0,4},{1,5},{2,6},{3,7},{4,0},{5,1},{6,2},{7,3},{8,12},{9,13},{10,... | collective-permute-start | bytes 196616 | tf_op jit(solution)/shard_map/ppermute | solution.py:39
  115.7 4.5 %collective-permute-start.20 = (bf16[1,2,8,1024]{3,2,1,0:T(8,128)(2,1)S(1)}, bf16[1,2,8,1024]{3,2,1,0:T(8,128)(2,1)S(1)}, u32[]{:S(2)}, u32[]{:S(2)}) collective-permute-start(bf16[1,2,8,1024]{3,2,1,0:T(8,128)(2,1)S(1)} %get-tuple-element.67), channel_id=1, source_target_pairs={{0,8},{1,9},{2,10},{3,11},{4,12},{5,13},{6,14},{7,15},{8,0},{9,1},... | collective-permute-start | bytes 98312 | tf_op jit(solution)/shard_map/ppermute | solution.py:39
  116.7 5.7 %collective-permute-start.22 = (bf16[1,2,8,1024]{3,2,1,0:T(8,128)(2,1)S(1)}, bf16[1,2,8,1024]{3,2,1,0:T(8,128)(2,1)S(1)}, u32[]{:S(2)}, u32[]{:S(2)}) collective-permute-start(bf16[1,2,8,1024]{3,2,1,0:T(8,128)(2,1)S(1)} %get-tuple-element.68), channel_id=1, source_target_pairs={{0,24},{1,25},{2,26},{3,27},{4,28},{5,29},{6,30},{7,31},{8,16},{9,... | collective-permute-start | bytes 98312 | tf_op jit(solution)/shard_map/ppermute | solution.py:39
  118.6 4.8 %collective-permute-start.21 = (bf16[1,2,8,1024]{3,2,1,0:T(8,128)(2,1)S(1)}, bf16[1,2,8,1024]{3,2,1,0:T(8,128)(2,1)S(1)}, u32[]{:S(2)}, u32[]{:S(2)}) collective-permute-start(bf16[1,2,8,1024]{3,2,1,0:T(8,128)(2,1)S(1)} %get-tuple-element.69), channel_id=1, source_target_pairs={{0,16},{1,17},{2,18},{3,19},{4,20},{5,21},{6,22},{7,23},{8,24},{9,... | collective-permute-start | bytes 98312 | tf_op jit(solution)/shard_map/ppermute | solution.py:39
  (5 other events, 26.9 us)

commit v2 on v1

--- a/solution.py
+++ b/solution.py
@@ -1,8 +1,11 @@
+import functools
 import math
 
 import jax
 import jax.numpy as jnp
 from jax import lax
+from jax.experimental import pallas as pl
+from jax.experimental.pallas import tpu as pltpu
 from jax.sharding import PartitionSpec as P
 
 FREQUENCY = 2.5
@@ -74,35 +77,6 @@
     return [(row, column) for row in range(count) for column in range(row, count)]
 
 
-def pack_upper(gram):
-    return jnp.stack(
-        [
-            gram[row * LANES : (row + 1) * LANES, column * LANES : (column + 1) * LANES]
-            for row, column in blocks_of(gram.shape[0])
-        ]
-    )
-
-
-def unpack_upper(packed, aux_count):
-    count = aux_count // LANES
-    where = {pair: n for n, pair in enumerate(blocks_of(aux_count))}
-    return jnp.concatenate(
-        [
-            jnp.concatenate(
-                [
-                    packed[where[row, column]]
-                    if row <= column
-                    else packed[where[column, row]].T
-                    for column in range(count)
-                ],
-                axis=1,
-            )
-            for row in range(count)
-        ],
-        axis=0,
-    )
-
-
 def split_float(value):
     high = lax.reduce_precision(value, 8, 7)
     middle = lax.reduce_precision(value - high, 8, 7)
@@ -112,7 +86,6 @@
 
 def fetch_partners(cube, occupied, occ_energy, partner):
     local_k, occ_count, grid_count = occupied.shape
-    transfers = partner.shape[0]
     width = grid_count // cube.band
     ka = lax.axis_index("ka")
     quarter = lax.dynamic_slice_in_dim(occupied, lax.axis_index("band") * width, width, axis=2)
@@ -125,23 +98,24 @@
         gathered = gather_differences(cube, gathered, bits).reshape((-1,) + payload.shape)
     gathered = gathered.reshape((-1,) + payload.shape[1:])
     side, upper = ka % 2, ka // 2
+    slots = jnp.arange(gathered.shape[0], dtype=jnp.int32)
+    held = (jnp.bitwise_xor(slots // local_k, upper) * 2 + side) * local_k + slots % local_k
+    every_k = jnp.arange(partner.shape[1], dtype=jnp.int32)
 
     def wanted(target_side):
-        target = (upper * 2 + target_side) * local_k
-        sources = lax.dynamic_slice_in_dim(partner, target, local_k, axis=1)
-        devices = sources // local_k
-        slots = jnp.bitwise_xor(devices // 2, upper) * local_k + sources % local_k
-        rows = [
-            pick(gathered, slots[transfer, k])
-            for transfer in range(transfers)
-            for k in range(local_k)
-        ]
-        return jnp.stack(rows), devices % 2
-
-    mine, sides = wanted(side)
-    theirs, _ = wanted(1 - side)
+        targets = (upper * 2 + target_side) * local_k + jnp.arange(local_k, dtype=jnp.int32)
+        at_target = every_k[None, None, :] == targets[None, :, None]
+        sources = jnp.sum(jnp.where(at_target, partner[:, None, :], 0), axis=2).reshape(-1)
+        hits = sources[:, None] == held[None, :]
+        rows = jnp.sum(
+            jnp.where(hits[:, :, None, None], gathered[None].astype(F32), 0.0), axis=1
+        ).astype(BF16)
+        return rows
+
+    mine = wanted(side)
+    theirs = wanted(1 - side)
     received = cube.swap(theirs, cube.x)
-    chosen = jnp.where((sides == side).reshape(-1, 1, 1), mine, received)
+    chosen = mine + received
     energy = chosen[:, :, width : width + 3].astype(F32)
     energy = (energy[:, :, 0] + energy[:, :, 1]) + energy[:, :, 2]
     part = chosen[:, :, :width]
@@ -151,29 +125,21 @@
         part = jnp.concatenate(
             [jnp.where(first, part, other), jnp.where(first, other, part)], axis=2
         )
-    shape = (transfers, local_k, occ_count)
-    return part.reshape(shape + (grid_count,)), energy.reshape(shape)
-
-
-def reduce_screen(cube, packed, coulomb, scale):
-    transfers, aux_count = coulomb.shape
-    core = cube.bit(cube.core)
+    return part, energy
+
+
+def reduce_screen(cube, packed):
     own = sum_scatter(cube, packed, [cube.core]).astype(BF16)
     rows = own.shape[0] * LANES
-    piece = sum_scatter(cube, own.reshape(4, rows // 4, LANES), [cube.y, cube.x])
+    piece = sum_scatter(cube, own.reshape(4, rows // 4, LANES), [cube.y, cube.x]).astype(BF16)
     for bits in cube.groups:
-        piece = piece.astype(BF16)
         arrived = [cube.swap(piece, mask) for mask in masks_of(bits)]
-        piece = piece.astype(F32)
+        total = piece.astype(F32)
         for term in arrived:
-            piece = piece + term.astype(F32)
-    factors = pick(coulomb, core)
-    scales = pack_upper(factors[:, None] * factors[None, :] * scale).reshape(4, rows // 4, LANES)
-    me = cube.bit(cube.y) + 2 * cube.bit(cube.x)
-    piece = (piece * pick(scales, me)).astype(BF16)
+            total = total + term.astype(F32)
+        piece = total.astype(BF16)
     own = gather_parts(cube, piece, [cube.y, cube.x])
-    both = gather_parts(cube, own, [cube.core])
-    return both.reshape(packed.shape)
+    return gather_parts(cube, own, [cube.core]).reshape(packed.shape)
 
 
 def return_occupied(cube, terms, partner):
@@ -218,12 +184,165 @@
     return value[0]
 
 
-def contract_grid(left, right):
-    return lax.dot_general(left, right, (((1,), (1,)), ((), ())), preferred_element_type=F32)
-
-
-def contract_rows(left, right):
-    return lax.dot_general(left, right, (((0,), (0,)), ((), ())), preferred_element_type=F32)
+def project_kernel(
+    occ_ref, virt_ref, basis_ref, occ_energy_ref, virt_energy_ref, coulomb_ref,
+    coeffs_ref, gram_ref, weighted_ref, *, scale,
+):
+    terms, occ_count, _ = occ_ref.shape
+    local_k, group_count, _ = virt_ref.shape
+    aux_count = basis_ref.shape[0]
+    rows = occ_count * group_count
+    per_transfer = local_k * rows
+    count = aux_count // LANES
+    for transfer in range(terms // local_k):
+        for k in range(local_k):
+            term = transfer * local_k + k
+            virt = virt_ref[k]
+            occ = occ_ref[term]
+            pair_rows = jnp.concatenate([occ[i : i + 1] * virt for i in range(occ_count)], axis=0)
+            coeffs = lax.dot_general(
+                pair_rows, basis_ref[...], (((1,), (1,)), ((), ())), preferred_element_type=F32
+            ).astype(BF16)
+            coeffs_ref[term * rows : (term + 1) * rows, :] = coeffs
+            for i in range(occ_count):
+                start = i * group_count
+                weights = response(virt_energy_ref[k] - occ_energy_ref[term][i : i + 1])
+                values = coeffs[start : start + group_count].astype(F32)
+                weighted_ref[k * rows + start : k * rows + start + group_count, :] = (
+                    jnp.concatenate(
+                        [values[:, n * LANES : (n + 1) * LANES] * weights for n in range(count)],
+                        axis=1,
+                    ).astype(BF16)
+                )
+        where = slice(transfer * per_transfer, (transfer + 1) * per_transfer)
+        coulomb = coulomb_ref[transfer : transfer + 1, :] * math.sqrt(scale)
+        for panel in range(0, count, 2):
+            height = min(2, count - panel)
+            gram = lax.dot_general(
+                weighted_ref[:, panel * LANES : (panel + height) * LANES],
+                coeffs_ref[where, panel * LANES :],
+                (((0,), (0,)), ((), ())),
+                preferred_element_type=F32,
+            )
+            for n, (row, column) in enumerate(blocks_of(aux_count)):
+                if not panel <= row < panel + height:
+                    continue
+                down, across = (row - panel) * LANES, (column - panel) * LANES
+                tile = gram[down : down + LANES, across : across + LANES]
+                first = jnp.broadcast_to(
+                    coulomb[:, row * LANES : (row + 1) * LANES], (LANES, LANES)
+                ).T
+                second = coulomb[:, column * LANES : (column + 1) * LANES]
+                gram_ref[transfer, n] = (first * tile * second).astype(BF16)
+
+
+def project(occ, virtual, basis, occ_energy, virt_energy, coulomb, scale):
+    terms, occ_count, grid_count = occ.shape
+    local_k, group_count, _ = virtual.shape
+    aux_count = basis.shape[0]
+    transfers = terms // local_k
+    rows = terms * occ_count * group_count
+    blocks = len(blocks_of(aux_count))
+    return pl.pallas_call(
+        functools.partial(project_kernel, scale=scale),
+        in_specs=[pl.BlockSpec(memory_space=pltpu.VMEM)] * 6,
+        out_specs=[pl.BlockSpec(memory_space=pltpu.VMEM)] * 2,
+        out_shape=[
+            jax.ShapeDtypeStruct((rows, aux_count), BF16),
+            jax.ShapeDtypeStruct((transfers, blocks, LANES, LANES), BF16),
+        ],
+        scratch_shapes=[pltpu.VMEM((rows // transfers, aux_count), BF16)],
+        compiler_params=pltpu.CompilerParams(vmem_limit_bytes=24 << 20),
+        cost_estimate=pl.CostEstimate(
+            flops=2 * rows * grid_count * aux_count, bytes_accessed=8 << 20, transcendentals=0
+        ),
+        name="project",
+    )(occ, virtual, basis, occ_energy, virt_energy, coulomb)
+
+
+def respond_kernel(
+    coeffs_ref, packed_ref, basis_ref, occ_ref, virt_ref,
+    term_ref, update_ref, screen_ref, screened_ref,
+):
+    terms, occ_count, _ = occ_ref.shape
+    local_k, group_count, _ = virt_ref.shape
+    aux_count = basis_ref.shape[0]
+    rows = occ_count * group_count
+    transfers = terms // local_k
+
+    @pl.when(pl.program_id(0) == 0)
+    def _():
+        for transfer in range(transfers):
+            for n, (row, column) in enumerate(blocks_of(aux_count)):
+                tile = packed_ref[transfer, n]
+                upper = slice(row * LANES, (row + 1) * LANES)
+                lower = slice(column * LANES, (column + 1) * LANES)
+                screen_ref[upper, lower] = tile
+                if row != column:
+                    screen_ref[lower, upper] = tile.T
+            where = slice(transfer * local_k * rows, (transfer + 1) * local_k * rows)
+            screened_ref[where, :] = jnp.dot(
+                coeffs_ref[where, :], screen_ref[...], preferred_element_type=F32
+            ).astype(BF16)
+
+    for k in range(local_k):
+        virt = virt_ref[k].astype(F32)
+        total = None
+        for transfer in range(transfers):
+            term = transfer * local_k + k
+            field = jnp.dot(
+                screened_ref[term * rows : (term + 1) * rows, :],
+                basis_ref[...],
+                preferred_element_type=F32,
+            ).astype(BF16)
+            occ = occ_ref[term].astype(F32)
+            virt_term = None
+            lines = []
+            for i in range(occ_count):
+                piece = field[i * group_count : (i + 1) * group_count].astype(F32)
+                lines.append(jnp.sum(piece * virt, axis=0, keepdims=True))
+                product = piece * occ[i : i + 1]
+                virt_term = product if virt_term is None else virt_term + product
+            term_ref[term] = jnp.concatenate(lines, axis=0).astype(BF16)
+            virt_term = virt_term.astype(BF16).astype(F32)
+            total = virt_term if total is None else total + virt_term
+        update_ref[k] = total.astype(BF16)
+
+
+def respond(coeffs, packed, basis, occ, virtual):
+    terms, occ_count, grid_count = occ.shape
+    local_k, group_count, _ = virtual.shape
+    aux_count = basis.shape[0]
+    rows = coeffs.shape[0]
+    width = min(1024, grid_count)
+    return pl.pallas_call(
+        respond_kernel,
+        grid=(grid_count // width,),
+        in_specs=[
+            pl.BlockSpec(coeffs.shape, lambda n: (0, 0)),
+            pl.BlockSpec(packed.shape, lambda n: (0, 0, 0, 0)),
+            pl.BlockSpec((aux_count, width), lambda n: (0, n)),
+            pl.BlockSpec((terms, occ_count, width), lambda n: (0, 0, n)),
+            pl.BlockSpec((local_k, group_count, width), lambda n: (0, 0, n)),
+        ],
+        out_specs=[
+            pl.BlockSpec((terms, occ_count, width), lambda n: (0, 0, n)),
+            pl.BlockSpec((local_k, group_count, width), lambda n: (0, 0, n)),
+        ],
+        out_shape=[
+            jax.ShapeDtypeStruct(occ.shape, BF16),
+            jax.ShapeDtypeStruct(virtual.shape, BF16),
+        ],
+        scratch_shapes=[
+            pltpu.VMEM((aux_count, aux_count), BF16),
+            pltpu.VMEM((rows, aux_count), BF16),
+        ],
+        compiler_params=pltpu.CompilerParams(vmem_limit_bytes=24 << 20),
+        cost_estimate=pl.CostEstimate(
+            flops=2 * rows * grid_count * aux_count, bytes_accessed=8 << 20, transcendentals=0
+        ),
+        name="respond",
+    )(coeffs, packed, basis, occ, virtual)
 
 
 def shards(occupied, virtual, occ_energy, virt_energy, partner, coulomb, basis):
@@ -238,30 +357,20 @@
     occ_scale = 1.0 / math.sqrt(transfers * virt_count)
     ka = lax.axis_index("ka")
 
+    own_energy = lax.dynamic_slice_in_dim(virt_energy, ka * local_k, local_k, axis=0)
+    own_energy = jnp.broadcast_to(own_energy[:, :, None], own_energy.shape + (LANES,))
     partner_occ, partner_energy = fetch_partners(cube, occupied, occ_energy, partner)
-    own_energy = lax.dynamic_slice_in_dim(virt_energy, ka * local_k, local_k, axis=0)
-    coeffs, grams = [], []
-    for transfer in range(transfers):
-        pair_rows = partner_occ[transfer][:, :, None, :] * virtual[:, None, :, :]
-        pair_coeffs = contract_grid(pair_rows.reshape(-1, grid_count), basis).astype(BF16)
-        gaps = own_energy[:, None, :] - partner_energy[transfer][:, :, None]
-        weights = response(gaps).reshape(-1, 1)
-        weighted = (pair_coeffs.astype(F32) * weights).astype(BF16)
-        grams.append(pack_upper(contract_rows(weighted, pair_coeffs)).astype(BF16))
-        coeffs.append(pair_coeffs)
-    screens = reduce_screen(cube, jnp.stack(grams), coulomb, gram_scale)
-    virt_total = jnp.zeros((local_k, group_count, grid_count), F32)
-    occ_terms = []
-    for transfer in range(transfers):
-        screen = unpack_upper(screens[transfer], aux_count)
-        screened = jnp.dot(coeffs[transfer], screen, preferred_element_type=F32).astype(BF16)
-        field = jnp.dot(screened, basis, preferred_element_type=F32).astype(BF16)
-        field = field.reshape(local_k, occ_count, group_count, grid_count).astype(F32)
-        occ_terms.append(jnp.sum(field * virtual[:, None].astype(F32), axis=2))
-        virt_term = jnp.sum(field * partner_occ[transfer][:, :, None, :].astype(F32), axis=1)
-        virt_total = virt_total + virt_term.astype(BF16).astype(F32)
-    occ_total = return_occupied(cube, jnp.stack(occ_terms), partner)
-    return ((occ_total * occ_scale).astype(BF16), virt_total.astype(BF16))
+    partner_energy = jnp.broadcast_to(
+        partner_energy[:, :, None], partner_energy.shape + (LANES,)
+    )
+    coeffs, packed = project(
+        partner_occ, virtual, basis, partner_energy, own_energy, coulomb, gram_scale
+    )
+    packed = reduce_screen(cube, packed)
+    terms, virt_update = respond(coeffs, packed, basis, partner_occ, virtual)
+    terms = terms.reshape(transfers, local_k, occ_count, grid_count)
+    occ_total = return_occupied(cube, terms, partner)
+    return ((occ_total * occ_scale).astype(BF16), virt_update)
 
 
 def solution(mesh):

time: 125 us -> 91.3 us (0.73)
  matrix products: 20.6 us -> 0 us
  between operations: 16.4 us -> 1.01 us
  Pallas kernels: 0 us -> 13.6 us
  other arithmetic: 13.4 us -> 4.33 us
  local copies, waits for them, and re-layouts: 13.4 us -> 6.55 us
  waiting for transfers between devices: 34 us -> 38.1 us
  starting transfers between devices: 26 us -> 27.4 us
    dot_general x6 -> x0, matrix products: 20.6 us -> none  [the longest x2 14.8 us: shards(): field = jnp.dot(screened, basis, preferred_element_type=F32).astype(BF16)]
    pallas_call x0 -> x2, Pallas kernels: none -> 13.6 us  [the longest x1 8.41 us: respond(): pl.pallas_call(respond_kernel, grid=(grid_count // width,), in_specs=[pl....]
    ppermute x23, waiting for transfers between devices: 34 us -> 38.1 us  [swap(): lax.ppermute(value, ('ka', 'band'), [(device, device ^ mask) for device i...]
    unnamed x47 -> x14, local copies, waits for them, and re-layouts: 8.34 us -> 4.59 us
    reduce_sum x2, other arithmetic: 3.91 us -> 1.09 us  [the longest x1 0.83 us: wanted(): jnp.sum(jnp.where(at_target, partner[:, None, :], 0), axis=2).reshape(-1)]
    convert_element_type x6 -> x4, other arithmetic: 2.7 us -> 0.77 us  [the longest x1 0.64 us: shards(): return ((occ_total * occ_scale).astype(BF16), virt_update)]
    ppermute x23, starting transfers between devices: 26 us -> 27.4 us  [swap(): lax.ppermute(value, ('ka', 'band'), [(device, device ^ mask) for device i...]
  transfers between devices with their start and end apart: 23 -> 23, of which waited for: 16 -> 19; matrix products, arithmetic and copies ran while one was open for 13% -> 4% of each run, Pallas kernels for 0% -> 0%
where the time goes in v2:
time: 91.3 us; the launch traced here: 91 us
  waiting for transfers between devices  38.1 us (42%)
  starting transfers between devices  27.4 us (30%)
  Pallas kernels  13.6 us (15%)
  local copies, waits for them, and re-layouts  6.55 us (7%)
  other arithmetic  4.33 us (5%)
  between operations  1.01 us (1%)
    ppermute x23, waiting for transfers between devices, swap(): lax.ppermute(value, ('ka', 'band'), [(device, device ^ mask) for device i...  38.1 us
    ppermute x23, starting transfers between devices, swap(): lax.ppermute(value, ('ka', 'band'), [(device, device ^ mask) for device i...  27.4 us
    pallas_call x1, Pallas kernels, respond(): pl.pallas_call(respond_kernel, grid=(grid_count // width,), in_specs=[pl....  8.41 us
    pallas_call x1, Pallas kernels, project(): pl.pallas_call(functools.partial(project_kernel, scale=scale), in_specs=[...  5.19 us
    unnamed x14, local copies, waits for them, and re-layouts  4.59 us
  transfers between devices with their start and end apart: 23, of which 19 were waited for; matrix products, arithmetic and copies ran while one was open for 4% of the time, Pallas kernels for 0%

profile of v2, /device:TPU:0, one launch (start us, length us, event | category | flops | bytes accessed | tf_op | source)
XLA Modules:
  0.0 91.0 jit_solution(5756841785744488524)
XLA Ops:
  1.6 4.1 %collective-permute-start.1 = (bf16[1,2,8,1152]{3,2,1,0:T(8,128)(2,1)S(1)}, bf16[1,2,8,1152]{3,2,1,0:T(8,128)(2,1)S(1)}, u32[]{:S(2)}, u32[]{:S(2)}) collective-permute-start(bf16[1,2,8,1152]{3,2,1,0:T(8,128)(2,1)S(1)} %get-tuple-element.33), channel_id=1, source_target_pairs={{0,16},{1,17},{2,18},{3,19},{4,20},{5,21},{6,22},{7,23},{8,24},{9,... | collective-permute-start | bytes 110600 | tf_op jit(solution)/shard_map/ppermute | solution.py:42
  8.4 3.0 %collective-permute-done.2 = bf16[1,2,8,1152]{3,2,1,0:T(8,128)(2,1)S(1)} collective-permute-done((bf16[1,2,8,1152]{3,2,1,0:T(8,128)(2,1)S(1)}, bf16[1,2,8,1152]{3,2,1,0:T(8,128)(2,1)S(1)}, u32[]{:S(2)}, u32[]{:S(2)}) %collective-permute-start.2) | collective-permute-done | bytes 36896 | tf_op jit(solution)/shard_map/ppermute | solution.py:42
  11.8 1.6 %collective-permute-start.3 = (bf16[4,8,1152]{2,1,0:T(8,128)(2,1)S(1)}, bf16[4,8,1152]{2,1,0:T(8,128)(2,1)S(1)}, u32[]{:S(2)}, u32[]{:S(2)}) collective-permute-start(bf16[4,8,1152]{2,1,0:T(8,128)(2,1)S(1)} %get-tuple-element.11), channel_id=1, source_target_pairs={{0,4},{1,5},{2,6},{3,7},{4,0},{5,1},{6,2},{7,3},{8,12},{9,13},{10,... | collective-permute-start | bytes 221192 | tf_op jit(solution)/shard_map/ppermute | solution.py:42
  13.3 2.9 %collective-permute-done.3 = bf16[4,8,1152]{2,1,0:T(8,128)(2,1)S(1)} collective-permute-done((bf16[4,8,1152]{2,1,0:T(8,128)(2,1)S(1)}, bf16[4,8,1152]{2,1,0:T(8,128)(2,1)S(1)}, u32[]{:S(2)}, u32[]{:S(2)}) %collective-permute-start.3) | collective-permute-done | bytes 73760 | tf_op jit(solution)/shard_map/ppermute | solution.py:42
  17.6 1.6 %collective-permute-start.5 = (bf16[4,8,2048]{2,1,0:T(8,128)(2,1)S(1)}, bf16[4,8,2048]{2,1,0:T(8,128)(2,1)S(1)}, u32[]{:S(2)}, u32[]{:S(2)}) collective-permute-start(bf16[4,8,2048]{2,1,0:T(8,128)(2,1)S(1)} %pad_maximum_fusion.5), channel_id=1, source_target_pairs={{0,2},{1,3},{2,0},{3,1},{4,6},{5,7},{6,4},{7,5},{8,10},{9,11},{10,... | collective-permute-start | bytes 393224 | tf_op jit(solution)/shard_map/ppermute | solution.py:42
  19.4 3.9 %collective-permute-done.5 = bf16[4,8,2048]{2,1,0:T(8,128)(2,1)S(1)} collective-permute-done((bf16[4,8,2048]{2,1,0:T(8,128)(2,1)S(1)}, bf16[4,8,2048]{2,1,0:T(8,128)(2,1)S(1)}, u32[]{:S(2)}, u32[]{:S(2)}) %collective-permute-start.5) | collective-permute-done | bytes 131104 | tf_op jit(solution)/shard_map/ppermute | solution.py:42
  23.5 2.2 %copy-done.1 = bf16[512,4096]{1,0:T(8,128)(2,1)S(1)} copy-done((bf16[512,4096]{1,0:T(8,128)(2,1)S(1)}, bf16[512,4096]{1,0:T(8,128)(2,1)}, u32[]{:S(2)}) %copy-start.1) | copy-done | bytes 4194328
  25.6 5.2 %project.1 = (bf16[1024,512]{1,0:T(8,128)(2,1)S(1)}, bf16[2,10,128,128]{3,2,1,0:T(8,128)(2,1)S(1)}) custom-call(bf16[4,8,4096]{2,1,0:T(8,128)(2,1)S(1)} %pad_maximum_fusion.3.occ_ref, bf16[2,32,4096]{2,1,0:T(8,128)(2,1)S(1)} %copy-done.3, bf16[512,4096]{1,0:T(8,128)(2,1)S(1)} %copy-done.1, f32[4,8,128]{2,1,0:T(8,128)S(1)} %broadcast_in_dim.129.occ_energy_ref, ...), custom_call_target="tpu_custom_call" | custom-call | flops 4294967296 | bytes 8388608 | tf_op jit(solution)/shard_map/project/pallas_call | solution.py:246
  31.0 1.6 %collective-permute-done.6 = bf16[10,128,128]{2,1,0:T(8,128)(2,1)S(1)} collective-permute-done((bf16[10,128,128]{2,1,0:T(8,128)(2,1)S(1)}, bf16[10,128,128]{2,1,0:T(8,128)(2,1)S(1)}, u32[]{:S(2)}, u32[]{:S(2)}) %collective-permute-start.6) | collective-permute-done | bytes 327712 | tf_op jit(solution)/shard_map/ppermute | solution.py:42
  32.7 1.6 %collective-permute-start.7 = (bf16[320,128]{1,0:T(8,128)(2,1)S(1)}, bf16[320,128]{1,0:T(8,128)(2,1)S(1)}, u32[]{:S(2)}, u32[]{:S(2)}) collective-permute-start(bf16[320,128]{1,0:T(8,128)(2,1)S(1)} %get-tuple-element.22), channel_id=1, source_target_pairs={{0,2},{1,3},{2,0},{3,1},{4,6},{5,7},{6,4},{7,5},{8,10},{9,11},{10,... | collective-permute-start | bytes 245768 | tf_op jit(solution)/shard_map/ppermute | solution.py:42
  34.3 1.5 %collective-permute-start.8 = (bf16[320,128]{1,0:T(8,128)(2,1)S(1)}, bf16[320,128]{1,0:T(8,128)(2,1)S(1)}, u32[]{:S(2)}, u32[]{:S(2)}) collective-permute-start(bf16[320,128]{1,0:T(8,128)(2,1)S(1)} %get-tuple-element.24), channel_id=1, source_target_pairs={{0,4},{1,5},{2,6},{3,7},{4,0},{5,1},{6,2},{7,3},{8,12},{9,13},{10,... | collective-permute-start | bytes 245768 | tf_op jit(solution)/shard_map/ppermute | solution.py:42
  37.3 2.3 %collective-permute-done.8 = bf16[320,128]{1,0:T(8,128)(2,1)S(1)} collective-permute-done((bf16[320,128]{1,0:T(8,128)(2,1)S(1)}, bf16[320,128]{1,0:T(8,128)(2,1)S(1)}, u32[]{:S(2)}, u32[]{:S(2)}) %collective-permute-start.8) | collective-permute-done | bytes 81952 | tf_op jit(solution)/shard_map/ppermute | solution.py:42
  39.6 1.6 %collective-permute-done.9 = bf16[320,128]{1,0:T(8,128)(2,1)S(1)} collective-permute-done((bf16[320,128]{1,0:T(8,128)(2,1)S(1)}, bf16[320,128]{1,0:T(8,128)(2,1)S(1)}, u32[]{:S(2)}, u32[]{:S(2)}) %collective-permute-start.9) | collective-permute-done | bytes 81952 | tf_op jit(solution)/shard_map/ppermute | solution.py:42
  41.3 2.6 %collective-permute-start.11 = (bf16[320,128]{1,0:T(8,128)(2,1)S(1)}, bf16[320,128]{1,0:T(8,128)(2,1)S(1)}, u32[]{:S(2)}, u32[]{:S(2)}) collective-permute-start(bf16[320,128]{1,0:T(8,128)(2,1)S(1)} %fusion.5), channel_id=1, source_target_pairs={{0,16},{1,17},{2,18},{3,19},{4,20},{5,21},{6,22},{7,23},{8,24},{9,... | collective-permute-start | bytes 245768 | tf_op jit(solution)/shard_map/ppermute | solution.py:42
  43.8 1.8 %collective-permute-start.12 = (bf16[320,128]{1,0:T(8,128)(2,1)S(1)}, bf16[320,128]{1,0:T(8,128)(2,1)S(1)}, u32[]{:S(2)}, u32[]{:S(2)}) collective-permute-start(bf16[320,128]{1,0:T(8,128)(2,1)S(1)} %fusion.5), channel_id=1, source_target_pairs={{0,24},{1,25},{2,26},{3,27},{4,28},{5,29},{6,30},{7,31},{8,16},{9,... | collective-permute-start | bytes 245768 | tf_op jit(solution)/shard_map/ppermute | solution.py:42
  45.7 3.0 %collective-permute-done.11 = bf16[320,128]{1,0:T(8,128)(2,1)S(1)} collective-permute-done((bf16[320,128]{1,0:T(8,128)(2,1)S(1)}, bf16[320,128]{1,0:T(8,128)(2,1)S(1)}, u32[]{:S(2)}, u32[]{:S(2)}) %collective-permute-start.11) | collective-permute-done | bytes 81952 | tf_op jit(solution)/shard_map/ppermute | solution.py:42
  55.9 1.9 %collective-permute-done.15 = bf16[320,128]{1,0:T(8,128)(2,1)S(1)} collective-permute-done((bf16[320,128]{1,0:T(8,128)(2,1)S(1)}, bf16[320,128]{1,0:T(8,128)(2,1)S(1)}, u32[]{:S(2)}, u32[]{:S(2)}) %collective-permute-start.15) | collective-permute-done | bytes 81952 | tf_op jit(solution)/shard_map/ppermute | solution.py:42
  59.9 2.2 %copy-done.2 = bf16[512,4096]{1,0:T(8,128)(2,1)S(1)} copy-done((bf16[512,4096]{1,0:T(8,128)(2,1)S(1)}, bf16[512,4096]{1,0:T(8,128)(2,1)}, u32[]{:S(2)}) %copy-start.2) | copy-done | bytes 4194328
  62.1 8.4 %respond.1 = (bf16[4,8,4096]{2,1,0:T(8,128)(2,1)S(1)}, bf16[2,32,4096]{2,1,0:T(8,128)(2,1)}) custom-call(bf16[1024,512]{1,0:T(8,128)(2,1)S(1)} %get-tuple-element.6.coeffs_ref, bf16[2,10,128,128]{3,2,1,0:T(8,128)(2,1)S(1)} %bitcast.53, bf16[512,4096]{1,0:T(8,128)(2,1)S(1)} %copy-done.2, bf16[4,8,4096]{2,1,0:T(8,128)(2,1)S(1)} %pad_maximum_fusion.3.occ_ref, ...), custom_call_target="tpu_custom_call" | custom-call | flops 4294967296 | bytes 8388608 | tf_op jit(solution)/shard_map/respond/pallas_call | solution.py:318
  71.7 4.4 %collective-permute-done.17 = bf16[4,8,2048]{2,1,0:T(8,128)(2,1)S(1)} collective-permute-done((bf16[4,8,2048]{2,1,0:T(8,128)(2,1)S(1)}, bf16[4,8,2048]{2,1,0:T(8,128)(2,1)S(1)}, u32[]{:S(2)}, u32[]{:S(2)}) %collective-permute-start.17) | collective-permute-done | bytes 131104 | tf_op jit(solution)/shard_map/ppermute | solution.py:42
  78.7 3.1 %collective-permute-done.19 = bf16[4,8,1024]{2,1,0:T(8,128)(2,1)S(1)} collective-permute-done((bf16[4,8,1024]{2,1,0:T(8,128)(2,1)S(1)}, bf16[4,8,1024]{2,1,0:T(8,128)(2,1)S(1)}, u32[]{:S(2)}, u32[]{:S(2)}) %collective-permute-start.19) | collective-permute-done | bytes 65568 | tf_op jit(solution)/shard_map/ppermute | solution.py:42
  84.7 2.0 %collective-permute-start.22 = (bf16[1,2,8,1024]{3,2,1,0:T(8,128)(2,1)S(1)}, bf16[1,2,8,1024]{3,2,1,0:T(8,128)(2,1)S(1)}, u32[]{:S(2)}, u32[]{:S(2)}) collective-permute-start(bf16[1,2,8,1024]{3,2,1,0:T(8,128)(2,1)S(1)} %get-tuple-element.30), channel_id=1, source_target_pairs={{0,24},{1,25},{2,26},{3,27},{4,28},{5,29},{6,30},{7,31},{8,16},{9,... | collective-permute-start | bytes 98312 | tf_op jit(solution)/shard_map/ppermute | solution.py:42
  86.7 1.6 %collective-permute-done.21 = bf16[1,2,8,1024]{3,2,1,0:T(8,128)(2,1)S(1)} collective-permute-done((bf16[1,2,8,1024]{3,2,1,0:T(8,128)(2,1)S(1)}, bf16[1,2,8,1024]{3,2,1,0:T(8,128)(2,1)S(1)}, u32[]{:S(2)}, u32[]{:S(2)}) %collective-permute-start.21) | collective-permute-done | bytes 32800 | tf_op jit(solution)/shard_map/ppermute | solution.py:42
  88.2 2.1 %collective-permute-done.22 = bf16[1,2,8,1024]{3,2,1,0:T(8,128)(2,1)S(1)} collective-permute-done((bf16[1,2,8,1024]{3,2,1,0:T(8,128)(2,1)S(1)}, bf16[1,2,8,1024]{3,2,1,0:T(8,128)(2,1)S(1)}, u32[]{:S(2)}, u32[]{:S(2)}) %collective-permute-start.22) | collective-permute-done | bytes 32800 | tf_op jit(solution)/shard_map/ppermute | solution.py:42
  (97 shorter events, 24.0 us)
Async XLA Ops:
  1.6 6.9 %collective-permute-start.1 = (bf16[1,2,8,1152]{3,2,1,0:T(8,128)(2,1)S(1)}, bf16[1,2,8,1152]{3,2,1,0:T(8,128)(2,1)S(1)}, u32[]{:S(2)}, u32[]{:S(2)}) collective-permute-start(bf16[1,2,8,1152]{3,2,1,0:T(8,128)(2,1)S(1)} %get-tuple-element.33), channel_id=1, source_target_pairs={{0,16},{1,17},{2,18},{3,19},{4,20},{5,21},{6,22},{7,23},{8,24},{9,... | collective-permute-start | bytes 110600 | tf_op jit(solution)/shard_map/ppermute | solution.py:42
  5.7 5.8 %collective-permute-start.2 = (bf16[1,2,8,1152]{3,2,1,0:T(8,128)(2,1)S(1)}, bf16[1,2,8,1152]{3,2,1,0:T(8,128)(2,1)S(1)}, u32[]{:S(2)}, u32[]{:S(2)}) collective-permute-start(bf16[1,2,8,1152]{3,2,1,0:T(8,128)(2,1)S(1)} %get-tuple-element.33), channel_id=1, source_target_pairs={{0,24},{1,25},{2,26},{3,27},{4,28},{5,29},{6,30},{7,31},{8,16},{9,... | collective-permute-start | bytes 110600 | tf_op jit(solution)/shard_map/ppermute | solution.py:42
  7.0 4.4 %collective-permute-start = (bf16[1,2,8,1152]{3,2,1,0:T(8,128)(2,1)S(1)}, bf16[1,2,8,1152]{3,2,1,0:T(8,128)(2,1)S(1)}, u32[]{:S(2)}, u32[]{:S(2)}) collective-permute-start(bf16[1,2,8,1152]{3,2,1,0:T(8,128)(2,1)S(1)} %get-tuple-element.33), channel_id=1, source_target_pairs={{0,8},{1,9},{2,10},{3,11},{4,12},{5,13},{6,14},{7,15},{8,0},{9,1},... | collective-permute-start | bytes 110600 | tf_op jit(solution)/shard_map/ppermute | solution.py:42
  11.8 4.4 %collective-permute-start.3 = (bf16[4,8,1152]{2,1,0:T(8,128)(2,1)S(1)}, bf16[4,8,1152]{2,1,0:T(8,128)(2,1)S(1)}, u32[]{:S(2)}, u32[]{:S(2)}) collective-permute-start(bf16[4,8,1152]{2,1,0:T(8,128)(2,1)S(1)} %get-tuple-element.11), channel_id=1, source_target_pairs={{0,4},{1,5},{2,6},{3,7},{4,0},{5,1},{6,2},{7,3},{8,12},{9,13},{10,... | collective-permute-start | bytes 221192 | tf_op jit(solution)/shard_map/ppermute | solution.py:42
  16.2 1.3 %collective-permute-start.4 = (bf16[4,8,1024]{2,1,0:T(8,128)(2,1)S(1)}, bf16[4,8,1024]{2,1,0:T(8,128)(2,1)S(1)}, u32[]{:S(2)}, u32[]{:S(2)}) collective-permute-start(bf16[4,8,1024]{2,1,0:T(8,128)(2,1)S(1)} %slice.45), channel_id=1, source_target_pairs={{0,1},{1,0},{2,3},{3,2},{4,5},{5,4},{6,7},{7,6},{8,9},{9,8},{10,11... | collective-permute-start | bytes 196616 | tf_op jit(solution)/shard_map/ppermute | solution.py:42
  17.6 5.6 %collective-permute-start.5 = (bf16[4,8,2048]{2,1,0:T(8,128)(2,1)S(1)}, bf16[4,8,2048]{2,1,0:T(8,128)(2,1)S(1)}, u32[]{:S(2)}, u32[]{:S(2)}) collective-permute-start(bf16[4,8,2048]{2,1,0:T(8,128)(2,1)S(1)} %pad_maximum_fusion.5), channel_id=1, source_target_pairs={{0,2},{1,3},{2,0},{3,1},{4,6},{5,7},{6,4},{7,5},{8,10},{9,11},{10,... | collective-permute-start | bytes 393224 | tf_op jit(solution)/shard_map/ppermute | solution.py:42
  30.8 23.0 %copy-start.5 = (s32[2,16]{1,0:T(2,128)S(1)}, s32[2,16]{1,0:T(2,128)}, u32[]{:S(2)}) copy-start(s32[2,16]{1,0:T(2,128)} %param.11) | copy-start | bytes 388
  30.9 1.7 %collective-permute-start.6 = (bf16[10,128,128]{2,1,0:T(8,128)(2,1)S(1)}, bf16[10,128,128]{2,1,0:T(8,128)(2,1)S(1)}, u32[]{:S(2)}, u32[]{:S(2)}) collective-permute-start(bf16[10,128,128]{2,1,0:T(8,128)(2,1)S(1)} %dynamic-slice_bitcast_fusion), channel_id=1, source_target_pairs={{0,1},{1,0},{2,3},{3,2},{4,5},{5,4},{6,7},{7,6},{8,9},{9,8},{10,11... | collective-permute-start | bytes 983048 | tf_op jit(solution)/shard_map/ppermute | solution.py:42
  32.7 4.6 %collective-permute-start.7 = (bf16[320,128]{1,0:T(8,128)(2,1)S(1)}, bf16[320,128]{1,0:T(8,128)(2,1)S(1)}, u32[]{:S(2)}, u32[]{:S(2)}) collective-permute-start(bf16[320,128]{1,0:T(8,128)(2,1)S(1)} %get-tuple-element.22), channel_id=1, source_target_pairs={{0,2},{1,3},{2,0},{3,1},{4,6},{5,7},{6,4},{7,5},{8,10},{9,11},{10,... | collective-permute-start | bytes 245768 | tf_op jit(solution)/shard_map/ppermute | solution.py:42
  34.3 5.3 %collective-permute-start.8 = (bf16[320,128]{1,0:T(8,128)(2,1)S(1)}, bf16[320,128]{1,0:T(8,128)(2,1)S(1)}, u32[]{:S(2)}, u32[]{:S(2)}) collective-permute-start(bf16[320,128]{1,0:T(8,128)(2,1)S(1)} %get-tuple-element.24), channel_id=1, source_target_pairs={{0,4},{1,5},{2,6},{3,7},{4,0},{5,1},{6,2},{7,3},{8,12},{9,13},{10,... | collective-permute-start | bytes 245768 | tf_op jit(solution)/shard_map/ppermute | solution.py:42
  35.8 5.3 %collective-permute-start.9 = (bf16[320,128]{1,0:T(8,128)(2,1)S(1)}, bf16[320,128]{1,0:T(8,128)(2,1)S(1)}, u32[]{:S(2)}, u32[]{:S(2)}) collective-permute-start(bf16[320,128]{1,0:T(8,128)(2,1)S(1)} %get-tuple-element.23), channel_id=1, source_target_pairs={{0,6},{1,7},{2,4},{3,5},{4,2},{5,3},{6,0},{7,1},{8,14},{9,15},{10,... | collective-permute-start | bytes 245768 | tf_op jit(solution)/shard_map/ppermute | solution.py:42
  41.2 4.5 %collective-permute-start.10 = (bf16[320,128]{1,0:T(8,128)(2,1)S(1)}, bf16[320,128]{1,0:T(8,128)(2,1)S(1)}, u32[]{:S(2)}, u32[]{:S(2)}) collective-permute-start(bf16[320,128]{1,0:T(8,128)(2,1)S(1)} %fusion.5), channel_id=1, source_target_pairs={{0,8},{1,9},{2,10},{3,11},{4,12},{5,13},{6,14},{7,15},{8,0},{9,1},... | collective-permute-start | bytes 245768 | tf_op jit(solution)/shard_map/ppermute | solution.py:42
  41.3 7.5 %collective-permute-start.11 = (bf16[320,128]{1,0:T(8,128)(2,1)S(1)}, bf16[320,128]{1,0:T(8,128)(2,1)S(1)}, u32[]{:S(2)}, u32[]{:S(2)}) collective-permute-start(bf16[320,128]{1,0:T(8,128)(2,1)S(1)} %fusion.5), channel_id=1, source_target_pairs={{0,16},{1,17},{2,18},{3,19},{4,20},{5,21},{6,22},{7,23},{8,24},{9,... | collective-permute-start | bytes 245768 | tf_op jit(solution)/shard_map/ppermute | solution.py:42
  43.8 6.3 %collective-permute-start.12 = (bf16[320,128]{1,0:T(8,128)(2,1)S(1)}, bf16[320,128]{1,0:T(8,128)(2,1)S(1)}, u32[]{:S(2)}, u32[]{:S(2)}) collective-permute-start(bf16[320,128]{1,0:T(8,128)(2,1)S(1)} %fusion.5), channel_id=1, source_target_pairs={{0,24},{1,25},{2,26},{3,27},{4,28},{5,29},{6,30},{7,31},{8,16},{9,... | collective-permute-start | bytes 245768 | tf_op jit(solution)/shard_map/ppermute | solution.py:42
  50.2 4.5 %collective-permute-start.13 = (bf16[320,128]{1,0:T(8,128)(2,1)S(1)}, bf16[320,128]{1,0:T(8,128)(2,1)S(1)}, u32[]{:S(2)}, u32[]{:S(2)}) collective-permute-start(bf16[320,128]{1,0:T(8,128)(2,1)S(1)} %add_convert_fusion.1), channel_id=1, source_target_pairs={{0,2},{1,3},{2,0},{3,1},{4,6},{5,7},{6,4},{7,5},{8,10},{9,11},{10,... | collective-permute-start | bytes 245768 | tf_op jit(solution)/shard_map/ppermute | solution.py:42
  51.4 4.4 %collective-permute-start.14 = (bf16[320,128]{1,0:T(8,128)(2,1)S(1)}, bf16[320,128]{1,0:T(8,128)(2,1)S(1)}, u32[]{:S(2)}, u32[]{:S(2)}) collective-permute-start(bf16[320,128]{1,0:T(8,128)(2,1)S(1)} %add_convert_fusion.1), channel_id=1, source_target_pairs={{0,4},{1,5},{2,6},{3,7},{4,0},{5,1},{6,2},{7,3},{8,12},{9,13},{10,... | collective-permute-start | bytes 245768 | tf_op jit(solution)/shard_map/ppermute | solution.py:42
  52.4 5.3 %collective-permute-start.15 = (bf16[320,128]{1,0:T(8,128)(2,1)S(1)}, bf16[320,128]{1,0:T(8,128)(2,1)S(1)}, u32[]{:S(2)}, u32[]{:S(2)}) collective-permute-start(bf16[320,128]{1,0:T(8,128)(2,1)S(1)} %add_convert_fusion.1), channel_id=1, source_target_pairs={{0,6},{1,7},{2,4},{3,5},{4,2},{5,3},{6,0},{7,1},{8,14},{9,15},{10,... | collective-permute-start | bytes 245768 | tf_op jit(solution)/shard_map/ppermute | solution.py:42
  57.9 1.7 %collective-permute-start.16 = (bf16[4,320,128]{2,1,0:T(8,128)(2,1)S(1)}, bf16[4,320,128]{2,1,0:T(8,128)(2,1)S(1)}, u32[]{:S(2)}, u32[]{:S(2)}) collective-permute-start(bf16[4,320,128]{2,1,0:T(8,128)(2,1)S(1)} %get-tuple-element.16), channel_id=1, source_target_pairs={{0,1},{1,0},{2,3},{3,2},{4,5},{5,4},{6,7},{7,6},{8,9},{9,8},{10,11... | collective-permute-start | bytes 983048 | tf_op jit(solution)/shard_map/ppermute | solution.py:42
  70.5 5.6 %collective-permute-start.17 = (bf16[4,8,2048]{2,1,0:T(8,128)(2,1)S(1)}, bf16[4,8,2048]{2,1,0:T(8,128)(2,1)S(1)}, u32[]{:S(2)}, u32[]{:S(2)}) collective-permute-start(bf16[4,8,2048]{2,1,0:T(8,128)(2,1)S(1)} %constant_dynamic-slice_fusion.1), channel_id=1, source_target_pairs={{0,2},{1,3},{2,0},{3,1},{4,6},{5,7},{6,4},{7,5},{8,10},{9,11},{10,... | collective-permute-start | bytes 393224 | tf_op jit(solution)/shard_map/ppermute | solution.py:42
  76.2 1.3 %collective-permute-start.18 = (bf16[4,8,1024]{2,1,0:T(8,128)(2,1)S(1)}, bf16[4,8,1024]{2,1,0:T(8,128)(2,1)S(1)}, u32[]{:S(2)}, u32[]{:S(2)}) collective-permute-start(bf16[4,8,1024]{2,1,0:T(8,128)(2,1)S(1)} %constant_dynamic-slice_fusion), channel_id=1, source_target_pairs={{0,1},{1,0},{2,3},{3,2},{4,5},{5,4},{6,7},{7,6},{8,9},{9,8},{10,11... | collective-permute-start | bytes 196616 | tf_op jit(solution)/shard_map/ppermute | solution.py:42
  77.5 4.3 %collective-permute-start.19 = (bf16[4,8,1024]{2,1,0:T(8,128)(2,1)S(1)}, bf16[4,8,1024]{2,1,0:T(8,128)(2,1)S(1)}, u32[]{:S(2)}, u32[]{:S(2)}) collective-permute-start(bf16[4,8,1024]{2,1,0:T(8,128)(2,1)S(1)} %add_convert_fusion.2), channel_id=1, source_target_pairs={{0,4},{1,5},{2,6},{3,7},{4,0},{5,1},{6,2},{7,3},{8,12},{9,13},{10,... | collective-permute-start | bytes 196616 | tf_op jit(solution)/shard_map/ppermute | solution.py:42
  82.2 4.5 %collective-permute-start.20 = (bf16[1,2,8,1024]{3,2,1,0:T(8,128)(2,1)S(1)}, bf16[1,2,8,1024]{3,2,1,0:T(8,128)(2,1)S(1)}, u32[]{:S(2)}, u32[]{:S(2)}) collective-permute-start(bf16[1,2,8,1024]{3,2,1,0:T(8,128)(2,1)S(1)} %get-tuple-element.29), channel_id=1, source_target_pairs={{0,8},{1,9},{2,10},{3,11},{4,12},{5,13},{6,14},{7,15},{8,0},{9,1},... | collective-permute-start | bytes 98312 | tf_op jit(solution)/shard_map/ppermute | solution.py:42
  83.4 4.8 %collective-permute-start.21 = (bf16[1,2,8,1024]{3,2,1,0:T(8,128)(2,1)S(1)}, bf16[1,2,8,1024]{3,2,1,0:T(8,128)(2,1)S(1)}, u32[]{:S(2)}, u32[]{:S(2)}) collective-permute-start(bf16[1,2,8,1024]{3,2,1,0:T(8,128)(2,1)S(1)} %get-tuple-element.31), channel_id=1, source_target_pairs={{0,16},{1,17},{2,18},{3,19},{4,20},{5,21},{6,22},{7,23},{8,24},{9,... | collective-permute-start | bytes 98312 | tf_op jit(solution)/shard_map/ppermute | solution.py:42
  84.7 5.7 %collective-permute-start.22 = (bf16[1,2,8,1024]{3,2,1,0:T(8,128)(2,1)S(1)}, bf16[1,2,8,1024]{3,2,1,0:T(8,128)(2,1)S(1)}, u32[]{:S(2)}, u32[]{:S(2)}) collective-permute-start(bf16[1,2,8,1024]{3,2,1,0:T(8,128)(2,1)S(1)} %get-tuple-element.30), channel_id=1, source_target_pairs={{0,24},{1,25},{2,26},{3,27},{4,28},{5,29},{6,30},{7,31},{8,16},{9,... | collective-permute-start | bytes 98312 | tf_op jit(solution)/shard_map/ppermute | solution.py:42
  (5 other events, 50.9 us)

commit v3 on v2

v3 whole, which is shorter than its diff:
```python
import functools
import math

import jax
import jax.numpy as jnp
from jax import lax
from jax.experimental import pallas as pl
from jax.experimental.pallas import tpu as pltpu
from jax.sharding import PartitionSpec as P

FREQUENCY = 2.5
BROADENING = 0.4
LANES = 128
KERNEL_VMEM = 50 << 20
VMEM_SPEC = pl.BlockSpec(memory_space=pltpu.VMEM)
BF16 = jnp.bfloat16
F32 = jnp.float32


def response(energy_gaps):
    shifted = FREQUENCY - energy_gaps
    return shifted / (shifted * shifted + BROADENING * BROADENING)


def pick(stack, index):
    return lax.dynamic_index_in_dim(stack, index, 0, keepdims=False)


class Hypercube:
    def __init__(self):
        self.ka = lax.axis_size("ka")
        self.band = lax.axis_size("band")
        self.count = self.ka * self.band
        assert self.band == 4 and self.ka >= 2 and self.ka & (self.ka - 1) == 0
        self.index = lax.axis_index("ka") * self.band + lax.axis_index("band")
        self.core, self.y, self.x = 1, 2, 4
        rest = [bit for bit in (1 << n for n in range(3, 31)) if bit < self.count]
        self.groups = [rest[n : n + 2] for n in range(0, len(rest), 2)]

    def bit(self, mask):
        return (self.index // mask) % 2

    def swap(self, value, mask):
        return lax.ppermute(
            value, ("ka", "band"), [(device, device ^ mask) for device in range(self.count)]
        )


def masks_of(bits):
    return [sum(bit for n, bit in enumerate(bits) if (d >> n) & 1) for d in range(1, 1 << len(bits))]


def sum_scatter(cube, parts, bits):
    me = sum(cube.bit(bit) << n for n, bit in enumerate(bits))
    total = pick(parts, me).astype(F32)
    arrived = [
        cube.swap(pick(parts, jnp.bitwise_xor(me, d + 1)), mask)
        for d, mask in enumerate(masks_of(bits))
    ]
    for term in arrived:
        total = total + term.astype(F32)
    return total


def gather_differences(cube, value, bits):
    return jnp.stack([value] + [cube.swap(value, mask) for mask in masks_of(bits)])


def gather_parts(cube, value, bits):
    me = sum(cube.bit(bit) << n for n, bit in enumerate(bits))
    differences = gather_differences(cube, value, bits)
    return jnp.stack(
        [pick(differences, jnp.bitwise_xor(me, d)) for d in range(1 << len(bits))]
    )


def blocks_of(aux_count):
    count = aux_count // LANES
    return [(row, column) for row in range(count) for column in range(row, count)]


def split_float(value):
    high = lax.reduce_precision(value, 8, 7)
    middle = lax.reduce_precision(value - high, 8, 7)
    low = value - high - middle
    return high.astype(BF16), middle.astype(BF16), low.astype(BF16)


def partners_of(partner, device, local_k):
    every_k = jnp.arange(partner.shape[1], dtype=jnp.int32)
    own_k = device * local_k + jnp.arange(local_k, dtype=jnp.int32)
    here = every_k[None, None, :] == own_k[None, :, None]
    return jnp.sum(jnp.where(here, partner[:, None, :], 0), axis=2).reshape(-1)


def fetch_partners(cube, occupied, occ_energy, sources, neighbour_sources):
    local_k, occ_count, grid_count = occupied.shape
    width = grid_count // 2
    ka = lax.axis_index("ka")
    first = cube.bit(cube.core) == 0
    half = jnp.where(first, occupied[:, :, :width], occupied[:, :, width:])
    pieces = jnp.stack(split_float(occ_energy), axis=2)
    payload = jnp.concatenate(
        [half, jnp.pad(pieces, ((0, 0), (0, 0), (0, LANES - pieces.shape[2])))], axis=2
    )
    gathered = payload[None]
    for bits in cube.groups:
        gathered = gather_differences(cube, gathered, bits).reshape((-1,) + payload.shape)
    gathered = gathered.reshape((-1,) + payload.shape[1:])
    side, upper = ka % 2, ka // 2
    slots = jnp.arange(gathered.shape[0], dtype=jnp.int32)
    held = (jnp.bitwise_xor(slots // local_k, upper) * 2 + side) * local_k + slots % local_k

    def held_of(wanted):
        hits = wanted[:, None] == held[None, :]
        return jnp.sum(
            jnp.where(hits[:, :, None, None], gathered[None].astype(F32), 0.0), axis=1
        ).astype(BF16)

    chosen = held_of(sources) + cube.swap(held_of(neighbour_sources), cube.x)
    energy = chosen[:, :, width : width + 3].astype(F32)
    energy = (energy[:, :, 0] + energy[:, :, 1]) + energy[:, :, 2]
    part = chosen[:, :, :width]
    other = cube.swap(part, cube.core)
    part = jnp.concatenate([jnp.where(first, part, other), jnp.where(first, other, part)], axis=2)
    return part, energy


def reduce_screen(cube, packed):
    own = sum_scatter(cube, packed, [cube.core]).astype(BF16)
    rows = own.shape[0] * LANES
    piece = sum_scatter(cube, own.reshape(4, rows // 4, LANES), [cube.y, cube.x]).astype(BF16)
    for bits in cube.groups:
        arrived = [cube.swap(piece, mask) for mask in masks_of(bits)]
        total = piece.astype(F32)
        for term in arrived:
            total = total + term.astype(F32)
        piece = total.astype(BF16)
    own = gather_parts(cube, piece, [cube.y, cube.x])
    return gather_parts(cube, own, [cube.core]).reshape(packed.shape)


def return_occupied(cube, part, local_k, targets, neighbour_targets):
    ka = lax.axis_index("ka")
    width = part.shape[2] // 2
    first = cube.bit(cube.core) == 0
    keep = jnp.where(first, part[:, :, :width], part[:, :, width:])
    give = jnp.where(first, part[:, :, width:], part[:, :, :width])
    part = (keep.astype(F32) + cube.swap(give, cube.core).astype(F32)).astype(BF16)
    side, upper = ka % 2, ka // 2
    received = cube.swap(part, cube.x)
    both = jnp.concatenate([part, received], axis=0)
    targets = jnp.concatenate([targets, neighbour_targets])

    def placed(uppers):
        wanted_k = ((uppers * 2 + side) * local_k)[:, None] + jnp.arange(local_k, dtype=jnp.int32)
        hits = targets[None, None, :] == wanted_k[:, :, None]
        return jnp.sum(
            jnp.where(hits[:, :, :, None, None], both[None, None].astype(F32), 0.0), axis=2
        )

    spans = 1
    for bits in cube.groups:
        spans *= 1 << len(bits)
    differences = jnp.arange(spans, dtype=jnp.int32)
    value = placed(jnp.bitwise_xor(differences, upper))
    for bits in reversed(cube.groups):
        size = 1 << len(bits)
        value = value.reshape((size, -1) + value.shape[1:])
        total = value[0]
        arrived = [
            cube.swap(value[d + 1].astype(BF16), mask) for d, mask in enumerate(masks_of(bits))
        ]
        for term in arrived:
            total = total + term.astype(F32)
        value = total
    return value[0]


def grid_copies(basis_ref, held_ref, sems, starts):
    ends = starts[1:] + [basis_ref.shape[1]]
    return [
        pltpu.make_async_copy(
            basis_ref.at[:, start:end], held_ref.at[:, start:end], sems.at[n]
        )
        for n, (start, end) in enumerate(zip(starts, ends))
    ]


def project_kernel(
    occ_ref, virt_ref, occ_energy_ref, virt_energy_ref, coulomb_ref, basis_ref,
    coeffs_ref, gram_ref, weighted_ref, held_ref, total_ref, sems, *, scale,
):
    terms, occ_count, grid_count = occ_ref.shape
    local_k, group_count, _ = virt_ref.shape
    aux_count = basis_ref.shape[0]
    rows = occ_count * group_count
    per_transfer = local_k * rows
    count = aux_count // LANES
    starts = [0, grid_count // 8]
    copies = grid_copies(basis_ref, held_ref, sems, starts)
    for copy in copies:
        copy.start()

    def contract(term, start, end):
        virt = virt_ref[term % local_k, :, start:end]
        occ = occ_ref[term, :, start:end]
        pair_rows = jnp.concatenate([occ[i : i + 1] * virt for i in range(occ_count)], axis=0)
        return lax.dot_general(
            pair_rows, held_ref[:, start:end], (((1,), (1,)), ((), ())), preferred_element_type=F32
        )

    copies[0].wait()
    for term in range(terms):
        total_ref[term * rows : (term + 1) * rows, :] = contract(term, 0, starts[1])
    copies[1].wait()
    for transfer in range(terms // local_k):
        for k in range(local_k):
            term = transfer * local_k + k
            here = slice(term * rows, (term + 1) * rows)
            coeffs = (total_ref[here, :] + contract(term, starts[1], grid_count)).astype(BF16)
            coeffs_ref[here, :] = coeffs
            for i in range(occ_count):
                start = i * group_count
                weights = response(virt_energy_ref[k] - occ_energy_ref[term][i : i + 1])
                values = coeffs[start : start + group_count].astype(F32)
                weighted_ref[k * rows + start : k * rows + start + group_count, :] = (
                    jnp.concatenate(
                        [values[:, n * LANES : (n + 1) * LANES] * weights for n in range(count)],
                        axis=1,
                    ).astype(BF16)
                )
        where = slice(transfer * per_transfer, (transfer + 1) * per_transfer)
        coulomb = coulomb_ref[transfer : transfer + 1, :] * math.sqrt(scale)
        for panel in range(0, count, 2):
            height = min(2, count - panel)
            gram = lax.dot_general(
                weighted_ref[:, panel * LANES : (panel + height) * LANES],
                coeffs_ref[where, panel * LANES :],
                (((0,), (0,)), ((), ())),
                preferred_element_type=F32,
            )
            for n, (row, column) in enumerate(blocks_of(aux_count)):
                if not panel <= row < panel + height:
                    continue
                down, across = (row - panel) * LANES, (column - panel) * LANES
                tile = gram[down : down + LANES, across : across + LANES]
                first = jnp.broadcast_to(
                    coulomb[:, row * LANES : (row + 1) * LANES], (LANES, LANES)
                ).T
                second = coulomb[:, column * LANES : (column + 1) * LANES]
                gram_ref[transfer, n] = (first * tile * second).astype(BF16)


def project(occ, virtual, basis, occ_energy, virt_energy, coulomb, scale):
    terms, occ_count, grid_count = occ.shape
    local_k, group_count, _ = virtual.shape
    aux_count = basis.shape[0]
    transfers = terms // local_k
    rows = terms * occ_count * group_count
    blocks = len(blocks_of(aux_count))
    return pl.pallas_call(
        functools.partial(project_kernel, scale=scale),
        in_specs=[VMEM_SPEC] * 5 + [pl.BlockSpec(memory_space=pl.ANY)],
        out_specs=[VMEM_SPEC] * 2,
        out_shape=[
            jax.ShapeDtypeStruct((rows, aux_count), BF16),
            jax.ShapeDtypeStruct((transfers, blocks, LANES, LANES), BF16),
        ],
        scratch_shapes=[
            pltpu.VMEM((rows // transfers, aux_count), BF16),
            pltpu.VMEM(basis.shape, BF16),
            pltpu.VMEM((rows, aux_count), F32),
            pltpu.SemaphoreType.DMA((2,)),
        ],
        compiler_params=pltpu.CompilerParams(vmem_limit_bytes=KERNEL_VMEM),
        cost_estimate=pl.CostEstimate(
            flops=2 * rows * grid_count * aux_count, bytes_accessed=8 << 20, transcendentals=0
        ),
        name="project",
    )(occ, virtual, occ_energy, virt_energy, coulomb, basis)


def screen_coeffs(coeffs_ref, packed_ref, screen_ref, screened_ref):
    transfers = packed_ref.shape[0]
    aux_count = coeffs_ref.shape[1]
    rows = coeffs_ref.shape[0] // transfers
    for transfer in range(transfers):
        for n, (row, column) in enumerate(blocks_of(aux_count)):
            tile = packed_ref[transfer, n]
            upper = slice(row * LANES, (row + 1) * LANES)
            lower = slice(column * LANES, (column + 1) * LANES)
            screen_ref[upper, lower] = tile
            if row != column:
                screen_ref[lower, upper] = tile.T
        where = slice(transfer * rows, (transfer + 1) * rows)
        screened_ref[where, :] = jnp.dot(
            coeffs_ref[where, :], screen_ref[...], preferred_element_type=F32
        ).astype(BF16)


def respond_half(screened_ref, basis_ref, held_ref, sems, occ_ref, virt_ref, outs, half, before=None):
    term_ref, update_ref = outs
    terms, occ_count, _ = occ_ref.shape
    local_k, group_count, _ = virt_ref.shape
    rows = occ_count * group_count
    transfers = terms // local_k
    span = term_ref.shape[2]
    width = min(512, span)

    def grid_of(step):
        return pl.ds(pl.multiple_of(half * span + step * width, width), width)

    def fetch(step):
        return pltpu.make_async_copy(
            basis_ref.at[:, grid_of(step)], held_ref.at[step], sems.at[step]
        )

    for step in range(span // width):
        fetch(step).start()
    if before is not None:
        before()

    def chunk(step, carry):
        to = pl.ds(pl.multiple_of(step * width, width), width)
        grid = grid_of(step)
        fetch(step).wait()
        for k in range(local_k):
            virt = virt_ref[k, :, grid].astype(F32)
            total = None
            for transfer in range(transfers):
                term = transfer * local_k + k
                field = jnp.dot(
                    screened_ref[term * rows : (term + 1) * rows, :],
                    held_ref[step],
                    preferred_element_type=F32,
                ).astype(BF16)
                occ = occ_ref[term, :, grid].astype(F32)
                virt_term = None
                lines = []
                for i in range(occ_count):
                    piece = field[i * group_count : (i + 1) * group_count].astype(F32)
                    lines.append(jnp.sum(piece * virt, axis=0, keepdims=True))
                    product = piece * occ[i : i + 1]
                    virt_term = product if virt_term is None else virt_term + product
                term_ref[term, :, to] = jnp.concatenate(lines, axis=0).astype(BF16)
                virt_term = virt_term.astype(BF16).astype(F32)
                total = virt_term if total is None else total + virt_term
            update_ref[k, :, to] = total.astype(BF16)
        return carry

    lax.fori_loop(0, span // width, chunk, 0)


def respond_far_kernel(
    coeffs_ref, packed_ref, occ_ref, virt_ref, basis_ref,
    term_ref, update_ref, screened_ref, screen_ref, held_ref, sems,
):
    y = (lax.axis_index("band") // 2) % 2
    respond_half(
        screened_ref, basis_ref, held_ref, sems, occ_ref, virt_ref, (term_ref, update_ref), 1 - y,
        lambda: screen_coeffs(coeffs_ref, packed_ref, screen_ref, screened_ref),
    )


def respond_near_kernel(
    screened_ref, occ_ref, virt_ref, basis_ref, term_ref, update_ref, held_ref, sems
):
    y = (lax.axis_index("band") // 2) % 2
    respond_half(
        screened_ref, basis_ref, held_ref, sems, occ_ref, virt_ref, (term_ref, update_ref), y
    )


def respond(coeffs, packed, basis, occ, virtual):
    terms, occ_count, grid_count = occ.shape
    local_k, group_count, _ = virtual.shape
    rows, aux_count = coeffs.shape
    half = grid_count // 2
    width = min(512, half)
    any_spec = pl.BlockSpec(memory_space=pl.ANY)
    shapes = [
        jax.ShapeDtypeStruct((terms, occ_count, half), BF16),
        jax.ShapeDtypeStruct((local_k, group_count, half), BF16),
    ]
    held = [
        pltpu.VMEM((half // width, aux_count, width), BF16),
        pltpu.SemaphoreType.DMA((half // width,)),
    ]
    params = pltpu.CompilerParams(vmem_limit_bytes=KERNEL_VMEM)
    cost = pl.CostEstimate(
        flops=rows * grid_count * aux_count, bytes_accessed=4 << 20, transcendentals=0
    )
    far_terms, far_update, screened = pl.pallas_call(
        respond_far_kernel,
        in_specs=[VMEM_SPEC] * 4 + [any_spec],
        out_specs=[VMEM_SPEC] * 3,
        out_shape=shapes + [jax.ShapeDtypeStruct(coeffs.shape, BF16)],
        scratch_shapes=[pltpu.VMEM((aux_count, aux_count), BF16)] + held,
        compiler_params=params,
        cost_estimate=cost,
        name="respond_far",
    )(coeffs, packed, occ, virtual, basis)
    near_terms, near_update = pl.pallas_call(
        respond_near_kernel,
        in_specs=[VMEM_SPEC] * 3 + [any_spec],
        out_specs=[VMEM_SPEC] * 2,
        out_shape=shapes,
        scratch_shapes=held,
        compiler_params=params,
        cost_estimate=cost,
        name="respond_near",
    )(screened, occ, virtual, basis)
    return (far_terms, near_terms), (far_update, near_update)


def shards(occupied, virtual, occ_energy, virt_energy, partner, coulomb, basis):
    local_k, occ_count, grid_count = occupied.shape
    group_count = virtual.shape[1]
    aux_count = basis.shape[0]
    transfers = partner.shape[0]
    cube = Hypercube()
    total_k = local_k * cube.ka
    virt_count = group_count * cube.band
    gram_scale = 1.0 / math.sqrt(total_k * occ_count * virt_count * aux_count)
    occ_scale = 1.0 / math.sqrt(transfers * virt_count)
    ka = lax.axis_index("ka")

    own_energy = lax.dynamic_slice_in_dim(virt_energy, ka * local_k, local_k, axis=0)
    own_energy = jnp.broadcast_to(own_energy[:, :, None], own_energy.shape + (LANES,))
    sources = partners_of(partner, ka, local_k)
    neighbour_sources = partners_of(partner, jnp.bitwise_xor(ka, 1), local_k)
    partner_occ, partner_energy = fetch_partners(
        cube, occupied, occ_energy, sources, neighbour_sources
    )
    partner_energy = jnp.broadcast_to(
        partner_energy[:, :, None], partner_energy.shape + (LANES,)
    )
    coeffs, packed = project(
        partner_occ, virtual, basis, partner_energy, own_energy, coulomb, gram_scale
    )
    packed = reduce_screen(cube, packed)
    (far_terms, near_terms), (far, near) = respond(coeffs, packed, basis, partner_occ, virtual)
    arrived = cube.swap(far_terms, cube.y)
    terms = (near_terms.astype(F32) + arrived.astype(F32)).astype(BF16)
    occ_total = return_occupied(cube, terms, local_k, sources, neighbour_sources)
    lower = cube.bit(cube.y) == 0
    virt_update = jnp.concatenate(
        [jnp.where(lower, near, far), jnp.where(lower, far, near)], axis=2
    )
    return ((occ_total * occ_scale).astype(BF16), virt_update)


def solution(mesh):
    in_specs = (
        P("ka", None, None),
        P("ka", "band", None),
        P("ka", None),
        P(None, "band"),
        P(),
        P(),
        P(),
    )
    out_specs = (P("ka", None, "band"), P("ka", "band", None))
    return jax.shard_map(shards, mesh=mesh, in_specs=in_specs, out_specs=out_specs, check_vma=False)
```

time: 91.3 us -> 81.5 us (0.89)
  local copies, waits for them, and re-layouts: 6.55 us -> 0.55 us
  waiting for transfers between devices: 38.1 us -> 33.3 us
  starting transfers between devices: 27.4 us -> 24.4 us
  Pallas kernels: 13.6 us -> 15.9 us
  other arithmetic: 4.33 us -> 6.16 us
    ppermute x23 -> x22, waiting for transfers between devices: 38.1 us -> 33.3 us  [swap(): lax.ppermute(value, ('ka', 'band'), [(device, device ^ mask) for device i...]
    unnamed x14 -> x7, local copies, waits for them, and re-layouts: 4.59 us -> 0.13 us
    ppermute x23 -> x22, starting transfers between devices: 27.4 us -> 24.4 us  [swap(): lax.ppermute(value, ('ka', 'band'), [(device, device ^ mask) for device i...]
    pallas_call x1, Pallas kernels: 5.19 us -> 7.05 us  [project(): pl.pallas_call(functools.partial(project_kernel, scale=scale), in_specs=[...]
    pallas_call x1 -> x2, Pallas kernels: 8.41 us -> 8.81 us  [the longest x1 4.61 us: respond(): pl.pallas_call(respond_far_kernel, in_specs=[VMEM_SPEC] * 4 + [any_spec],...]
  transfers between devices with their start and end apart: 23 -> 22, of which waited for: 19 -> 19; matrix products, arithmetic and copies ran while one was open for 4% -> 3% of each run, Pallas kernels for 0% -> 5%
where the time goes in v3:
time: 81.5 us; the launch traced here: 81.2 us
  waiting for transfers between devices  33.3 us (41%)
  starting transfers between devices  24.4 us (30%)
  Pallas kernels  15.9 us (20%)
  other arithmetic  6.16 us (8%)
  between operations  0.93 us (1%)
    ppermute x22, waiting for transfers between devices, swap(): lax.ppermute(value, ('ka', 'band'), [(device, device ^ mask) for device i...  33.3 us
    ppermute x22, starting transfers between devices, swap(): lax.ppermute(value, ('ka', 'band'), [(device, device ^ mask) for device i...  24.4 us
    pallas_call x1, Pallas kernels, project(): pl.pallas_call(functools.partial(project_kernel, scale=scale), in_specs=[...  7.05 us
    pallas_call x1, Pallas kernels, respond(): pl.pallas_call(respond_far_kernel, in_specs=[VMEM_SPEC] * 4 + [any_spec],...  4.61 us
    pallas_call x1, Pallas kernels, respond(): pl.pallas_call(respond_near_kernel, in_specs=[VMEM_SPEC] * 3 + [any_spec]...  4.21 us
  transfers between devices with their start and end apart: 22, of which 19 were waited for; matrix products, arithmetic and copies ran while one was open for 3% of the time, Pallas kernels for 5%

profile of v3, /device:TPU:0, one launch (start us, length us, event | category | flops | bytes accessed | tf_op | source)
XLA Modules:
  0.0 81.2 jit_solution(7157662921036514470)
XLA Ops:
  2.4 5.1 %collective-permute-start.2 = (bf16[1,2,8,2176]{3,2,1,0:T(8,128)(2,1)S(1)}, bf16[1,2,8,2176]{3,2,1,0:T(8,128)(2,1)S(1)}, u32[]{:S(2)}, u32[]{:S(2)}) collective-permute-start(bf16[1,2,8,2176]{3,2,1,0:T(8,128)(2,1)S(1)} %get-tuple-element.39), channel_id=1, source_target_pairs={{0,24},{1,25},{2,26},{3,27},{4,28},{5,29},{6,30},{7,31},{8,16},{9,... | collective-permute-start | bytes 208904 | tf_op jit(solution)/shard_map/ppermute | solution.py:44
  10.1 3.3 %collective-permute-done.1 = bf16[1,2,8,2176]{3,2,1,0:T(8,128)(2,1)S(1)} collective-permute-done((bf16[1,2,8,2176]{3,2,1,0:T(8,128)(2,1)S(1)}, bf16[1,2,8,2176]{3,2,1,0:T(8,128)(2,1)S(1)}, u32[]{:S(2)}, u32[]{:S(2)}) %collective-permute-start.1) | collective-permute-done | bytes 69664 | tf_op jit(solution)/shard_map/ppermute | solution.py:44
  14.1 1.6 %collective-permute-start.3 = (bf16[4,8,2176]{2,1,0:T(8,128)(2,1)S(1)}, bf16[4,8,2176]{2,1,0:T(8,128)(2,1)S(1)}, u32[]{:S(2)}, u32[]{:S(2)}) collective-permute-start(bf16[4,8,2176]{2,1,0:T(8,128)(2,1)S(1)} %get-tuple-element.17), channel_id=1, source_target_pairs={{0,4},{1,5},{2,6},{3,7},{4,0},{5,1},{6,2},{7,3},{8,12},{9,13},{10,... | collective-permute-start | bytes 417800 | tf_op jit(solution)/shard_map/ppermute | solution.py:44
  15.7 3.6 %collective-permute-done.3 = bf16[4,8,2176]{2,1,0:T(8,128)(2,1)S(1)} collective-permute-done((bf16[4,8,2176]{2,1,0:T(8,128)(2,1)S(1)}, bf16[4,8,2176]{2,1,0:T(8,128)(2,1)S(1)}, u32[]{:S(2)}, u32[]{:S(2)}) %collective-permute-start.3) | collective-permute-done | bytes 139296 | tf_op jit(solution)/shard_map/ppermute | solution.py:44
  20.9 7.0 %project.1 = (bf16[1024,512]{1,0:T(8,128)(2,1)S(1)}, bf16[2,10,128,128]{3,2,1,0:T(8,128)(2,1)S(1)}) custom-call(bf16[4,8,4096]{2,1,0:T(8,128)(2,1)S(1)} %pad_maximum_fusion.5.occ_ref, bf16[2,32,4096]{2,1,0:T(8,128)(2,1)S(1)} %copy-done.1, f32[4,8,128]{2,1,0:T(8,128)S(1)} %broadcast_in_dim.122.occ_energy_ref, ...), custom_call_target="tpu_custom_call" | custom-call | flops 4294967296 | bytes 8388608 | tf_op jit(solution)/shard_map/project/pallas_call | solution.py:262
  28.3 1.5 %collective-permute-done.5 = bf16[10,128,128]{2,1,0:T(8,128)(2,1)S(1)} collective-permute-done((bf16[10,128,128]{2,1,0:T(8,128)(2,1)S(1)}, bf16[10,128,128]{2,1,0:T(8,128)(2,1)S(1)}, u32[]{:S(2)}, u32[]{:S(2)}) %collective-permute-start.5) | collective-permute-done | bytes 327712 | tf_op jit(solution)/shard_map/ppermute | solution.py:44
  29.9 1.8 %collective-permute-start.6 = (bf16[320,128]{1,0:T(8,128)(2,1)S(1)}, bf16[320,128]{1,0:T(8,128)(2,1)S(1)}, u32[]{:S(2)}, u32[]{:S(2)}) collective-permute-start(bf16[320,128]{1,0:T(8,128)(2,1)S(1)} %get-tuple-element.30), channel_id=1, source_target_pairs={{0,2},{1,3},{2,0},{3,1},{4,6},{5,7},{6,4},{7,5},{8,10},{9,11},{10,... | collective-permute-start | bytes 245768 | tf_op jit(solution)/shard_map/ppermute | solution.py:44
  31.7 1.4 %collective-permute-start.8 = (bf16[320,128]{1,0:T(8,128)(2,1)S(1)}, bf16[320,128]{1,0:T(8,128)(2,1)S(1)}, u32[]{:S(2)}, u32[]{:S(2)}) collective-permute-start(bf16[320,128]{1,0:T(8,128)(2,1)S(1)} %get-tuple-element.31), channel_id=1, source_target_pairs={{0,6},{1,7},{2,4},{3,5},{4,2},{5,3},{6,0},{7,1},{8,14},{9,15},{10,... | collective-permute-start | bytes 245768 | tf_op jit(solution)/shard_map/ppermute | solution.py:44
  33.4 1.9 %collective-permute-done.6 = bf16[320,128]{1,0:T(8,128)(2,1)S(1)} collective-permute-done((bf16[320,128]{1,0:T(8,128)(2,1)S(1)}, bf16[320,128]{1,0:T(8,128)(2,1)S(1)}, u32[]{:S(2)}, u32[]{:S(2)}) %collective-permute-start.6) | collective-permute-done | bytes 81952 | tf_op jit(solution)/shard_map/ppermute | solution.py:44
  35.3 2.4 %collective-permute-done.8 = bf16[320,128]{1,0:T(8,128)(2,1)S(1)} collective-permute-done((bf16[320,128]{1,0:T(8,128)(2,1)S(1)}, bf16[320,128]{1,0:T(8,128)(2,1)S(1)}, u32[]{:S(2)}, u32[]{:S(2)}) %collective-permute-start.8) | collective-permute-done | bytes 81952 | tf_op jit(solution)/shard_map/ppermute | solution.py:44
  37.8 2.6 %collective-permute-start.11 = (bf16[320,128]{1,0:T(8,128)(2,1)S(1)}, bf16[320,128]{1,0:T(8,128)(2,1)S(1)}, u32[]{:S(2)}, u32[]{:S(2)}) collective-permute-start(bf16[320,128]{1,0:T(8,128)(2,1)S(1)} %fusion.5), channel_id=1, source_target_pairs={{0,24},{1,25},{2,26},{3,27},{4,28},{5,29},{6,30},{7,31},{8,16},{9,... | collective-permute-start | bytes 245768 | tf_op jit(solution)/shard_map/ppermute | solution.py:44
  40.4 1.8 %collective-permute-start.9 = (bf16[320,128]{1,0:T(8,128)(2,1)S(1)}, bf16[320,128]{1,0:T(8,128)(2,1)S(1)}, u32[]{:S(2)}, u32[]{:S(2)}) collective-permute-start(bf16[320,128]{1,0:T(8,128)(2,1)S(1)} %fusion.5), channel_id=1, source_target_pairs={{0,8},{1,9},{2,10},{3,11},{4,12},{5,13},{6,14},{7,15},{8,0},{9,1},... | collective-permute-start | bytes 245768 | tf_op jit(solution)/shard_map/ppermute | solution.py:44
  42.3 1.9 %collective-permute-done.11 = bf16[320,128]{1,0:T(8,128)(2,1)S(1)} collective-permute-done((bf16[320,128]{1,0:T(8,128)(2,1)S(1)}, bf16[320,128]{1,0:T(8,128)(2,1)S(1)}, u32[]{:S(2)}, u32[]{:S(2)}) %collective-permute-start.11) | collective-permute-done | bytes 81952 | tf_op jit(solution)/shard_map/ppermute | solution.py:44
  44.1 3.4 %collective-permute-done.10 = bf16[320,128]{1,0:T(8,128)(2,1)S(1)} collective-permute-done((bf16[320,128]{1,0:T(8,128)(2,1)S(1)}, bf16[320,128]{1,0:T(8,128)(2,1)S(1)}, u32[]{:S(2)}, u32[]{:S(2)}) %collective-permute-start.10) | collective-permute-done | bytes 81952 | tf_op jit(solution)/shard_map/ppermute | solution.py:44
  47.6 2.2 %collective-permute-start.14 = (bf16[320,128]{1,0:T(8,128)(2,1)S(1)}, bf16[320,128]{1,0:T(8,128)(2,1)S(1)}, u32[]{:S(2)}, u32[]{:S(2)}) collective-permute-start(bf16[320,128]{1,0:T(8,128)(2,1)S(1)} %add_convert_fusion.1), channel_id=1, source_target_pairs={{0,6},{1,7},{2,4},{3,5},{4,2},{5,3},{6,0},{7,1},{8,14},{9,15},{10,... | collective-permute-start | bytes 245768 | tf_op jit(solution)/shard_map/ppermute | solution.py:44
  51.2 2.1 %collective-permute-done.14 = bf16[320,128]{1,0:T(8,128)(2,1)S(1)} collective-permute-done((bf16[320,128]{1,0:T(8,128)(2,1)S(1)}, bf16[320,128]{1,0:T(8,128)(2,1)S(1)}, u32[]{:S(2)}, u32[]{:S(2)}) %collective-permute-start.14) | collective-permute-done | bytes 81952 | tf_op jit(solution)/shard_map/ppermute | solution.py:44
  55.7 1.5 %collective-permute-done.15 = bf16[4,320,128]{2,1,0:T(8,128)(2,1)S(1)} collective-permute-done((bf16[4,320,128]{2,1,0:T(8,128)(2,1)S(1)}, bf16[4,320,128]{2,1,0:T(8,128)(2,1)S(1)}, u32[]{:S(2)}, u32[]{:S(2)}) %collective-permute-start.15) | collective-permute-done | bytes 327712 | tf_op jit(solution)/shard_map/ppermute | solution.py:44
  57.5 4.6 %respond_far.1 = (bf16[4,8,2048]{2,1,0:T(8,128)(2,1)S(1)}, bf16[2,32,2048]{2,1,0:T(8,128)(2,1)S(1)}, bf16[1024,512]{1,0:T(8,128)(2,1)S(1)}) custom-call(bf16[1024,512]{1,0:T(8,128)(2,1)S(1)} %get-tuple-element.9.coeffs_ref, bf16[2,10,128,128]{3,2,1,0:T(8,128)(2,1)S(1)} %bitcast.41, bf16[4,8,4096]{2,1,0:T(8,128)(2,1)S(1)} %pad_maximum_fusion.5.occ_ref, ...), custom_call_target="tpu_custom_call" | custom-call | flops 2147483648 | bytes 4194304 | tf_op jit(solution)/shard_map/respond_far/pallas_call | solution.py:394
  62.6 4.2 %respond_near.1 = (bf16[4,8,2048]{2,1,0:T(8,128)(2,1)S(1)}, bf16[2,32,2048]{2,1,0:T(8,128)(2,1)S(1)}) custom-call(bf16[1024,512]{1,0:T(8,128)(2,1)S(1)} %get-tuple-element.11.screened_ref, bf16[4,8,4096]{2,1,0:T(8,128)(2,1)S(1)} %pad_maximum_fusion.5.occ_ref, bf16[2,32,4096]{2,1,0:T(8,128)(2,1)S(1)} %copy-done.1, bf16[512,4096]{1,0:T(8,128)(2,1)} %basis_ref.5), custom_call_target="tpu_custom_call" | custom-call | flops 2147483648 | bytes 4194304 | tf_op jit(solution)/shard_map/respond_near/pallas_call | solution.py:404
  67.9 1.2 %collective-permute-done.17 = bf16[4,8,1024]{2,1,0:T(8,128)(2,1)S(1)} collective-permute-done((bf16[4,8,1024]{2,1,0:T(8,128)(2,1)S(1)}, bf16[4,8,1024]{2,1,0:T(8,128)(2,1)S(1)}, u32[]{:S(2)}, u32[]{:S(2)}) %collective-permute-start.17) | collective-permute-done | bytes 65568 | tf_op jit(solution)/shard_map/ppermute | solution.py:44
  70.2 3.3 %collective-permute-done.18 = bf16[4,8,1024]{2,1,0:T(8,128)(2,1)S(1)} collective-permute-done((bf16[4,8,1024]{2,1,0:T(8,128)(2,1)S(1)}, bf16[4,8,1024]{2,1,0:T(8,128)(2,1)S(1)}, u32[]{:S(2)}, u32[]{:S(2)}) %collective-permute-start.18) | collective-permute-done | bytes 65568 | tf_op jit(solution)/shard_map/ppermute | solution.py:44
  73.9 1.9 %collective-permute-start.21 = (bf16[1,2,8,1024]{3,2,1,0:T(8,128)(2,1)S(1)}, bf16[1,2,8,1024]{3,2,1,0:T(8,128)(2,1)S(1)}, u32[]{:S(2)}, u32[]{:S(2)}) collective-permute-start(bf16[1,2,8,1024]{3,2,1,0:T(8,128)(2,1)S(1)} %get-tuple-element.36), channel_id=1, source_target_pairs={{0,24},{1,25},{2,26},{3,27},{4,28},{5,29},{6,30},{7,31},{8,16},{9,... | collective-permute-start | bytes 98312 | tf_op jit(solution)/shard_map/ppermute | solution.py:44
  75.8 1.6 %collective-permute-start.20 = (bf16[1,2,8,1024]{3,2,1,0:T(8,128)(2,1)S(1)}, bf16[1,2,8,1024]{3,2,1,0:T(8,128)(2,1)S(1)}, u32[]{:S(2)}, u32[]{:S(2)}) collective-permute-start(bf16[1,2,8,1024]{3,2,1,0:T(8,128)(2,1)S(1)} %get-tuple-element.37), channel_id=1, source_target_pairs={{0,16},{1,17},{2,18},{3,19},{4,20},{5,21},{6,22},{7,23},{8,24},{9,... | collective-permute-start | bytes 98312 | tf_op jit(solution)/shard_map/ppermute | solution.py:44
  78.4 1.3 %collective-permute-done.21 = bf16[1,2,8,1024]{3,2,1,0:T(8,128)(2,1)S(1)} collective-permute-done((bf16[1,2,8,1024]{3,2,1,0:T(8,128)(2,1)S(1)}, bf16[1,2,8,1024]{3,2,1,0:T(8,128)(2,1)S(1)}, u32[]{:S(2)}, u32[]{:S(2)}) %collective-permute-start.21) | collective-permute-done | bytes 32800 | tf_op jit(solution)/shard_map/ppermute | solution.py:44
  (78 shorter events, 17.1 us)
Async XLA Ops:
  2.4 18.6 %copy-start.1 = (bf16[2,32,4096]{2,1,0:T(8,128)(2,1)S(1)}, bf16[2,32,4096]{2,1,0:T(8,128)(2,1)}, u32[]{:S(2)}) copy-start(bf16[2,32,4096]{2,1,0:T(8,128)(2,1)} %virt_ref.5) | copy-start | bytes 1572868
  2.4 18.6 %copy-start.2 = (f32[2,512]{1,0:T(2,128)S(1)}, f32[2,512]{1,0:T(2,128)}, u32[]{:S(2)}) copy-start(f32[2,512]{1,0:T(2,128)} %coulomb_ref.1) | copy-start | bytes 12292
  2.4 7.7 %collective-permute-start.2 = (bf16[1,2,8,2176]{3,2,1,0:T(8,128)(2,1)S(1)}, bf16[1,2,8,2176]{3,2,1,0:T(8,128)(2,1)S(1)}, u32[]{:S(2)}, u32[]{:S(2)}) collective-permute-start(bf16[1,2,8,2176]{3,2,1,0:T(8,128)(2,1)S(1)} %get-tuple-element.39), channel_id=1, source_target_pairs={{0,24},{1,25},{2,26},{3,27},{4,28},{5,29},{6,30},{7,31},{8,16},{9,... | collective-permute-start | bytes 208904 | tf_op jit(solution)/shard_map/ppermute | solution.py:44
  7.5 5.9 %collective-permute-start.1 = (bf16[1,2,8,2176]{3,2,1,0:T(8,128)(2,1)S(1)}, bf16[1,2,8,2176]{3,2,1,0:T(8,128)(2,1)S(1)}, u32[]{:S(2)}, u32[]{:S(2)}) collective-permute-start(bf16[1,2,8,2176]{3,2,1,0:T(8,128)(2,1)S(1)} %get-tuple-element.39), channel_id=1, source_target_pairs={{0,16},{1,17},{2,18},{3,19},{4,20},{5,21},{6,22},{7,23},{8,24},{9,... | collective-permute-start | bytes 208904 | tf_op jit(solution)/shard_map/ppermute | solution.py:44
  7.5 5.9 %collective-permute-start = (bf16[1,2,8,2176]{3,2,1,0:T(8,128)(2,1)S(1)}, bf16[1,2,8,2176]{3,2,1,0:T(8,128)(2,1)S(1)}, u32[]{:S(2)}, u32[]{:S(2)}) collective-permute-start(bf16[1,2,8,2176]{3,2,1,0:T(8,128)(2,1)S(1)} %get-tuple-element.39), channel_id=1, source_target_pairs={{0,8},{1,9},{2,10},{3,11},{4,12},{5,13},{6,14},{7,15},{8,0},{9,1},... | collective-permute-start | bytes 208904 | tf_op jit(solution)/shard_map/ppermute | solution.py:44
  14.1 5.1 %collective-permute-start.3 = (bf16[4,8,2176]{2,1,0:T(8,128)(2,1)S(1)}, bf16[4,8,2176]{2,1,0:T(8,128)(2,1)S(1)}, u32[]{:S(2)}, u32[]{:S(2)}) collective-permute-start(bf16[4,8,2176]{2,1,0:T(8,128)(2,1)S(1)} %get-tuple-element.17), channel_id=1, source_target_pairs={{0,4},{1,5},{2,6},{3,7},{4,0},{5,1},{6,2},{7,3},{8,12},{9,13},{10,... | collective-permute-start | bytes 417800 | tf_op jit(solution)/shard_map/ppermute | solution.py:44
  19.3 1.4 %collective-permute-start.4 = (bf16[4,8,2048]{2,1,0:T(8,128)(2,1)S(1)}, bf16[4,8,2048]{2,1,0:T(8,128)(2,1)S(1)}, u32[]{:S(2)}, u32[]{:S(2)}) collective-permute-start(bf16[4,8,2048]{2,1,0:T(8,128)(2,1)S(1)} %slice.61), channel_id=1, source_target_pairs={{0,1},{1,0},{2,3},{3,2},{4,5},{5,4},{6,7},{7,6},{8,9},{9,8},{10,11... | collective-permute-start | bytes 393224 | tf_op jit(solution)/shard_map/ppermute | solution.py:44
  28.0 1.7 %collective-permute-start.5 = (bf16[10,128,128]{2,1,0:T(8,128)(2,1)S(1)}, bf16[10,128,128]{2,1,0:T(8,128)(2,1)S(1)}, u32[]{:S(2)}, u32[]{:S(2)}) collective-permute-start(bf16[10,128,128]{2,1,0:T(8,128)(2,1)S(1)} %dynamic-slice_bitcast_fusion), channel_id=1, source_target_pairs={{0,1},{1,0},{2,3},{3,2},{4,5},{5,4},{6,7},{7,6},{8,9},{9,8},{10,11... | collective-permute-start | bytes 983048 | tf_op jit(solution)/shard_map/ppermute | solution.py:44
  29.9 5.5 %collective-permute-start.6 = (bf16[320,128]{1,0:T(8,128)(2,1)S(1)}, bf16[320,128]{1,0:T(8,128)(2,1)S(1)}, u32[]{:S(2)}, u32[]{:S(2)}) collective-permute-start(bf16[320,128]{1,0:T(8,128)(2,1)S(1)} %get-tuple-element.30), channel_id=1, source_target_pairs={{0,2},{1,3},{2,0},{3,1},{4,6},{5,7},{6,4},{7,5},{8,10},{9,11},{10,... | collective-permute-start | bytes 245768 | tf_op jit(solution)/shard_map/ppermute | solution.py:44
  31.7 6.1 %collective-permute-start.8 = (bf16[320,128]{1,0:T(8,128)(2,1)S(1)}, bf16[320,128]{1,0:T(8,128)(2,1)S(1)}, u32[]{:S(2)}, u32[]{:S(2)}) collective-permute-start(bf16[320,128]{1,0:T(8,128)(2,1)S(1)} %get-tuple-element.31), channel_id=1, source_target_pairs={{0,6},{1,7},{2,4},{3,5},{4,2},{5,3},{6,0},{7,1},{8,14},{9,15},{10,... | collective-permute-start | bytes 245768 | tf_op jit(solution)/shard_map/ppermute | solution.py:44
  33.1 4.7 %collective-permute-start.7 = (bf16[320,128]{1,0:T(8,128)(2,1)S(1)}, bf16[320,128]{1,0:T(8,128)(2,1)S(1)}, u32[]{:S(2)}, u32[]{:S(2)}) collective-permute-start(bf16[320,128]{1,0:T(8,128)(2,1)S(1)} %get-tuple-element.32), channel_id=1, source_target_pairs={{0,4},{1,5},{2,6},{3,7},{4,0},{5,1},{6,2},{7,3},{8,12},{9,13},{10,... | collective-permute-start | bytes 245768 | tf_op jit(solution)/shard_map/ppermute | solution.py:44
  37.8 6.3 %collective-permute-start.11 = (bf16[320,128]{1,0:T(8,128)(2,1)S(1)}, bf16[320,128]{1,0:T(8,128)(2,1)S(1)}, u32[]{:S(2)}, u32[]{:S(2)}) collective-permute-start(bf16[320,128]{1,0:T(8,128)(2,1)S(1)} %fusion.5), channel_id=1, source_target_pairs={{0,24},{1,25},{2,26},{3,27},{4,28},{5,29},{6,30},{7,31},{8,16},{9,... | collective-permute-start | bytes 245768 | tf_op jit(solution)/shard_map/ppermute | solution.py:44
  40.4 7.1 %collective-permute-start.10 = (bf16[320,128]{1,0:T(8,128)(2,1)S(1)}, bf16[320,128]{1,0:T(8,128)(2,1)S(1)}, u32[]{:S(2)}, u32[]{:S(2)}) collective-permute-start(bf16[320,128]{1,0:T(8,128)(2,1)S(1)} %fusion.5), channel_id=1, source_target_pairs={{0,16},{1,17},{2,18},{3,19},{4,20},{5,21},{6,22},{7,23},{8,24},{9,... | collective-permute-start | bytes 245768 | tf_op jit(solution)/shard_map/ppermute | solution.py:44
  40.4 7.1 %collective-permute-start.9 = (bf16[320,128]{1,0:T(8,128)(2,1)S(1)}, bf16[320,128]{1,0:T(8,128)(2,1)S(1)}, u32[]{:S(2)}, u32[]{:S(2)}) collective-permute-start(bf16[320,128]{1,0:T(8,128)(2,1)S(1)} %fusion.5), channel_id=1, source_target_pairs={{0,8},{1,9},{2,10},{3,11},{4,12},{5,13},{6,14},{7,15},{8,0},{9,1},... | collective-permute-start | bytes 245768 | tf_op jit(solution)/shard_map/ppermute | solution.py:44
  47.6 5.6 %collective-permute-start.14 = (bf16[320,128]{1,0:T(8,128)(2,1)S(1)}, bf16[320,128]{1,0:T(8,128)(2,1)S(1)}, u32[]{:S(2)}, u32[]{:S(2)}) collective-permute-start(bf16[320,128]{1,0:T(8,128)(2,1)S(1)} %add_convert_fusion.1), channel_id=1, source_target_pairs={{0,6},{1,7},{2,4},{3,5},{4,2},{5,3},{6,0},{7,1},{8,14},{9,15},{10,... | collective-permute-start | bytes 245768 | tf_op jit(solution)/shard_map/ppermute | solution.py:44
  49.8 4.5 %collective-permute-start.13 = (bf16[320,128]{1,0:T(8,128)(2,1)S(1)}, bf16[320,128]{1,0:T(8,128)(2,1)S(1)}, u32[]{:S(2)}, u32[]{:S(2)}) collective-permute-start(bf16[320,128]{1,0:T(8,128)(2,1)S(1)} %add_convert_fusion.1), channel_id=1, source_target_pairs={{0,4},{1,5},{2,6},{3,7},{4,0},{5,1},{6,2},{7,3},{8,12},{9,13},{10,... | collective-permute-start | bytes 245768 | tf_op jit(solution)/shard_map/ppermute | solution.py:44
  50.9 4.4 %collective-permute-start.12 = (bf16[320,128]{1,0:T(8,128)(2,1)S(1)}, bf16[320,128]{1,0:T(8,128)(2,1)S(1)}, u32[]{:S(2)}, u32[]{:S(2)}) collective-permute-start(bf16[320,128]{1,0:T(8,128)(2,1)S(1)} %add_convert_fusion.1), channel_id=1, source_target_pairs={{0,2},{1,3},{2,0},{3,1},{4,6},{5,7},{6,4},{7,5},{8,10},{9,11},{10,... | collective-permute-start | bytes 245768 | tf_op jit(solution)/shard_map/ppermute | solution.py:44
  55.5 1.7 %collective-permute-start.15 = (bf16[4,320,128]{2,1,0:T(8,128)(2,1)S(1)}, bf16[4,320,128]{2,1,0:T(8,128)(2,1)S(1)}, u32[]{:S(2)}, u32[]{:S(2)}) collective-permute-start(bf16[4,320,128]{2,1,0:T(8,128)(2,1)S(1)} %get-tuple-element.24), channel_id=1, source_target_pairs={{0,1},{1,0},{2,3},{3,2},{4,5},{5,4},{6,7},{7,6},{8,9},{9,8},{10,11... | collective-permute-start | bytes 983048 | tf_op jit(solution)/shard_map/ppermute | solution.py:44
  62.1 5.6 %collective-permute-start.16 = (bf16[4,8,2048]{2,1,0:T(8,128)(2,1)S(1)}, bf16[4,8,2048]{2,1,0:T(8,128)(2,1)S(1)}, u32[]{:S(2)}, u32[]{:S(2)}) collective-permute-start(bf16[4,8,2048]{2,1,0:T(8,128)(2,1)S(1)} %get-tuple-element.13), channel_id=1, source_target_pairs={{0,2},{1,3},{2,0},{3,1},{4,6},{5,7},{6,4},{7,5},{8,10},{9,11},{10,... | collective-permute-start | bytes 393224 | tf_op jit(solution)/shard_map/ppermute | solution.py:44
  67.8 1.3 %collective-permute-start.17 = (bf16[4,8,1024]{2,1,0:T(8,128)(2,1)S(1)}, bf16[4,8,1024]{2,1,0:T(8,128)(2,1)S(1)}, u32[]{:S(2)}, u32[]{:S(2)}) collective-permute-start(bf16[4,8,1024]{2,1,0:T(8,128)(2,1)S(1)} %broadcast_select_fusion.4), channel_id=1, source_target_pairs={{0,1},{1,0},{2,3},{3,2},{4,5},{5,4},{6,7},{7,6},{8,9},{9,8},{10,11... | collective-permute-start | bytes 196616 | tf_op jit(solution)/shard_map/ppermute | solution.py:44
  69.1 4.3 %collective-permute-start.18 = (bf16[4,8,1024]{2,1,0:T(8,128)(2,1)S(1)}, bf16[4,8,1024]{2,1,0:T(8,128)(2,1)S(1)}, u32[]{:S(2)}, u32[]{:S(2)}) collective-permute-start(bf16[4,8,1024]{2,1,0:T(8,128)(2,1)S(1)} %add_convert_fusion.2), channel_id=1, source_target_pairs={{0,4},{1,5},{2,6},{3,7},{4,0},{5,1},{6,2},{7,3},{8,12},{9,13},{10,... | collective-permute-start | bytes 196616 | tf_op jit(solution)/shard_map/ppermute | solution.py:44
  73.8 4.6 %collective-permute-start.19 = (bf16[1,2,8,1024]{3,2,1,0:T(8,128)(2,1)S(1)}, bf16[1,2,8,1024]{3,2,1,0:T(8,128)(2,1)S(1)}, u32[]{:S(2)}, u32[]{:S(2)}) collective-permute-start(bf16[1,2,8,1024]{3,2,1,0:T(8,128)(2,1)S(1)} %get-tuple-element.35), channel_id=1, source_target_pairs={{0,8},{1,9},{2,10},{3,11},{4,12},{5,13},{6,14},{7,15},{8,0},{9,1},... | collective-permute-start | bytes 98312 | tf_op jit(solution)/shard_map/ppermute | solution.py:44
  73.9 5.8 %collective-permute-start.21 = (bf16[1,2,8,1024]{3,2,1,0:T(8,128)(2,1)S(1)}, bf16[1,2,8,1024]{3,2,1,0:T(8,128)(2,1)S(1)}, u32[]{:S(2)}, u32[]{:S(2)}) collective-permute-start(bf16[1,2,8,1024]{3,2,1,0:T(8,128)(2,1)S(1)} %get-tuple-element.36), channel_id=1, source_target_pairs={{0,24},{1,25},{2,26},{3,27},{4,28},{5,29},{6,30},{7,31},{8,16},{9,... | collective-permute-start | bytes 98312 | tf_op jit(solution)/shard_map/ppermute | solution.py:44
  75.8 4.8 %collective-permute-start.20 = (bf16[1,2,8,1024]{3,2,1,0:T(8,128)(2,1)S(1)}, bf16[1,2,8,1024]{3,2,1,0:T(8,128)(2,1)S(1)}, u32[]{:S(2)}, u32[]{:S(2)}) collective-permute-start(bf16[1,2,8,1024]{3,2,1,0:T(8,128)(2,1)S(1)} %get-tuple-element.37), channel_id=1, source_target_pairs={{0,16},{1,17},{2,18},{3,19},{4,20},{5,21},{6,22},{7,23},{8,24},{9,... | collective-permute-start | bytes 98312 | tf_op jit(solution)/shard_map/ppermute | solution.py:44
  (1 other events, 15.1 us)

commit v4 on v3

v4 whole, which is shorter than its diff:
```python
import functools
import math

import jax
import jax.numpy as jnp
from jax import lax
from jax.experimental import pallas as pl
from jax.experimental.pallas import tpu as pltpu
from jax.sharding import PartitionSpec as P

FREQUENCY = 2.5
BROADENING = 0.4
LANES = 128
KERNEL_VMEM = 48 << 20
VMEM_SPEC = pl.BlockSpec(memory_space=pltpu.VMEM)
BF16 = jnp.bfloat16
F32 = jnp.float32


def response(energy_gaps):
    shifted = FREQUENCY - energy_gaps
    return shifted / (shifted * shifted + BROADENING * BROADENING)


def pick(stack, index):
    return lax.dynamic_index_in_dim(stack, index, 0, keepdims=False)


class Hypercube:
    def __init__(self):
        self.ka = lax.axis_size("ka")
        self.band = lax.axis_size("band")
        self.count = self.ka * self.band
        assert self.band == 4 and self.ka >= 2 and self.ka & (self.ka - 1) == 0
        self.index = lax.axis_index("ka") * self.band + lax.axis_index("band")
        self.core, self.y, self.x = 1, 2, 4
        rest = [bit for bit in (1 << n for n in range(3, 31)) if bit < self.count]
        self.groups = [rest[n : n + 2] for n in range(0, len(rest), 2)]

    def bit(self, mask):
        return (self.index // mask) % 2

    def swap(self, value, mask):
        return lax.ppermute(
            value, ("ka", "band"), [(device, device ^ mask) for device in range(self.count)]
        )


def masks_of(bits):
    return [sum(bit for n, bit in enumerate(bits) if (d >> n) & 1) for d in range(1, 1 << len(bits))]


def sum_scatter(cube, parts, bits):
    me = sum(cube.bit(bit) << n for n, bit in enumerate(bits))
    total = pick(parts, me).astype(F32)
    arrived = [
        cube.swap(pick(parts, jnp.bitwise_xor(me, d + 1)), mask)
        for d, mask in enumerate(masks_of(bits))
    ]
    for term in arrived:
        total = total + term.astype(F32)
    return total


def gather_differences(cube, value, bits):
    return jnp.stack([value] + [cube.swap(value, mask) for mask in masks_of(bits)])


def gather_parts(cube, value, bits):
    me = sum(cube.bit(bit) << n for n, bit in enumerate(bits))
    differences = gather_differences(cube, value, bits)
    return jnp.stack(
        [pick(differences, jnp.bitwise_xor(me, d)) for d in range(1 << len(bits))]
    )


def blocks_of(aux_count):
    count = aux_count // LANES
    return [(row, column) for row in range(count) for column in range(row, count)]


def split_float(value):
    high = lax.reduce_precision(value, 8, 7)
    middle = lax.reduce_precision(value - high, 8, 7)
    low = value - high - middle
    return high.astype(BF16), middle.astype(BF16), low.astype(BF16)


def partners_of(partner, device, local_k):
    every_k = jnp.arange(partner.shape[1], dtype=jnp.int32)
    own_k = device * local_k + jnp.arange(local_k, dtype=jnp.int32)
    here = every_k[None, None, :] == own_k[None, :, None]
    return jnp.sum(jnp.where(here, partner[:, None, :], 0), axis=2).reshape(-1)


def fetch_partners(cube, occupied, occ_energy, sources, neighbour_sources):
    local_k, occ_count, grid_count = occupied.shape
    width = grid_count // 2
    ka = lax.axis_index("ka")
    first = cube.bit(cube.core) == 0
    half = jnp.where(first, occupied[:, :, :width], occupied[:, :, width:])
    pieces = jnp.stack(split_float(occ_energy), axis=2)
    payload = jnp.concatenate(
        [half, jnp.pad(pieces, ((0, 0), (0, 0), (0, LANES - pieces.shape[2])))], axis=2
    )
    gathered = payload[None]
    for bits in cube.groups:
        gathered = gather_differences(cube, gathered, bits).reshape((-1,) + payload.shape)
    gathered = gathered.reshape((-1,) + payload.shape[1:])
    side, upper = ka % 2, ka // 2
    slots = jnp.arange(gathered.shape[0], dtype=jnp.int32)
    held = (jnp.bitwise_xor(slots // local_k, upper) * 2 + side) * local_k + slots % local_k

    def held_of(wanted):
        hits = wanted[:, None] == held[None, :]
        return jnp.sum(
            jnp.where(hits[:, :, None, None], gathered[None].astype(F32), 0.0), axis=1
        ).astype(BF16)

    chosen = held_of(sources) + cube.swap(held_of(neighbour_sources), cube.x)
    mine = jnp.where(first, chosen[:local_k], chosen[local_k:])
    theirs = jnp.where(first, chosen[local_k:], chosen[:local_k])
    energy = mine[:, :, width : width + 3].astype(F32)
    energy = (energy[:, :, 0] + energy[:, :, 1]) + energy[:, :, 2]
    part = mine[:, :, :width]
    other = cube.swap(theirs[:, :, :width], cube.core)
    part = jnp.concatenate([jnp.where(first, part, other), jnp.where(first, other, part)], axis=2)
    return part, energy


def reduce_screen(cube, own):
    rows = own.shape[0] * LANES
    piece = sum_scatter(cube, own.reshape(4, rows // 4, LANES), [cube.y, cube.x]).astype(BF16)
    for bits in cube.groups:
        arrived = [cube.swap(piece, mask) for mask in masks_of(bits)]
        total = piece.astype(F32)
        for term in arrived:
            total = total + term.astype(F32)
        piece = total.astype(BF16)
    return gather_parts(cube, piece, [cube.y, cube.x]).reshape(own.shape)


def return_occupied(cube, part, local_k, sources, neighbour_sources, beside):
    ka = lax.axis_index("ka")
    width = part.shape[2] // 2
    first = cube.bit(cube.core) == 0
    keep = jnp.where(first, part[:, :, :width], part[:, :, width:])
    give = jnp.where(first, part[:, :, width:], part[:, :, :width])
    part = jnp.concatenate([keep, cube.swap(give, cube.core)], axis=0)
    side, upper = ka % 2, ka // 2
    received = cube.swap(part, cube.x)
    both = jnp.concatenate([part, received], axis=0)

    def own_transfer_first(targets):
        turned = jnp.concatenate([targets[local_k:], targets[:local_k]])
        return jnp.where(first, targets, turned)

    targets = jnp.concatenate(
        [own_transfer_first(sources), own_transfer_first(neighbour_sources)]
    )

    def placed(uppers):
        wanted_k = ((uppers * 2 + side) * local_k)[:, None] + jnp.arange(local_k, dtype=jnp.int32)
        hits = targets[None, None, :] == wanted_k[:, :, None]
        return jnp.sum(
            jnp.where(hits[:, :, :, None, None], both[None, None].astype(F32), 0.0), axis=2
        )

    spans = 1
    for bits in cube.groups:
        spans *= 1 << len(bits)
    differences = jnp.arange(spans, dtype=jnp.int32)
    value = placed(jnp.bitwise_xor(differences, upper))
    for bits in reversed(cube.groups):
        size = 1 << len(bits)
        value = value.reshape((size, -1) + value.shape[1:])
        total = value[0]
        arrived = [
            cube.swap(value[d + 1].astype(BF16), mask) for d, mask in enumerate(masks_of(bits))
        ]
        arrived[-1], beside = lax.optimization_barrier((arrived[-1], beside))
        for term in arrived:
            total = total + term.astype(F32)
        value = total
    return value[0], beside


def grid_copies(basis_ref, held_ref, sems, starts):
    ends = starts[1:] + [basis_ref.shape[1]]
    return [
        pltpu.make_async_copy(
            basis_ref.at[:, start:end], held_ref.at[:, start:end], sems.at[n]
        )
        for n, (start, end) in enumerate(zip(starts, ends))
    ]


def project_kernel(
    occ_ref, own_ref, other_ref, occ_energy_ref, levels_ref, coulomb_ref, basis_ref,
    coeffs_ref, gram_ref, weighted_ref, held_ref, total_ref, sems, *, scale, starts,
):
    local_k, occ_count, grid_count = occ_ref.shape
    group_count = own_ref.shape[1]
    aux_count = basis_ref.shape[0]
    rows = occ_count * group_count
    count = aux_count // LANES
    parts = list(zip(starts, starts[1:] + (grid_count,)))
    copies = [
        pltpu.make_async_copy(basis_ref.at[:, start:end], held_ref.at[:, start:end], sems.at[n])
        for n, (start, end) in enumerate(parts)
    ]
    for copy in copies:
        copy.start()
    terms = [(virt_ref, k) for virt_ref in (own_ref, other_ref) for k in range(local_k)]
    for n, (start, end) in enumerate(parts):
        copies[n].wait()
        for term, (virt_ref, k) in enumerate(terms):
            virt = virt_ref[k, :, start:end]
            occ = occ_ref[k, :, start:end]
            pair_rows = jnp.concatenate([occ[i : i + 1] * virt for i in range(occ_count)], axis=0)
            coeffs = lax.dot_general(
                pair_rows,
                held_ref[:, start:end],
                (((1,), (1,)), ((), ())),
                preferred_element_type=F32,
            )
            here = slice(term * rows, (term + 1) * rows)
            if n > 0:
                coeffs = total_ref[here, :] + coeffs
            if n < len(parts) - 1:
                total_ref[here, :] = coeffs
                continue
            coeffs_ref[here, :] = coeffs.astype(BF16)
            coeffs = coeffs.astype(BF16)
            for i in range(occ_count):
                first = i * group_count
                weights = response(levels_ref[term] - occ_energy_ref[k][i : i + 1])
                values = coeffs[first : first + group_count].astype(F32)
                weighted_ref[term * rows + first : term * rows + first + group_count, :] = (
                    jnp.concatenate(
                        [values[:, n * LANES : (n + 1) * LANES] * weights for n in range(count)],
                        axis=1,
                    ).astype(BF16)
                )
    coulomb = coulomb_ref[...] * math.sqrt(scale)
    for panel in range(0, count, 2):
        height = min(2, count - panel)
        gram = lax.dot_general(
            weighted_ref[:, panel * LANES : (panel + height) * LANES],
            coeffs_ref[:, panel * LANES :],
            (((0,), (0,)), ((), ())),
            preferred_element_type=F32,
        )
        for n, (row, column) in enumerate(blocks_of(aux_count)):
            if not panel <= row < panel + height:
                continue
            down, across = (row - panel) * LANES, (column - panel) * LANES
            tile = gram[down : down + LANES, across : across + LANES]
            left = jnp.broadcast_to(coulomb[:, row * LANES : (row + 1) * LANES], (LANES, LANES)).T
            right = coulomb[:, column * LANES : (column + 1) * LANES]
            gram_ref[n] = (left * tile * right).astype(BF16)


def project(occ, own, other, basis, occ_energy, levels, coulomb, scale):
    local_k, occ_count, grid_count = occ.shape
    group_count = own.shape[1]
    aux_count = basis.shape[0]
    rows = 2 * local_k * occ_count * group_count
    blocks = len(blocks_of(aux_count))
    starts = (0, grid_count // 8, 3 * grid_count // 8)
    return pl.pallas_call(
        functools.partial(project_kernel, scale=scale, starts=starts),
        in_specs=[VMEM_SPEC] * 6 + [pl.BlockSpec(memory_space=pl.ANY)],
        out_specs=[VMEM_SPEC] * 2,
        out_shape=[
            jax.ShapeDtypeStruct((rows, aux_count), BF16),
            jax.ShapeDtypeStruct((blocks, LANES, LANES), BF16),
        ],
        scratch_shapes=[
            pltpu.VMEM((rows, aux_count), BF16),
            pltpu.VMEM(basis.shape, BF16),
            pltpu.VMEM((rows, aux_count), F32),
            pltpu.SemaphoreType.DMA((len(starts),)),
        ],
        compiler_params=pltpu.CompilerParams(vmem_limit_bytes=KERNEL_VMEM),
        cost_estimate=pl.CostEstimate(
            flops=2 * rows * grid_count * aux_count, bytes_accessed=8 << 20, transcendentals=0
        ),
        name="project",
    )(occ, own, other, occ_energy, levels, coulomb, basis)


def screen_coeffs(coeffs_ref, packed_ref, screen_ref, screened_ref):
    for n, (row, column) in enumerate(blocks_of(coeffs_ref.shape[1])):
        tile = packed_ref[n]
        upper = slice(row * LANES, (row + 1) * LANES)
        lower = slice(column * LANES, (column + 1) * LANES)
        screen_ref[upper, lower] = tile
        if row != column:
            screen_ref[lower, upper] = tile.T
    screened_ref[...] = jnp.dot(
        coeffs_ref[...], screen_ref[...], preferred_element_type=F32
    ).astype(BF16)


def respond_half(screened_ref, basis_ref, held_ref, sems, inputs, outs, half, before=None):
    occ_ref, own_ref, other_ref = inputs
    term_ref, own_update_ref, other_update_ref = outs
    local_k, occ_count, _ = occ_ref.shape
    group_count = own_ref.shape[1]
    rows = occ_count * group_count
    span = term_ref.shape[2]
    width = held_ref.shape[2]

    def grid_of(step):
        return pl.ds(pl.multiple_of(half * span + step * width, width), width)

    def fetch(step):
        return pltpu.make_async_copy(
            basis_ref.at[:, grid_of(step)], held_ref.at[step], sems.at[step]
        )

    for step in range(span // width):
        fetch(step).start()
    if before is not None:
        before()

    def chunk(step, carry):
        to = pl.ds(pl.multiple_of(step * width, width), width)
        grid = grid_of(step)
        fetch(step).wait()
        for k in range(local_k):
            occ = occ_ref[k, :, grid].astype(F32)
            sums = [None] * occ_count
            sides = ((own_ref, own_update_ref), (other_ref, other_update_ref))
            for side, (virt_ref, update_ref) in enumerate(sides):
                virt = virt_ref[k, :, grid].astype(F32)
                term = side * local_k + k
                field = jnp.dot(
                    screened_ref[term * rows : (term + 1) * rows, :],
                    held_ref[step],
                    preferred_element_type=F32,
                ).astype(BF16)
                virt_term = None
                for i in range(occ_count):
                    piece = field[i * group_count : (i + 1) * group_count].astype(F32)
                    line = jnp.sum((piece * virt).reshape(group_count // 8, 8, width), axis=0)
                    sums[i] = line if side == 0 else sums[i] + line
                    product = piece * occ[i : i + 1]
                    virt_term = product if virt_term is None else virt_term + product
                update_ref[k, :, to] = virt_term.astype(BF16)
            term_ref[k, :, to] = jnp.concatenate(
                [jnp.sum(line, axis=0, keepdims=True) for line in sums], axis=0
            ).astype(BF16)
        return carry

    lax.fori_loop(0, span // width, chunk, 0)


def upper_half():
    return (lax.axis_index("band") // 2) % 2


def respond_far_kernel(
    coeffs_ref, packed_ref, occ_ref, own_ref, other_ref, basis_ref,
    term_ref, own_update_ref, other_update_ref, screened_ref, screen_ref, held_ref, sems,
):
    respond_half(
        screened_ref, basis_ref, held_ref, sems, (occ_ref, own_ref, other_ref),
        (term_ref, own_update_ref, other_update_ref), 1 - upper_half(),
        lambda: screen_coeffs(coeffs_ref, packed_ref, screen_ref, screened_ref),
    )


def respond_near_kernel(
    screened_ref, occ_ref, own_ref, other_ref, basis_ref,
    term_ref, own_update_ref, other_update_ref, held_ref, sems,
):
    respond_half(
        screened_ref, basis_ref, held_ref, sems, (occ_ref, own_ref, other_ref),
        (term_ref, own_update_ref, other_update_ref), upper_half(),
    )


def respond(coeffs, packed, basis, occ, own, other):
    local_k, occ_count, grid_count = occ.shape
    group_count = own.shape[1]
    rows, aux_count = coeffs.shape
    half = grid_count // 2
    width = min(512, half)
    any_spec = pl.BlockSpec(memory_space=pl.ANY)
    shapes = [
        jax.ShapeDtypeStruct((local_k, occ_count, half), BF16),
        jax.ShapeDtypeStruct((local_k, group_count, half), BF16),
        jax.ShapeDtypeStruct((local_k, group_count, half), BF16),
    ]
    held = [
        pltpu.VMEM((half // width, aux_count, width), BF16),
        pltpu.SemaphoreType.DMA((half // width,)),
    ]
    params = pltpu.CompilerParams(vmem_limit_bytes=KERNEL_VMEM)
    cost = pl.CostEstimate(
        flops=rows * grid_count * aux_count, bytes_accessed=4 << 20, transcendentals=0
    )
    *far, screened = pl.pallas_call(
        respond_far_kernel,
        in_specs=[VMEM_SPEC] * 5 + [any_spec],
        out_specs=[VMEM_SPEC] * 4,
        out_shape=shapes + [jax.ShapeDtypeStruct(coeffs.shape, BF16)],
        scratch_shapes=[pltpu.VMEM((aux_count, aux_count), BF16)] + held,
        compiler_params=params,
        cost_estimate=cost,
        name="respond_far",
    )(coeffs, packed, occ, own, other, basis)
    near = pl.pallas_call(
        respond_near_kernel,
        in_specs=[VMEM_SPEC] * 4 + [any_spec],
        out_specs=[VMEM_SPEC] * 3,
        out_shape=shapes,
        scratch_shapes=held,
        compiler_params=params,
        cost_estimate=cost,
        name="respond_near",
    )(screened, occ, own, other, basis)
    return far, near


def shards(occupied, virtual, occ_energy, virt_energy, partner, coulomb, basis):
    local_k, occ_count, grid_count = occupied.shape
    group_count = virtual.shape[1]
    aux_count = basis.shape[0]
    transfers = partner.shape[0]
    assert transfers == 2
    cube = Hypercube()
    total_k = local_k * cube.ka
    virt_count = group_count * cube.band
    gram_scale = 1.0 / math.sqrt(total_k * occ_count * virt_count * aux_count)
    occ_scale = 1.0 / math.sqrt(transfers * virt_count)
    ka = lax.axis_index("ka")

    first = cube.bit(cube.core) == 0
    other_virtual = cube.swap(virtual, cube.core)

    def level_rows(energy):
        rows = lax.dynamic_slice_in_dim(energy, ka * local_k, local_k, axis=0)
        return jnp.broadcast_to(rows[:, :, None], rows.shape + (LANES,))

    levels = jnp.concatenate(
        [level_rows(virt_energy), level_rows(cube.swap(virt_energy, cube.core))]
    )
    sources = partners_of(partner, ka, local_k)
    neighbour_sources = partners_of(partner, jnp.bitwise_xor(ka, 1), local_k)
    partner_occ, partner_energy = fetch_partners(
        cube, occupied, occ_energy, sources, neighbour_sources
    )
    partner_energy = jnp.broadcast_to(
        partner_energy[:, :, None], partner_energy.shape + (LANES,)
    )
    factors = jnp.where(first, coulomb[:1], coulomb[1:])
    coeffs, packed = project(
        partner_occ, virtual, other_virtual, basis, partner_energy, levels, factors, gram_scale
    )
    packed = reduce_screen(cube, packed)
    far, near = respond(coeffs, packed, basis, partner_occ, virtual, other_virtual)
    arrived = cube.swap(far[0], cube.y)
    terms = (near[0].astype(F32) + arrived.astype(F32)).astype(BF16)
    updates = [
        (own.astype(F32) + cube.swap(other, cube.core).astype(F32)).astype(BF16)
        for _, own, other in (far, near)
    ]
    lower = cube.bit(cube.y) == 0
    virt_update = jnp.concatenate(
        [jnp.where(lower, updates[1], updates[0]), jnp.where(lower, updates[0], updates[1])],
        axis=2,
    )
    occ_total, virt_update = return_occupied(
        cube, terms, local_k, sources, neighbour_sources, virt_update
    )
    return ((occ_total * occ_scale).astype(BF16), virt_update)


def solution(mesh):
    in_specs = (
        P("ka", None, None),
        P("ka", "band", None),
        P("ka", None),
        P(None, "band"),
        P(),
        P(),
        P(),
    )
    out_specs = (P("ka", None, "band"), P("ka", "band", None))
    return jax.shard_map(shards, mesh=mesh, in_specs=in_specs, out_specs=out_specs, check_vma=False)
```

time: 81.5 us -> 76.8 us (0.942)
  waiting for transfers between devices: 33.3 us -> 26.9 us
    ppermute x22 -> x24, waiting for transfers between devices: 33.3 us -> 26.9 us  [swap(): lax.ppermute(value, ('ka', 'band'), [(device, device ^ mask) for device i...]
    select_n x2 -> x6, other arithmetic: 0.05 us -> 1.05 us  [the longest x1 0.77 us: shards(): factors = jnp.where(first, coulomb[:1], coulomb[1:])]
    ppermute x22 -> x24, starting transfers between devices: 24.4 us -> 25.2 us  [swap(): lax.ppermute(value, ('ka', 'band'), [(device, device ^ mask) for device i...]
  transfers between devices with their start and end apart: 22 -> 24, of which waited for: 19 -> 14; matrix products, arithmetic and copies ran while one was open for 3% -> 7% of each run, Pallas kernels for 5% -> 5%
where the time goes in v4:
time: 76.8 us; the launch traced here: 76.5 us
  waiting for transfers between devices  26.9 us (35%)
  starting transfers between devices  25.2 us (33%)
  Pallas kernels  15.5 us (20%)
  other arithmetic  6.76 us (9%)
  local copies, waits for them, and re-layouts  1.27 us (2%)
  between operations  0.94 us (1%)
    ppermute x24, waiting for transfers between devices, swap(): lax.ppermute(value, ('ka', 'band'), [(device, device ^ mask) for device i...  26.9 us
    ppermute x24, starting transfers between devices, swap(): lax.ppermute(value, ('ka', 'band'), [(device, device ^ mask) for device i...  25.2 us
    pallas_call x1, Pallas kernels, project(): pl.pallas_call(functools.partial(project_kernel, scale=scale, starts=star...  6.45 us
    pallas_call x1, Pallas kernels, respond(): pl.pallas_call(respond_far_kernel, in_specs=[VMEM_SPEC] * 5 + [any_spec],...  4.83 us
    pallas_call x1, Pallas kernels, respond(): pl.pallas_call(respond_near_kernel, in_specs=[VMEM_SPEC] * 4 + [any_spec]...  4.2 us
  transfers between devices with their start and end apart: 24, of which 14 were waited for; matrix products, arithmetic and copies ran while one was open for 7% of the time, Pallas kernels for 5%

profile of v4, /device:TPU:0, one launch (start us, length us, event | category | flops | bytes accessed | tf_op | source)
XLA Modules:
  0.0 76.5 jit_solution(8965410540580041263)
XLA Ops:
  2.4 5.1 %collective-permute-start.2 = (bf16[1,2,8,2176]{3,2,1,0:T(8,128)(2,1)S(1)}, bf16[1,2,8,2176]{3,2,1,0:T(8,128)(2,1)S(1)}, u32[]{:S(2)}, u32[]{:S(2)}) collective-permute-start(bf16[1,2,8,2176]{3,2,1,0:T(8,128)(2,1)S(1)} %get-tuple-element.46), channel_id=1, source_target_pairs={{0,24},{1,25},{2,26},{3,27},{4,28},{5,29},{6,30},{7,31},{8,16},{9,... | collective-permute-start | bytes 208904 | tf_op jit(solution)/shard_map/ppermute | solution.py:44
  11.5 2.0 %collective-permute-done.1 = bf16[1,2,8,2176]{3,2,1,0:T(8,128)(2,1)S(1)} collective-permute-done((bf16[1,2,8,2176]{3,2,1,0:T(8,128)(2,1)S(1)}, bf16[1,2,8,2176]{3,2,1,0:T(8,128)(2,1)S(1)}, u32[]{:S(2)}, u32[]{:S(2)}) %collective-permute-start.1) | collective-permute-done | bytes 69664 | tf_op jit(solution)/shard_map/ppermute | solution.py:44
  14.1 1.6 %collective-permute-start.3 = (bf16[4,8,2176]{2,1,0:T(8,128)(2,1)S(1)}, bf16[4,8,2176]{2,1,0:T(8,128)(2,1)S(1)}, u32[]{:S(2)}, u32[]{:S(2)}) collective-permute-start(bf16[4,8,2176]{2,1,0:T(8,128)(2,1)S(1)} %get-tuple-element.25), channel_id=1, source_target_pairs={{0,4},{1,5},{2,6},{3,7},{4,0},{5,1},{6,2},{7,3},{8,12},{9,13},{10,... | collective-permute-start | bytes 417800 | tf_op jit(solution)/shard_map/ppermute | solution.py:44
  15.8 3.4 %collective-permute-done.3 = bf16[4,8,2176]{2,1,0:T(8,128)(2,1)S(1)} collective-permute-done((bf16[4,8,2176]{2,1,0:T(8,128)(2,1)S(1)}, bf16[4,8,2176]{2,1,0:T(8,128)(2,1)S(1)}, u32[]{:S(2)}, u32[]{:S(2)}) %collective-permute-start.3) | collective-permute-done | bytes 139296 | tf_op jit(solution)/shard_map/ppermute | solution.py:44
  19.6 1.1 %collective-permute-done.4 = bf16[2,8,2048]{2,1,0:T(8,128)(2,1)S(1)} collective-permute-done((bf16[2,8,2048]{2,1,0:T(8,128)(2,1)S(1)}, bf16[2,8,2048]{2,1,0:T(8,128)(2,1)S(1)}, u32[]{:S(2)}, u32[]{:S(2)}) %collective-permute-start.4) | collective-permute-done | bytes 65568 | tf_op jit(solution)/shard_map/ppermute | solution.py:44
  20.8 6.5 %project.1 = (bf16[1024,512]{1,0:T(8,128)(2,1)S(1)}, bf16[10,128,128]{2,1,0:T(8,128)(2,1)S(1)}) custom-call(bf16[2,8,4096]{2,1,0:T(8,128)(2,1)S(1)} %pad_maximum_fusion.4.occ_ref, bf16[2,32,4096]{2,1,0:T(8,128)(2,1)S(1)} %copy-done, bf16[2,32,4096]{2,1,0:T(8,128)(2,1)S(1)} %collective-permute-done.5.other_ref, ...), custom_call_target="tpu_custom_call" | custom-call | flops 4294967296 | bytes 8388608 | tf_op jit(solution)/shard_map/project/pallas_call | solution.py:271
  27.3 1.8 %collective-permute-start.7 = (bf16[320,128]{1,0:T(8,128)(2,1)S(1)}, bf16[320,128]{1,0:T(8,128)(2,1)S(1)}, u32[]{:S(2)}, u32[]{:S(2)}) collective-permute-start(bf16[320,128]{1,0:T(8,128)(2,1)S(1)} %get-tuple-element.34), channel_id=1, source_target_pairs={{0,2},{1,3},{2,0},{3,1},{4,6},{5,7},{6,4},{7,5},{8,10},{9,11},{10,... | collective-permute-start | bytes 245768 | tf_op jit(solution)/shard_map/ppermute | solution.py:44
  29.1 1.4 %collective-permute-start.9 = (bf16[320,128]{1,0:T(8,128)(2,1)S(1)}, bf16[320,128]{1,0:T(8,128)(2,1)S(1)}, u32[]{:S(2)}, u32[]{:S(2)}) collective-permute-start(bf16[320,128]{1,0:T(8,128)(2,1)S(1)} %get-tuple-element.35), channel_id=1, source_target_pairs={{0,6},{1,7},{2,4},{3,5},{4,2},{5,3},{6,0},{7,1},{8,14},{9,15},{10,... | collective-permute-start | bytes 245768 | tf_op jit(solution)/shard_map/ppermute | solution.py:44
  30.8 1.9 %collective-permute-done.7 = bf16[320,128]{1,0:T(8,128)(2,1)S(1)} collective-permute-done((bf16[320,128]{1,0:T(8,128)(2,1)S(1)}, bf16[320,128]{1,0:T(8,128)(2,1)S(1)}, u32[]{:S(2)}, u32[]{:S(2)}) %collective-permute-start.7) | collective-permute-done | bytes 81952 | tf_op jit(solution)/shard_map/ppermute | solution.py:44
  32.8 2.4 %collective-permute-done.9 = bf16[320,128]{1,0:T(8,128)(2,1)S(1)} collective-permute-done((bf16[320,128]{1,0:T(8,128)(2,1)S(1)}, bf16[320,128]{1,0:T(8,128)(2,1)S(1)}, u32[]{:S(2)}, u32[]{:S(2)}) %collective-permute-start.9) | collective-permute-done | bytes 81952 | tf_op jit(solution)/shard_map/ppermute | solution.py:44
  35.2 2.6 %collective-permute-start.12 = (bf16[320,128]{1,0:T(8,128)(2,1)S(1)}, bf16[320,128]{1,0:T(8,128)(2,1)S(1)}, u32[]{:S(2)}, u32[]{:S(2)}) collective-permute-start(bf16[320,128]{1,0:T(8,128)(2,1)S(1)} %fusion.2), channel_id=1, source_target_pairs={{0,24},{1,25},{2,26},{3,27},{4,28},{5,29},{6,30},{7,31},{8,16},{9,... | collective-permute-start | bytes 245768 | tf_op jit(solution)/shard_map/ppermute | solution.py:44
  37.8 1.8 %collective-permute-start.10 = (bf16[320,128]{1,0:T(8,128)(2,1)S(1)}, bf16[320,128]{1,0:T(8,128)(2,1)S(1)}, u32[]{:S(2)}, u32[]{:S(2)}) collective-permute-start(bf16[320,128]{1,0:T(8,128)(2,1)S(1)} %fusion.2), channel_id=1, source_target_pairs={{0,8},{1,9},{2,10},{3,11},{4,12},{5,13},{6,14},{7,15},{8,0},{9,1},... | collective-permute-start | bytes 245768 | tf_op jit(solution)/shard_map/ppermute | solution.py:44
  39.7 1.9 %collective-permute-done.12 = bf16[320,128]{1,0:T(8,128)(2,1)S(1)} collective-permute-done((bf16[320,128]{1,0:T(8,128)(2,1)S(1)}, bf16[320,128]{1,0:T(8,128)(2,1)S(1)}, u32[]{:S(2)}, u32[]{:S(2)}) %collective-permute-start.12) | collective-permute-done | bytes 81952 | tf_op jit(solution)/shard_map/ppermute | solution.py:44
  41.5 3.4 %collective-permute-done.11 = bf16[320,128]{1,0:T(8,128)(2,1)S(1)} collective-permute-done((bf16[320,128]{1,0:T(8,128)(2,1)S(1)}, bf16[320,128]{1,0:T(8,128)(2,1)S(1)}, u32[]{:S(2)}, u32[]{:S(2)}) %collective-permute-start.11) | collective-permute-done | bytes 81952 | tf_op jit(solution)/shard_map/ppermute | solution.py:44
  45.0 2.2 %collective-permute-start.15 = (bf16[320,128]{1,0:T(8,128)(2,1)S(1)}, bf16[320,128]{1,0:T(8,128)(2,1)S(1)}, u32[]{:S(2)}, u32[]{:S(2)}) collective-permute-start(bf16[320,128]{1,0:T(8,128)(2,1)S(1)} %add_convert_fusion.2), channel_id=1, source_target_pairs={{0,6},{1,7},{2,4},{3,5},{4,2},{5,3},{6,0},{7,1},{8,14},{9,15},{10,... | collective-permute-start | bytes 245768 | tf_op jit(solution)/shard_map/ppermute | solution.py:44
  47.2 1.1 %collective-permute-start.14 = (bf16[320,128]{1,0:T(8,128)(2,1)S(1)}, bf16[320,128]{1,0:T(8,128)(2,1)S(1)}, u32[]{:S(2)}, u32[]{:S(2)}) collective-permute-start(bf16[320,128]{1,0:T(8,128)(2,1)S(1)} %add_convert_fusion.2), channel_id=1, source_target_pairs={{0,4},{1,5},{2,6},{3,7},{4,0},{5,1},{6,2},{7,3},{8,12},{9,13},{10,... | collective-permute-start | bytes 245768 | tf_op jit(solution)/shard_map/ppermute | solution.py:44
  48.6 2.0 %collective-permute-done.15 = bf16[320,128]{1,0:T(8,128)(2,1)S(1)} collective-permute-done((bf16[320,128]{1,0:T(8,128)(2,1)S(1)}, bf16[320,128]{1,0:T(8,128)(2,1)S(1)}, u32[]{:S(2)}, u32[]{:S(2)}) %collective-permute-start.15) | collective-permute-done | bytes 81952 | tf_op jit(solution)/shard_map/ppermute | solution.py:44
  52.9 4.8 %respond_far.1 = (bf16[2,8,2048]{2,1,0:T(8,128)(2,1)S(1)}, bf16[2,32,2048]{2,1,0:T(8,128)(2,1)S(1)}, bf16[2,32,2048]{2,1,0:T(8,128)(2,1)S(1)}, bf16[1024,512]{1,0:T(8,128)(2,1)S(1)}) custom-call(bf16[1024,512]{1,0:T(8,128)(2,1)S(1)} %get-tuple-element.13.coeffs_ref, bf16[10,128,128]{2,1,0:T(8,128)(2,1)S(1)} %bitcast.43, ...), custom_call_target="tpu_custom_call" | custom-call | flops 2147483648 | bytes 4194304 | tf_op jit(solution)/shard_map/respond_far/pallas_call | solution.py:405
  58.2 4.2 %respond_near.1 = (bf16[2,8,2048]{2,1,0:T(8,128)(2,1)S(1)}, bf16[2,32,2048]{2,1,0:T(8,128)(2,1)S(1)}, bf16[2,32,2048]{2,1,0:T(8,128)(2,1)S(1)}) custom-call(bf16[1024,512]{1,0:T(8,128)(2,1)S(1)} %get-tuple-element.15.screened_ref, bf16[2,8,4096]{2,1,0:T(8,128)(2,1)S(1)} %pad_maximum_fusion.4.occ_ref, bf16[2,32,4096]{2,1,0:T(8,128)(2,1)S(1)} %copy-done, ...), custom_call_target="tpu_custom_call" | custom-call | flops 2147483648 | bytes 4194304 | tf_op jit(solution)/shard_map/respond_near/pallas_call | solution.py:415
  62.6 1.1 %collective-permute-done.17 = bf16[2,8,1024]{2,1,0:T(8,128)(2,1)S(1)} collective-permute-done((bf16[2,8,1024]{2,1,0:T(8,128)(2,1)S(1)}, bf16[2,8,1024]{2,1,0:T(8,128)(2,1)S(1)}, u32[]{:S(2)}, u32[]{:S(2)}) %collective-permute-start.17) | collective-permute-done | bytes 32800 | tf_op jit(solution)/shard_map/ppermute | solution.py:44
  65.4 2.7 %collective-permute-done.18 = bf16[4,8,1024]{2,1,0:T(8,128)(2,1)S(1)} collective-permute-done((bf16[4,8,1024]{2,1,0:T(8,128)(2,1)S(1)}, bf16[4,8,1024]{2,1,0:T(8,128)(2,1)S(1)}, u32[]{:S(2)}, u32[]{:S(2)}) %collective-permute-start.18) | collective-permute-done | bytes 65568 | tf_op jit(solution)/shard_map/ppermute | solution.py:44
  68.5 2.6 %collective-permute-start.21 = (bf16[1,2,8,1024]{3,2,1,0:T(8,128)(2,1)S(1)}, bf16[1,2,8,1024]{3,2,1,0:T(8,128)(2,1)S(1)}, u32[]{:S(2)}, u32[]{:S(2)}) collective-permute-start(bf16[1,2,8,1024]{3,2,1,0:T(8,128)(2,1)S(1)} %get-tuple-element.43), channel_id=1, source_target_pairs={{0,24},{1,25},{2,26},{3,27},{4,28},{5,29},{6,30},{7,31},{8,16},{9,... | collective-permute-start | bytes 98312 | tf_op jit(solution)/shard_map/ppermute | solution.py:44
  73.0 1.3 %collective-permute-done.21 = bf16[1,2,8,1024]{3,2,1,0:T(8,128)(2,1)S(1)} collective-permute-done((bf16[1,2,8,1024]{3,2,1,0:T(8,128)(2,1)S(1)}, bf16[1,2,8,1024]{3,2,1,0:T(8,128)(2,1)S(1)}, u32[]{:S(2)}, u32[]{:S(2)}) %collective-permute-start.21) | collective-permute-done | bytes 32800 | tf_op jit(solution)/shard_map/ppermute | solution.py:44
  74.3 1.6 %collective-permute-done.20 = bf16[1,2,8,1024]{3,2,1,0:T(8,128)(2,1)S(1)} collective-permute-done((bf16[1,2,8,1024]{3,2,1,0:T(8,128)(2,1)S(1)}, bf16[1,2,8,1024]{3,2,1,0:T(8,128)(2,1)S(1)}, u32[]{:S(2)}, u32[]{:S(2)}) %collective-permute-start.20) | collective-permute-done | bytes 32800 | tf_op jit(solution)/shard_map/ppermute | solution.py:44
  (83 shorter events, 15.1 us)
Async XLA Ops:
  2.4 9.1 %collective-permute-start.2 = (bf16[1,2,8,2176]{3,2,1,0:T(8,128)(2,1)S(1)}, bf16[1,2,8,2176]{3,2,1,0:T(8,128)(2,1)S(1)}, u32[]{:S(2)}, u32[]{:S(2)}) collective-permute-start(bf16[1,2,8,2176]{3,2,1,0:T(8,128)(2,1)S(1)} %get-tuple-element.46), channel_id=1, source_target_pairs={{0,24},{1,25},{2,26},{3,27},{4,28},{5,29},{6,30},{7,31},{8,16},{9,... | collective-permute-start | bytes 208904 | tf_op jit(solution)/shard_map/ppermute | solution.py:44
  7.5 5.9 %collective-permute-start.1 = (bf16[1,2,8,2176]{3,2,1,0:T(8,128)(2,1)S(1)}, bf16[1,2,8,2176]{3,2,1,0:T(8,128)(2,1)S(1)}, u32[]{:S(2)}, u32[]{:S(2)}) collective-permute-start(bf16[1,2,8,2176]{3,2,1,0:T(8,128)(2,1)S(1)} %get-tuple-element.46), channel_id=1, source_target_pairs={{0,16},{1,17},{2,18},{3,19},{4,20},{5,21},{6,22},{7,23},{8,24},{9,... | collective-permute-start | bytes 208904 | tf_op jit(solution)/shard_map/ppermute | solution.py:44
  7.5 5.9 %collective-permute-start = (bf16[1,2,8,2176]{3,2,1,0:T(8,128)(2,1)S(1)}, bf16[1,2,8,2176]{3,2,1,0:T(8,128)(2,1)S(1)}, u32[]{:S(2)}, u32[]{:S(2)}) collective-permute-start(bf16[1,2,8,2176]{3,2,1,0:T(8,128)(2,1)S(1)} %get-tuple-element.46), channel_id=1, source_target_pairs={{0,8},{1,9},{2,10},{3,11},{4,12},{5,13},{6,14},{7,15},{8,0},{9,1},... | collective-permute-start | bytes 208904 | tf_op jit(solution)/shard_map/ppermute | solution.py:44
  8.2 7.5 %collective-permute-start.6 = (f32[16,32]{1,0:T(8,128)}, f32[16,32]{1,0:T(8,128)S(1)}, u32[]{:S(2)}, u32[]{:S(2)}) collective-permute-start(f32[16,32]{1,0:T(8,128)} %param.10), channel_id=1, source_target_pairs={{0,1},{1,0},{2,3},{3,2},{4,5},{5,4},{6,7},{7,6},{8,9},{9,8},{10,11... | collective-permute-start | bytes 6152 | tf_op jit(solution)/shard_map/ppermute | solution.py:44
  8.2 12.5 %collective-permute-start.5 = (bf16[2,32,4096]{2,1,0:T(8,128)(2,1)}, bf16[2,32,4096]{2,1,0:T(8,128)(2,1)S(1)}, u32[]{:S(2)}, u32[]{:S(2)}) collective-permute-start(bf16[2,32,4096]{2,1,0:T(8,128)(2,1)} %own_ref.5), channel_id=1, source_target_pairs={{0,1},{1,0},{2,3},{3,2},{4,5},{5,4},{6,7},{7,6},{8,9},{9,8},{10,11... | collective-permute-start | bytes 1572872 | tf_op jit(solution)/shard_map/ppermute | solution.py:44
  14.1 5.1 %collective-permute-start.3 = (bf16[4,8,2176]{2,1,0:T(8,128)(2,1)S(1)}, bf16[4,8,2176]{2,1,0:T(8,128)(2,1)S(1)}, u32[]{:S(2)}, u32[]{:S(2)}) collective-permute-start(bf16[4,8,2176]{2,1,0:T(8,128)(2,1)S(1)} %get-tuple-element.25), channel_id=1, source_target_pairs={{0,4},{1,5},{2,6},{3,7},{4,0},{5,1},{6,2},{7,3},{8,12},{9,13},{10,... | collective-permute-start | bytes 417800 | tf_op jit(solution)/shard_map/ppermute | solution.py:44
  19.3 1.3 %collective-permute-start.4 = (bf16[2,8,2048]{2,1,0:T(8,128)(2,1)S(1)}, bf16[2,8,2048]{2,1,0:T(8,128)(2,1)S(1)}, u32[]{:S(2)}, u32[]{:S(2)}) collective-permute-start(bf16[2,8,2048]{2,1,0:T(8,128)(2,1)S(1)} %slice_select_fusion), channel_id=1, source_target_pairs={{0,1},{1,0},{2,3},{3,2},{4,5},{5,4},{6,7},{7,6},{8,9},{9,8},{10,11... | collective-permute-start | bytes 196616 | tf_op jit(solution)/shard_map/ppermute | solution.py:44
  27.3 5.5 %collective-permute-start.7 = (bf16[320,128]{1,0:T(8,128)(2,1)S(1)}, bf16[320,128]{1,0:T(8,128)(2,1)S(1)}, u32[]{:S(2)}, u32[]{:S(2)}) collective-permute-start(bf16[320,128]{1,0:T(8,128)(2,1)S(1)} %get-tuple-element.34), channel_id=1, source_target_pairs={{0,2},{1,3},{2,0},{3,1},{4,6},{5,7},{6,4},{7,5},{8,10},{9,11},{10,... | collective-permute-start | bytes 245768 | tf_op jit(solution)/shard_map/ppermute | solution.py:44
  29.1 6.1 %collective-permute-start.9 = (bf16[320,128]{1,0:T(8,128)(2,1)S(1)}, bf16[320,128]{1,0:T(8,128)(2,1)S(1)}, u32[]{:S(2)}, u32[]{:S(2)}) collective-permute-start(bf16[320,128]{1,0:T(8,128)(2,1)S(1)} %get-tuple-element.35), channel_id=1, source_target_pairs={{0,6},{1,7},{2,4},{3,5},{4,2},{5,3},{6,0},{7,1},{8,14},{9,15},{10,... | collective-permute-start | bytes 245768 | tf_op jit(solution)/shard_map/ppermute | solution.py:44
  30.5 4.7 %collective-permute-start.8 = (bf16[320,128]{1,0:T(8,128)(2,1)S(1)}, bf16[320,128]{1,0:T(8,128)(2,1)S(1)}, u32[]{:S(2)}, u32[]{:S(2)}) collective-permute-start(bf16[320,128]{1,0:T(8,128)(2,1)S(1)} %get-tuple-element.36), channel_id=1, source_target_pairs={{0,4},{1,5},{2,6},{3,7},{4,0},{5,1},{6,2},{7,3},{8,12},{9,13},{10,... | collective-permute-start | bytes 245768 | tf_op jit(solution)/shard_map/ppermute | solution.py:44
  35.2 6.3 %collective-permute-start.12 = (bf16[320,128]{1,0:T(8,128)(2,1)S(1)}, bf16[320,128]{1,0:T(8,128)(2,1)S(1)}, u32[]{:S(2)}, u32[]{:S(2)}) collective-permute-start(bf16[320,128]{1,0:T(8,128)(2,1)S(1)} %fusion.2), channel_id=1, source_target_pairs={{0,24},{1,25},{2,26},{3,27},{4,28},{5,29},{6,30},{7,31},{8,16},{9,... | collective-permute-start | bytes 245768 | tf_op jit(solution)/shard_map/ppermute | solution.py:44
  37.8 7.1 %collective-permute-start.11 = (bf16[320,128]{1,0:T(8,128)(2,1)S(1)}, bf16[320,128]{1,0:T(8,128)(2,1)S(1)}, u32[]{:S(2)}, u32[]{:S(2)}) collective-permute-start(bf16[320,128]{1,0:T(8,128)(2,1)S(1)} %fusion.2), channel_id=1, source_target_pairs={{0,16},{1,17},{2,18},{3,19},{4,20},{5,21},{6,22},{7,23},{8,24},{9,... | collective-permute-start | bytes 245768 | tf_op jit(solution)/shard_map/ppermute | solution.py:44
  37.8 7.1 %collective-permute-start.10 = (bf16[320,128]{1,0:T(8,128)(2,1)S(1)}, bf16[320,128]{1,0:T(8,128)(2,1)S(1)}, u32[]{:S(2)}, u32[]{:S(2)}) collective-permute-start(bf16[320,128]{1,0:T(8,128)(2,1)S(1)} %fusion.2), channel_id=1, source_target_pairs={{0,8},{1,9},{2,10},{3,11},{4,12},{5,13},{6,14},{7,15},{8,0},{9,1},... | collective-permute-start | bytes 245768 | tf_op jit(solution)/shard_map/ppermute | solution.py:44
  45.0 5.7 %collective-permute-start.15 = (bf16[320,128]{1,0:T(8,128)(2,1)S(1)}, bf16[320,128]{1,0:T(8,128)(2,1)S(1)}, u32[]{:S(2)}, u32[]{:S(2)}) collective-permute-start(bf16[320,128]{1,0:T(8,128)(2,1)S(1)} %add_convert_fusion.2), channel_id=1, source_target_pairs={{0,6},{1,7},{2,4},{3,5},{4,2},{5,3},{6,0},{7,1},{8,14},{9,15},{10,... | collective-permute-start | bytes 245768 | tf_op jit(solution)/shard_map/ppermute | solution.py:44
  47.2 4.5 %collective-permute-start.14 = (bf16[320,128]{1,0:T(8,128)(2,1)S(1)}, bf16[320,128]{1,0:T(8,128)(2,1)S(1)}, u32[]{:S(2)}, u32[]{:S(2)}) collective-permute-start(bf16[320,128]{1,0:T(8,128)(2,1)S(1)} %add_convert_fusion.2), channel_id=1, source_target_pairs={{0,4},{1,5},{2,6},{3,7},{4,0},{5,1},{6,2},{7,3},{8,12},{9,13},{10,... | collective-permute-start | bytes 245768 | tf_op jit(solution)/shard_map/ppermute | solution.py:44
  48.3 4.4 %collective-permute-start.13 = (bf16[320,128]{1,0:T(8,128)(2,1)S(1)}, bf16[320,128]{1,0:T(8,128)(2,1)S(1)}, u32[]{:S(2)}, u32[]{:S(2)}) collective-permute-start(bf16[320,128]{1,0:T(8,128)(2,1)S(1)} %add_convert_fusion.2), channel_id=1, source_target_pairs={{0,2},{1,3},{2,0},{3,1},{4,6},{5,7},{6,4},{7,5},{8,10},{9,11},{10,... | collective-permute-start | bytes 245768 | tf_op jit(solution)/shard_map/ppermute | solution.py:44
  57.7 4.7 %collective-permute-start.16 = (bf16[2,8,2048]{2,1,0:T(8,128)(2,1)S(1)}, bf16[2,8,2048]{2,1,0:T(8,128)(2,1)S(1)}, u32[]{:S(2)}, u32[]{:S(2)}) collective-permute-start(bf16[2,8,2048]{2,1,0:T(8,128)(2,1)S(1)} %get-tuple-element.17), channel_id=1, source_target_pairs={{0,2},{1,3},{2,0},{3,1},{4,6},{5,7},{6,4},{7,5},{8,10},{9,11},{10,... | collective-permute-start | bytes 196616 | tf_op jit(solution)/shard_map/ppermute | solution.py:44
  62.5 1.3 %collective-permute-start.17 = (bf16[2,8,1024]{2,1,0:T(8,128)(2,1)S(1)}, bf16[2,8,1024]{2,1,0:T(8,128)(2,1)S(1)}, u32[]{:S(2)}, u32[]{:S(2)}) collective-permute-start(bf16[2,8,1024]{2,1,0:T(8,128)(2,1)S(1)} %get-tuple-element.48), channel_id=1, source_target_pairs={{0,1},{1,0},{2,3},{3,2},{4,5},{5,4},{6,7},{7,6},{8,9},{9,8},{10,11... | collective-permute-start | bytes 98312 | tf_op jit(solution)/shard_map/ppermute | solution.py:44
  63.8 4.3 %collective-permute-start.18 = (bf16[4,8,1024]{2,1,0:T(8,128)(2,1)S(1)}, bf16[4,8,1024]{2,1,0:T(8,128)(2,1)S(1)}, u32[]{:S(2)}, u32[]{:S(2)}) collective-permute-start(bf16[4,8,1024]{2,1,0:T(8,128)(2,1)S(1)} %pad_maximum_fusion.6), channel_id=1, source_target_pairs={{0,4},{1,5},{2,6},{3,7},{4,0},{5,1},{6,2},{7,3},{8,12},{9,13},{10,... | collective-permute-start | bytes 196616 | tf_op jit(solution)/shard_map/ppermute | solution.py:44
  64.9 7.1 %collective-permute-start.22 = (bf16[2,32,2048]{2,1,0:T(8,128)(2,1)S(1)}, bf16[2,32,2048]{2,1,0:T(8,128)(2,1)S(1)}, u32[]{:S(2)}, u32[]{:S(2)}) collective-permute-start(bf16[2,32,2048]{2,1,0:T(8,128)(2,1)S(1)} %get-tuple-element.19), channel_id=1, source_target_pairs={{0,1},{1,0},{2,3},{3,2},{4,5},{5,4},{6,7},{7,6},{8,9},{9,8},{10,11... | collective-permute-start | bytes 786440 | tf_op jit(solution)/shard_map/ppermute | solution.py:44
  65.0 7.0 %collective-permute-start.23 = (bf16[2,32,2048]{2,1,0:T(8,128)(2,1)S(1)}, bf16[2,32,2048]{2,1,0:T(8,128)(2,1)S(1)}, u32[]{:S(2)}, u32[]{:S(2)}) collective-permute-start(bf16[2,32,2048]{2,1,0:T(8,128)(2,1)S(1)} %get-tuple-element.21), channel_id=1, source_target_pairs={{0,1},{1,0},{2,3},{3,2},{4,5},{5,4},{6,7},{7,6},{8,9},{9,8},{10,11... | collective-permute-start | bytes 786440 | tf_op jit(solution)/shard_map/ppermute | solution.py:44
  68.4 5.9 %collective-permute-start.19 = (bf16[1,2,8,1024]{3,2,1,0:T(8,128)(2,1)S(1)}, bf16[1,2,8,1024]{3,2,1,0:T(8,128)(2,1)S(1)}, u32[]{:S(2)}, u32[]{:S(2)}) collective-permute-start(bf16[1,2,8,1024]{3,2,1,0:T(8,128)(2,1)S(1)} %get-tuple-element.42), channel_id=1, source_target_pairs={{0,8},{1,9},{2,10},{3,11},{4,12},{5,13},{6,14},{7,15},{8,0},{9,1},... | collective-permute-start | bytes 98312 | tf_op jit(solution)/shard_map/ppermute | solution.py:44
  68.5 5.8 %collective-permute-start.21 = (bf16[1,2,8,1024]{3,2,1,0:T(8,128)(2,1)S(1)}, bf16[1,2,8,1024]{3,2,1,0:T(8,128)(2,1)S(1)}, u32[]{:S(2)}, u32[]{:S(2)}) collective-permute-start(bf16[1,2,8,1024]{3,2,1,0:T(8,128)(2,1)S(1)} %get-tuple-element.43), channel_id=1, source_target_pairs={{0,24},{1,25},{2,26},{3,27},{4,28},{5,29},{6,30},{7,31},{8,16},{9,... | collective-permute-start | bytes 98312 | tf_op jit(solution)/shard_map/ppermute | solution.py:44
  71.1 4.8 %collective-permute-start.20 = (bf16[1,2,8,1024]{3,2,1,0:T(8,128)(2,1)S(1)}, bf16[1,2,8,1024]{3,2,1,0:T(8,128)(2,1)S(1)}, u32[]{:S(2)}, u32[]{:S(2)}) collective-permute-start(bf16[1,2,8,1024]{3,2,1,0:T(8,128)(2,1)S(1)} %get-tuple-element.44), channel_id=1, source_target_pairs={{0,16},{1,17},{2,18},{3,19},{4,20},{5,21},{6,22},{7,23},{8,24},{9,... | collective-permute-start | bytes 98312 | tf_op jit(solution)/shard_map/ppermute | solution.py:44
  (1 other events, 18.4 us)

commit v5 on v4

--- a/solution.py
+++ b/solution.py
@@ -11,7 +11,9 @@
 FREQUENCY = 2.5
 BROADENING = 0.4
 LANES = 128
-KERNEL_VMEM = 48 << 20
+PROJECT_VMEM = 48 << 20
+FAR_VMEM = 45 << 20
+NEAR_VMEM = 32 << 20
 VMEM_SPEC = pl.BlockSpec(memory_space=pltpu.VMEM)
 BF16 = jnp.bfloat16
 F32 = jnp.float32
@@ -93,7 +95,7 @@
     return jnp.sum(jnp.where(here, partner[:, None, :], 0), axis=2).reshape(-1)
 
 
-def fetch_partners(cube, occupied, occ_energy, sources, neighbour_sources):
+def fetch_partners(cube, occupied, occ_energy, sources, neighbour_sources, beside):
     local_k, occ_count, grid_count = occupied.shape
     width = grid_count // 2
     ka = lax.axis_index("ka")
@@ -117,7 +119,9 @@
             jnp.where(hits[:, :, None, None], gathered[None].astype(F32), 0.0), axis=1
         ).astype(BF16)
 
-    chosen = held_of(sources) + cube.swap(held_of(neighbour_sources), cube.x)
+    received = cube.swap(held_of(neighbour_sources), cube.x)
+    received, beside = lax.optimization_barrier((received, beside))
+    chosen = held_of(sources) + received
     mine = jnp.where(first, chosen[:local_k], chosen[local_k:])
     theirs = jnp.where(first, chosen[local_k:], chosen[:local_k])
     energy = mine[:, :, width : width + 3].astype(F32)
@@ -125,7 +129,7 @@
     part = mine[:, :, :width]
     other = cube.swap(theirs[:, :, :width], cube.core)
     part = jnp.concatenate([jnp.where(first, part, other), jnp.where(first, other, part)], axis=2)
-    return part, energy
+    return part, energy, beside
 
 
 def reduce_screen(cube, own):
@@ -196,7 +200,7 @@
 
 
 def project_kernel(
-    occ_ref, own_ref, other_ref, occ_energy_ref, levels_ref, coulomb_ref, basis_ref,
+    occ_ref, own_ref, other_ref, occ_energy_ref, levels_ref, coulomb_ref, first_ref, basis_ref,
     coeffs_ref, gram_ref, weighted_ref, held_ref, total_ref, sems, *, scale, starts,
 ):
     local_k, occ_count, grid_count = occ_ref.shape
@@ -205,22 +209,28 @@
     rows = occ_count * group_count
     count = aux_count // LANES
     parts = list(zip(starts, starts[1:] + (grid_count,)))
-    copies = [
-        pltpu.make_async_copy(basis_ref.at[:, start:end], held_ref.at[:, start:end], sems.at[n])
-        for n, (start, end) in enumerate(parts)
+    offset = starts[1]
+    copies = [None] + [
+        pltpu.make_async_copy(
+            basis_ref.at[:, start:end],
+            held_ref.at[:, start - offset : end - offset],
+            sems.at[n],
+        )
+        for n, (start, end) in enumerate(parts[1:])
     ]
-    for copy in copies:
+    for copy in copies[1:]:
         copy.start()
     terms = [(virt_ref, k) for virt_ref in (own_ref, other_ref) for k in range(local_k)]
     for n, (start, end) in enumerate(parts):
-        copies[n].wait()
+        if n > 0:
+            copies[n].wait()
         for term, (virt_ref, k) in enumerate(terms):
             virt = virt_ref[k, :, start:end]
             occ = occ_ref[k, :, start:end]
             pair_rows = jnp.concatenate([occ[i : i + 1] * virt for i in range(occ_count)], axis=0)
             coeffs = lax.dot_general(
                 pair_rows,
-                held_ref[:, start:end],
+                held_ref[:, start - offset : end - offset] if n > 0 else first_ref[...],
                 (((1,), (1,)), ((), ())),
                 preferred_element_type=F32,
             )
@@ -261,16 +271,16 @@
             gram_ref[n] = (left * tile * right).astype(BF16)
 
 
-def project(occ, own, other, basis, occ_energy, levels, coulomb, scale):
+def project(occ, own, other, first, basis, occ_energy, levels, coulomb, scale):
     local_k, occ_count, grid_count = occ.shape
     group_count = own.shape[1]
     aux_count = basis.shape[0]
     rows = 2 * local_k * occ_count * group_count
     blocks = len(blocks_of(aux_count))
-    starts = (0, grid_count // 8, 3 * grid_count // 8)
+    starts = (0, first.shape[1], 3 * first.shape[1])
     return pl.pallas_call(
         functools.partial(project_kernel, scale=scale, starts=starts),
-        in_specs=[VMEM_SPEC] * 6 + [pl.BlockSpec(memory_space=pl.ANY)],
+        in_specs=[VMEM_SPEC] * 7 + [pl.BlockSpec(memory_space=pl.ANY)],
         out_specs=[VMEM_SPEC] * 2,
         out_shape=[
             jax.ShapeDtypeStruct((rows, aux_count), BF16),
@@ -278,16 +288,16 @@
         ],
         scratch_shapes=[
             pltpu.VMEM((rows, aux_count), BF16),
-            pltpu.VMEM(basis.shape, BF16),
+            pltpu.VMEM((aux_count, grid_count - starts[1]), BF16),
             pltpu.VMEM((rows, aux_count), F32),
-            pltpu.SemaphoreType.DMA((len(starts),)),
+            pltpu.SemaphoreType.DMA((len(starts) - 1,)),
         ],
-        compiler_params=pltpu.CompilerParams(vmem_limit_bytes=KERNEL_VMEM),
+        compiler_params=pltpu.CompilerParams(vmem_limit_bytes=PROJECT_VMEM),
         cost_estimate=pl.CostEstimate(
             flops=2 * rows * grid_count * aux_count, bytes_accessed=8 << 20, transcendentals=0
         ),
         name="project",
-    )(occ, own, other, occ_energy, levels, coulomb, basis)
+    )(occ, own, other, occ_energy, levels, coulomb, first, basis)
 
 
 def screen_coeffs(coeffs_ref, packed_ref, screen_ref, screened_ref):
@@ -303,7 +313,7 @@
     ).astype(BF16)
 
 
-def respond_half(screened_ref, basis_ref, held_ref, sems, inputs, outs, half, before=None):
+def respond_half(screened_ref, held_ref, field_ref, inputs, outs, half, arrived=None):
     occ_ref, own_ref, other_ref = inputs
     term_ref, own_update_ref, other_update_ref = outs
     local_k, occ_count, _ = occ_ref.shape
@@ -315,35 +325,25 @@
     def grid_of(step):
         return pl.ds(pl.multiple_of(half * span + step * width, width), width)
 
-    def fetch(step):
-        return pltpu.make_async_copy(
-            basis_ref.at[:, grid_of(step)], held_ref.at[step], sems.at[step]
-        )
-
-    for step in range(span // width):
-        fetch(step).start()
-    if before is not None:
-        before()
-
     def chunk(step, carry):
         to = pl.ds(pl.multiple_of(step * width, width), width)
         grid = grid_of(step)
-        fetch(step).wait()
+        if arrived is not None:
+            arrived(step)
+        field_ref[...] = jnp.dot(
+            screened_ref[...], held_ref[step], preferred_element_type=F32
+        ).astype(BF16)
         for k in range(local_k):
             occ = occ_ref[k, :, grid].astype(F32)
             sums = [None] * occ_count
             sides = ((own_ref, own_update_ref), (other_ref, other_update_ref))
             for side, (virt_ref, update_ref) in enumerate(sides):
                 virt = virt_ref[k, :, grid].astype(F32)
-                term = side * local_k + k
-                field = jnp.dot(
-                    screened_ref[term * rows : (term + 1) * rows, :],
-                    held_ref[step],
-                    preferred_element_type=F32,
-                ).astype(BF16)
+                first = (side * local_k + k) * rows
                 virt_term = None
                 for i in range(occ_count):
-                    piece = field[i * group_count : (i + 1) * group_count].astype(F32)
+                    here = slice(first + i * group_count, first + (i + 1) * group_count)
+                    piece = field_ref[here, :].astype(F32)
                     line = jnp.sum((piece * virt).reshape(group_count // 8, 8, width), axis=0)
                     sums[i] = line if side == 0 else sums[i] + line
                     product = piece * occ[i : i + 1]
@@ -363,21 +363,38 @@
 
 def respond_far_kernel(
     coeffs_ref, packed_ref, occ_ref, own_ref, other_ref, basis_ref,
-    term_ref, own_update_ref, other_update_ref, screened_ref, screen_ref, held_ref, sems,
+    term_ref, own_update_ref, other_update_ref, screened_ref, near_ref,
+    screen_ref, far_ref, field_ref, far_sems, near_sem,
+):
+    steps, _, width = far_ref.shape
+    far, near = 1 - upper_half(), upper_half()
+
+    def fetch(half, step, held_ref, sem):
+        start = pl.multiple_of((half * steps + step) * width, width)
+        return pltpu.make_async_copy(
+            basis_ref.at[:, pl.ds(start, width)], held_ref.at[step], sem
+        )
+
+    for step in range(steps):
+        fetch(far, step, far_ref, far_sems.at[step]).start()
+    for step in range(steps):
+        fetch(near, step, near_ref, near_sem.at[step]).start()
+    screen_coeffs(coeffs_ref, packed_ref, screen_ref, screened_ref)
+    respond_half(
+        screened_ref, far_ref, field_ref, (occ_ref, own_ref, other_ref),
+        (term_ref, own_update_ref, other_update_ref), far,
+        lambda step: fetch(far, step, far_ref, far_sems.at[step]).wait(),
+    )
+    for step in range(steps):
+        fetch(near, step, near_ref, near_sem.at[step]).wait()
+
+
+def respond_near_kernel(
+    screened_ref, occ_ref, own_ref, other_ref, near_ref,
+    term_ref, own_update_ref, other_update_ref, field_ref,
 ):
     respond_half(
-        screened_ref, basis_ref, held_ref, sems, (occ_ref, own_ref, other_ref),
-        (term_ref, own_update_ref, other_update_ref), 1 - upper_half(),
-        lambda: screen_coeffs(coeffs_ref, packed_ref, screen_ref, screened_ref),
-    )
-
-
-def respond_near_kernel(
-    screened_ref, occ_ref, own_ref, other_ref, basis_ref,
-    term_ref, own_update_ref, other_update_ref, held_ref, sems,
-):
-    respond_half(
-        screened_ref, basis_ref, held_ref, sems, (occ_ref, own_ref, other_ref),
+        screened_ref, near_ref, field_ref, (occ_ref, own_ref, other_ref),
         (term_ref, own_update_ref, other_update_ref), upper_half(),
     )
 
@@ -387,41 +404,44 @@
     group_count = own.shape[1]
     rows, aux_count = coeffs.shape
     half = grid_count // 2
-    width = min(512, half)
+    width = min(1024, half)
     any_spec = pl.BlockSpec(memory_space=pl.ANY)
     shapes = [
         jax.ShapeDtypeStruct((local_k, occ_count, half), BF16),
         jax.ShapeDtypeStruct((local_k, group_count, half), BF16),
         jax.ShapeDtypeStruct((local_k, group_count, half), BF16),
     ]
-    held = [
-        pltpu.VMEM((half // width, aux_count, width), BF16),
-        pltpu.SemaphoreType.DMA((half // width,)),
-    ]
-    params = pltpu.CompilerParams(vmem_limit_bytes=KERNEL_VMEM)
+    held = (half // width, aux_count, width)
     cost = pl.CostEstimate(
         flops=rows * grid_count * aux_count, bytes_accessed=4 << 20, transcendentals=0
     )
-    *far, screened = pl.pallas_call(
+    *far, screened, near_basis = pl.pallas_call(
         respond_far_kernel,
         in_specs=[VMEM_SPEC] * 5 + [any_spec],
-        out_specs=[VMEM_SPEC] * 4,
-        out_shape=shapes + [jax.ShapeDtypeStruct(coeffs.shape, BF16)],
-        scratch_shapes=[pltpu.VMEM((aux_count, aux_count), BF16)] + held,
-        compiler_params=params,
+        out_specs=[VMEM_SPEC] * 5,
+        out_shape=shapes
+        + [jax.ShapeDtypeStruct(coeffs.shape, BF16), jax.ShapeDtypeStruct(held, BF16)],
+        scratch_shapes=[
+            pltpu.VMEM((aux_count, aux_count), BF16),
+            pltpu.VMEM(held, BF16),
+            pltpu.VMEM((rows, width), BF16),
+            pltpu.SemaphoreType.DMA((held[0],)),
+            pltpu.SemaphoreType.DMA((held[0],)),
+        ],
+        compiler_params=pltpu.CompilerParams(vmem_limit_bytes=FAR_VMEM),
         cost_estimate=cost,
         name="respond_far",
     )(coeffs, packed, occ, own, other, basis)
     near = pl.pallas_call(
         respond_near_kernel,
-        in_specs=[VMEM_SPEC] * 4 + [any_spec],
+        in_specs=[VMEM_SPEC] * 5,
         out_specs=[VMEM_SPEC] * 3,
         out_shape=shapes,
-        scratch_shapes=held,
-        compiler_params=params,
+        scratch_shapes=[pltpu.VMEM((rows, width), BF16)],
+        compiler_params=pltpu.CompilerParams(vmem_limit_bytes=NEAR_VMEM),
         cost_estimate=cost,
         name="respond_near",
-    )(screened, occ, own, other, basis)
+    )(screened, occ, own, other, near_basis)
     return far, near
 
 
@@ -450,15 +470,16 @@
     )
     sources = partners_of(partner, ka, local_k)
     neighbour_sources = partners_of(partner, jnp.bitwise_xor(ka, 1), local_k)
-    partner_occ, partner_energy = fetch_partners(
-        cube, occupied, occ_energy, sources, neighbour_sources
+    partner_occ, partner_energy, first_basis = fetch_partners(
+        cube, occupied, occ_energy, sources, neighbour_sources, basis[:, : grid_count // 8]
     )
     partner_energy = jnp.broadcast_to(
         partner_energy[:, :, None], partner_energy.shape + (LANES,)
     )
     factors = jnp.where(first, coulomb[:1], coulomb[1:])
     coeffs, packed = project(
-        partner_occ, virtual, other_virtual, basis, partner_energy, levels, factors, gram_scale
+        partner_occ, virtual, other_virtual, first_basis, basis, partner_energy, levels, factors,
+        gram_scale,
     )
     packed = reduce_screen(cube, packed)
     far, near = respond(coeffs, packed, basis, partner_occ, virtual, other_virtual)

time: 76.8 us -> 75.4 us (0.982)
  Pallas kernels: 15.5 us -> 13.1 us
  local copies, waits for them, and re-layouts: 1.27 us -> 2.39 us
    pallas_call x1, Pallas kernels: 4.2 us -> 2.81 us  [respond(): pl.pallas_call(respond_near_kernel, in_specs=[VMEM_SPEC] * 5, out_specs=[...]
    slice x0 -> x1, local copies, waits for them, and re-layouts: none -> 1.08 us  [shards(): basis[:, :grid_count // 8]]
  transfers between devices with their start and end apart: 24 -> 24, of which waited for: 14 -> 15; matrix products, arithmetic and copies ran while one was open for 7% -> 9% of each run, Pallas kernels for 5% -> 4%
where the time goes in v5:
time: 75.4 us; the launch traced here: 75.1 us
  waiting for transfers between devices  26.8 us (36%)
  starting transfers between devices  25.1 us (33%)
  Pallas kernels  13.1 us (17%)
  other arithmetic  6.78 us (9%)
  local copies, waits for them, and re-layouts  2.39 us (3%)
  between operations  0.94 us (1%)
    ppermute x24, waiting for transfers between devices, swap(): lax.ppermute(value, ('ka', 'band'), [(device, device ^ mask) for device i...  26.8 us
    ppermute x24, starting transfers between devices, swap(): lax.ppermute(value, ('ka', 'band'), [(device, device ^ mask) for device i...  25.1 us
    pallas_call x1, Pallas kernels, project(): pl.pallas_call(functools.partial(project_kernel, scale=scale, starts=star...  5.91 us
    pallas_call x1, Pallas kernels, respond(): pl.pallas_call(respond_far_kernel, in_specs=[VMEM_SPEC] * 5 + [any_spec],...  4.36 us
    pallas_call x1, Pallas kernels, respond(): pl.pallas_call(respond_near_kernel, in_specs=[VMEM_SPEC] * 5, out_specs=[...  2.81 us
  transfers between devices with their start and end apart: 24, of which 15 were waited for; matrix products, arithmetic and copies ran while one was open for 9% of the time, Pallas kernels for 4%

profile of v5, /device:TPU:0, one launch (start us, length us, event | category | flops | bytes accessed | tf_op | source)
XLA Modules:
  0.0 75.1 jit_solution(9430158341647108636)
XLA Ops:
  2.4 5.1 %collective-permute-start.2 = (bf16[1,2,8,2176]{3,2,1,0:T(8,128)(2,1)S(1)}, bf16[1,2,8,2176]{3,2,1,0:T(8,128)(2,1)S(1)}, u32[]{:S(2)}, u32[]{:S(2)}) collective-permute-start(bf16[1,2,8,2176]{3,2,1,0:T(8,128)(2,1)S(1)} %get-tuple-element.52), channel_id=1, source_target_pairs={{0,24},{1,25},{2,26},{3,27},{4,28},{5,29},{6,30},{7,31},{8,16},{9,... | collective-permute-start | bytes 208904 | tf_op jit(solution)/shard_map/ppermute | solution.py:46
  10.7 1.1 %slice.102.first_ref = bf16[512,512]{1,0:T(8,128)(2,1)S(1)} slice(bf16[512,4096]{1,0:T(8,128)(2,1)} %basis_ref.3), slice={[0:512], [0:512]} | slice | bytes 1048576 | tf_op jit(solution)/shard_map/slice | solution.py:474
  14.1 1.6 %collective-permute-start.3 = (bf16[4,8,2176]{2,1,0:T(8,128)(2,1)S(1)}, bf16[4,8,2176]{2,1,0:T(8,128)(2,1)S(1)}, u32[]{:S(2)}, u32[]{:S(2)}) collective-permute-start(bf16[4,8,2176]{2,1,0:T(8,128)(2,1)S(1)} %get-tuple-element.31), channel_id=1, source_target_pairs={{0,4},{1,5},{2,6},{3,7},{4,0},{5,1},{6,2},{7,3},{8,12},{9,13},{10,... | collective-permute-start | bytes 417800 | tf_op jit(solution)/shard_map/ppermute | solution.py:46
  15.8 3.4 %collective-permute-done.3 = bf16[4,8,2176]{2,1,0:T(8,128)(2,1)S(1)} collective-permute-done((bf16[4,8,2176]{2,1,0:T(8,128)(2,1)S(1)}, bf16[4,8,2176]{2,1,0:T(8,128)(2,1)S(1)}, u32[]{:S(2)}, u32[]{:S(2)}) %collective-permute-start.3) | collective-permute-done | bytes 139296 | tf_op jit(solution)/shard_map/ppermute | solution.py:46
  19.6 1.1 %collective-permute-done.4 = bf16[2,8,2048]{2,1,0:T(8,128)(2,1)S(1)} collective-permute-done((bf16[2,8,2048]{2,1,0:T(8,128)(2,1)S(1)}, bf16[2,8,2048]{2,1,0:T(8,128)(2,1)S(1)}, u32[]{:S(2)}, u32[]{:S(2)}) %collective-permute-start.4) | collective-permute-done | bytes 65568 | tf_op jit(solution)/shard_map/ppermute | solution.py:46
  20.8 5.9 %project.1 = (bf16[1024,512]{1,0:T(8,128)(2,1)S(1)}, bf16[10,128,128]{2,1,0:T(8,128)(2,1)S(1)}) custom-call(bf16[2,8,4096]{2,1,0:T(8,128)(2,1)S(1)} %pad_maximum_fusion.4.occ_ref, bf16[2,32,4096]{2,1,0:T(8,128)(2,1)S(1)} %copy-done, bf16[2,32,4096]{2,1,0:T(8,128)(2,1)S(1)} %collective-permute-done.5.other_ref, ...), custom_call_target="tpu_custom_call" | custom-call | flops 4294967296 | bytes 8388608 | tf_op jit(solution)/shard_map/project/pallas_call | solution.py:281
  26.7 1.8 %collective-permute-start.7 = (bf16[320,128]{1,0:T(8,128)(2,1)S(1)}, bf16[320,128]{1,0:T(8,128)(2,1)S(1)}, u32[]{:S(2)}, u32[]{:S(2)}) collective-permute-start(bf16[320,128]{1,0:T(8,128)(2,1)S(1)} %get-tuple-element.40), channel_id=1, source_target_pairs={{0,2},{1,3},{2,0},{3,1},{4,6},{5,7},{6,4},{7,5},{8,10},{9,11},{10,... | collective-permute-start | bytes 245768 | tf_op jit(solution)/shard_map/ppermute | solution.py:46
  28.5 1.4 %collective-permute-start.9 = (bf16[320,128]{1,0:T(8,128)(2,1)S(1)}, bf16[320,128]{1,0:T(8,128)(2,1)S(1)}, u32[]{:S(2)}, u32[]{:S(2)}) collective-permute-start(bf16[320,128]{1,0:T(8,128)(2,1)S(1)} %get-tuple-element.41), channel_id=1, source_target_pairs={{0,6},{1,7},{2,4},{3,5},{4,2},{5,3},{6,0},{7,1},{8,14},{9,15},{10,... | collective-permute-start | bytes 245768 | tf_op jit(solution)/shard_map/ppermute | solution.py:46
  30.3 1.9 %collective-permute-done.7 = bf16[320,128]{1,0:T(8,128)(2,1)S(1)} collective-permute-done((bf16[320,128]{1,0:T(8,128)(2,1)S(1)}, bf16[320,128]{1,0:T(8,128)(2,1)S(1)}, u32[]{:S(2)}, u32[]{:S(2)}) %collective-permute-start.7) | collective-permute-done | bytes 81952 | tf_op jit(solution)/shard_map/ppermute | solution.py:46
  32.2 2.4 %collective-permute-done.9 = bf16[320,128]{1,0:T(8,128)(2,1)S(1)} collective-permute-done((bf16[320,128]{1,0:T(8,128)(2,1)S(1)}, bf16[320,128]{1,0:T(8,128)(2,1)S(1)}, u32[]{:S(2)}, u32[]{:S(2)}) %collective-permute-start.9) | collective-permute-done | bytes 81952 | tf_op jit(solution)/shard_map/ppermute | solution.py:46
  34.7 3.4 %collective-permute-start.12 = (bf16[320,128]{1,0:T(8,128)(2,1)S(1)}, bf16[320,128]{1,0:T(8,128)(2,1)S(1)}, u32[]{:S(2)}, u32[]{:S(2)}) collective-permute-start(bf16[320,128]{1,0:T(8,128)(2,1)S(1)} %fusion.2), channel_id=1, source_target_pairs={{0,24},{1,25},{2,26},{3,27},{4,28},{5,29},{6,30},{7,31},{8,16},{9,... | collective-permute-start | bytes 245768 | tf_op jit(solution)/shard_map/ppermute | solution.py:46
  38.0 1.1 %collective-permute-start.10 = (bf16[320,128]{1,0:T(8,128)(2,1)S(1)}, bf16[320,128]{1,0:T(8,128)(2,1)S(1)}, u32[]{:S(2)}, u32[]{:S(2)}) collective-permute-start(bf16[320,128]{1,0:T(8,128)(2,1)S(1)} %fusion.2), channel_id=1, source_target_pairs={{0,8},{1,9},{2,10},{3,11},{4,12},{5,13},{6,14},{7,15},{8,0},{9,1},... | collective-permute-start | bytes 245768 | tf_op jit(solution)/shard_map/ppermute | solution.py:46
  39.1 2.0 %collective-permute-done.12 = bf16[320,128]{1,0:T(8,128)(2,1)S(1)} collective-permute-done((bf16[320,128]{1,0:T(8,128)(2,1)S(1)}, bf16[320,128]{1,0:T(8,128)(2,1)S(1)}, u32[]{:S(2)}, u32[]{:S(2)}) %collective-permute-start.12) | collective-permute-done | bytes 81952 | tf_op jit(solution)/shard_map/ppermute | solution.py:46
  41.1 3.3 %collective-permute-done.11 = bf16[320,128]{1,0:T(8,128)(2,1)S(1)} collective-permute-done((bf16[320,128]{1,0:T(8,128)(2,1)S(1)}, bf16[320,128]{1,0:T(8,128)(2,1)S(1)}, u32[]{:S(2)}, u32[]{:S(2)}) %collective-permute-start.11) | collective-permute-done | bytes 81952 | tf_op jit(solution)/shard_map/ppermute | solution.py:46
  44.4 2.2 %collective-permute-start.15 = (bf16[320,128]{1,0:T(8,128)(2,1)S(1)}, bf16[320,128]{1,0:T(8,128)(2,1)S(1)}, u32[]{:S(2)}, u32[]{:S(2)}) collective-permute-start(bf16[320,128]{1,0:T(8,128)(2,1)S(1)} %add_convert_fusion.2), channel_id=1, source_target_pairs={{0,6},{1,7},{2,4},{3,5},{4,2},{5,3},{6,0},{7,1},{8,14},{9,15},{10,... | collective-permute-start | bytes 245768 | tf_op jit(solution)/shard_map/ppermute | solution.py:46
  46.7 1.1 %collective-permute-start.14 = (bf16[320,128]{1,0:T(8,128)(2,1)S(1)}, bf16[320,128]{1,0:T(8,128)(2,1)S(1)}, u32[]{:S(2)}, u32[]{:S(2)}) collective-permute-start(bf16[320,128]{1,0:T(8,128)(2,1)S(1)} %add_convert_fusion.2), channel_id=1, source_target_pairs={{0,4},{1,5},{2,6},{3,7},{4,0},{5,1},{6,2},{7,3},{8,12},{9,13},{10,... | collective-permute-start | bytes 245768 | tf_op jit(solution)/shard_map/ppermute | solution.py:46
  48.1 2.2 %collective-permute-done.15 = bf16[320,128]{1,0:T(8,128)(2,1)S(1)} collective-permute-done((bf16[320,128]{1,0:T(8,128)(2,1)S(1)}, bf16[320,128]{1,0:T(8,128)(2,1)S(1)}, u32[]{:S(2)}, u32[]{:S(2)}) %collective-permute-start.15) | collective-permute-done | bytes 81952 | tf_op jit(solution)/shard_map/ppermute | solution.py:46
  52.3 4.4 %respond_far.1 = (bf16[2,8,2048]{2,1,0:T(8,128)(2,1)S(1)}, bf16[2,32,2048]{2,1,0:T(8,128)(2,1)S(1)}, bf16[2,32,2048]{2,1,0:T(8,128)(2,1)S(1)}, bf16[1024,512]{1,0:T(8,128)(2,1)S(1)}, bf16[2,512,1024]{2,1,0:T(8,128)(2,1)S(1)}) custom-call(bf16[1024,512]{1,0:T(8,128)(2,1)S(1)} %get-tuple-element.18.coeffs_ref, bf16[10,128,128]{2,1,0:T(8,128)(2,1)S(1)} %bitcast.43, ...), custom_call_target="tpu_custom_call" | custom-call | flops 2147483648 | bytes 4194304 | tf_op jit(solution)/shard_map/respond_far/pallas_call | solution.py:418
  57.2 2.8 %respond_near.1 = (bf16[2,8,2048]{2,1,0:T(8,128)(2,1)S(1)}, bf16[2,32,2048]{2,1,0:T(8,128)(2,1)S(1)}, bf16[2,32,2048]{2,1,0:T(8,128)(2,1)S(1)}) custom-call(bf16[1024,512]{1,0:T(8,128)(2,1)S(1)} %get-tuple-element.20.screened_ref, bf16[2,8,4096]{2,1,0:T(8,128)(2,1)S(1)} %pad_maximum_fusion.4.occ_ref, bf16[2,32,4096]{2,1,0:T(8,128)(2,1)S(1)} %copy-done, ...), custom_call_target="tpu_custom_call" | custom-call | flops 2147483648 | bytes 4194304 | tf_op jit(solution)/shard_map/respond_near/pallas_call | solution.py:435
  61.2 1.1 %collective-permute-done.17 = bf16[2,8,1024]{2,1,0:T(8,128)(2,1)S(1)} collective-permute-done((bf16[2,8,1024]{2,1,0:T(8,128)(2,1)S(1)}, bf16[2,8,1024]{2,1,0:T(8,128)(2,1)S(1)}, u32[]{:S(2)}, u32[]{:S(2)}) %collective-permute-start.17) | collective-permute-done | bytes 32800 | tf_op jit(solution)/shard_map/ppermute | solution.py:46
  63.9 2.7 %collective-permute-done.18 = bf16[4,8,1024]{2,1,0:T(8,128)(2,1)S(1)} collective-permute-done((bf16[4,8,1024]{2,1,0:T(8,128)(2,1)S(1)}, bf16[4,8,1024]{2,1,0:T(8,128)(2,1)S(1)}, u32[]{:S(2)}, u32[]{:S(2)}) %collective-permute-start.18) | collective-permute-done | bytes 65568 | tf_op jit(solution)/shard_map/ppermute | solution.py:46
  67.7 2.0 %collective-permute-start.21 = (bf16[1,2,8,1024]{3,2,1,0:T(8,128)(2,1)S(1)}, bf16[1,2,8,1024]{3,2,1,0:T(8,128)(2,1)S(1)}, u32[]{:S(2)}, u32[]{:S(2)}) collective-permute-start(bf16[1,2,8,1024]{3,2,1,0:T(8,128)(2,1)S(1)} %get-tuple-element.49), channel_id=1, source_target_pairs={{0,24},{1,25},{2,26},{3,27},{4,28},{5,29},{6,30},{7,31},{8,16},{9,... | collective-permute-start | bytes 98312 | tf_op jit(solution)/shard_map/ppermute | solution.py:46
  71.6 1.9 %collective-permute-done.21 = bf16[1,2,8,1024]{3,2,1,0:T(8,128)(2,1)S(1)} collective-permute-done((bf16[1,2,8,1024]{3,2,1,0:T(8,128)(2,1)S(1)}, bf16[1,2,8,1024]{3,2,1,0:T(8,128)(2,1)S(1)}, u32[]{:S(2)}, u32[]{:S(2)}) %collective-permute-start.21) | collective-permute-done | bytes 32800 | tf_op jit(solution)/shard_map/ppermute | solution.py:46
  73.4 1.1 %collective-permute-done.20 = bf16[1,2,8,1024]{3,2,1,0:T(8,128)(2,1)S(1)} collective-permute-done((bf16[1,2,8,1024]{3,2,1,0:T(8,128)(2,1)S(1)}, bf16[1,2,8,1024]{3,2,1,0:T(8,128)(2,1)S(1)}, u32[]{:S(2)}, u32[]{:S(2)}) %collective-permute-start.20) | collective-permute-done | bytes 32800 | tf_op jit(solution)/shard_map/ppermute | solution.py:46
  (84 shorter events, 17.3 us)
Async XLA Ops:
  2.4 10.2 %collective-permute-start.2 = (bf16[1,2,8,2176]{3,2,1,0:T(8,128)(2,1)S(1)}, bf16[1,2,8,2176]{3,2,1,0:T(8,128)(2,1)S(1)}, u32[]{:S(2)}, u32[]{:S(2)}) collective-permute-start(bf16[1,2,8,2176]{3,2,1,0:T(8,128)(2,1)S(1)} %get-tuple-element.52), channel_id=1, source_target_pairs={{0,24},{1,25},{2,26},{3,27},{4,28},{5,29},{6,30},{7,31},{8,16},{9,... | collective-permute-start | bytes 208904 | tf_op jit(solution)/shard_map/ppermute | solution.py:46
  7.5 5.9 %collective-permute-start.1 = (bf16[1,2,8,2176]{3,2,1,0:T(8,128)(2,1)S(1)}, bf16[1,2,8,2176]{3,2,1,0:T(8,128)(2,1)S(1)}, u32[]{:S(2)}, u32[]{:S(2)}) collective-permute-start(bf16[1,2,8,2176]{3,2,1,0:T(8,128)(2,1)S(1)} %get-tuple-element.52), channel_id=1, source_target_pairs={{0,16},{1,17},{2,18},{3,19},{4,20},{5,21},{6,22},{7,23},{8,24},{9,... | collective-permute-start | bytes 208904 | tf_op jit(solution)/shard_map/ppermute | solution.py:46
  7.5 5.9 %collective-permute-start = (bf16[1,2,8,2176]{3,2,1,0:T(8,128)(2,1)S(1)}, bf16[1,2,8,2176]{3,2,1,0:T(8,128)(2,1)S(1)}, u32[]{:S(2)}, u32[]{:S(2)}) collective-permute-start(bf16[1,2,8,2176]{3,2,1,0:T(8,128)(2,1)S(1)} %get-tuple-element.52), channel_id=1, source_target_pairs={{0,8},{1,9},{2,10},{3,11},{4,12},{5,13},{6,14},{7,15},{8,0},{9,1},... | collective-permute-start | bytes 208904 | tf_op jit(solution)/shard_map/ppermute | solution.py:46
  8.1 7.5 %collective-permute-start.6 = (f32[16,32]{1,0:T(8,128)}, f32[16,32]{1,0:T(8,128)S(1)}, u32[]{:S(2)}, u32[]{:S(2)}) collective-permute-start(f32[16,32]{1,0:T(8,128)} %param.10), channel_id=1, source_target_pairs={{0,1},{1,0},{2,3},{3,2},{4,5},{5,4},{6,7},{7,6},{8,9},{9,8},{10,11... | collective-permute-start | bytes 6152 | tf_op jit(solution)/shard_map/ppermute | solution.py:46
  8.1 12.5 %collective-permute-start.5 = (bf16[2,32,4096]{2,1,0:T(8,128)(2,1)}, bf16[2,32,4096]{2,1,0:T(8,128)(2,1)S(1)}, u32[]{:S(2)}, u32[]{:S(2)}) collective-permute-start(bf16[2,32,4096]{2,1,0:T(8,128)(2,1)} %own_ref.5), channel_id=1, source_target_pairs={{0,1},{1,0},{2,3},{3,2},{4,5},{5,4},{6,7},{7,6},{8,9},{9,8},{10,11... | collective-permute-start | bytes 1572872 | tf_op jit(solution)/shard_map/ppermute | solution.py:46
  14.1 5.1 %collective-permute-start.3 = (bf16[4,8,2176]{2,1,0:T(8,128)(2,1)S(1)}, bf16[4,8,2176]{2,1,0:T(8,128)(2,1)S(1)}, u32[]{:S(2)}, u32[]{:S(2)}) collective-permute-start(bf16[4,8,2176]{2,1,0:T(8,128)(2,1)S(1)} %get-tuple-element.31), channel_id=1, source_target_pairs={{0,4},{1,5},{2,6},{3,7},{4,0},{5,1},{6,2},{7,3},{8,12},{9,13},{10,... | collective-permute-start | bytes 417800 | tf_op jit(solution)/shard_map/ppermute | solution.py:46
  19.3 1.3 %collective-permute-start.4 = (bf16[2,8,2048]{2,1,0:T(8,128)(2,1)S(1)}, bf16[2,8,2048]{2,1,0:T(8,128)(2,1)S(1)}, u32[]{:S(2)}, u32[]{:S(2)}) collective-permute-start(bf16[2,8,2048]{2,1,0:T(8,128)(2,1)S(1)} %slice_select_fusion), channel_id=1, source_target_pairs={{0,1},{1,0},{2,3},{3,2},{4,5},{5,4},{6,7},{7,6},{8,9},{9,8},{10,11... | collective-permute-start | bytes 196616 | tf_op jit(solution)/shard_map/ppermute | solution.py:46
  26.7 5.5 %collective-permute-start.7 = (bf16[320,128]{1,0:T(8,128)(2,1)S(1)}, bf16[320,128]{1,0:T(8,128)(2,1)S(1)}, u32[]{:S(2)}, u32[]{:S(2)}) collective-permute-start(bf16[320,128]{1,0:T(8,128)(2,1)S(1)} %get-tuple-element.40), channel_id=1, source_target_pairs={{0,2},{1,3},{2,0},{3,1},{4,6},{5,7},{6,4},{7,5},{8,10},{9,11},{10,... | collective-permute-start | bytes 245768 | tf_op jit(solution)/shard_map/ppermute | solution.py:46
  28.5 6.1 %collective-permute-start.9 = (bf16[320,128]{1,0:T(8,128)(2,1)S(1)}, bf16[320,128]{1,0:T(8,128)(2,1)S(1)}, u32[]{:S(2)}, u32[]{:S(2)}) collective-permute-start(bf16[320,128]{1,0:T(8,128)(2,1)S(1)} %get-tuple-element.41), channel_id=1, source_target_pairs={{0,6},{1,7},{2,4},{3,5},{4,2},{5,3},{6,0},{7,1},{8,14},{9,15},{10,... | collective-permute-start | bytes 245768 | tf_op jit(solution)/shard_map/ppermute | solution.py:46
  29.9 4.7 %collective-permute-start.8 = (bf16[320,128]{1,0:T(8,128)(2,1)S(1)}, bf16[320,128]{1,0:T(8,128)(2,1)S(1)}, u32[]{:S(2)}, u32[]{:S(2)}) collective-permute-start(bf16[320,128]{1,0:T(8,128)(2,1)S(1)} %get-tuple-element.42), channel_id=1, source_target_pairs={{0,4},{1,5},{2,6},{3,7},{4,0},{5,1},{6,2},{7,3},{8,12},{9,13},{10,... | collective-permute-start | bytes 245768 | tf_op jit(solution)/shard_map/ppermute | solution.py:46
  34.7 6.4 %collective-permute-start.12 = (bf16[320,128]{1,0:T(8,128)(2,1)S(1)}, bf16[320,128]{1,0:T(8,128)(2,1)S(1)}, u32[]{:S(2)}, u32[]{:S(2)}) collective-permute-start(bf16[320,128]{1,0:T(8,128)(2,1)S(1)} %fusion.2), channel_id=1, source_target_pairs={{0,24},{1,25},{2,26},{3,27},{4,28},{5,29},{6,30},{7,31},{8,16},{9,... | collective-permute-start | bytes 245768 | tf_op jit(solution)/shard_map/ppermute | solution.py:46
  38.0 6.4 %collective-permute-start.11 = (bf16[320,128]{1,0:T(8,128)(2,1)S(1)}, bf16[320,128]{1,0:T(8,128)(2,1)S(1)}, u32[]{:S(2)}, u32[]{:S(2)}) collective-permute-start(bf16[320,128]{1,0:T(8,128)(2,1)S(1)} %fusion.2), channel_id=1, source_target_pairs={{0,16},{1,17},{2,18},{3,19},{4,20},{5,21},{6,22},{7,23},{8,24},{9,... | collective-permute-start | bytes 245768 | tf_op jit(solution)/shard_map/ppermute | solution.py:46
  38.0 6.4 %collective-permute-start.10 = (bf16[320,128]{1,0:T(8,128)(2,1)S(1)}, bf16[320,128]{1,0:T(8,128)(2,1)S(1)}, u32[]{:S(2)}, u32[]{:S(2)}) collective-permute-start(bf16[320,128]{1,0:T(8,128)(2,1)S(1)} %fusion.2), channel_id=1, source_target_pairs={{0,8},{1,9},{2,10},{3,11},{4,12},{5,13},{6,14},{7,15},{8,0},{9,1},... | collective-permute-start | bytes 245768 | tf_op jit(solution)/shard_map/ppermute | solution.py:46
  44.4 5.8 %collective-permute-start.15 = (bf16[320,128]{1,0:T(8,128)(2,1)S(1)}, bf16[320,128]{1,0:T(8,128)(2,1)S(1)}, u32[]{:S(2)}, u32[]{:S(2)}) collective-permute-start(bf16[320,128]{1,0:T(8,128)(2,1)S(1)} %add_convert_fusion.2), channel_id=1, source_target_pairs={{0,6},{1,7},{2,4},{3,5},{4,2},{5,3},{6,0},{7,1},{8,14},{9,15},{10,... | collective-permute-start | bytes 245768 | tf_op jit(solution)/shard_map/ppermute | solution.py:46
  46.7 4.5 %collective-permute-start.14 = (bf16[320,128]{1,0:T(8,128)(2,1)S(1)}, bf16[320,128]{1,0:T(8,128)(2,1)S(1)}, u32[]{:S(2)}, u32[]{:S(2)}) collective-permute-start(bf16[320,128]{1,0:T(8,128)(2,1)S(1)} %add_convert_fusion.2), channel_id=1, source_target_pairs={{0,4},{1,5},{2,6},{3,7},{4,0},{5,1},{6,2},{7,3},{8,12},{9,13},{10,... | collective-permute-start | bytes 245768 | tf_op jit(solution)/shard_map/ppermute | solution.py:46
  47.7 4.4 %collective-permute-start.13 = (bf16[320,128]{1,0:T(8,128)(2,1)S(1)}, bf16[320,128]{1,0:T(8,128)(2,1)S(1)}, u32[]{:S(2)}, u32[]{:S(2)}) collective-permute-start(bf16[320,128]{1,0:T(8,128)(2,1)S(1)} %add_convert_fusion.2), channel_id=1, source_target_pairs={{0,2},{1,3},{2,0},{3,1},{4,6},{5,7},{6,4},{7,5},{8,10},{9,11},{10,... | collective-permute-start | bytes 245768 | tf_op jit(solution)/shard_map/ppermute | solution.py:46
  56.7 4.3 %collective-permute-start.16 = (bf16[2,8,2048]{2,1,0:T(8,128)(2,1)S(1)}, bf16[2,8,2048]{2,1,0:T(8,128)(2,1)S(1)}, u32[]{:S(2)}, u32[]{:S(2)}) collective-permute-start(bf16[2,8,2048]{2,1,0:T(8,128)(2,1)S(1)} %get-tuple-element.23), channel_id=1, source_target_pairs={{0,2},{1,3},{2,0},{3,1},{4,6},{5,7},{6,4},{7,5},{8,10},{9,11},{10,... | collective-permute-start | bytes 196616 | tf_op jit(solution)/shard_map/ppermute | solution.py:46
  61.1 1.3 %collective-permute-start.17 = (bf16[2,8,1024]{2,1,0:T(8,128)(2,1)S(1)}, bf16[2,8,1024]{2,1,0:T(8,128)(2,1)S(1)}, u32[]{:S(2)}, u32[]{:S(2)}) collective-permute-start(bf16[2,8,1024]{2,1,0:T(8,128)(2,1)S(1)} %get-tuple-element.54), channel_id=1, source_target_pairs={{0,1},{1,0},{2,3},{3,2},{4,5},{5,4},{6,7},{7,6},{8,9},{9,8},{10,11... | collective-permute-start | bytes 98312 | tf_op jit(solution)/shard_map/ppermute | solution.py:46
  62.3 4.3 %collective-permute-start.18 = (bf16[4,8,1024]{2,1,0:T(8,128)(2,1)S(1)}, bf16[4,8,1024]{2,1,0:T(8,128)(2,1)S(1)}, u32[]{:S(2)}, u32[]{:S(2)}) collective-permute-start(bf16[4,8,1024]{2,1,0:T(8,128)(2,1)S(1)} %pad_maximum_fusion.6), channel_id=1, source_target_pairs={{0,4},{1,5},{2,6},{3,7},{4,0},{5,1},{6,2},{7,3},{8,12},{9,13},{10,... | collective-permute-start | bytes 196616 | tf_op jit(solution)/shard_map/ppermute | solution.py:46
  63.4 7.1 %collective-permute-start.22 = (bf16[2,32,2048]{2,1,0:T(8,128)(2,1)S(1)}, bf16[2,32,2048]{2,1,0:T(8,128)(2,1)S(1)}, u32[]{:S(2)}, u32[]{:S(2)}) collective-permute-start(bf16[2,32,2048]{2,1,0:T(8,128)(2,1)S(1)} %get-tuple-element.25), channel_id=1, source_target_pairs={{0,1},{1,0},{2,3},{3,2},{4,5},{5,4},{6,7},{7,6},{8,9},{9,8},{10,11... | collective-permute-start | bytes 786440 | tf_op jit(solution)/shard_map/ppermute | solution.py:46
  63.5 7.1 %collective-permute-start.23 = (bf16[2,32,2048]{2,1,0:T(8,128)(2,1)S(1)}, bf16[2,32,2048]{2,1,0:T(8,128)(2,1)S(1)}, u32[]{:S(2)}, u32[]{:S(2)}) collective-permute-start(bf16[2,32,2048]{2,1,0:T(8,128)(2,1)S(1)} %get-tuple-element.27), channel_id=1, source_target_pairs={{0,1},{1,0},{2,3},{3,2},{4,5},{5,4},{6,7},{7,6},{8,9},{9,8},{10,11... | collective-permute-start | bytes 786440 | tf_op jit(solution)/shard_map/ppermute | solution.py:46
  67.0 6.4 %collective-permute-start.19 = (bf16[1,2,8,1024]{3,2,1,0:T(8,128)(2,1)S(1)}, bf16[1,2,8,1024]{3,2,1,0:T(8,128)(2,1)S(1)}, u32[]{:S(2)}, u32[]{:S(2)}) collective-permute-start(bf16[1,2,8,1024]{3,2,1,0:T(8,128)(2,1)S(1)} %get-tuple-element.48), channel_id=1, source_target_pairs={{0,8},{1,9},{2,10},{3,11},{4,12},{5,13},{6,14},{7,15},{8,0},{9,1},... | collective-permute-start | bytes 98312 | tf_op jit(solution)/shard_map/ppermute | solution.py:46
  67.7 5.7 %collective-permute-start.21 = (bf16[1,2,8,1024]{3,2,1,0:T(8,128)(2,1)S(1)}, bf16[1,2,8,1024]{3,2,1,0:T(8,128)(2,1)S(1)}, u32[]{:S(2)}, u32[]{:S(2)}) collective-permute-start(bf16[1,2,8,1024]{3,2,1,0:T(8,128)(2,1)S(1)} %get-tuple-element.49), channel_id=1, source_target_pairs={{0,24},{1,25},{2,26},{3,27},{4,28},{5,29},{6,30},{7,31},{8,16},{9,... | collective-permute-start | bytes 98312 | tf_op jit(solution)/shard_map/ppermute | solution.py:46
  69.7 4.8 %collective-permute-start.20 = (bf16[1,2,8,1024]{3,2,1,0:T(8,128)(2,1)S(1)}, bf16[1,2,8,1024]{3,2,1,0:T(8,128)(2,1)S(1)}, u32[]{:S(2)}, u32[]{:S(2)}) collective-permute-start(bf16[1,2,8,1024]{3,2,1,0:T(8,128)(2,1)S(1)} %get-tuple-element.50), channel_id=1, source_target_pairs={{0,16},{1,17},{2,18},{3,19},{4,20},{5,21},{6,22},{7,23},{8,24},{9,... | collective-permute-start | bytes 98312 | tf_op jit(solution)/shard_map/ppermute | solution.py:46
  (1 other events, 9.0 us)

commit v6 on v5

--- a/solution.py
+++ b/solution.py
@@ -78,7 +78,14 @@
 
 def blocks_of(aux_count):
     count = aux_count // LANES
-    return [(row, column) for row in range(count) for column in range(row, count)]
+    return [(row, column) for row in range(count) for column in range(row + 1, count)]
+
+
+def packed_rows(aux_count):
+    count = aux_count // LANES
+    assert count % 2 == 0
+    blocks = (len(blocks_of(aux_count)) + count // 2) * LANES
+    return blocks, blocks + 64
 
 
 def split_float(value):
@@ -93,6 +100,12 @@
     own_k = device * local_k + jnp.arange(local_k, dtype=jnp.int32)
     here = every_k[None, None, :] == own_k[None, :, None]
     return jnp.sum(jnp.where(here, partner[:, None, :], 0), axis=2).reshape(-1)
+
+
+def own_transfer_first(cube, values, local_k):
+    first = cube.bit(cube.core) == 0
+    low, high = values[:local_k], values[local_k:]
+    return jnp.where(first, low, high), jnp.where(first, high, low)
 
 
 def fetch_partners(cube, occupied, occ_energy, sources, neighbour_sources, beside):
@@ -119,21 +132,23 @@
             jnp.where(hits[:, :, None, None], gathered[None].astype(F32), 0.0), axis=1
         ).astype(BF16)
 
-    received = cube.swap(held_of(neighbour_sources), cube.x)
-    received, beside = lax.optimization_barrier((received, beside))
-    chosen = held_of(sources) + received
-    mine = jnp.where(first, chosen[:local_k], chosen[local_k:])
-    theirs = jnp.where(first, chosen[local_k:], chosen[:local_k])
+    own_sources, other_sources = own_transfer_first(cube, sources, local_k)
+    own_neighbour, other_neighbour = own_transfer_first(cube, neighbour_sources, local_k)
+    along_x = cube.swap(held_of(own_neighbour), cube.x)
+    across = cube.swap(held_of(other_neighbour)[:, :, :width], cube.x | cube.core)
+    beside_core = cube.swap(held_of(other_sources)[:, :, :width], cube.core)
+    along_x, beside = lax.optimization_barrier((along_x, beside))
+    mine = held_of(own_sources) + along_x
+    other = beside_core + across
     energy = mine[:, :, width : width + 3].astype(F32)
     energy = (energy[:, :, 0] + energy[:, :, 1]) + energy[:, :, 2]
     part = mine[:, :, :width]
-    other = cube.swap(theirs[:, :, :width], cube.core)
     part = jnp.concatenate([jnp.where(first, part, other), jnp.where(first, other, part)], axis=2)
     return part, energy, beside
 
 
 def reduce_screen(cube, own):
-    rows = own.shape[0] * LANES
+    rows = own.shape[0]
     piece = sum_scatter(cube, own.reshape(4, rows // 4, LANES), [cube.y, cube.x]).astype(BF16)
     for bits in cube.groups:
         arrived = [cube.swap(piece, mask) for mask in masks_of(bits)]
@@ -150,17 +165,14 @@
     first = cube.bit(cube.core) == 0
     keep = jnp.where(first, part[:, :, :width], part[:, :, width:])
     give = jnp.where(first, part[:, :, width:], part[:, :, :width])
-    part = jnp.concatenate([keep, cube.swap(give, cube.core)], axis=0)
+    along_x = cube.swap(keep, cube.x)
+    across = cube.swap(give, cube.x | cube.core)
+    beside_core = cube.swap(give, cube.core)
     side, upper = ka % 2, ka // 2
-    received = cube.swap(part, cube.x)
-    both = jnp.concatenate([part, received], axis=0)
-
-    def own_transfer_first(targets):
-        turned = jnp.concatenate([targets[local_k:], targets[:local_k]])
-        return jnp.where(first, targets, turned)
-
+    both = jnp.concatenate([keep, beside_core, along_x, across], axis=0)
     targets = jnp.concatenate(
-        [own_transfer_first(sources), own_transfer_first(neighbour_sources)]
+        own_transfer_first(cube, sources, local_k)
+        + own_transfer_first(cube, neighbour_sources, local_k)
     )
 
     def placed(uppers):
@@ -253,22 +265,38 @@
                     ).astype(BF16)
                 )
     coulomb = coulomb_ref[...] * math.sqrt(scale)
+    tiles = {}
     for panel in range(0, count, 2):
-        height = min(2, count - panel)
         gram = lax.dot_general(
-            weighted_ref[:, panel * LANES : (panel + height) * LANES],
+            weighted_ref[:, panel * LANES : (panel + 2) * LANES],
             coeffs_ref[:, panel * LANES :],
             (((0,), (0,)), ((), ())),
             preferred_element_type=F32,
         )
-        for n, (row, column) in enumerate(blocks_of(aux_count)):
-            if not panel <= row < panel + height:
-                continue
-            down, across = (row - panel) * LANES, (column - panel) * LANES
-            tile = gram[down : down + LANES, across : across + LANES]
+        for row in (panel, panel + 1):
             left = jnp.broadcast_to(coulomb[:, row * LANES : (row + 1) * LANES], (LANES, LANES)).T
-            right = coulomb[:, column * LANES : (column + 1) * LANES]
-            gram_ref[n] = (left * tile * right).astype(BF16)
+            for column in range(row, count):
+                down, across = (row - panel) * LANES, (column - panel) * LANES
+                right = coulomb[:, column * LANES : (column + 1) * LANES]
+                tiles[row, column] = (
+                    left * gram[down : down + LANES, across : across + LANES] * right
+                )
+    places = blocks_of(aux_count)
+    for n, place in enumerate(places):
+        gram_ref[n * LANES : (n + 1) * LANES, :] = tiles[place].astype(BF16)
+    down = lax.broadcasted_iota(jnp.int32, (LANES, LANES), 0)
+    across = lax.broadcasted_iota(jnp.int32, (LANES, LANES), 1)
+    lines = []
+    for pair in range(count // 2):
+        upper, lower = tiles[2 * pair, 2 * pair], tiles[2 * pair + 1, 2 * pair + 1]
+        n = len(places) + pair
+        gram_ref[n * LANES : (n + 1) * LANES, :] = jnp.where(across >= down, upper, lower).astype(
+            BF16
+        )
+        lines.append(jnp.sum(jnp.where(across == down, lower, 0.0), axis=0, keepdims=True))
+    blocks, total_rows = packed_rows(aux_count)
+    lines.append(jnp.zeros((total_rows - blocks - len(lines), LANES), F32))
+    gram_ref[blocks:, :] = jnp.concatenate(lines, axis=0).astype(BF16)
 
 
 def project(occ, own, other, first, basis, occ_energy, levels, coulomb, scale):
@@ -276,7 +304,6 @@
     group_count = own.shape[1]
     aux_count = basis.shape[0]
     rows = 2 * local_k * occ_count * group_count
-    blocks = len(blocks_of(aux_count))
     starts = (0, first.shape[1], 3 * first.shape[1])
     return pl.pallas_call(
         functools.partial(project_kernel, scale=scale, starts=starts),
@@ -284,7 +311,7 @@
         out_specs=[VMEM_SPEC] * 2,
         out_shape=[
             jax.ShapeDtypeStruct((rows, aux_count), BF16),
-            jax.ShapeDtypeStruct((blocks, LANES, LANES), BF16),
+            jax.ShapeDtypeStruct((packed_rows(aux_count)[1], LANES), BF16),
         ],
         scratch_shapes=[
             pltpu.VMEM((rows, aux_count), BF16),
@@ -301,13 +328,28 @@
 
 
 def screen_coeffs(coeffs_ref, packed_ref, screen_ref, screened_ref):
-    for n, (row, column) in enumerate(blocks_of(coeffs_ref.shape[1])):
-        tile = packed_ref[n]
+    aux_count = coeffs_ref.shape[1]
+    places = blocks_of(aux_count)
+    for n, (row, column) in enumerate(places):
+        tile = packed_ref[n * LANES : (n + 1) * LANES, :]
         upper = slice(row * LANES, (row + 1) * LANES)
         lower = slice(column * LANES, (column + 1) * LANES)
         screen_ref[upper, lower] = tile
-        if row != column:
-            screen_ref[lower, upper] = tile.T
+        screen_ref[lower, upper] = tile.T
+    down = lax.broadcasted_iota(jnp.int32, (LANES, LANES), 0)
+    across = lax.broadcasted_iota(jnp.int32, (LANES, LANES), 1)
+    lines = packed_ref[packed_rows(aux_count)[0] :, :].astype(F32)
+    for pair in range(aux_count // LANES // 2):
+        n = len(places) + pair
+        tile = packed_ref[n * LANES : (n + 1) * LANES, :].astype(F32)
+        turned = tile.T
+        first = slice(2 * pair * LANES, (2 * pair + 1) * LANES)
+        second = slice((2 * pair + 1) * LANES, (2 * pair + 2) * LANES)
+        screen_ref[first, first] = jnp.where(across >= down, tile, turned).astype(BF16)
+        strict = jnp.where(across < down, tile, turned)
+        screen_ref[second, second] = jnp.where(
+            across == down, lines[pair : pair + 1], strict
+        ).astype(BF16)
     screened_ref[...] = jnp.dot(
         coeffs_ref[...], screen_ref[...], preferred_element_type=F32
     ).astype(BF16)

time: 75.4 us -> 72.5 us (0.962)
  waiting for transfers between devices: 26.8 us -> 22.5 us
  starting transfers between devices: 25.1 us -> 27 us
    ppermute x24 -> x26, waiting for transfers between devices: 26.8 us -> 22.5 us  [swap(): lax.ppermute(value, ('ka', 'band'), [(device, device ^ mask) for device i...]
    ppermute x24 -> x26, starting transfers between devices: 25.1 us -> 27 us  [swap(): lax.ppermute(value, ('ka', 'band'), [(device, device ^ mask) for device i...]
  transfers between devices with their start and end apart: 24 -> 26, of which waited for: 15 -> 14; matrix products, arithmetic and copies ran while one was open for 9% -> 9% of each run, Pallas kernels for 4% -> 4%
where the time goes in v6:
time: 72.5 us; the launch traced here: 72.2 us
  starting transfers between devices  27 us (37%)
  waiting for transfers between devices  22.5 us (31%)
  Pallas kernels  12.9 us (18%)
  other arithmetic  6.69 us (9%)
  local copies, waits for them, and re-layouts  2.19 us (3%)
  between operations  0.97 us (1%)
    ppermute x26, starting transfers between devices, swap(): lax.ppermute(value, ('ka', 'band'), [(device, device ^ mask) for device i...  27 us
    ppermute x26, waiting for transfers between devices, swap(): lax.ppermute(value, ('ka', 'band'), [(device, device ^ mask) for device i...  22.5 us
    pallas_call x1, Pallas kernels, project(): pl.pallas_call(functools.partial(project_kernel, scale=scale, starts=star...  5.89 us
    pallas_call x1, Pallas kernels, respond(): pl.pallas_call(respond_far_kernel, in_specs=[VMEM_SPEC] * 5 + [any_spec],...  4.16 us
    pallas_call x1, Pallas kernels, respond(): pl.pallas_call(respond_near_kernel, in_specs=[VMEM_SPEC] * 5, out_specs=[...  2.8 us
  transfers between devices with their start and end apart: 26, of which 14 were waited for; matrix products, arithmetic and copies ran while one was open for 9% of the time, Pallas kernels for 4%

profile of v6, /device:TPU:0, one launch (start us, length us, event | category | flops | bytes accessed | tf_op | source)
XLA Modules:
  0.0 72.2 jit_solution(1110359325605726739)
XLA Ops:
  2.4 5.1 %collective-permute-start.2 = (bf16[1,2,8,2176]{3,2,1,0:T(8,128)(2,1)S(1)}, bf16[1,2,8,2176]{3,2,1,0:T(8,128)(2,1)S(1)}, u32[]{:S(2)}, u32[]{:S(2)}) collective-permute-start(bf16[1,2,8,2176]{3,2,1,0:T(8,128)(2,1)S(1)} %get-tuple-element.51), channel_id=1, source_target_pairs={{0,24},{1,25},{2,26},{3,27},{4,28},{5,29},{6,30},{7,31},{8,16},{9,... | collective-permute-start | bytes 208904 | tf_op jit(solution)/shard_map/ppermute | solution.py:46
  11.2 1.1 %slice.89.first_ref = bf16[512,512]{1,0:T(8,128)(2,1)S(1)} slice(bf16[512,4096]{1,0:T(8,128)(2,1)} %basis_ref.3), slice={[0:512], [0:512]} | slice | bytes 1048576 | tf_op jit(solution)/shard_map/slice | solution.py:516
  14.2 1.6 %collective-permute-start.3 = (bf16[2,8,2176]{2,1,0:T(8,128)(2,1)S(1)}, bf16[2,8,2176]{2,1,0:T(8,128)(2,1)S(1)}, u32[]{:S(2)}, u32[]{:S(2)}) collective-permute-start(bf16[2,8,2176]{2,1,0:T(8,128)(2,1)S(1)} %get-tuple-element.31), channel_id=1, source_target_pairs={{0,4},{1,5},{2,6},{3,7},{4,0},{5,1},{6,2},{7,3},{8,12},{9,13},{10,... | collective-permute-start | bytes 208904 | tf_op jit(solution)/shard_map/ppermute | solution.py:46
  16.6 1.9 %collective-permute-done.3 = bf16[2,8,2176]{2,1,0:T(8,128)(2,1)S(1)} collective-permute-done((bf16[2,8,2176]{2,1,0:T(8,128)(2,1)S(1)}, bf16[2,8,2176]{2,1,0:T(8,128)(2,1)S(1)}, u32[]{:S(2)}, u32[]{:S(2)}) %collective-permute-start.3) | collective-permute-done | bytes 69664 | tf_op jit(solution)/shard_map/ppermute | solution.py:46
  18.6 1.2 %collective-permute-done.5 = bf16[2,8,2048]{2,1,0:T(8,128)(2,1)S(1)} collective-permute-done((bf16[2,8,2048]{2,1,0:T(8,128)(2,1)S(1)}, bf16[2,8,2048]{2,1,0:T(8,128)(2,1)S(1)}, u32[]{:S(2)}, u32[]{:S(2)}) %collective-permute-start.5) | collective-permute-done | bytes 65568 | tf_op jit(solution)/shard_map/ppermute | solution.py:46
  20.1 5.9 %project.1 = (bf16[1024,512]{1,0:T(8,128)(2,1)S(1)}, bf16[1088,128]{1,0:T(8,128)(2,1)S(1)}) custom-call(bf16[2,8,4096]{2,1,0:T(8,128)(2,1)S(1)} %pad_maximum_fusion.4.occ_ref, bf16[2,32,4096]{2,1,0:T(8,128)(2,1)S(1)} %copy-done, bf16[2,32,4096]{2,1,0:T(8,128)(2,1)S(1)} %collective-permute-done.6.other_ref, ...), custom_call_target="tpu_custom_call" | custom-call | flops 4294967296 | bytes 8388608 | tf_op jit(solution)/shard_map/project/pallas_call | solution.py:308
  26.0 1.6 %collective-permute-start.8 = (bf16[272,128]{1,0:T(8,128)(2,1)S(1)}, bf16[272,128]{1,0:T(8,128)(2,1)S(1)}, u32[]{:S(2)}, u32[]{:S(2)}) collective-permute-start(bf16[272,128]{1,0:T(8,128)(2,1)S(1)} %get-tuple-element.42), channel_id=1, source_target_pairs={{0,2},{1,3},{2,0},{3,1},{4,6},{5,7},{6,4},{7,5},{8,10},{9,11},{10,... | collective-permute-start | bytes 208904 | tf_op jit(solution)/shard_map/ppermute | solution.py:46
  27.6 1.1 %collective-permute-start.10 = (bf16[272,128]{1,0:T(8,128)(2,1)S(1)}, bf16[272,128]{1,0:T(8,128)(2,1)S(1)}, u32[]{:S(2)}, u32[]{:S(2)}) collective-permute-start(bf16[272,128]{1,0:T(8,128)(2,1)S(1)} %get-tuple-element.43), channel_id=1, source_target_pairs={{0,6},{1,7},{2,4},{3,5},{4,2},{5,3},{6,0},{7,1},{8,14},{9,15},{10,... | collective-permute-start | bytes 208904 | tf_op jit(solution)/shard_map/ppermute | solution.py:46
  30.6 2.9 %collective-permute-done.10 = bf16[272,128]{1,0:T(8,128)(2,1)S(1)} collective-permute-done((bf16[272,128]{1,0:T(8,128)(2,1)S(1)}, bf16[272,128]{1,0:T(8,128)(2,1)S(1)}, u32[]{:S(2)}, u32[]{:S(2)}) %collective-permute-start.10) | collective-permute-done | bytes 69664 | tf_op jit(solution)/shard_map/ppermute | solution.py:46
  33.6 2.8 %collective-permute-start.13 = (bf16[272,128]{1,0:T(8,128)(2,1)S(1)}, bf16[272,128]{1,0:T(8,128)(2,1)S(1)}, u32[]{:S(2)}, u32[]{:S(2)}) collective-permute-start(bf16[272,128]{1,0:T(8,128)(2,1)S(1)} %fusion.2), channel_id=1, source_target_pairs={{0,24},{1,25},{2,26},{3,27},{4,28},{5,29},{6,30},{7,31},{8,16},{9,... | collective-permute-start | bytes 208904 | tf_op jit(solution)/shard_map/ppermute | solution.py:46
  36.3 1.7 %collective-permute-start.11 = (bf16[272,128]{1,0:T(8,128)(2,1)S(1)}, bf16[272,128]{1,0:T(8,128)(2,1)S(1)}, u32[]{:S(2)}, u32[]{:S(2)}) collective-permute-start(bf16[272,128]{1,0:T(8,128)(2,1)S(1)} %fusion.2), channel_id=1, source_target_pairs={{0,8},{1,9},{2,10},{3,11},{4,12},{5,13},{6,14},{7,15},{8,0},{9,1},... | collective-permute-start | bytes 208904 | tf_op jit(solution)/shard_map/ppermute | solution.py:46
  38.1 1.7 %collective-permute-done.13 = bf16[272,128]{1,0:T(8,128)(2,1)S(1)} collective-permute-done((bf16[272,128]{1,0:T(8,128)(2,1)S(1)}, bf16[272,128]{1,0:T(8,128)(2,1)S(1)}, u32[]{:S(2)}, u32[]{:S(2)}) %collective-permute-start.13) | collective-permute-done | bytes 69664 | tf_op jit(solution)/shard_map/ppermute | solution.py:46
  39.7 2.6 %collective-permute-done.12 = bf16[272,128]{1,0:T(8,128)(2,1)S(1)} collective-permute-done((bf16[272,128]{1,0:T(8,128)(2,1)S(1)}, bf16[272,128]{1,0:T(8,128)(2,1)S(1)}, u32[]{:S(2)}, u32[]{:S(2)}) %collective-permute-start.12) | collective-permute-done | bytes 69664 | tf_op jit(solution)/shard_map/ppermute | solution.py:46
  42.4 1.9 %collective-permute-start.16 = (bf16[272,128]{1,0:T(8,128)(2,1)S(1)}, bf16[272,128]{1,0:T(8,128)(2,1)S(1)}, u32[]{:S(2)}, u32[]{:S(2)}) collective-permute-start(bf16[272,128]{1,0:T(8,128)(2,1)S(1)} %add_convert_fusion.2), channel_id=1, source_target_pairs={{0,6},{1,7},{2,4},{3,5},{4,2},{5,3},{6,0},{7,1},{8,14},{9,15},{10,... | collective-permute-start | bytes 208904 | tf_op jit(solution)/shard_map/ppermute | solution.py:46
  44.2 1.2 %collective-permute-start.15 = (bf16[272,128]{1,0:T(8,128)(2,1)S(1)}, bf16[272,128]{1,0:T(8,128)(2,1)S(1)}, u32[]{:S(2)}, u32[]{:S(2)}) collective-permute-start(bf16[272,128]{1,0:T(8,128)(2,1)S(1)} %add_convert_fusion.2), channel_id=1, source_target_pairs={{0,4},{1,5},{2,6},{3,7},{4,0},{5,1},{6,2},{7,3},{8,12},{9,13},{10,... | collective-permute-start | bytes 208904 | tf_op jit(solution)/shard_map/ppermute | solution.py:46
  46.0 1.7 %collective-permute-done.16 = bf16[272,128]{1,0:T(8,128)(2,1)S(1)} collective-permute-done((bf16[272,128]{1,0:T(8,128)(2,1)S(1)}, bf16[272,128]{1,0:T(8,128)(2,1)S(1)}, u32[]{:S(2)}, u32[]{:S(2)}) %collective-permute-start.16) | collective-permute-done | bytes 69664 | tf_op jit(solution)/shard_map/ppermute | solution.py:46
  48.6 1.2 %collective-permute-done.14 = bf16[272,128]{1,0:T(8,128)(2,1)S(1)} collective-permute-done((bf16[272,128]{1,0:T(8,128)(2,1)S(1)}, bf16[272,128]{1,0:T(8,128)(2,1)S(1)}, u32[]{:S(2)}, u32[]{:S(2)}) %collective-permute-start.14) | collective-permute-done | bytes 69664 | tf_op jit(solution)/shard_map/ppermute | solution.py:46
  49.9 4.2 %respond_far.1 = (bf16[2,8,2048]{2,1,0:T(8,128)(2,1)S(1)}, bf16[2,32,2048]{2,1,0:T(8,128)(2,1)S(1)}, bf16[2,32,2048]{2,1,0:T(8,128)(2,1)S(1)}, bf16[1024,512]{1,0:T(8,128)(2,1)S(1)}, bf16[2,512,1024]{2,1,0:T(8,128)(2,1)S(1)}) custom-call(bf16[1024,512]{1,0:T(8,128)(2,1)S(1)} %get-tuple-element.18.coeffs_ref, bf16[1088,128]{1,0:T(8,128)(2,1)S(1)} %bitcast.43, ...), custom_call_target="tpu_custom_call" | custom-call | flops 2147483648 | bytes 4194304 | tf_op jit(solution)/shard_map/respond_far/pallas_call | solution.py:460
  54.6 2.8 %respond_near.1 = (bf16[2,8,2048]{2,1,0:T(8,128)(2,1)S(1)}, bf16[2,32,2048]{2,1,0:T(8,128)(2,1)S(1)}, bf16[2,32,2048]{2,1,0:T(8,128)(2,1)S(1)}) custom-call(bf16[1024,512]{1,0:T(8,128)(2,1)S(1)} %get-tuple-element.20.screened_ref, bf16[2,8,4096]{2,1,0:T(8,128)(2,1)S(1)} %pad_maximum_fusion.4.occ_ref, bf16[2,32,4096]{2,1,0:T(8,128)(2,1)S(1)} %copy-done, ...), custom_call_target="tpu_custom_call" | custom-call | flops 2147483648 | bytes 4194304 | tf_op jit(solution)/shard_map/respond_near/pallas_call | solution.py:477
  59.4 1.2 %collective-permute-start.19 = (bf16[2,8,1024]{2,1,0:T(8,128)(2,1)S(1)}, bf16[2,8,1024]{2,1,0:T(8,128)(2,1)S(1)}, u32[]{:S(2)}, u32[]{:S(2)}) collective-permute-start(bf16[2,8,1024]{2,1,0:T(8,128)(2,1)S(1)} %get-tuple-element.52), channel_id=1, source_target_pairs={{0,4},{1,5},{2,6},{3,7},{4,0},{5,1},{6,2},{7,3},{8,12},{9,13},{10,... | collective-permute-start | bytes 98312 | tf_op jit(solution)/shard_map/ppermute | solution.py:46
  61.2 2.1 %collective-permute-done.19 = bf16[2,8,1024]{2,1,0:T(8,128)(2,1)S(1)} collective-permute-done((bf16[2,8,1024]{2,1,0:T(8,128)(2,1)S(1)}, bf16[2,8,1024]{2,1,0:T(8,128)(2,1)S(1)}, u32[]{:S(2)}, u32[]{:S(2)}) %collective-permute-start.19) | collective-permute-done | bytes 32800 | tf_op jit(solution)/shard_map/ppermute | solution.py:46
  63.9 2.4 %collective-permute-start.23 = (bf16[1,2,8,1024]{3,2,1,0:T(8,128)(2,1)S(1)}, bf16[1,2,8,1024]{3,2,1,0:T(8,128)(2,1)S(1)}, u32[]{:S(2)}, u32[]{:S(2)}) collective-permute-start(bf16[1,2,8,1024]{3,2,1,0:T(8,128)(2,1)S(1)} %get-tuple-element.48), channel_id=1, source_target_pairs={{0,24},{1,25},{2,26},{3,27},{4,28},{5,29},{6,30},{7,31},{8,16},{9,... | collective-permute-start | bytes 98312 | tf_op jit(solution)/shard_map/ppermute | solution.py:46
  68.2 1.4 %collective-permute-done.23 = bf16[1,2,8,1024]{3,2,1,0:T(8,128)(2,1)S(1)} collective-permute-done((bf16[1,2,8,1024]{3,2,1,0:T(8,128)(2,1)S(1)}, bf16[1,2,8,1024]{3,2,1,0:T(8,128)(2,1)S(1)}, u32[]{:S(2)}, u32[]{:S(2)}) %collective-permute-start.23) | collective-permute-done | bytes 32800 | tf_op jit(solution)/shard_map/ppermute | solution.py:46
  69.7 1.9 %collective-permute-done.22 = bf16[1,2,8,1024]{3,2,1,0:T(8,128)(2,1)S(1)} collective-permute-done((bf16[1,2,8,1024]{3,2,1,0:T(8,128)(2,1)S(1)}, bf16[1,2,8,1024]{3,2,1,0:T(8,128)(2,1)S(1)}, u32[]{:S(2)}, u32[]{:S(2)}) %collective-permute-start.22) | collective-permute-done | bytes 32800 | tf_op jit(solution)/shard_map/ppermute | solution.py:46
  (83 shorter events, 18.2 us)
Async XLA Ops:
  2.4 10.0 %collective-permute-start.2 = (bf16[1,2,8,2176]{3,2,1,0:T(8,128)(2,1)S(1)}, bf16[1,2,8,2176]{3,2,1,0:T(8,128)(2,1)S(1)}, u32[]{:S(2)}, u32[]{:S(2)}) collective-permute-start(bf16[1,2,8,2176]{3,2,1,0:T(8,128)(2,1)S(1)} %get-tuple-element.51), channel_id=1, source_target_pairs={{0,24},{1,25},{2,26},{3,27},{4,28},{5,29},{6,30},{7,31},{8,16},{9,... | collective-permute-start | bytes 208904 | tf_op jit(solution)/shard_map/ppermute | solution.py:46
  7.5 5.9 %collective-permute-start.1 = (bf16[1,2,8,2176]{3,2,1,0:T(8,128)(2,1)S(1)}, bf16[1,2,8,2176]{3,2,1,0:T(8,128)(2,1)S(1)}, u32[]{:S(2)}, u32[]{:S(2)}) collective-permute-start(bf16[1,2,8,2176]{3,2,1,0:T(8,128)(2,1)S(1)} %get-tuple-element.51), channel_id=1, source_target_pairs={{0,16},{1,17},{2,18},{3,19},{4,20},{5,21},{6,22},{7,23},{8,24},{9,... | collective-permute-start | bytes 208904 | tf_op jit(solution)/shard_map/ppermute | solution.py:46
  7.5 5.9 %collective-permute-start = (bf16[1,2,8,2176]{3,2,1,0:T(8,128)(2,1)S(1)}, bf16[1,2,8,2176]{3,2,1,0:T(8,128)(2,1)S(1)}, u32[]{:S(2)}, u32[]{:S(2)}) collective-permute-start(bf16[1,2,8,2176]{3,2,1,0:T(8,128)(2,1)S(1)} %get-tuple-element.51), channel_id=1, source_target_pairs={{0,8},{1,9},{2,10},{3,11},{4,12},{5,13},{6,14},{7,15},{8,0},{9,1},... | collective-permute-start | bytes 208904 | tf_op jit(solution)/shard_map/ppermute | solution.py:46
  8.1 4.2 %collective-permute-start.7 = (f32[16,32]{1,0:T(8,128)}, f32[16,32]{1,0:T(8,128)S(1)}, u32[]{:S(2)}, u32[]{:S(2)}) collective-permute-start(f32[16,32]{1,0:T(8,128)} %param.10), channel_id=1, source_target_pairs={{0,1},{1,0},{2,3},{3,2},{4,5},{5,4},{6,7},{7,6},{8,9},{9,8},{10,11... | collective-permute-start | bytes 6152 | tf_op jit(solution)/shard_map/ppermute | solution.py:46
  8.1 11.9 %collective-permute-start.6 = (bf16[2,32,4096]{2,1,0:T(8,128)(2,1)}, bf16[2,32,4096]{2,1,0:T(8,128)(2,1)S(1)}, u32[]{:S(2)}, u32[]{:S(2)}) collective-permute-start(bf16[2,32,4096]{2,1,0:T(8,128)(2,1)} %own_ref.5), channel_id=1, source_target_pairs={{0,1},{1,0},{2,3},{3,2},{4,5},{5,4},{6,7},{7,6},{8,9},{9,8},{10,11... | collective-permute-start | bytes 1572872 | tf_op jit(solution)/shard_map/ppermute | solution.py:46
  14.2 4.4 %collective-permute-start.3 = (bf16[2,8,2176]{2,1,0:T(8,128)(2,1)S(1)}, bf16[2,8,2176]{2,1,0:T(8,128)(2,1)S(1)}, u32[]{:S(2)}, u32[]{:S(2)}) collective-permute-start(bf16[2,8,2176]{2,1,0:T(8,128)(2,1)S(1)} %get-tuple-element.31), channel_id=1, source_target_pairs={{0,4},{1,5},{2,6},{3,7},{4,0},{5,1},{6,2},{7,3},{8,12},{9,13},{10,... | collective-permute-start | bytes 208904 | tf_op jit(solution)/shard_map/ppermute | solution.py:46
  26.0 4.6 %collective-permute-start.8 = (bf16[272,128]{1,0:T(8,128)(2,1)S(1)}, bf16[272,128]{1,0:T(8,128)(2,1)S(1)}, u32[]{:S(2)}, u32[]{:S(2)}) collective-permute-start(bf16[272,128]{1,0:T(8,128)(2,1)S(1)} %get-tuple-element.42), channel_id=1, source_target_pairs={{0,2},{1,3},{2,0},{3,1},{4,6},{5,7},{6,4},{7,5},{8,10},{9,11},{10,... | collective-permute-start | bytes 208904 | tf_op jit(solution)/shard_map/ppermute | solution.py:46
  27.6 5.9 %collective-permute-start.10 = (bf16[272,128]{1,0:T(8,128)(2,1)S(1)}, bf16[272,128]{1,0:T(8,128)(2,1)S(1)}, u32[]{:S(2)}, u32[]{:S(2)}) collective-permute-start(bf16[272,128]{1,0:T(8,128)(2,1)S(1)} %get-tuple-element.43), channel_id=1, source_target_pairs={{0,6},{1,7},{2,4},{3,5},{4,2},{5,3},{6,0},{7,1},{8,14},{9,15},{10,... | collective-permute-start | bytes 208904 | tf_op jit(solution)/shard_map/ppermute | solution.py:46
  28.7 4.8 %collective-permute-start.9 = (bf16[272,128]{1,0:T(8,128)(2,1)S(1)}, bf16[272,128]{1,0:T(8,128)(2,1)S(1)}, u32[]{:S(2)}, u32[]{:S(2)}) collective-permute-start(bf16[272,128]{1,0:T(8,128)(2,1)S(1)} %get-tuple-element.44), channel_id=1, source_target_pairs={{0,4},{1,5},{2,6},{3,7},{4,0},{5,1},{6,2},{7,3},{8,12},{9,13},{10,... | collective-permute-start | bytes 208904 | tf_op jit(solution)/shard_map/ppermute | solution.py:46
  33.6 6.2 %collective-permute-start.13 = (bf16[272,128]{1,0:T(8,128)(2,1)S(1)}, bf16[272,128]{1,0:T(8,128)(2,1)S(1)}, u32[]{:S(2)}, u32[]{:S(2)}) collective-permute-start(bf16[272,128]{1,0:T(8,128)(2,1)S(1)} %fusion.2), channel_id=1, source_target_pairs={{0,24},{1,25},{2,26},{3,27},{4,28},{5,29},{6,30},{7,31},{8,16},{9,... | collective-permute-start | bytes 208904 | tf_op jit(solution)/shard_map/ppermute | solution.py:46
  36.3 6.0 %collective-permute-start.12 = (bf16[272,128]{1,0:T(8,128)(2,1)S(1)}, bf16[272,128]{1,0:T(8,128)(2,1)S(1)}, u32[]{:S(2)}, u32[]{:S(2)}) collective-permute-start(bf16[272,128]{1,0:T(8,128)(2,1)S(1)} %fusion.2), channel_id=1, source_target_pairs={{0,16},{1,17},{2,18},{3,19},{4,20},{5,21},{6,22},{7,23},{8,24},{9,... | collective-permute-start | bytes 208904 | tf_op jit(solution)/shard_map/ppermute | solution.py:46
  36.3 6.0 %collective-permute-start.11 = (bf16[272,128]{1,0:T(8,128)(2,1)S(1)}, bf16[272,128]{1,0:T(8,128)(2,1)S(1)}, u32[]{:S(2)}, u32[]{:S(2)}) collective-permute-start(bf16[272,128]{1,0:T(8,128)(2,1)S(1)} %fusion.2), channel_id=1, source_target_pairs={{0,8},{1,9},{2,10},{3,11},{4,12},{5,13},{6,14},{7,15},{8,0},{9,1},... | collective-permute-start | bytes 208904 | tf_op jit(solution)/shard_map/ppermute | solution.py:46
  42.4 5.4 %collective-permute-start.16 = (bf16[272,128]{1,0:T(8,128)(2,1)S(1)}, bf16[272,128]{1,0:T(8,128)(2,1)S(1)}, u32[]{:S(2)}, u32[]{:S(2)}) collective-permute-start(bf16[272,128]{1,0:T(8,128)(2,1)S(1)} %add_convert_fusion.2), channel_id=1, source_target_pairs={{0,6},{1,7},{2,4},{3,5},{4,2},{5,3},{6,0},{7,1},{8,14},{9,15},{10,... | collective-permute-start | bytes 208904 | tf_op jit(solution)/shard_map/ppermute | solution.py:46
  44.2 4.3 %collective-permute-start.15 = (bf16[272,128]{1,0:T(8,128)(2,1)S(1)}, bf16[272,128]{1,0:T(8,128)(2,1)S(1)}, u32[]{:S(2)}, u32[]{:S(2)}) collective-permute-start(bf16[272,128]{1,0:T(8,128)(2,1)S(1)} %add_convert_fusion.2), channel_id=1, source_target_pairs={{0,4},{1,5},{2,6},{3,7},{4,0},{5,1},{6,2},{7,3},{8,12},{9,13},{10,... | collective-permute-start | bytes 208904 | tf_op jit(solution)/shard_map/ppermute | solution.py:46
  45.4 4.3 %collective-permute-start.14 = (bf16[272,128]{1,0:T(8,128)(2,1)S(1)}, bf16[272,128]{1,0:T(8,128)(2,1)S(1)}, u32[]{:S(2)}, u32[]{:S(2)}) collective-permute-start(bf16[272,128]{1,0:T(8,128)(2,1)S(1)} %add_convert_fusion.2), channel_id=1, source_target_pairs={{0,2},{1,3},{2,0},{3,1},{4,6},{5,7},{6,4},{7,5},{8,10},{9,11},{10,... | collective-permute-start | bytes 208904 | tf_op jit(solution)/shard_map/ppermute | solution.py:46
  54.0 4.3 %collective-permute-start.17 = (bf16[2,8,2048]{2,1,0:T(8,128)(2,1)S(1)}, bf16[2,8,2048]{2,1,0:T(8,128)(2,1)S(1)}, u32[]{:S(2)}, u32[]{:S(2)}) collective-permute-start(bf16[2,8,2048]{2,1,0:T(8,128)(2,1)S(1)} %get-tuple-element.23), channel_id=1, source_target_pairs={{0,2},{1,3},{2,0},{3,1},{4,6},{5,7},{6,4},{7,5},{8,10},{9,11},{10,... | collective-permute-start | bytes 196616 | tf_op jit(solution)/shard_map/ppermute | solution.py:46
  58.4 4.9 %collective-permute-start.20 = (bf16[2,8,1024]{2,1,0:T(8,128)(2,1)S(1)}, bf16[2,8,1024]{2,1,0:T(8,128)(2,1)S(1)}, u32[]{:S(2)}, u32[]{:S(2)}) collective-permute-start(bf16[2,8,1024]{2,1,0:T(8,128)(2,1)S(1)} %get-tuple-element.53), channel_id=1, source_target_pairs={{0,5},{1,4},{2,7},{3,6},{4,1},{5,0},{6,3},{7,2},{8,13},{9,12},{10,... | collective-permute-start | bytes 98312 | tf_op jit(solution)/shard_map/ppermute | solution.py:46
  58.5 4.9 %collective-permute-start.18 = (bf16[2,8,1024]{2,1,0:T(8,128)(2,1)S(1)}, bf16[2,8,1024]{2,1,0:T(8,128)(2,1)S(1)}, u32[]{:S(2)}, u32[]{:S(2)}) collective-permute-start(bf16[2,8,1024]{2,1,0:T(8,128)(2,1)S(1)} %get-tuple-element.53), channel_id=1, source_target_pairs={{0,1},{1,0},{2,3},{3,2},{4,5},{5,4},{6,7},{7,6},{8,9},{9,8},{10,11... | collective-permute-start | bytes 98312 | tf_op jit(solution)/shard_map/ppermute | solution.py:46
  59.4 3.9 %collective-permute-start.19 = (bf16[2,8,1024]{2,1,0:T(8,128)(2,1)S(1)}, bf16[2,8,1024]{2,1,0:T(8,128)(2,1)S(1)}, u32[]{:S(2)}, u32[]{:S(2)}) collective-permute-start(bf16[2,8,1024]{2,1,0:T(8,128)(2,1)S(1)} %get-tuple-element.52), channel_id=1, source_target_pairs={{0,4},{1,5},{2,6},{3,7},{4,0},{5,1},{6,2},{7,3},{8,12},{9,13},{10,... | collective-permute-start | bytes 98312 | tf_op jit(solution)/shard_map/ppermute | solution.py:46
  60.7 6.5 %collective-permute-start.24 = (bf16[2,32,2048]{2,1,0:T(8,128)(2,1)S(1)}, bf16[2,32,2048]{2,1,0:T(8,128)(2,1)S(1)}, u32[]{:S(2)}, u32[]{:S(2)}) collective-permute-start(bf16[2,32,2048]{2,1,0:T(8,128)(2,1)S(1)} %get-tuple-element.25), channel_id=1, source_target_pairs={{0,1},{1,0},{2,3},{3,2},{4,5},{5,4},{6,7},{7,6},{8,9},{9,8},{10,11... | collective-permute-start | bytes 786440 | tf_op jit(solution)/shard_map/ppermute | solution.py:46
  60.7 6.5 %collective-permute-start.25 = (bf16[2,32,2048]{2,1,0:T(8,128)(2,1)S(1)}, bf16[2,32,2048]{2,1,0:T(8,128)(2,1)S(1)}, u32[]{:S(2)}, u32[]{:S(2)}) collective-permute-start(bf16[2,32,2048]{2,1,0:T(8,128)(2,1)S(1)} %get-tuple-element.27), channel_id=1, source_target_pairs={{0,1},{1,0},{2,3},{3,2},{4,5},{5,4},{6,7},{7,6},{8,9},{9,8},{10,11... | collective-permute-start | bytes 786440 | tf_op jit(solution)/shard_map/ppermute | solution.py:46
  63.7 6.0 %collective-permute-start.21 = (bf16[1,2,8,1024]{3,2,1,0:T(8,128)(2,1)S(1)}, bf16[1,2,8,1024]{3,2,1,0:T(8,128)(2,1)S(1)}, u32[]{:S(2)}, u32[]{:S(2)}) collective-permute-start(bf16[1,2,8,1024]{3,2,1,0:T(8,128)(2,1)S(1)} %get-tuple-element.47), channel_id=1, source_target_pairs={{0,8},{1,9},{2,10},{3,11},{4,12},{5,13},{6,14},{7,15},{8,0},{9,1},... | collective-permute-start | bytes 98312 | tf_op jit(solution)/shard_map/ppermute | solution.py:46
  63.9 5.7 %collective-permute-start.23 = (bf16[1,2,8,1024]{3,2,1,0:T(8,128)(2,1)S(1)}, bf16[1,2,8,1024]{3,2,1,0:T(8,128)(2,1)S(1)}, u32[]{:S(2)}, u32[]{:S(2)}) collective-permute-start(bf16[1,2,8,1024]{3,2,1,0:T(8,128)(2,1)S(1)} %get-tuple-element.48), channel_id=1, source_target_pairs={{0,24},{1,25},{2,26},{3,27},{4,28},{5,29},{6,30},{7,31},{8,16},{9,... | collective-permute-start | bytes 98312 | tf_op jit(solution)/shard_map/ppermute | solution.py:46
  66.4 5.2 %collective-permute-start.22 = (bf16[1,2,8,1024]{3,2,1,0:T(8,128)(2,1)S(1)}, bf16[1,2,8,1024]{3,2,1,0:T(8,128)(2,1)S(1)}, u32[]{:S(2)}, u32[]{:S(2)}) collective-permute-start(bf16[1,2,8,1024]{3,2,1,0:T(8,128)(2,1)S(1)} %get-tuple-element.49), channel_id=1, source_target_pairs={{0,16},{1,17},{2,18},{3,19},{4,20},{5,21},{6,22},{7,23},{8,24},{9,... | collective-permute-start | bytes 98312 | tf_op jit(solution)/shard_map/ppermute | solution.py:46
  (3 other events, 13.1 us)

commit v7 on v6

--- a/solution.py
+++ b/solution.py
@@ -108,20 +108,22 @@
     return jnp.where(first, low, high), jnp.where(first, high, low)
 
 
-def fetch_partners(cube, occupied, occ_energy, sources, neighbour_sources, beside):
+def fetch_partners(cube, occupied, occ_energy, sources, neighbour_sources, make_beside):
     local_k, occ_count, grid_count = occupied.shape
-    width = grid_count // 2
+    width = grid_count // cube.band
     ka = lax.axis_index("ka")
     first = cube.bit(cube.core) == 0
-    half = jnp.where(first, occupied[:, :, :width], occupied[:, :, width:])
+    quarter = lax.dynamic_slice_in_dim(occupied, lax.axis_index("band") * width, width, axis=2)
     pieces = jnp.stack(split_float(occ_energy), axis=2)
     payload = jnp.concatenate(
-        [half, jnp.pad(pieces, ((0, 0), (0, 0), (0, LANES - pieces.shape[2])))], axis=2
+        [quarter, jnp.pad(pieces, ((0, 0), (0, 0), (0, LANES - pieces.shape[2])))], axis=2
     )
     gathered = payload[None]
     for bits in cube.groups:
         gathered = gather_differences(cube, gathered, bits).reshape((-1,) + payload.shape)
     gathered = gathered.reshape((-1,) + payload.shape[1:])
+    gathered, late_ka, late_band = lax.optimization_barrier((gathered, ka, lax.axis_index("band")))
+    beside = make_beside(late_ka, late_band)
     side, upper = ka % 2, ka // 2
     slots = jnp.arange(gathered.shape[0], dtype=jnp.int32)
     held = (jnp.bitwise_xor(slots // local_k, upper) * 2 + side) * local_k + slots % local_k
@@ -144,7 +146,7 @@
     energy = (energy[:, :, 0] + energy[:, :, 1]) + energy[:, :, 2]
     part = mine[:, :, :width]
     part = jnp.concatenate([jnp.where(first, part, other), jnp.where(first, other, part)], axis=2)
-    return part, energy, beside
+    return part, cube.swap(part, cube.y), energy, beside
 
 
 def reduce_screen(cube, own):
@@ -211,59 +213,80 @@
     ]
 
 
+def pair_coeffs(occ, virt, basis):
+    pair_rows = jnp.concatenate([occ[i : i + 1] * virt for i in range(occ.shape[0])], axis=0)
+    return lax.dot_general(
+        pair_rows, basis, (((1,), (1,)), ((), ())), preferred_element_type=F32
+    )
+
+
+def upper_half():
+    return (lax.axis_index("band") // 2) % 2
+
+
+def project_near_kernel(
+    occ_ref, own_ref, other_ref, first_ref, basis_ref, total_ref, far_ref, held_ref, sems, *, starts
+):
+    local_k, occ_count, half = occ_ref.shape
+    rows = occ_count * own_ref.shape[1]
+    near = pl.multiple_of(upper_half() * half, half)
+    far = pl.multiple_of((1 - upper_half()) * half, half)
+    parts = list(zip(starts, starts[1:] + (half,)))
+    offset = starts[1]
+    copies = [
+        pltpu.make_async_copy(
+            basis_ref.at[:, pl.ds(near + start, end - start)],
+            held_ref.at[:, start - offset : end - offset],
+            sems.at[n],
+        )
+        for n, (start, end) in enumerate(parts[1:])
+    ]
+    copies.append(
+        pltpu.make_async_copy(basis_ref.at[:, pl.ds(far, half)], far_ref, sems.at[len(copies)])
+    )
+    for copy in copies:
+        copy.start()
+    terms = [(virt_ref, k) for virt_ref in (own_ref, other_ref) for k in range(local_k)]
+    for n, (start, end) in enumerate(parts):
+        if n > 0:
+            copies[n - 1].wait()
+        for term, (virt_ref, k) in enumerate(terms):
+            part = pair_coeffs(
+                occ_ref[k, :, start:end],
+                virt_ref[k, :, pl.ds(near + start, end - start)],
+                held_ref[:, start - offset : end - offset] if n > 0 else first_ref[...],
+            )
+            here = slice(term * rows, (term + 1) * rows)
+            total_ref[here, :] = total_ref[here, :] + part if n > 0 else part
+    copies[-1].wait()
+
+
 def project_kernel(
-    occ_ref, own_ref, other_ref, occ_energy_ref, levels_ref, coulomb_ref, first_ref, basis_ref,
-    coeffs_ref, gram_ref, weighted_ref, held_ref, total_ref, sems, *, scale, starts,
+    occ_ref, own_ref, other_ref, occ_energy_ref, levels_ref, coulomb_ref, total_ref, basis_ref,
+    coeffs_ref, gram_ref, weighted_ref, *, scale,
 ):
-    local_k, occ_count, grid_count = occ_ref.shape
+    local_k, occ_count, half = occ_ref.shape
     group_count = own_ref.shape[1]
     aux_count = basis_ref.shape[0]
     rows = occ_count * group_count
     count = aux_count // LANES
-    parts = list(zip(starts, starts[1:] + (grid_count,)))
-    offset = starts[1]
-    copies = [None] + [
-        pltpu.make_async_copy(
-            basis_ref.at[:, start:end],
-            held_ref.at[:, start - offset : end - offset],
-            sems.at[n],
-        )
-        for n, (start, end) in enumerate(parts[1:])
-    ]
-    for copy in copies[1:]:
-        copy.start()
+    far = pl.multiple_of((1 - upper_half()) * half, half)
     terms = [(virt_ref, k) for virt_ref in (own_ref, other_ref) for k in range(local_k)]
-    for n, (start, end) in enumerate(parts):
-        if n > 0:
-            copies[n].wait()
-        for term, (virt_ref, k) in enumerate(terms):
-            virt = virt_ref[k, :, start:end]
-            occ = occ_ref[k, :, start:end]
-            pair_rows = jnp.concatenate([occ[i : i + 1] * virt for i in range(occ_count)], axis=0)
-            coeffs = lax.dot_general(
-                pair_rows,
-                held_ref[:, start - offset : end - offset] if n > 0 else first_ref[...],
-                (((1,), (1,)), ((), ())),
-                preferred_element_type=F32,
+    for term, (virt_ref, k) in enumerate(terms):
+        here = slice(term * rows, (term + 1) * rows)
+        part = pair_coeffs(occ_ref[k], virt_ref[k, :, pl.ds(far, half)], basis_ref[...])
+        coeffs = (total_ref[here, :] + part).astype(BF16)
+        coeffs_ref[here, :] = coeffs
+        for i in range(occ_count):
+            first = i * group_count
+            weights = response(levels_ref[term] - occ_energy_ref[k][i : i + 1])
+            values = coeffs[first : first + group_count].astype(F32)
+            weighted_ref[term * rows + first : term * rows + first + group_count, :] = (
+                jnp.concatenate(
+                    [values[:, n * LANES : (n + 1) * LANES] * weights for n in range(count)],
+                    axis=1,
+                ).astype(BF16)
             )
-            here = slice(term * rows, (term + 1) * rows)
-            if n > 0:
-                coeffs = total_ref[here, :] + coeffs
-            if n < len(parts) - 1:
-                total_ref[here, :] = coeffs
-                continue
-            coeffs_ref[here, :] = coeffs.astype(BF16)
-            coeffs = coeffs.astype(BF16)
-            for i in range(occ_count):
-                first = i * group_count
-                weights = response(levels_ref[term] - occ_energy_ref[k][i : i + 1])
-                values = coeffs[first : first + group_count].astype(F32)
-                weighted_ref[term * rows + first : term * rows + first + group_count, :] = (
-                    jnp.concatenate(
-                        [values[:, n * LANES : (n + 1) * LANES] * weights for n in range(count)],
-                        axis=1,
-                    ).astype(BF16)
-                )
     coulomb = coulomb_ref[...] * math.sqrt(scale)
     tiles = {}
     for panel in range(0, count, 2):
@@ -299,32 +322,45 @@
     gram_ref[blocks:, :] = jnp.concatenate(lines, axis=0).astype(BF16)
 
 
-def project(occ, own, other, first, basis, occ_energy, levels, coulomb, scale):
-    local_k, occ_count, grid_count = occ.shape
+def project(near_occ, far_occ, own, other, first, basis, occ_energy, levels, coulomb, scale):
+    local_k, occ_count, half = near_occ.shape
     group_count = own.shape[1]
     aux_count = basis.shape[0]
     rows = 2 * local_k * occ_count * group_count
-    starts = (0, first.shape[1], 3 * first.shape[1])
+    width = first.shape[1]
+    starts = (0, width, 2 * width)
+    cost = pl.CostEstimate(
+        flops=2 * rows * half * aux_count, bytes_accessed=4 << 20, transcendentals=0
+    )
+    total, far_basis = pl.pallas_call(
+        functools.partial(project_near_kernel, starts=starts),
+        in_specs=[VMEM_SPEC] * 4 + [pl.BlockSpec(memory_space=pl.ANY)],
+        out_specs=[VMEM_SPEC] * 2,
+        out_shape=[
+            jax.ShapeDtypeStruct((rows, aux_count), F32),
+            jax.ShapeDtypeStruct((aux_count, half), BF16),
+        ],
+        scratch_shapes=[
+            pltpu.VMEM((aux_count, half - width), BF16),
+            pltpu.SemaphoreType.DMA((len(starts),)),
+        ],
+        compiler_params=pltpu.CompilerParams(vmem_limit_bytes=PROJECT_VMEM),
+        cost_estimate=cost,
+        name="project_near",
+    )(near_occ, own, other, first, basis)
     return pl.pallas_call(
-        functools.partial(project_kernel, scale=scale, starts=starts),
-        in_specs=[VMEM_SPEC] * 7 + [pl.BlockSpec(memory_space=pl.ANY)],
+        functools.partial(project_kernel, scale=scale),
+        in_specs=[VMEM_SPEC] * 8,
         out_specs=[VMEM_SPEC] * 2,
         out_shape=[
             jax.ShapeDtypeStruct((rows, aux_count), BF16),
             jax.ShapeDtypeStruct((packed_rows(aux_count)[1], LANES), BF16),
         ],
-        scratch_shapes=[
-            pltpu.VMEM((rows, aux_count), BF16),
-            pltpu.VMEM((aux_count, grid_count - starts[1]), BF16),
-            pltpu.VMEM((rows, aux_count), F32),
-            pltpu.SemaphoreType.DMA((len(starts) - 1,)),
-        ],
-        compiler_params=pltpu.CompilerParams(vmem_limit_bytes=PROJECT_VMEM),
-        cost_estimate=pl.CostEstimate(
-            flops=2 * rows * grid_count * aux_count, bytes_accessed=8 << 20, transcendentals=0
-        ),
+        scratch_shapes=[pltpu.VMEM((rows, aux_count), BF16)],
+        compiler_params=pltpu.CompilerParams(vmem_limit_bytes=NEAR_VMEM),
+        cost_estimate=cost,
         name="project",
-    )(occ, own, other, occ_energy, levels, coulomb, first, basis)
+    )(far_occ, own, other, occ_energy, levels, coulomb, total, far_basis)
 
 
 def screen_coeffs(coeffs_ref, packed_ref, screen_ref, screened_ref):
@@ -376,7 +412,7 @@
             screened_ref[...], held_ref[step], preferred_element_type=F32
         ).astype(BF16)
         for k in range(local_k):
-            occ = occ_ref[k, :, grid].astype(F32)
+            occ = occ_ref[k, :, to].astype(F32)
             sums = [None] * occ_count
             sides = ((own_ref, own_update_ref), (other_ref, other_update_ref))
             for side, (virt_ref, update_ref) in enumerate(sides):
@@ -399,10 +435,6 @@
     lax.fori_loop(0, span // width, chunk, 0)
 
 
-def upper_half():
-    return (lax.axis_index("band") // 2) % 2
-
-
 def respond_far_kernel(
     coeffs_ref, packed_ref, occ_ref, own_ref, other_ref, basis_ref,
     term_ref, own_update_ref, other_update_ref, screened_ref, near_ref,
@@ -441,11 +473,11 @@
     )
 
 
-def respond(coeffs, packed, basis, occ, own, other):
-    local_k, occ_count, grid_count = occ.shape
+def respond(coeffs, packed, basis, near_occ, far_occ, own, other):
+    local_k, occ_count, half = near_occ.shape
+    grid_count = 2 * half
     group_count = own.shape[1]
     rows, aux_count = coeffs.shape
-    half = grid_count // 2
     width = min(1024, half)
     any_spec = pl.BlockSpec(memory_space=pl.ANY)
     shapes = [
@@ -473,7 +505,7 @@
         compiler_params=pltpu.CompilerParams(vmem_limit_bytes=FAR_VMEM),
         cost_estimate=cost,
         name="respond_far",
-    )(coeffs, packed, occ, own, other, basis)
+    )(coeffs, packed, far_occ, own, other, basis)
     near = pl.pallas_call(
         respond_near_kernel,
         in_specs=[VMEM_SPEC] * 5,
@@ -483,7 +515,7 @@
         compiler_params=pltpu.CompilerParams(vmem_limit_bytes=NEAR_VMEM),
         cost_estimate=cost,
         name="respond_near",
-    )(screened, occ, own, other, near_basis)
+    )(screened, near_occ, own, other, near_basis)
     return far, near
 
 
@@ -500,31 +532,34 @@
     occ_scale = 1.0 / math.sqrt(transfers * virt_count)
     ka = lax.axis_index("ka")
 
-    first = cube.bit(cube.core) == 0
     other_virtual = cube.swap(virtual, cube.core)
-
-    def level_rows(energy):
-        rows = lax.dynamic_slice_in_dim(energy, ka * local_k, local_k, axis=0)
-        return jnp.broadcast_to(rows[:, :, None], rows.shape + (LANES,))
-
-    levels = jnp.concatenate(
-        [level_rows(virt_energy), level_rows(cube.swap(virt_energy, cube.core))]
-    )
+    other_energy = cube.swap(virt_energy, cube.core)
+
+    def operands(late_ka, late_band):
+        def level_rows(energy):
+            rows = lax.dynamic_slice_in_dim(energy, late_ka * local_k, local_k, axis=0)
+            return jnp.broadcast_to(rows[:, :, None], rows.shape + (LANES,))
+
+        levels = jnp.concatenate([level_rows(virt_energy), level_rows(other_energy)])
+        near_start = (late_band // 2) % 2 * (grid_count // 2)
+        first_basis = lax.dynamic_slice_in_dim(basis, near_start, grid_count // 8, axis=1)
+        factors = jnp.where(late_band % 2 == 0, coulomb[:1], coulomb[1:])
+        return levels, first_basis, factors
+
     sources = partners_of(partner, ka, local_k)
     neighbour_sources = partners_of(partner, jnp.bitwise_xor(ka, 1), local_k)
-    partner_occ, partner_energy, first_basis = fetch_partners(
-        cube, occupied, occ_energy, sources, neighbour_sources, basis[:, : grid_count // 8]
+    near_occ, far_occ, partner_energy, (levels, first_basis, factors) = fetch_partners(
+        cube, occupied, occ_energy, sources, neighbour_sources, operands
     )
     partner_energy = jnp.broadcast_to(
         partner_energy[:, :, None], partner_energy.shape + (LANES,)
     )
-    factors = jnp.where(first, coulomb[:1], coulomb[1:])
     coeffs, packed = project(
-        partner_occ, virtual, other_virtual, first_basis, basis, partner_energy, levels, factors,
+        near_occ, far_occ, virtual, other_virtual, first_basis, basis, partner_energy, levels, factors,
         gram_scale,
     )
     packed = reduce_screen(cube, packed)
-    far, near = respond(coeffs, packed, basis, partner_occ, virtual, other_virtual)
+    far, near = respond(coeffs, packed, basis, near_occ, far_occ, virtual, other_virtual)
     arrived = cube.swap(far[0], cube.y)
     terms = (near[0].astype(F32) + arrived.astype(F32)).astype(BF16)
     updates = [

time: 72.5 us -> 69.5 us (0.959)
  waiting for transfers between devices: 22.5 us -> 18.3 us
  starting transfers between devices: 27 us -> 29.1 us
  other arithmetic: 6.69 us -> 5.49 us
    ppermute x26 -> x27, waiting for transfers between devices: 22.5 us -> 18.3 us  [swap(): lax.ppermute(value, ('ka', 'band'), [(device, device ^ mask) for device i...]
    ppermute x26 -> x27, starting transfers between devices: 27 us -> 29.1 us  [swap(): lax.ppermute(value, ('ka', 'band'), [(device, device ^ mask) for device i...]
    dynamic_slice x2 -> x4, local copies, waits for them, and re-layouts: 0.7 us -> 1.78 us  [the longest x1 1.08 us: operands(): lax.dynamic_slice_in_dim(basis, near_start, grid_count // 8, axis=1)]
    slice x1 -> x0, local copies, waits for them, and re-layouts: 1.08 us -> none  [shards(): basis[:, :grid_count // 8]]
    select_n x2 -> x1, other arithmetic: 1.65 us -> 0.77 us  [operands(): factors = jnp.where(late_band % 2 == 0, coulomb[:1], coulomb[1:])]
    pallas_call x1 -> x2, Pallas kernels: 5.89 us -> 6.11 us  [the longest x1 3.23 us: project(): pl.pallas_call(functools.partial(project_near_kernel, starts=starts), in_...]
  transfers between devices with their start and end apart: 26 -> 27, of which waited for: 14 -> 14; matrix products, arithmetic and copies ran while one was open for 9% -> 8% of each run, Pallas kernels for 4% -> 9%
where the time goes in v7:
time: 69.5 us; the launch traced here: 69.2 us
  starting transfers between devices  29.1 us (42%)
  waiting for transfers between devices  18.3 us (26%)
  Pallas kernels  13.1 us (19%)
  other arithmetic  5.49 us (8%)
  local copies, waits for them, and re-layouts  2.21 us (3%)
  between operations  0.98 us (1%)
    ppermute x27, starting transfers between devices, swap(): lax.ppermute(value, ('ka', 'band'), [(device, device ^ mask) for device i...  29.1 us
    ppermute x27, waiting for transfers between devices, swap(): lax.ppermute(value, ('ka', 'band'), [(device, device ^ mask) for device i...  18.3 us
    pallas_call x1, Pallas kernels, respond(): pl.pallas_call(respond_far_kernel, in_specs=[VMEM_SPEC] * 5 + [any_spec],...  4.16 us
    pallas_call x1, Pallas kernels, project(): pl.pallas_call(functools.partial(project_near_kernel, starts=starts), in_...  3.23 us
    pallas_call x1, Pallas kernels, project(): pl.pallas_call(functools.partial(project_kernel, scale=scale), in_specs=[...  2.89 us
    pallas_call x1, Pallas kernels, respond(): pl.pallas_call(respond_near_kernel, in_specs=[VMEM_SPEC] * 5, out_specs=[...  2.8 us
  transfers between devices with their start and end apart: 27, of which 14 were waited for; matrix products, arithmetic and copies ran while one was open for 8% of the time, Pallas kernels for 9%

profile of v7, /device:TPU:0, one launch (start us, length us, event | category | flops | bytes accessed | tf_op | source)
XLA Modules:
  0.0 69.2 jit_solution(329022037078545244)
XLA Ops:
  1.6 5.1 %collective-permute-start.2 = (bf16[1,2,8,1152]{3,2,1,0:T(8,128)(2,1)S(1)}, bf16[1,2,8,1152]{3,2,1,0:T(8,128)(2,1)S(1)}, u32[]{:S(2)}, u32[]{:S(2)}) collective-permute-start(bf16[1,2,8,1152]{3,2,1,0:T(8,128)(2,1)S(1)} %get-tuple-element.67), channel_id=1, source_target_pairs={{0,24},{1,25},{2,26},{3,27},{4,28},{5,29},{6,30},{7,31},{8,16},{9,... | collective-permute-start | bytes 110600 | tf_op jit(solution)/shard_map/ppermute | solution.py:46
  9.0 2.6 %collective-permute-done.1 = bf16[1,2,8,1152]{3,2,1,0:T(8,128)(2,1)S(1)} collective-permute-done((bf16[1,2,8,1152]{3,2,1,0:T(8,128)(2,1)S(1)}, bf16[1,2,8,1152]{3,2,1,0:T(8,128)(2,1)S(1)}, u32[]{:S(2)}, u32[]{:S(2)}) %collective-permute-start.1) | collective-permute-done | bytes 36896 | tf_op jit(solution)/shard_map/ppermute | solution.py:46
  12.1 1.6 %collective-permute-start.6 = (bf16[2,8,1024]{2,1,0:T(8,128)(2,1)S(1)}, bf16[2,8,1024]{2,1,0:T(8,128)(2,1)S(1)}, u32[]{:S(2)}, u32[]{:S(2)}) collective-permute-start(bf16[2,8,1024]{2,1,0:T(8,128)(2,1)S(1)} %slice.143), channel_id=1, source_target_pairs={{0,5},{1,4},{2,7},{3,6},{4,1},{5,0},{6,3},{7,2},{8,13},{9,12},{10,... | collective-permute-start | bytes 98312 | tf_op jit(solution)/shard_map/ppermute | solution.py:46
  17.7 1.6 %collective-permute-start.7 = (bf16[2,8,2048]{2,1,0:T(8,128)(2,1)S(1)}, bf16[2,8,2048]{2,1,0:T(8,128)(2,1)S(1)}, u32[]{:S(2)}, u32[]{:S(2)}) collective-permute-start(bf16[2,8,2048]{2,1,0:T(8,128)(2,1)S(1)} %pad_maximum_fusion.5.occ_ref), channel_id=1, source_target_pairs={{0,2},{1,3},{2,0},{3,1},{4,6},{5,7},{6,4},{7,5},{8,10},{9,11},{10,... | collective-permute-start | bytes 196616 | tf_op jit(solution)/shard_map/ppermute | solution.py:46
  19.4 3.2 %project_near.1 = (f32[1024,512]{1,0:T(8,128)S(1)}, bf16[512,2048]{1,0:T(8,128)(2,1)S(1)}) custom-call(bf16[2,8,2048]{2,1,0:T(8,128)(2,1)S(1)} %pad_maximum_fusion.5.occ_ref, bf16[2,32,4096]{2,1,0:T(8,128)(2,1)S(1)} %copy-done.1, bf16[2,32,4096]{2,1,0:T(8,128)(2,1)S(1)} %collective-permute-done.8.other_ref, ...), custom_call_target="tpu_custom_call" | custom-call | flops 2147483648 | bytes 4194304 | tf_op jit(solution)/shard_map/project_near/pallas_call | solution.py:335
  22.8 2.9 %project.1 = (bf16[1024,512]{1,0:T(8,128)(2,1)S(1)}, bf16[1088,128]{1,0:T(8,128)(2,1)S(1)}) custom-call(bf16[2,8,2048]{2,1,0:T(8,128)(2,1)S(1)} %collective-permute-done.7.occ_ref, bf16[2,32,4096]{2,1,0:T(8,128)(2,1)S(1)} %copy-done.1, bf16[2,32,4096]{2,1,0:T(8,128)(2,1)S(1)} %collective-permute-done.8.other_ref, ...), custom_call_target="tpu_custom_call" | custom-call | flops 2147483648 | bytes 4194304 | tf_op jit(solution)/shard_map/project/pallas_call | solution.py:351
  26.6 1.4 %collective-permute-start.11 = (bf16[272,128]{1,0:T(8,128)(2,1)S(1)}, bf16[272,128]{1,0:T(8,128)(2,1)S(1)}, u32[]{:S(2)}, u32[]{:S(2)}) collective-permute-start(bf16[272,128]{1,0:T(8,128)(2,1)S(1)} %get-tuple-element.57), channel_id=1, source_target_pairs={{0,6},{1,7},{2,4},{3,5},{4,2},{5,3},{6,0},{7,1},{8,14},{9,15},{10,... | collective-permute-start | bytes 208904 | tf_op jit(solution)/shard_map/ppermute | solution.py:46
  28.0 1.2 %collective-permute-start.10 = (bf16[272,128]{1,0:T(8,128)(2,1)S(1)}, bf16[272,128]{1,0:T(8,128)(2,1)S(1)}, u32[]{:S(2)}, u32[]{:S(2)}) collective-permute-start(bf16[272,128]{1,0:T(8,128)(2,1)S(1)} %get-tuple-element.58), channel_id=1, source_target_pairs={{0,4},{1,5},{2,6},{3,7},{4,0},{5,1},{6,2},{7,3},{8,12},{9,13},{10,... | collective-permute-start | bytes 208904 | tf_op jit(solution)/shard_map/ppermute | solution.py:46
  30.1 1.8 %collective-permute-done.11 = bf16[272,128]{1,0:T(8,128)(2,1)S(1)} collective-permute-done((bf16[272,128]{1,0:T(8,128)(2,1)S(1)}, bf16[272,128]{1,0:T(8,128)(2,1)S(1)}, u32[]{:S(2)}, u32[]{:S(2)}) %collective-permute-start.11) | collective-permute-done | bytes 69664 | tf_op jit(solution)/shard_map/ppermute | solution.py:46
  32.4 1.5 %collective-permute-start.14 = (bf16[272,128]{1,0:T(8,128)(2,1)S(1)}, bf16[272,128]{1,0:T(8,128)(2,1)S(1)}, u32[]{:S(2)}, u32[]{:S(2)}) collective-permute-start(bf16[272,128]{1,0:T(8,128)(2,1)S(1)} %fusion.2), channel_id=1, source_target_pairs={{0,24},{1,25},{2,26},{3,27},{4,28},{5,29},{6,30},{7,31},{8,16},{9,... | collective-permute-start | bytes 208904 | tf_op jit(solution)/shard_map/ppermute | solution.py:46
  34.5 2.3 %collective-permute-start.12 = (bf16[272,128]{1,0:T(8,128)(2,1)S(1)}, bf16[272,128]{1,0:T(8,128)(2,1)S(1)}, u32[]{:S(2)}, u32[]{:S(2)}) collective-permute-start(bf16[272,128]{1,0:T(8,128)(2,1)S(1)} %fusion.2), channel_id=1, source_target_pairs={{0,8},{1,9},{2,10},{3,11},{4,12},{5,13},{6,14},{7,15},{8,0},{9,1},... | collective-permute-start | bytes 208904 | tf_op jit(solution)/shard_map/ppermute | solution.py:46
  36.9 1.7 %collective-permute-done.14 = bf16[272,128]{1,0:T(8,128)(2,1)S(1)} collective-permute-done((bf16[272,128]{1,0:T(8,128)(2,1)S(1)}, bf16[272,128]{1,0:T(8,128)(2,1)S(1)}, u32[]{:S(2)}, u32[]{:S(2)}) %collective-permute-start.14) | collective-permute-done | bytes 69664 | tf_op jit(solution)/shard_map/ppermute | solution.py:46
  38.6 1.5 %collective-permute-done.13 = bf16[272,128]{1,0:T(8,128)(2,1)S(1)} collective-permute-done((bf16[272,128]{1,0:T(8,128)(2,1)S(1)}, bf16[272,128]{1,0:T(8,128)(2,1)S(1)}, u32[]{:S(2)}, u32[]{:S(2)}) %collective-permute-start.13) | collective-permute-done | bytes 69664 | tf_op jit(solution)/shard_map/ppermute | solution.py:46
  40.1 1.6 %collective-permute-start.17 = (bf16[272,128]{1,0:T(8,128)(2,1)S(1)}, bf16[272,128]{1,0:T(8,128)(2,1)S(1)}, u32[]{:S(2)}, u32[]{:S(2)}) collective-permute-start(bf16[272,128]{1,0:T(8,128)(2,1)S(1)} %add_convert_fusion.2), channel_id=1, source_target_pairs={{0,6},{1,7},{2,4},{3,5},{4,2},{5,3},{6,0},{7,1},{8,14},{9,15},{10,... | collective-permute-start | bytes 208904 | tf_op jit(solution)/shard_map/ppermute | solution.py:46
  42.5 1.2 %collective-permute-start.15 = (bf16[272,128]{1,0:T(8,128)(2,1)S(1)}, bf16[272,128]{1,0:T(8,128)(2,1)S(1)}, u32[]{:S(2)}, u32[]{:S(2)}) collective-permute-start(bf16[272,128]{1,0:T(8,128)(2,1)S(1)} %add_convert_fusion.2), channel_id=1, source_target_pairs={{0,2},{1,3},{2,0},{3,1},{4,6},{5,7},{6,4},{7,5},{8,10},{9,11},{10,... | collective-permute-start | bytes 208904 | tf_op jit(solution)/shard_map/ppermute | solution.py:46
  43.7 1.6 %collective-permute-done.17 = bf16[272,128]{1,0:T(8,128)(2,1)S(1)} collective-permute-done((bf16[272,128]{1,0:T(8,128)(2,1)S(1)}, bf16[272,128]{1,0:T(8,128)(2,1)S(1)}, u32[]{:S(2)}, u32[]{:S(2)}) %collective-permute-start.17) | collective-permute-done | bytes 69664 | tf_op jit(solution)/shard_map/ppermute | solution.py:46
  46.9 4.2 %respond_far.1 = (bf16[2,8,2048]{2,1,0:T(8,128)(2,1)S(1)}, bf16[2,32,2048]{2,1,0:T(8,128)(2,1)S(1)}, bf16[2,32,2048]{2,1,0:T(8,128)(2,1)S(1)}, bf16[1024,512]{1,0:T(8,128)(2,1)S(1)}, bf16[2,512,1024]{2,1,0:T(8,128)(2,1)S(1)}) custom-call(bf16[1024,512]{1,0:T(8,128)(2,1)S(1)} %get-tuple-element.32.coeffs_ref, bf16[1088,128]{1,0:T(8,128)(2,1)S(1)} %bitcast.41, ...), custom_call_target="tpu_custom_call" | custom-call | flops 2147483648 | bytes 4194304 | tf_op jit(solution)/shard_map/respond_far/pallas_call | solution.py:492
  51.1 1.2 %collective-permute-start.18 = (bf16[2,8,2048]{2,1,0:T(8,128)(2,1)S(1)}, bf16[2,8,2048]{2,1,0:T(8,128)(2,1)S(1)}, u32[]{:S(2)}, u32[]{:S(2)}) collective-permute-start(bf16[2,8,2048]{2,1,0:T(8,128)(2,1)S(1)} %get-tuple-element.37), channel_id=1, source_target_pairs={{0,2},{1,3},{2,0},{3,1},{4,6},{5,7},{6,4},{7,5},{8,10},{9,11},{10,... | collective-permute-start | bytes 196616 | tf_op jit(solution)/shard_map/ppermute | solution.py:46
  52.3 2.8 %respond_near.1 = (bf16[2,8,2048]{2,1,0:T(8,128)(2,1)S(1)}, bf16[2,32,2048]{2,1,0:T(8,128)(2,1)S(1)}, bf16[2,32,2048]{2,1,0:T(8,128)(2,1)S(1)}) custom-call(bf16[1024,512]{1,0:T(8,128)(2,1)S(1)} %get-tuple-element.34.screened_ref, bf16[2,8,2048]{2,1,0:T(8,128)(2,1)S(1)} %pad_maximum_fusion.5.occ_ref, bf16[2,32,4096]{2,1,0:T(8,128)(2,1)S(1)} %copy-done.1, ...), custom_call_target="tpu_custom_call" | custom-call | flops 2147483648 | bytes 4194304 | tf_op jit(solution)/shard_map/respond_near/pallas_call | solution.py:509
  55.5 1.3 %collective-permute-start.19 = (bf16[2,8,1024]{2,1,0:T(8,128)(2,1)S(1)}, bf16[2,8,1024]{2,1,0:T(8,128)(2,1)S(1)}, u32[]{:S(2)}, u32[]{:S(2)}) collective-permute-start(bf16[2,8,1024]{2,1,0:T(8,128)(2,1)S(1)} %get-tuple-element.65), channel_id=1, source_target_pairs={{0,1},{1,0},{2,3},{3,2},{4,5},{5,4},{6,7},{7,6},{8,9},{9,8},{10,11... | collective-permute-start | bytes 98312 | tf_op jit(solution)/shard_map/ppermute | solution.py:46
  58.2 2.5 %collective-permute-done.20 = bf16[2,8,1024]{2,1,0:T(8,128)(2,1)S(1)} collective-permute-done((bf16[2,8,1024]{2,1,0:T(8,128)(2,1)S(1)}, bf16[2,8,1024]{2,1,0:T(8,128)(2,1)S(1)}, u32[]{:S(2)}, u32[]{:S(2)}) %collective-permute-start.20) | collective-permute-done | bytes 32800 | tf_op jit(solution)/shard_map/ppermute | solution.py:46
  61.1 1.2 %collective-permute-start.22 = (bf16[1,2,8,1024]{3,2,1,0:T(8,128)(2,1)S(1)}, bf16[1,2,8,1024]{3,2,1,0:T(8,128)(2,1)S(1)}, u32[]{:S(2)}, u32[]{:S(2)}) collective-permute-start(bf16[1,2,8,1024]{3,2,1,0:T(8,128)(2,1)S(1)} %get-tuple-element.59), channel_id=1, source_target_pairs={{0,8},{1,9},{2,10},{3,11},{4,12},{5,13},{6,14},{7,15},{8,0},{9,1},... | collective-permute-start | bytes 98312 | tf_op jit(solution)/shard_map/ppermute | solution.py:46
  62.3 1.5 %collective-permute-start.24 = (bf16[1,2,8,1024]{3,2,1,0:T(8,128)(2,1)S(1)}, bf16[1,2,8,1024]{3,2,1,0:T(8,128)(2,1)S(1)}, u32[]{:S(2)}, u32[]{:S(2)}) collective-permute-start(bf16[1,2,8,1024]{3,2,1,0:T(8,128)(2,1)S(1)} %get-tuple-element.60), channel_id=1, source_target_pairs={{0,24},{1,25},{2,26},{3,27},{4,28},{5,29},{6,30},{7,31},{8,16},{9,... | collective-permute-start | bytes 98312 | tf_op jit(solution)/shard_map/ppermute | solution.py:46
  65.7 2.3 %collective-permute-done.24 = bf16[1,2,8,1024]{3,2,1,0:T(8,128)(2,1)S(1)} collective-permute-done((bf16[1,2,8,1024]{3,2,1,0:T(8,128)(2,1)S(1)}, bf16[1,2,8,1024]{3,2,1,0:T(8,128)(2,1)S(1)}, u32[]{:S(2)}, u32[]{:S(2)}) %collective-permute-start.24) | collective-permute-done | bytes 32800 | tf_op jit(solution)/shard_map/ppermute | solution.py:46
  (88 shorter events, 18.5 us)
Async XLA Ops:
  1.6 7.4 %collective-permute-start.2 = (bf16[1,2,8,1152]{3,2,1,0:T(8,128)(2,1)S(1)}, bf16[1,2,8,1152]{3,2,1,0:T(8,128)(2,1)S(1)}, u32[]{:S(2)}, u32[]{:S(2)}) collective-permute-start(bf16[1,2,8,1152]{3,2,1,0:T(8,128)(2,1)S(1)} %get-tuple-element.67), channel_id=1, source_target_pairs={{0,24},{1,25},{2,26},{3,27},{4,28},{5,29},{6,30},{7,31},{8,16},{9,... | collective-permute-start | bytes 110600 | tf_op jit(solution)/shard_map/ppermute | solution.py:46
  6.7 4.9 %collective-permute-start.1 = (bf16[1,2,8,1152]{3,2,1,0:T(8,128)(2,1)S(1)}, bf16[1,2,8,1152]{3,2,1,0:T(8,128)(2,1)S(1)}, u32[]{:S(2)}, u32[]{:S(2)}) collective-permute-start(bf16[1,2,8,1152]{3,2,1,0:T(8,128)(2,1)S(1)} %get-tuple-element.67), channel_id=1, source_target_pairs={{0,16},{1,17},{2,18},{3,19},{4,20},{5,21},{6,22},{7,23},{8,24},{9,... | collective-permute-start | bytes 110600 | tf_op jit(solution)/shard_map/ppermute | solution.py:46
  6.7 4.9 %collective-permute-start = (bf16[1,2,8,1152]{3,2,1,0:T(8,128)(2,1)S(1)}, bf16[1,2,8,1152]{3,2,1,0:T(8,128)(2,1)S(1)}, u32[]{:S(2)}, u32[]{:S(2)}) collective-permute-start(bf16[1,2,8,1152]{3,2,1,0:T(8,128)(2,1)S(1)} %get-tuple-element.67), channel_id=1, source_target_pairs={{0,8},{1,9},{2,10},{3,11},{4,12},{5,13},{6,14},{7,15},{8,0},{9,1},... | collective-permute-start | bytes 110600 | tf_op jit(solution)/shard_map/ppermute | solution.py:46
  7.3 9.4 %collective-permute-start.4 = (f32[16,32]{1,0:T(8,128)}, f32[16,32]{1,0:T(8,128)S(1)}, u32[]{:S(2)}, u32[]{:S(2)}) collective-permute-start(f32[16,32]{1,0:T(8,128)} %param.10), channel_id=1, source_target_pairs={{0,1},{1,0},{2,3},{3,2},{4,5},{5,4},{6,7},{7,6},{8,9},{9,8},{10,11... | collective-permute-start | bytes 6152 | tf_op jit(solution)/shard_map/ppermute | solution.py:46
  7.3 12.1 %collective-permute-start.8 = (bf16[2,32,4096]{2,1,0:T(8,128)(2,1)}, bf16[2,32,4096]{2,1,0:T(8,128)(2,1)S(1)}, u32[]{:S(2)}, u32[]{:S(2)}) collective-permute-start(bf16[2,32,4096]{2,1,0:T(8,128)(2,1)} %own_ref.7), channel_id=1, source_target_pairs={{0,1},{1,0},{2,3},{3,2},{4,5},{5,4},{6,7},{7,6},{8,9},{9,8},{10,11... | collective-permute-start | bytes 1572872 | tf_op jit(solution)/shard_map/ppermute | solution.py:46
  12.0 5.6 %collective-permute-start.5 = (bf16[2,8,1024]{2,1,0:T(8,128)(2,1)S(1)}, bf16[2,8,1024]{2,1,0:T(8,128)(2,1)S(1)}, u32[]{:S(2)}, u32[]{:S(2)}) collective-permute-start(bf16[2,8,1024]{2,1,0:T(8,128)(2,1)S(1)} %slice.144), channel_id=1, source_target_pairs={{0,1},{1,0},{2,3},{3,2},{4,5},{5,4},{6,7},{7,6},{8,9},{9,8},{10,11... | collective-permute-start | bytes 98312 | tf_op jit(solution)/shard_map/ppermute | solution.py:46
  12.1 5.6 %collective-permute-start.6 = (bf16[2,8,1024]{2,1,0:T(8,128)(2,1)S(1)}, bf16[2,8,1024]{2,1,0:T(8,128)(2,1)S(1)}, u32[]{:S(2)}, u32[]{:S(2)}) collective-permute-start(bf16[2,8,1024]{2,1,0:T(8,128)(2,1)S(1)} %slice.143), channel_id=1, source_target_pairs={{0,5},{1,4},{2,7},{3,6},{4,1},{5,0},{6,3},{7,2},{8,13},{9,12},{10,... | collective-permute-start | bytes 98312 | tf_op jit(solution)/shard_map/ppermute | solution.py:46
  17.7 5.0 %collective-permute-start.7 = (bf16[2,8,2048]{2,1,0:T(8,128)(2,1)S(1)}, bf16[2,8,2048]{2,1,0:T(8,128)(2,1)S(1)}, u32[]{:S(2)}, u32[]{:S(2)}) collective-permute-start(bf16[2,8,2048]{2,1,0:T(8,128)(2,1)S(1)} %pad_maximum_fusion.5.occ_ref), channel_id=1, source_target_pairs={{0,2},{1,3},{2,0},{3,1},{4,6},{5,7},{6,4},{7,5},{8,10},{9,11},{10,... | collective-permute-start | bytes 196616 | tf_op jit(solution)/shard_map/ppermute | solution.py:46
  25.7 4.4 %collective-permute-start.9 = (bf16[272,128]{1,0:T(8,128)(2,1)S(1)}, bf16[272,128]{1,0:T(8,128)(2,1)S(1)}, u32[]{:S(2)}, u32[]{:S(2)}) collective-permute-start(bf16[272,128]{1,0:T(8,128)(2,1)S(1)} %get-tuple-element.56), channel_id=1, source_target_pairs={{0,2},{1,3},{2,0},{3,1},{4,6},{5,7},{6,4},{7,5},{8,10},{9,11},{10,... | collective-permute-start | bytes 208904 | tf_op jit(solution)/shard_map/ppermute | solution.py:46
  26.6 5.2 %collective-permute-start.11 = (bf16[272,128]{1,0:T(8,128)(2,1)S(1)}, bf16[272,128]{1,0:T(8,128)(2,1)S(1)}, u32[]{:S(2)}, u32[]{:S(2)}) collective-permute-start(bf16[272,128]{1,0:T(8,128)(2,1)S(1)} %get-tuple-element.57), channel_id=1, source_target_pairs={{0,6},{1,7},{2,4},{3,5},{4,2},{5,3},{6,0},{7,1},{8,14},{9,15},{10,... | collective-permute-start | bytes 208904 | tf_op jit(solution)/shard_map/ppermute | solution.py:46
  28.0 4.3 %collective-permute-start.10 = (bf16[272,128]{1,0:T(8,128)(2,1)S(1)}, bf16[272,128]{1,0:T(8,128)(2,1)S(1)}, u32[]{:S(2)}, u32[]{:S(2)}) collective-permute-start(bf16[272,128]{1,0:T(8,128)(2,1)S(1)} %get-tuple-element.58), channel_id=1, source_target_pairs={{0,4},{1,5},{2,6},{3,7},{4,0},{5,1},{6,2},{7,3},{8,12},{9,13},{10,... | collective-permute-start | bytes 208904 | tf_op jit(solution)/shard_map/ppermute | solution.py:46
  32.4 6.2 %collective-permute-start.14 = (bf16[272,128]{1,0:T(8,128)(2,1)S(1)}, bf16[272,128]{1,0:T(8,128)(2,1)S(1)}, u32[]{:S(2)}, u32[]{:S(2)}) collective-permute-start(bf16[272,128]{1,0:T(8,128)(2,1)S(1)} %fusion.2), channel_id=1, source_target_pairs={{0,24},{1,25},{2,26},{3,27},{4,28},{5,29},{6,30},{7,31},{8,16},{9,... | collective-permute-start | bytes 208904 | tf_op jit(solution)/shard_map/ppermute | solution.py:46
  33.9 6.1 %collective-permute-start.13 = (bf16[272,128]{1,0:T(8,128)(2,1)S(1)}, bf16[272,128]{1,0:T(8,128)(2,1)S(1)}, u32[]{:S(2)}, u32[]{:S(2)}) collective-permute-start(bf16[272,128]{1,0:T(8,128)(2,1)S(1)} %fusion.2), channel_id=1, source_target_pairs={{0,16},{1,17},{2,18},{3,19},{4,20},{5,21},{6,22},{7,23},{8,24},{9,... | collective-permute-start | bytes 208904 | tf_op jit(solution)/shard_map/ppermute | solution.py:46
  34.5 5.5 %collective-permute-start.12 = (bf16[272,128]{1,0:T(8,128)(2,1)S(1)}, bf16[272,128]{1,0:T(8,128)(2,1)S(1)}, u32[]{:S(2)}, u32[]{:S(2)}) collective-permute-start(bf16[272,128]{1,0:T(8,128)(2,1)S(1)} %fusion.2), channel_id=1, source_target_pairs={{0,8},{1,9},{2,10},{3,11},{4,12},{5,13},{6,14},{7,15},{8,0},{9,1},... | collective-permute-start | bytes 208904 | tf_op jit(solution)/shard_map/ppermute | solution.py:46
  40.1 5.3 %collective-permute-start.17 = (bf16[272,128]{1,0:T(8,128)(2,1)S(1)}, bf16[272,128]{1,0:T(8,128)(2,1)S(1)}, u32[]{:S(2)}, u32[]{:S(2)}) collective-permute-start(bf16[272,128]{1,0:T(8,128)(2,1)S(1)} %add_convert_fusion.2), channel_id=1, source_target_pairs={{0,6},{1,7},{2,4},{3,5},{4,2},{5,3},{6,0},{7,1},{8,14},{9,15},{10,... | collective-permute-start | bytes 208904 | tf_op jit(solution)/shard_map/ppermute | solution.py:46
  42.5 4.3 %collective-permute-start.15 = (bf16[272,128]{1,0:T(8,128)(2,1)S(1)}, bf16[272,128]{1,0:T(8,128)(2,1)S(1)}, u32[]{:S(2)}, u32[]{:S(2)}) collective-permute-start(bf16[272,128]{1,0:T(8,128)(2,1)S(1)} %add_convert_fusion.2), channel_id=1, source_target_pairs={{0,2},{1,3},{2,0},{3,1},{4,6},{5,7},{6,4},{7,5},{8,10},{9,11},{10,... | collective-permute-start | bytes 208904 | tf_op jit(solution)/shard_map/ppermute | solution.py:46
  51.1 4.3 %collective-permute-start.18 = (bf16[2,8,2048]{2,1,0:T(8,128)(2,1)S(1)}, bf16[2,8,2048]{2,1,0:T(8,128)(2,1)S(1)}, u32[]{:S(2)}, u32[]{:S(2)}) collective-permute-start(bf16[2,8,2048]{2,1,0:T(8,128)(2,1)S(1)} %get-tuple-element.37), channel_id=1, source_target_pairs={{0,2},{1,3},{2,0},{3,1},{4,6},{5,7},{6,4},{7,5},{8,10},{9,11},{10,... | collective-permute-start | bytes 196616 | tf_op jit(solution)/shard_map/ppermute | solution.py:46
  55.4 5.3 %collective-permute-start.21 = (bf16[2,8,1024]{2,1,0:T(8,128)(2,1)S(1)}, bf16[2,8,1024]{2,1,0:T(8,128)(2,1)S(1)}, u32[]{:S(2)}, u32[]{:S(2)}) collective-permute-start(bf16[2,8,1024]{2,1,0:T(8,128)(2,1)S(1)} %get-tuple-element.65), channel_id=1, source_target_pairs={{0,5},{1,4},{2,7},{3,6},{4,1},{5,0},{6,3},{7,2},{8,13},{9,12},{10,... | collective-permute-start | bytes 98312 | tf_op jit(solution)/shard_map/ppermute | solution.py:46
  55.5 5.3 %collective-permute-start.19 = (bf16[2,8,1024]{2,1,0:T(8,128)(2,1)S(1)}, bf16[2,8,1024]{2,1,0:T(8,128)(2,1)S(1)}, u32[]{:S(2)}, u32[]{:S(2)}) collective-permute-start(bf16[2,8,1024]{2,1,0:T(8,128)(2,1)S(1)} %get-tuple-element.65), channel_id=1, source_target_pairs={{0,1},{1,0},{2,3},{3,2},{4,5},{5,4},{6,7},{7,6},{8,9},{9,8},{10,11... | collective-permute-start | bytes 98312 | tf_op jit(solution)/shard_map/ppermute | solution.py:46
  57.7 6.9 %collective-permute-start.25 = (bf16[2,32,2048]{2,1,0:T(8,128)(2,1)S(1)}, bf16[2,32,2048]{2,1,0:T(8,128)(2,1)S(1)}, u32[]{:S(2)}, u32[]{:S(2)}) collective-permute-start(bf16[2,32,2048]{2,1,0:T(8,128)(2,1)S(1)} %get-tuple-element.39), channel_id=1, source_target_pairs={{0,1},{1,0},{2,3},{3,2},{4,5},{5,4},{6,7},{7,6},{8,9},{9,8},{10,11... | collective-permute-start | bytes 786440 | tf_op jit(solution)/shard_map/ppermute | solution.py:46
  57.8 6.9 %collective-permute-start.26 = (bf16[2,32,2048]{2,1,0:T(8,128)(2,1)S(1)}, bf16[2,32,2048]{2,1,0:T(8,128)(2,1)S(1)}, u32[]{:S(2)}, u32[]{:S(2)}) collective-permute-start(bf16[2,32,2048]{2,1,0:T(8,128)(2,1)S(1)} %get-tuple-element.41), channel_id=1, source_target_pairs={{0,1},{1,0},{2,3},{3,2},{4,5},{5,4},{6,7},{7,6},{8,9},{9,8},{10,11... | collective-permute-start | bytes 786440 | tf_op jit(solution)/shard_map/ppermute | solution.py:46
  61.1 6.9 %collective-permute-start.22 = (bf16[1,2,8,1024]{3,2,1,0:T(8,128)(2,1)S(1)}, bf16[1,2,8,1024]{3,2,1,0:T(8,128)(2,1)S(1)}, u32[]{:S(2)}, u32[]{:S(2)}) collective-permute-start(bf16[1,2,8,1024]{3,2,1,0:T(8,128)(2,1)S(1)} %get-tuple-element.59), channel_id=1, source_target_pairs={{0,8},{1,9},{2,10},{3,11},{4,12},{5,13},{6,14},{7,15},{8,0},{9,1},... | collective-permute-start | bytes 98312 | tf_op jit(solution)/shard_map/ppermute | solution.py:46
  62.3 5.7 %collective-permute-start.24 = (bf16[1,2,8,1024]{3,2,1,0:T(8,128)(2,1)S(1)}, bf16[1,2,8,1024]{3,2,1,0:T(8,128)(2,1)S(1)}, u32[]{:S(2)}, u32[]{:S(2)}) collective-permute-start(bf16[1,2,8,1024]{3,2,1,0:T(8,128)(2,1)S(1)} %get-tuple-element.60), channel_id=1, source_target_pairs={{0,24},{1,25},{2,26},{3,27},{4,28},{5,29},{6,30},{7,31},{8,16},{9,... | collective-permute-start | bytes 98312 | tf_op jit(solution)/shard_map/ppermute | solution.py:46
  63.7 4.8 %collective-permute-start.23 = (bf16[1,2,8,1024]{3,2,1,0:T(8,128)(2,1)S(1)}, bf16[1,2,8,1024]{3,2,1,0:T(8,128)(2,1)S(1)}, u32[]{:S(2)}, u32[]{:S(2)}) collective-permute-start(bf16[1,2,8,1024]{3,2,1,0:T(8,128)(2,1)S(1)} %get-tuple-element.61), channel_id=1, source_target_pairs={{0,16},{1,17},{2,18},{3,19},{4,20},{5,21},{6,22},{7,23},{8,24},{9,... | collective-permute-start | bytes 98312 | tf_op jit(solution)/shard_map/ppermute | solution.py:46
  (5 other events, 31.9 us)

commit v8 on v7

--- a/solution.py
+++ b/solution.py
@@ -244,12 +244,14 @@
     copies.append(
         pltpu.make_async_copy(basis_ref.at[:, pl.ds(far, half)], far_ref, sems.at[len(copies)])
     )
-    for copy in copies:
+    for copy in copies[:-1]:
         copy.start()
     terms = [(virt_ref, k) for virt_ref in (own_ref, other_ref) for k in range(local_k)]
     for n, (start, end) in enumerate(parts):
         if n > 0:
             copies[n - 1].wait()
+        if n == 1:
+            copies[-1].start()
         for term, (virt_ref, k) in enumerate(terms):
             part = pair_coeffs(
                 occ_ref[k, :, start:end],
@@ -287,7 +289,8 @@
                     axis=1,
                 ).astype(BF16)
             )
-    coulomb = coulomb_ref[...] * math.sqrt(scale)
+    own_transfer = lax.axis_index("band") % 2
+    coulomb = coulomb_ref[pl.ds(own_transfer, 1), :] * math.sqrt(scale)
     tiles = {}
     for panel in range(0, count, 2):
         gram = lax.dot_general(
@@ -451,9 +454,9 @@
 
     for step in range(steps):
         fetch(far, step, far_ref, far_sems.at[step]).start()
+    screen_coeffs(coeffs_ref, packed_ref, screen_ref, screened_ref)
     for step in range(steps):
         fetch(near, step, near_ref, near_sem.at[step]).start()
-    screen_coeffs(coeffs_ref, packed_ref, screen_ref, screened_ref)
     respond_half(
         screened_ref, far_ref, field_ref, (occ_ref, own_ref, other_ref),
         (term_ref, own_update_ref, other_update_ref), far,
@@ -543,19 +546,18 @@
         levels = jnp.concatenate([level_rows(virt_energy), level_rows(other_energy)])
         near_start = (late_band // 2) % 2 * (grid_count // 2)
         first_basis = lax.dynamic_slice_in_dim(basis, near_start, grid_count // 8, axis=1)
-        factors = jnp.where(late_band % 2 == 0, coulomb[:1], coulomb[1:])
-        return levels, first_basis, factors
+        return levels, first_basis
 
     sources = partners_of(partner, ka, local_k)
     neighbour_sources = partners_of(partner, jnp.bitwise_xor(ka, 1), local_k)
-    near_occ, far_occ, partner_energy, (levels, first_basis, factors) = fetch_partners(
+    near_occ, far_occ, partner_energy, (levels, first_basis) = fetch_partners(
         cube, occupied, occ_energy, sources, neighbour_sources, operands
     )
     partner_energy = jnp.broadcast_to(
         partner_energy[:, :, None], partner_energy.shape + (LANES,)
     )
     coeffs, packed = project(
-        near_occ, far_occ, virtual, other_virtual, first_basis, basis, partner_energy, levels, factors,
+        near_occ, far_occ, virtual, other_virtual, first_basis, basis, partner_energy, levels, coulomb,
         gram_scale,
     )
     packed = reduce_screen(cube, packed)

time: 69.5 us -> 69.4 us (level)
  waiting for transfers between devices: 18.3 us -> 19.3 us
  other arithmetic: 5.49 us -> 4.72 us
    ppermute x27, waiting for transfers between devices: 18.3 us -> 19.3 us  [swap(): lax.ppermute(value, ('ka', 'band'), [(device, device ^ mask) for device i...]
    select_n x1 -> x0, other arithmetic: 0.77 us -> none  [operands(): factors = jnp.where(late_band % 2 == 0, coulomb[:1], coulomb[1:])]
  transfers between devices with their start and end apart: 27 -> 27, of which waited for: 14 -> 14; matrix products, arithmetic and copies ran while one was open for 8% -> 7% of each run, Pallas kernels for 9% -> 9%
where the time goes in v8:
time: 69.4 us; the launch traced here: 69.2 us
  starting transfers between devices  29 us (42%)
  waiting for transfers between devices  19.3 us (28%)
  Pallas kernels  13 us (19%)
  other arithmetic  4.72 us (7%)
  local copies, waits for them, and re-layouts  2.21 us (3%)
  between operations  0.98 us (1%)
    ppermute x27, starting transfers between devices, swap(): lax.ppermute(value, ('ka', 'band'), [(device, device ^ mask) for device i...  29 us
    ppermute x27, waiting for transfers between devices, swap(): lax.ppermute(value, ('ka', 'band'), [(device, device ^ mask) for device i...  19.3 us
    pallas_call x1, Pallas kernels, respond(): pl.pallas_call(respond_far_kernel, in_specs=[VMEM_SPEC] * 5 + [any_spec],...  4.16 us
    pallas_call x1, Pallas kernels, project(): pl.pallas_call(functools.partial(project_near_kernel, starts=starts), in_...  3.1 us
    pallas_call x1, Pallas kernels, project(): pl.pallas_call(functools.partial(project_kernel, scale=scale), in_specs=[...  2.9 us
    pallas_call x1, Pallas kernels, respond(): pl.pallas_call(respond_near_kernel, in_specs=[VMEM_SPEC] * 5, out_specs=[...  2.8 us
  transfers between devices with their start and end apart: 27, of which 14 were waited for; matrix products, arithmetic and copies ran while one was open for 7% of the time, Pallas kernels for 9%

profile of v8, /device:TPU:0, one launch (start us, length us, event | category | flops | bytes accessed | tf_op | source)
XLA Modules:
  0.0 69.2 jit_solution(10143492960039868005)
XLA Ops:
  1.6 5.1 %collective-permute-start.2 = (bf16[1,2,8,1152]{3,2,1,0:T(8,128)(2,1)S(1)}, bf16[1,2,8,1152]{3,2,1,0:T(8,128)(2,1)S(1)}, u32[]{:S(2)}, u32[]{:S(2)}) collective-permute-start(bf16[1,2,8,1152]{3,2,1,0:T(8,128)(2,1)S(1)} %get-tuple-element.65), channel_id=1, source_target_pairs={{0,24},{1,25},{2,26},{3,27},{4,28},{5,29},{6,30},{7,31},{8,16},{9,... | collective-permute-start | bytes 110600 | tf_op jit(solution)/shard_map/ppermute | solution.py:46
  9.0 2.6 %collective-permute-done.1 = bf16[1,2,8,1152]{3,2,1,0:T(8,128)(2,1)S(1)} collective-permute-done((bf16[1,2,8,1152]{3,2,1,0:T(8,128)(2,1)S(1)}, bf16[1,2,8,1152]{3,2,1,0:T(8,128)(2,1)S(1)}, u32[]{:S(2)}, u32[]{:S(2)}) %collective-permute-start.1) | collective-permute-done | bytes 36896 | tf_op jit(solution)/shard_map/ppermute | solution.py:46
  12.1 1.6 %collective-permute-start.6 = (bf16[2,8,1024]{2,1,0:T(8,128)(2,1)S(1)}, bf16[2,8,1024]{2,1,0:T(8,128)(2,1)S(1)}, u32[]{:S(2)}, u32[]{:S(2)}) collective-permute-start(bf16[2,8,1024]{2,1,0:T(8,128)(2,1)S(1)} %slice.133), channel_id=1, source_target_pairs={{0,5},{1,4},{2,7},{3,6},{4,1},{5,0},{6,3},{7,2},{8,13},{9,12},{10,... | collective-permute-start | bytes 98312 | tf_op jit(solution)/shard_map/ppermute | solution.py:46
  14.2 1.1 %constant_dynamic-slice_fusion.4.first_ref = bf16[512,512]{1,0:T(8,128)(2,1)S(1)} fusion(bf16[512,4096]{1,0:T(8,128)(2,1)} %basis_ref.3, s32[]{:T(128)S(6)} %select_n.245), kind=kLoop, calls=%fused_computation.51 | loop fusion | bytes 1048580 | tf_op jit(solution)/shard_map/dynamic_slice | solution.py:548
  16.1 1.5 %collective-permute-done.3 = bf16[2,8,1152]{2,1,0:T(8,128)(2,1)S(1)} collective-permute-done((bf16[2,8,1152]{2,1,0:T(8,128)(2,1)S(1)}, bf16[2,8,1152]{2,1,0:T(8,128)(2,1)S(1)}, u32[]{:S(2)}, u32[]{:S(2)}) %collective-permute-start.3) | collective-permute-done | bytes 36896 | tf_op jit(solution)/shard_map/ppermute | solution.py:46
  17.7 1.6 %collective-permute-start.7 = (bf16[2,8,2048]{2,1,0:T(8,128)(2,1)S(1)}, bf16[2,8,2048]{2,1,0:T(8,128)(2,1)S(1)}, u32[]{:S(2)}, u32[]{:S(2)}) collective-permute-start(bf16[2,8,2048]{2,1,0:T(8,128)(2,1)S(1)} %pad_maximum_fusion.5.occ_ref), channel_id=1, source_target_pairs={{0,2},{1,3},{2,0},{3,1},{4,6},{5,7},{6,4},{7,5},{8,10},{9,11},{10,... | collective-permute-start | bytes 196616 | tf_op jit(solution)/shard_map/ppermute | solution.py:46
  19.4 3.1 %project_near.1 = (f32[1024,512]{1,0:T(8,128)S(1)}, bf16[512,2048]{1,0:T(8,128)(2,1)S(1)}) custom-call(bf16[2,8,2048]{2,1,0:T(8,128)(2,1)S(1)} %pad_maximum_fusion.5.occ_ref, bf16[2,32,4096]{2,1,0:T(8,128)(2,1)S(1)} %copy-done.1, bf16[2,32,4096]{2,1,0:T(8,128)(2,1)S(1)} %collective-permute-done.8.other_ref, ...), custom_call_target="tpu_custom_call" | custom-call | flops 2147483648 | bytes 4194304 | tf_op jit(solution)/shard_map/project_near/pallas_call | solution.py:338
  22.6 2.9 %project.1 = (bf16[1024,512]{1,0:T(8,128)(2,1)S(1)}, bf16[1088,128]{1,0:T(8,128)(2,1)S(1)}) custom-call(bf16[2,8,2048]{2,1,0:T(8,128)(2,1)S(1)} %collective-permute-done.7.occ_ref, bf16[2,32,4096]{2,1,0:T(8,128)(2,1)S(1)} %copy-done.1, bf16[2,32,4096]{2,1,0:T(8,128)(2,1)S(1)} %collective-permute-done.8.other_ref, ...), custom_call_target="tpu_custom_call" | custom-call | flops 2147483648 | bytes 4194304 | tf_op jit(solution)/shard_map/project/pallas_call | solution.py:354
  27.6 1.5 %collective-permute-start.10 = (bf16[272,128]{1,0:T(8,128)(2,1)S(1)}, bf16[272,128]{1,0:T(8,128)(2,1)S(1)}, u32[]{:S(2)}, u32[]{:S(2)}) collective-permute-start(bf16[272,128]{1,0:T(8,128)(2,1)S(1)} %get-tuple-element.56), channel_id=1, source_target_pairs={{0,4},{1,5},{2,6},{3,7},{4,0},{5,1},{6,2},{7,3},{8,12},{9,13},{10,... | collective-permute-start | bytes 208904 | tf_op jit(solution)/shard_map/ppermute | solution.py:46
  29.9 1.9 %collective-permute-done.11 = bf16[272,128]{1,0:T(8,128)(2,1)S(1)} collective-permute-done((bf16[272,128]{1,0:T(8,128)(2,1)S(1)}, bf16[272,128]{1,0:T(8,128)(2,1)S(1)}, u32[]{:S(2)}, u32[]{:S(2)}) %collective-permute-start.11) | collective-permute-done | bytes 69664 | tf_op jit(solution)/shard_map/ppermute | solution.py:46
  32.2 1.5 %collective-permute-start.14 = (bf16[272,128]{1,0:T(8,128)(2,1)S(1)}, bf16[272,128]{1,0:T(8,128)(2,1)S(1)}, u32[]{:S(2)}, u32[]{:S(2)}) collective-permute-start(bf16[272,128]{1,0:T(8,128)(2,1)S(1)} %fusion.2), channel_id=1, source_target_pairs={{0,24},{1,25},{2,26},{3,27},{4,28},{5,29},{6,30},{7,31},{8,16},{9,... | collective-permute-start | bytes 208904 | tf_op jit(solution)/shard_map/ppermute | solution.py:46
  34.4 2.3 %collective-permute-start.12 = (bf16[272,128]{1,0:T(8,128)(2,1)S(1)}, bf16[272,128]{1,0:T(8,128)(2,1)S(1)}, u32[]{:S(2)}, u32[]{:S(2)}) collective-permute-start(bf16[272,128]{1,0:T(8,128)(2,1)S(1)} %fusion.2), channel_id=1, source_target_pairs={{0,8},{1,9},{2,10},{3,11},{4,12},{5,13},{6,14},{7,15},{8,0},{9,1},... | collective-permute-start | bytes 208904 | tf_op jit(solution)/shard_map/ppermute | solution.py:46
  36.7 1.7 %collective-permute-done.14 = bf16[272,128]{1,0:T(8,128)(2,1)S(1)} collective-permute-done((bf16[272,128]{1,0:T(8,128)(2,1)S(1)}, bf16[272,128]{1,0:T(8,128)(2,1)S(1)}, u32[]{:S(2)}, u32[]{:S(2)}) %collective-permute-start.14) | collective-permute-done | bytes 69664 | tf_op jit(solution)/shard_map/ppermute | solution.py:46
  38.4 1.5 %collective-permute-done.13 = bf16[272,128]{1,0:T(8,128)(2,1)S(1)} collective-permute-done((bf16[272,128]{1,0:T(8,128)(2,1)S(1)}, bf16[272,128]{1,0:T(8,128)(2,1)S(1)}, u32[]{:S(2)}, u32[]{:S(2)}) %collective-permute-start.13) | collective-permute-done | bytes 69664 | tf_op jit(solution)/shard_map/ppermute | solution.py:46
  39.9 1.8 %collective-permute-start.17 = (bf16[272,128]{1,0:T(8,128)(2,1)S(1)}, bf16[272,128]{1,0:T(8,128)(2,1)S(1)}, u32[]{:S(2)}, u32[]{:S(2)}) collective-permute-start(bf16[272,128]{1,0:T(8,128)(2,1)S(1)} %add_convert_fusion.2), channel_id=1, source_target_pairs={{0,6},{1,7},{2,4},{3,5},{4,2},{5,3},{6,0},{7,1},{8,14},{9,15},{10,... | collective-permute-start | bytes 208904 | tf_op jit(solution)/shard_map/ppermute | solution.py:46
  43.5 1.6 %collective-permute-done.17 = bf16[272,128]{1,0:T(8,128)(2,1)S(1)} collective-permute-done((bf16[272,128]{1,0:T(8,128)(2,1)S(1)}, bf16[272,128]{1,0:T(8,128)(2,1)S(1)}, u32[]{:S(2)}, u32[]{:S(2)}) %collective-permute-start.17) | collective-permute-done | bytes 69664 | tf_op jit(solution)/shard_map/ppermute | solution.py:46
  46.9 4.2 %respond_far.1 = (bf16[2,8,2048]{2,1,0:T(8,128)(2,1)S(1)}, bf16[2,32,2048]{2,1,0:T(8,128)(2,1)S(1)}, bf16[2,32,2048]{2,1,0:T(8,128)(2,1)S(1)}, bf16[1024,512]{1,0:T(8,128)(2,1)S(1)}, bf16[2,512,1024]{2,1,0:T(8,128)(2,1)S(1)}) custom-call(bf16[1024,512]{1,0:T(8,128)(2,1)S(1)} %get-tuple-element.30.coeffs_ref, bf16[1088,128]{1,0:T(8,128)(2,1)S(1)} %bitcast.41, ...), custom_call_target="tpu_custom_call" | custom-call | flops 2147483648 | bytes 4194304 | tf_op jit(solution)/shard_map/respond_far/pallas_call | solution.py:495
  51.0 1.1 %collective-permute-start.18 = (bf16[2,8,2048]{2,1,0:T(8,128)(2,1)S(1)}, bf16[2,8,2048]{2,1,0:T(8,128)(2,1)S(1)}, u32[]{:S(2)}, u32[]{:S(2)}) collective-permute-start(bf16[2,8,2048]{2,1,0:T(8,128)(2,1)S(1)} %get-tuple-element.35), channel_id=1, source_target_pairs={{0,2},{1,3},{2,0},{3,1},{4,6},{5,7},{6,4},{7,5},{8,10},{9,11},{10,... | collective-permute-start | bytes 196616 | tf_op jit(solution)/shard_map/ppermute | solution.py:46
  52.1 2.8 %respond_near.1 = (bf16[2,8,2048]{2,1,0:T(8,128)(2,1)S(1)}, bf16[2,32,2048]{2,1,0:T(8,128)(2,1)S(1)}, bf16[2,32,2048]{2,1,0:T(8,128)(2,1)S(1)}) custom-call(bf16[1024,512]{1,0:T(8,128)(2,1)S(1)} %get-tuple-element.32.screened_ref, bf16[2,8,2048]{2,1,0:T(8,128)(2,1)S(1)} %pad_maximum_fusion.5.occ_ref, bf16[2,32,4096]{2,1,0:T(8,128)(2,1)S(1)} %copy-done.1, ...), custom_call_target="tpu_custom_call" | custom-call | flops 2147483648 | bytes 4194304 | tf_op jit(solution)/shard_map/respond_near/pallas_call | solution.py:512
  55.5 1.4 %collective-permute-start.19 = (bf16[2,8,1024]{2,1,0:T(8,128)(2,1)S(1)}, bf16[2,8,1024]{2,1,0:T(8,128)(2,1)S(1)}, u32[]{:S(2)}, u32[]{:S(2)}) collective-permute-start(bf16[2,8,1024]{2,1,0:T(8,128)(2,1)S(1)} %get-tuple-element.63), channel_id=1, source_target_pairs={{0,1},{1,0},{2,3},{3,2},{4,5},{5,4},{6,7},{7,6},{8,9},{9,8},{10,11... | collective-permute-start | bytes 98312 | tf_op jit(solution)/shard_map/ppermute | solution.py:46
  58.2 2.6 %collective-permute-done.20 = bf16[2,8,1024]{2,1,0:T(8,128)(2,1)S(1)} collective-permute-done((bf16[2,8,1024]{2,1,0:T(8,128)(2,1)S(1)}, bf16[2,8,1024]{2,1,0:T(8,128)(2,1)S(1)}, u32[]{:S(2)}, u32[]{:S(2)}) %collective-permute-start.20) | collective-permute-done | bytes 32800 | tf_op jit(solution)/shard_map/ppermute | solution.py:46
  61.1 1.2 %collective-permute-start.22 = (bf16[1,2,8,1024]{3,2,1,0:T(8,128)(2,1)S(1)}, bf16[1,2,8,1024]{3,2,1,0:T(8,128)(2,1)S(1)}, u32[]{:S(2)}, u32[]{:S(2)}) collective-permute-start(bf16[1,2,8,1024]{3,2,1,0:T(8,128)(2,1)S(1)} %get-tuple-element.57), channel_id=1, source_target_pairs={{0,8},{1,9},{2,10},{3,11},{4,12},{5,13},{6,14},{7,15},{8,0},{9,1},... | collective-permute-start | bytes 98312 | tf_op jit(solution)/shard_map/ppermute | solution.py:46
  62.3 1.5 %collective-permute-start.24 = (bf16[1,2,8,1024]{3,2,1,0:T(8,128)(2,1)S(1)}, bf16[1,2,8,1024]{3,2,1,0:T(8,128)(2,1)S(1)}, u32[]{:S(2)}, u32[]{:S(2)}) collective-permute-start(bf16[1,2,8,1024]{3,2,1,0:T(8,128)(2,1)S(1)} %get-tuple-element.58), channel_id=1, source_target_pairs={{0,24},{1,25},{2,26},{3,27},{4,28},{5,29},{6,30},{7,31},{8,16},{9,... | collective-permute-start | bytes 98312 | tf_op jit(solution)/shard_map/ppermute | solution.py:46
  65.7 2.3 %collective-permute-done.24 = bf16[1,2,8,1024]{3,2,1,0:T(8,128)(2,1)S(1)} collective-permute-done((bf16[1,2,8,1024]{3,2,1,0:T(8,128)(2,1)S(1)}, bf16[1,2,8,1024]{3,2,1,0:T(8,128)(2,1)S(1)}, u32[]{:S(2)}, u32[]{:S(2)}) %collective-permute-start.24) | collective-permute-done | bytes 32800 | tf_op jit(solution)/shard_map/ppermute | solution.py:46
  (89 shorter events, 18.1 us)
Async XLA Ops:
  1.6 7.4 %collective-permute-start.2 = (bf16[1,2,8,1152]{3,2,1,0:T(8,128)(2,1)S(1)}, bf16[1,2,8,1152]{3,2,1,0:T(8,128)(2,1)S(1)}, u32[]{:S(2)}, u32[]{:S(2)}) collective-permute-start(bf16[1,2,8,1152]{3,2,1,0:T(8,128)(2,1)S(1)} %get-tuple-element.65), channel_id=1, source_target_pairs={{0,24},{1,25},{2,26},{3,27},{4,28},{5,29},{6,30},{7,31},{8,16},{9,... | collective-permute-start | bytes 110600 | tf_op jit(solution)/shard_map/ppermute | solution.py:46
  6.7 4.9 %collective-permute-start.1 = (bf16[1,2,8,1152]{3,2,1,0:T(8,128)(2,1)S(1)}, bf16[1,2,8,1152]{3,2,1,0:T(8,128)(2,1)S(1)}, u32[]{:S(2)}, u32[]{:S(2)}) collective-permute-start(bf16[1,2,8,1152]{3,2,1,0:T(8,128)(2,1)S(1)} %get-tuple-element.65), channel_id=1, source_target_pairs={{0,16},{1,17},{2,18},{3,19},{4,20},{5,21},{6,22},{7,23},{8,24},{9,... | collective-permute-start | bytes 110600 | tf_op jit(solution)/shard_map/ppermute | solution.py:46
  6.7 4.9 %collective-permute-start = (bf16[1,2,8,1152]{3,2,1,0:T(8,128)(2,1)S(1)}, bf16[1,2,8,1152]{3,2,1,0:T(8,128)(2,1)S(1)}, u32[]{:S(2)}, u32[]{:S(2)}) collective-permute-start(bf16[1,2,8,1152]{3,2,1,0:T(8,128)(2,1)S(1)} %get-tuple-element.65), channel_id=1, source_target_pairs={{0,8},{1,9},{2,10},{3,11},{4,12},{5,13},{6,14},{7,15},{8,0},{9,1},... | collective-permute-start | bytes 110600 | tf_op jit(solution)/shard_map/ppermute | solution.py:46
  7.3 8.6 %collective-permute-start.4 = (f32[16,32]{1,0:T(8,128)}, f32[16,32]{1,0:T(8,128)S(1)}, u32[]{:S(2)}, u32[]{:S(2)}) collective-permute-start(f32[16,32]{1,0:T(8,128)} %param.10), channel_id=1, source_target_pairs={{0,1},{1,0},{2,3},{3,2},{4,5},{5,4},{6,7},{7,6},{8,9},{9,8},{10,11... | collective-permute-start | bytes 6152 | tf_op jit(solution)/shard_map/ppermute | solution.py:46
  7.3 12.1 %collective-permute-start.8 = (bf16[2,32,4096]{2,1,0:T(8,128)(2,1)}, bf16[2,32,4096]{2,1,0:T(8,128)(2,1)S(1)}, u32[]{:S(2)}, u32[]{:S(2)}) collective-permute-start(bf16[2,32,4096]{2,1,0:T(8,128)(2,1)} %own_ref.7), channel_id=1, source_target_pairs={{0,1},{1,0},{2,3},{3,2},{4,5},{5,4},{6,7},{7,6},{8,9},{9,8},{10,11... | collective-permute-start | bytes 1572872 | tf_op jit(solution)/shard_map/ppermute | solution.py:46
  12.0 5.6 %collective-permute-start.5 = (bf16[2,8,1024]{2,1,0:T(8,128)(2,1)S(1)}, bf16[2,8,1024]{2,1,0:T(8,128)(2,1)S(1)}, u32[]{:S(2)}, u32[]{:S(2)}) collective-permute-start(bf16[2,8,1024]{2,1,0:T(8,128)(2,1)S(1)} %slice.134), channel_id=1, source_target_pairs={{0,1},{1,0},{2,3},{3,2},{4,5},{5,4},{6,7},{7,6},{8,9},{9,8},{10,11... | collective-permute-start | bytes 98312 | tf_op jit(solution)/shard_map/ppermute | solution.py:46
  12.1 5.6 %collective-permute-start.6 = (bf16[2,8,1024]{2,1,0:T(8,128)(2,1)S(1)}, bf16[2,8,1024]{2,1,0:T(8,128)(2,1)S(1)}, u32[]{:S(2)}, u32[]{:S(2)}) collective-permute-start(bf16[2,8,1024]{2,1,0:T(8,128)(2,1)S(1)} %slice.133), channel_id=1, source_target_pairs={{0,5},{1,4},{2,7},{3,6},{4,1},{5,0},{6,3},{7,2},{8,13},{9,12},{10,... | collective-permute-start | bytes 98312 | tf_op jit(solution)/shard_map/ppermute | solution.py:46
  17.7 4.9 %collective-permute-start.7 = (bf16[2,8,2048]{2,1,0:T(8,128)(2,1)S(1)}, bf16[2,8,2048]{2,1,0:T(8,128)(2,1)S(1)}, u32[]{:S(2)}, u32[]{:S(2)}) collective-permute-start(bf16[2,8,2048]{2,1,0:T(8,128)(2,1)S(1)} %pad_maximum_fusion.5.occ_ref), channel_id=1, source_target_pairs={{0,2},{1,3},{2,0},{3,1},{4,6},{5,7},{6,4},{7,5},{8,10},{9,11},{10,... | collective-permute-start | bytes 196616 | tf_op jit(solution)/shard_map/ppermute | solution.py:46
  25.6 4.4 %collective-permute-start.9 = (bf16[272,128]{1,0:T(8,128)(2,1)S(1)}, bf16[272,128]{1,0:T(8,128)(2,1)S(1)}, u32[]{:S(2)}, u32[]{:S(2)}) collective-permute-start(bf16[272,128]{1,0:T(8,128)(2,1)S(1)} %get-tuple-element.54), channel_id=1, source_target_pairs={{0,2},{1,3},{2,0},{3,1},{4,6},{5,7},{6,4},{7,5},{8,10},{9,11},{10,... | collective-permute-start | bytes 208904 | tf_op jit(solution)/shard_map/ppermute | solution.py:46
  26.6 5.2 %collective-permute-start.11 = (bf16[272,128]{1,0:T(8,128)(2,1)S(1)}, bf16[272,128]{1,0:T(8,128)(2,1)S(1)}, u32[]{:S(2)}, u32[]{:S(2)}) collective-permute-start(bf16[272,128]{1,0:T(8,128)(2,1)S(1)} %get-tuple-element.55), channel_id=1, source_target_pairs={{0,6},{1,7},{2,4},{3,5},{4,2},{5,3},{6,0},{7,1},{8,14},{9,15},{10,... | collective-permute-start | bytes 208904 | tf_op jit(solution)/shard_map/ppermute | solution.py:46
  27.6 4.5 %collective-permute-start.10 = (bf16[272,128]{1,0:T(8,128)(2,1)S(1)}, bf16[272,128]{1,0:T(8,128)(2,1)S(1)}, u32[]{:S(2)}, u32[]{:S(2)}) collective-permute-start(bf16[272,128]{1,0:T(8,128)(2,1)S(1)} %get-tuple-element.56), channel_id=1, source_target_pairs={{0,4},{1,5},{2,6},{3,7},{4,0},{5,1},{6,2},{7,3},{8,12},{9,13},{10,... | collective-permute-start | bytes 208904 | tf_op jit(solution)/shard_map/ppermute | solution.py:46
  32.2 6.2 %collective-permute-start.14 = (bf16[272,128]{1,0:T(8,128)(2,1)S(1)}, bf16[272,128]{1,0:T(8,128)(2,1)S(1)}, u32[]{:S(2)}, u32[]{:S(2)}) collective-permute-start(bf16[272,128]{1,0:T(8,128)(2,1)S(1)} %fusion.2), channel_id=1, source_target_pairs={{0,24},{1,25},{2,26},{3,27},{4,28},{5,29},{6,30},{7,31},{8,16},{9,... | collective-permute-start | bytes 208904 | tf_op jit(solution)/shard_map/ppermute | solution.py:46
  33.7 6.1 %collective-permute-start.13 = (bf16[272,128]{1,0:T(8,128)(2,1)S(1)}, bf16[272,128]{1,0:T(8,128)(2,1)S(1)}, u32[]{:S(2)}, u32[]{:S(2)}) collective-permute-start(bf16[272,128]{1,0:T(8,128)(2,1)S(1)} %fusion.2), channel_id=1, source_target_pairs={{0,16},{1,17},{2,18},{3,19},{4,20},{5,21},{6,22},{7,23},{8,24},{9,... | collective-permute-start | bytes 208904 | tf_op jit(solution)/shard_map/ppermute | solution.py:46
  34.4 5.5 %collective-permute-start.12 = (bf16[272,128]{1,0:T(8,128)(2,1)S(1)}, bf16[272,128]{1,0:T(8,128)(2,1)S(1)}, u32[]{:S(2)}, u32[]{:S(2)}) collective-permute-start(bf16[272,128]{1,0:T(8,128)(2,1)S(1)} %fusion.2), channel_id=1, source_target_pairs={{0,8},{1,9},{2,10},{3,11},{4,12},{5,13},{6,14},{7,15},{8,0},{9,1},... | collective-permute-start | bytes 208904 | tf_op jit(solution)/shard_map/ppermute | solution.py:46
  39.9 5.3 %collective-permute-start.17 = (bf16[272,128]{1,0:T(8,128)(2,1)S(1)}, bf16[272,128]{1,0:T(8,128)(2,1)S(1)}, u32[]{:S(2)}, u32[]{:S(2)}) collective-permute-start(bf16[272,128]{1,0:T(8,128)(2,1)S(1)} %add_convert_fusion.2), channel_id=1, source_target_pairs={{0,6},{1,7},{2,4},{3,5},{4,2},{5,3},{6,0},{7,1},{8,14},{9,15},{10,... | collective-permute-start | bytes 208904 | tf_op jit(solution)/shard_map/ppermute | solution.py:46
  42.4 4.3 %collective-permute-start.15 = (bf16[272,128]{1,0:T(8,128)(2,1)S(1)}, bf16[272,128]{1,0:T(8,128)(2,1)S(1)}, u32[]{:S(2)}, u32[]{:S(2)}) collective-permute-start(bf16[272,128]{1,0:T(8,128)(2,1)S(1)} %add_convert_fusion.2), channel_id=1, source_target_pairs={{0,2},{1,3},{2,0},{3,1},{4,6},{5,7},{6,4},{7,5},{8,10},{9,11},{10,... | collective-permute-start | bytes 208904 | tf_op jit(solution)/shard_map/ppermute | solution.py:46
  51.0 4.3 %collective-permute-start.18 = (bf16[2,8,2048]{2,1,0:T(8,128)(2,1)S(1)}, bf16[2,8,2048]{2,1,0:T(8,128)(2,1)S(1)}, u32[]{:S(2)}, u32[]{:S(2)}) collective-permute-start(bf16[2,8,2048]{2,1,0:T(8,128)(2,1)S(1)} %get-tuple-element.35), channel_id=1, source_target_pairs={{0,2},{1,3},{2,0},{3,1},{4,6},{5,7},{6,4},{7,5},{8,10},{9,11},{10,... | collective-permute-start | bytes 196616 | tf_op jit(solution)/shard_map/ppermute | solution.py:46
  55.4 5.4 %collective-permute-start.21 = (bf16[2,8,1024]{2,1,0:T(8,128)(2,1)S(1)}, bf16[2,8,1024]{2,1,0:T(8,128)(2,1)S(1)}, u32[]{:S(2)}, u32[]{:S(2)}) collective-permute-start(bf16[2,8,1024]{2,1,0:T(8,128)(2,1)S(1)} %get-tuple-element.63), channel_id=1, source_target_pairs={{0,5},{1,4},{2,7},{3,6},{4,1},{5,0},{6,3},{7,2},{8,13},{9,12},{10,... | collective-permute-start | bytes 98312 | tf_op jit(solution)/shard_map/ppermute | solution.py:46
  55.5 5.3 %collective-permute-start.19 = (bf16[2,8,1024]{2,1,0:T(8,128)(2,1)S(1)}, bf16[2,8,1024]{2,1,0:T(8,128)(2,1)S(1)}, u32[]{:S(2)}, u32[]{:S(2)}) collective-permute-start(bf16[2,8,1024]{2,1,0:T(8,128)(2,1)S(1)} %get-tuple-element.63), channel_id=1, source_target_pairs={{0,1},{1,0},{2,3},{3,2},{4,5},{5,4},{6,7},{7,6},{8,9},{9,8},{10,11... | collective-permute-start | bytes 98312 | tf_op jit(solution)/shard_map/ppermute | solution.py:46
  57.7 7.0 %collective-permute-start.25 = (bf16[2,32,2048]{2,1,0:T(8,128)(2,1)S(1)}, bf16[2,32,2048]{2,1,0:T(8,128)(2,1)S(1)}, u32[]{:S(2)}, u32[]{:S(2)}) collective-permute-start(bf16[2,32,2048]{2,1,0:T(8,128)(2,1)S(1)} %get-tuple-element.37), channel_id=1, source_target_pairs={{0,1},{1,0},{2,3},{3,2},{4,5},{5,4},{6,7},{7,6},{8,9},{9,8},{10,11... | collective-permute-start | bytes 786440 | tf_op jit(solution)/shard_map/ppermute | solution.py:46
  57.7 7.0 %collective-permute-start.26 = (bf16[2,32,2048]{2,1,0:T(8,128)(2,1)S(1)}, bf16[2,32,2048]{2,1,0:T(8,128)(2,1)S(1)}, u32[]{:S(2)}, u32[]{:S(2)}) collective-permute-start(bf16[2,32,2048]{2,1,0:T(8,128)(2,1)S(1)} %get-tuple-element.39), channel_id=1, source_target_pairs={{0,1},{1,0},{2,3},{3,2},{4,5},{5,4},{6,7},{7,6},{8,9},{9,8},{10,11... | collective-permute-start | bytes 786440 | tf_op jit(solution)/shard_map/ppermute | solution.py:46
  61.1 6.9 %collective-permute-start.22 = (bf16[1,2,8,1024]{3,2,1,0:T(8,128)(2,1)S(1)}, bf16[1,2,8,1024]{3,2,1,0:T(8,128)(2,1)S(1)}, u32[]{:S(2)}, u32[]{:S(2)}) collective-permute-start(bf16[1,2,8,1024]{3,2,1,0:T(8,128)(2,1)S(1)} %get-tuple-element.57), channel_id=1, source_target_pairs={{0,8},{1,9},{2,10},{3,11},{4,12},{5,13},{6,14},{7,15},{8,0},{9,1},... | collective-permute-start | bytes 98312 | tf_op jit(solution)/shard_map/ppermute | solution.py:46
  62.3 5.7 %collective-permute-start.24 = (bf16[1,2,8,1024]{3,2,1,0:T(8,128)(2,1)S(1)}, bf16[1,2,8,1024]{3,2,1,0:T(8,128)(2,1)S(1)}, u32[]{:S(2)}, u32[]{:S(2)}) collective-permute-start(bf16[1,2,8,1024]{3,2,1,0:T(8,128)(2,1)S(1)} %get-tuple-element.58), channel_id=1, source_target_pairs={{0,24},{1,25},{2,26},{3,27},{4,28},{5,29},{6,30},{7,31},{8,16},{9,... | collective-permute-start | bytes 98312 | tf_op jit(solution)/shard_map/ppermute | solution.py:46
  63.7 4.8 %collective-permute-start.23 = (bf16[1,2,8,1024]{3,2,1,0:T(8,128)(2,1)S(1)}, bf16[1,2,8,1024]{3,2,1,0:T(8,128)(2,1)S(1)}, u32[]{:S(2)}, u32[]{:S(2)}) collective-permute-start(bf16[1,2,8,1024]{3,2,1,0:T(8,128)(2,1)S(1)} %get-tuple-element.59), channel_id=1, source_target_pairs={{0,16},{1,17},{2,18},{3,19},{4,20},{5,21},{6,22},{7,23},{8,24},{9,... | collective-permute-start | bytes 98312 | tf_op jit(solution)/shard_map/ppermute | solution.py:46
  (6 other events, 35.1 us)

commit v9 on v7

--- a/solution.py
+++ b/solution.py
@@ -7,6 +7,7 @@
 from jax.experimental import pallas as pl
 from jax.experimental.pallas import tpu as pltpu
 from jax.sharding import PartitionSpec as P
+
 
 FREQUENCY = 2.5
 BROADENING = 0.4
@@ -55,10 +56,9 @@
 def sum_scatter(cube, parts, bits):
     me = sum(cube.bit(bit) << n for n, bit in enumerate(bits))
     total = pick(parts, me).astype(F32)
-    arrived = [
-        cube.swap(pick(parts, jnp.bitwise_xor(me, d + 1)), mask)
-        for d, mask in enumerate(masks_of(bits))
-    ]
+    arrived = []
+    for d, mask in enumerate(masks_of(bits)):
+        arrived.append(cube.swap(pick(parts, jnp.bitwise_xor(me, d + 1)), mask))
     for term in arrived:
         total = total + term.astype(F32)
     return total
@@ -109,7 +109,7 @@
 
 
 def fetch_partners(cube, occupied, occ_energy, sources, neighbour_sources, make_beside):
-    local_k, occ_count, grid_count = occupied.shape
+    local_k, _, grid_count = occupied.shape
     width = grid_count // cube.band
     ka = lax.axis_index("ka")
     first = cube.bit(cube.core) == 0
@@ -201,16 +201,6 @@
             total = total + term.astype(F32)
         value = total
     return value[0], beside
-
-
-def grid_copies(basis_ref, held_ref, sems, starts):
-    ends = starts[1:] + [basis_ref.shape[1]]
-    return [
-        pltpu.make_async_copy(
-            basis_ref.at[:, start:end], held_ref.at[:, start:end], sems.at[n]
-        )
-        for n, (start, end) in enumerate(zip(starts, ends))
-    ]
 
 
 def pair_coeffs(occ, virt, basis):
@@ -588,4 +578,5 @@
         P(),
     )
     out_specs = (P("ka", None, "band"), P("ka", "band", None))
+
     return jax.shard_map(shards, mesh=mesh, in_specs=in_specs, out_specs=out_specs, check_vma=False)

time: 69.5 us -> 69.5 us (level)
  no operation moved by 1% of the time
where the time goes in v9:
time: 69.5 us; the launch traced here: 69.2 us
  starting transfers between devices  29.1 us (42%)
  waiting for transfers between devices  18.3 us (26%)
  Pallas kernels  13.1 us (19%)
  other arithmetic  5.49 us (8%)
  local copies, waits for them, and re-layouts  2.21 us (3%)
  between operations  0.98 us (1%)
    ppermute x27, starting transfers between devices, swap(): lax.ppermute(value, ('ka', 'band'), [(device, device ^ mask) for device i...  29.1 us
    ppermute x27, waiting for transfers between devices, swap(): lax.ppermute(value, ('ka', 'band'), [(device, device ^ mask) for device i...  18.3 us
    pallas_call x1, Pallas kernels, respond(): pl.pallas_call(respond_far_kernel, in_specs=[VMEM_SPEC] * 5 + [any_spec],...  4.16 us
    pallas_call x1, Pallas kernels, project(): pl.pallas_call(functools.partial(project_near_kernel, starts=starts), in_...  3.23 us
    pallas_call x1, Pallas kernels, project(): pl.pallas_call(functools.partial(project_kernel, scale=scale), in_specs=[...  2.89 us
    pallas_call x1, Pallas kernels, respond(): pl.pallas_call(respond_near_kernel, in_specs=[VMEM_SPEC] * 5, out_specs=[...  2.8 us
  transfers between devices with their start and end apart: 27, of which 14 were waited for; matrix products, arithmetic and copies ran while one was open for 8% of the time, Pallas kernels for 9%

profile of v9, /device:TPU:0, one launch (start us, length us, event | category | flops | bytes accessed | tf_op | source)
XLA Modules:
  0.0 69.2 jit_solution(329022037078545244)
XLA Ops:
  1.6 5.1 %collective-permute-start.2 = (bf16[1,2,8,1152]{3,2,1,0:T(8,128)(2,1)S(1)}, bf16[1,2,8,1152]{3,2,1,0:T(8,128)(2,1)S(1)}, u32[]{:S(2)}, u32[]{:S(2)}) collective-permute-start(bf16[1,2,8,1152]{3,2,1,0:T(8,128)(2,1)S(1)} %get-tuple-element.67), channel_id=1, source_target_pairs={{0,24},{1,25},{2,26},{3,27},{4,28},{5,29},{6,30},{7,31},{8,16},{9,... | collective-permute-start | bytes 110600 | tf_op jit(solution)/shard_map/ppermute | solution.py:47
  9.0 2.6 %collective-permute-done.1 = bf16[1,2,8,1152]{3,2,1,0:T(8,128)(2,1)S(1)} collective-permute-done((bf16[1,2,8,1152]{3,2,1,0:T(8,128)(2,1)S(1)}, bf16[1,2,8,1152]{3,2,1,0:T(8,128)(2,1)S(1)}, u32[]{:S(2)}, u32[]{:S(2)}) %collective-permute-start.1) | collective-permute-done | bytes 36896 | tf_op jit(solution)/shard_map/ppermute | solution.py:47
  12.1 1.6 %collective-permute-start.6 = (bf16[2,8,1024]{2,1,0:T(8,128)(2,1)S(1)}, bf16[2,8,1024]{2,1,0:T(8,128)(2,1)S(1)}, u32[]{:S(2)}, u32[]{:S(2)}) collective-permute-start(bf16[2,8,1024]{2,1,0:T(8,128)(2,1)S(1)} %slice.143), channel_id=1, source_target_pairs={{0,5},{1,4},{2,7},{3,6},{4,1},{5,0},{6,3},{7,2},{8,13},{9,12},{10,... | collective-permute-start | bytes 98312 | tf_op jit(solution)/shard_map/ppermute | solution.py:47
  17.7 1.6 %collective-permute-start.7 = (bf16[2,8,2048]{2,1,0:T(8,128)(2,1)S(1)}, bf16[2,8,2048]{2,1,0:T(8,128)(2,1)S(1)}, u32[]{:S(2)}, u32[]{:S(2)}) collective-permute-start(bf16[2,8,2048]{2,1,0:T(8,128)(2,1)S(1)} %pad_maximum_fusion.5.occ_ref), channel_id=1, source_target_pairs={{0,2},{1,3},{2,0},{3,1},{4,6},{5,7},{6,4},{7,5},{8,10},{9,11},{10,... | collective-permute-start | bytes 196616 | tf_op jit(solution)/shard_map/ppermute | solution.py:47
  19.4 3.2 %project_near.1 = (f32[1024,512]{1,0:T(8,128)S(1)}, bf16[512,2048]{1,0:T(8,128)(2,1)S(1)}) custom-call(bf16[2,8,2048]{2,1,0:T(8,128)(2,1)S(1)} %pad_maximum_fusion.5.occ_ref, bf16[2,32,4096]{2,1,0:T(8,128)(2,1)S(1)} %copy-done.1, bf16[2,32,4096]{2,1,0:T(8,128)(2,1)S(1)} %collective-permute-done.8.other_ref, ...), custom_call_target="tpu_custom_call" | custom-call | flops 2147483648 | bytes 4194304 | tf_op jit(solution)/shard_map/project_near/pallas_call | solution.py:325
  22.8 2.9 %project.1 = (bf16[1024,512]{1,0:T(8,128)(2,1)S(1)}, bf16[1088,128]{1,0:T(8,128)(2,1)S(1)}) custom-call(bf16[2,8,2048]{2,1,0:T(8,128)(2,1)S(1)} %collective-permute-done.7.occ_ref, bf16[2,32,4096]{2,1,0:T(8,128)(2,1)S(1)} %copy-done.1, bf16[2,32,4096]{2,1,0:T(8,128)(2,1)S(1)} %collective-permute-done.8.other_ref, ...), custom_call_target="tpu_custom_call" | custom-call | flops 2147483648 | bytes 4194304 | tf_op jit(solution)/shard_map/project/pallas_call | solution.py:341
  26.6 1.4 %collective-permute-start.11 = (bf16[272,128]{1,0:T(8,128)(2,1)S(1)}, bf16[272,128]{1,0:T(8,128)(2,1)S(1)}, u32[]{:S(2)}, u32[]{:S(2)}) collective-permute-start(bf16[272,128]{1,0:T(8,128)(2,1)S(1)} %get-tuple-element.57), channel_id=1, source_target_pairs={{0,6},{1,7},{2,4},{3,5},{4,2},{5,3},{6,0},{7,1},{8,14},{9,15},{10,... | collective-permute-start | bytes 208904 | tf_op jit(solution)/shard_map/ppermute | solution.py:47
  28.0 1.2 %collective-permute-start.10 = (bf16[272,128]{1,0:T(8,128)(2,1)S(1)}, bf16[272,128]{1,0:T(8,128)(2,1)S(1)}, u32[]{:S(2)}, u32[]{:S(2)}) collective-permute-start(bf16[272,128]{1,0:T(8,128)(2,1)S(1)} %get-tuple-element.58), channel_id=1, source_target_pairs={{0,4},{1,5},{2,6},{3,7},{4,0},{5,1},{6,2},{7,3},{8,12},{9,13},{10,... | collective-permute-start | bytes 208904 | tf_op jit(solution)/shard_map/ppermute | solution.py:47
  30.1 1.8 %collective-permute-done.11 = bf16[272,128]{1,0:T(8,128)(2,1)S(1)} collective-permute-done((bf16[272,128]{1,0:T(8,128)(2,1)S(1)}, bf16[272,128]{1,0:T(8,128)(2,1)S(1)}, u32[]{:S(2)}, u32[]{:S(2)}) %collective-permute-start.11) | collective-permute-done | bytes 69664 | tf_op jit(solution)/shard_map/ppermute | solution.py:47
  32.4 1.5 %collective-permute-start.14 = (bf16[272,128]{1,0:T(8,128)(2,1)S(1)}, bf16[272,128]{1,0:T(8,128)(2,1)S(1)}, u32[]{:S(2)}, u32[]{:S(2)}) collective-permute-start(bf16[272,128]{1,0:T(8,128)(2,1)S(1)} %fusion.2), channel_id=1, source_target_pairs={{0,24},{1,25},{2,26},{3,27},{4,28},{5,29},{6,30},{7,31},{8,16},{9,... | collective-permute-start | bytes 208904 | tf_op jit(solution)/shard_map/ppermute | solution.py:47
  34.5 2.3 %collective-permute-start.12 = (bf16[272,128]{1,0:T(8,128)(2,1)S(1)}, bf16[272,128]{1,0:T(8,128)(2,1)S(1)}, u32[]{:S(2)}, u32[]{:S(2)}) collective-permute-start(bf16[272,128]{1,0:T(8,128)(2,1)S(1)} %fusion.2), channel_id=1, source_target_pairs={{0,8},{1,9},{2,10},{3,11},{4,12},{5,13},{6,14},{7,15},{8,0},{9,1},... | collective-permute-start | bytes 208904 | tf_op jit(solution)/shard_map/ppermute | solution.py:47
  36.9 1.7 %collective-permute-done.14 = bf16[272,128]{1,0:T(8,128)(2,1)S(1)} collective-permute-done((bf16[272,128]{1,0:T(8,128)(2,1)S(1)}, bf16[272,128]{1,0:T(8,128)(2,1)S(1)}, u32[]{:S(2)}, u32[]{:S(2)}) %collective-permute-start.14) | collective-permute-done | bytes 69664 | tf_op jit(solution)/shard_map/ppermute | solution.py:47
  38.6 1.5 %collective-permute-done.13 = bf16[272,128]{1,0:T(8,128)(2,1)S(1)} collective-permute-done((bf16[272,128]{1,0:T(8,128)(2,1)S(1)}, bf16[272,128]{1,0:T(8,128)(2,1)S(1)}, u32[]{:S(2)}, u32[]{:S(2)}) %collective-permute-start.13) | collective-permute-done | bytes 69664 | tf_op jit(solution)/shard_map/ppermute | solution.py:47
  40.1 1.6 %collective-permute-start.17 = (bf16[272,128]{1,0:T(8,128)(2,1)S(1)}, bf16[272,128]{1,0:T(8,128)(2,1)S(1)}, u32[]{:S(2)}, u32[]{:S(2)}) collective-permute-start(bf16[272,128]{1,0:T(8,128)(2,1)S(1)} %add_convert_fusion.2), channel_id=1, source_target_pairs={{0,6},{1,7},{2,4},{3,5},{4,2},{5,3},{6,0},{7,1},{8,14},{9,15},{10,... | collective-permute-start | bytes 208904 | tf_op jit(solution)/shard_map/ppermute | solution.py:47
  42.5 1.2 %collective-permute-start.15 = (bf16[272,128]{1,0:T(8,128)(2,1)S(1)}, bf16[272,128]{1,0:T(8,128)(2,1)S(1)}, u32[]{:S(2)}, u32[]{:S(2)}) collective-permute-start(bf16[272,128]{1,0:T(8,128)(2,1)S(1)} %add_convert_fusion.2), channel_id=1, source_target_pairs={{0,2},{1,3},{2,0},{3,1},{4,6},{5,7},{6,4},{7,5},{8,10},{9,11},{10,... | collective-permute-start | bytes 208904 | tf_op jit(solution)/shard_map/ppermute | solution.py:47
  43.7 1.6 %collective-permute-done.17 = bf16[272,128]{1,0:T(8,128)(2,1)S(1)} collective-permute-done((bf16[272,128]{1,0:T(8,128)(2,1)S(1)}, bf16[272,128]{1,0:T(8,128)(2,1)S(1)}, u32[]{:S(2)}, u32[]{:S(2)}) %collective-permute-start.17) | collective-permute-done | bytes 69664 | tf_op jit(solution)/shard_map/ppermute | solution.py:47
  46.9 4.2 %respond_far.1 = (bf16[2,8,2048]{2,1,0:T(8,128)(2,1)S(1)}, bf16[2,32,2048]{2,1,0:T(8,128)(2,1)S(1)}, bf16[2,32,2048]{2,1,0:T(8,128)(2,1)S(1)}, bf16[1024,512]{1,0:T(8,128)(2,1)S(1)}, bf16[2,512,1024]{2,1,0:T(8,128)(2,1)S(1)}) custom-call(bf16[1024,512]{1,0:T(8,128)(2,1)S(1)} %get-tuple-element.32.coeffs_ref, bf16[1088,128]{1,0:T(8,128)(2,1)S(1)} %bitcast.41, ...), custom_call_target="tpu_custom_call" | custom-call | flops 2147483648 | bytes 4194304 | tf_op jit(solution)/shard_map/respond_far/pallas_call | solution.py:482
  51.1 1.2 %collective-permute-start.18 = (bf16[2,8,2048]{2,1,0:T(8,128)(2,1)S(1)}, bf16[2,8,2048]{2,1,0:T(8,128)(2,1)S(1)}, u32[]{:S(2)}, u32[]{:S(2)}) collective-permute-start(bf16[2,8,2048]{2,1,0:T(8,128)(2,1)S(1)} %get-tuple-element.37), channel_id=1, source_target_pairs={{0,2},{1,3},{2,0},{3,1},{4,6},{5,7},{6,4},{7,5},{8,10},{9,11},{10,... | collective-permute-start | bytes 196616 | tf_op jit(solution)/shard_map/ppermute | solution.py:47
  52.3 2.8 %respond_near.1 = (bf16[2,8,2048]{2,1,0:T(8,128)(2,1)S(1)}, bf16[2,32,2048]{2,1,0:T(8,128)(2,1)S(1)}, bf16[2,32,2048]{2,1,0:T(8,128)(2,1)S(1)}) custom-call(bf16[1024,512]{1,0:T(8,128)(2,1)S(1)} %get-tuple-element.34.screened_ref, bf16[2,8,2048]{2,1,0:T(8,128)(2,1)S(1)} %pad_maximum_fusion.5.occ_ref, bf16[2,32,4096]{2,1,0:T(8,128)(2,1)S(1)} %copy-done.1, ...), custom_call_target="tpu_custom_call" | custom-call | flops 2147483648 | bytes 4194304 | tf_op jit(solution)/shard_map/respond_near/pallas_call | solution.py:499
  55.5 1.3 %collective-permute-start.19 = (bf16[2,8,1024]{2,1,0:T(8,128)(2,1)S(1)}, bf16[2,8,1024]{2,1,0:T(8,128)(2,1)S(1)}, u32[]{:S(2)}, u32[]{:S(2)}) collective-permute-start(bf16[2,8,1024]{2,1,0:T(8,128)(2,1)S(1)} %get-tuple-element.65), channel_id=1, source_target_pairs={{0,1},{1,0},{2,3},{3,2},{4,5},{5,4},{6,7},{7,6},{8,9},{9,8},{10,11... | collective-permute-start | bytes 98312 | tf_op jit(solution)/shard_map/ppermute | solution.py:47
  58.2 2.5 %collective-permute-done.20 = bf16[2,8,1024]{2,1,0:T(8,128)(2,1)S(1)} collective-permute-done((bf16[2,8,1024]{2,1,0:T(8,128)(2,1)S(1)}, bf16[2,8,1024]{2,1,0:T(8,128)(2,1)S(1)}, u32[]{:S(2)}, u32[]{:S(2)}) %collective-permute-start.20) | collective-permute-done | bytes 32800 | tf_op jit(solution)/shard_map/ppermute | solution.py:47
  61.1 1.2 %collective-permute-start.22 = (bf16[1,2,8,1024]{3,2,1,0:T(8,128)(2,1)S(1)}, bf16[1,2,8,1024]{3,2,1,0:T(8,128)(2,1)S(1)}, u32[]{:S(2)}, u32[]{:S(2)}) collective-permute-start(bf16[1,2,8,1024]{3,2,1,0:T(8,128)(2,1)S(1)} %get-tuple-element.59), channel_id=1, source_target_pairs={{0,8},{1,9},{2,10},{3,11},{4,12},{5,13},{6,14},{7,15},{8,0},{9,1},... | collective-permute-start | bytes 98312 | tf_op jit(solution)/shard_map/ppermute | solution.py:47
  62.3 1.5 %collective-permute-start.24 = (bf16[1,2,8,1024]{3,2,1,0:T(8,128)(2,1)S(1)}, bf16[1,2,8,1024]{3,2,1,0:T(8,128)(2,1)S(1)}, u32[]{:S(2)}, u32[]{:S(2)}) collective-permute-start(bf16[1,2,8,1024]{3,2,1,0:T(8,128)(2,1)S(1)} %get-tuple-element.60), channel_id=1, source_target_pairs={{0,24},{1,25},{2,26},{3,27},{4,28},{5,29},{6,30},{7,31},{8,16},{9,... | collective-permute-start | bytes 98312 | tf_op jit(solution)/shard_map/ppermute | solution.py:47
  65.7 2.3 %collective-permute-done.24 = bf16[1,2,8,1024]{3,2,1,0:T(8,128)(2,1)S(1)} collective-permute-done((bf16[1,2,8,1024]{3,2,1,0:T(8,128)(2,1)S(1)}, bf16[1,2,8,1024]{3,2,1,0:T(8,128)(2,1)S(1)}, u32[]{:S(2)}, u32[]{:S(2)}) %collective-permute-start.24) | collective-permute-done | bytes 32800 | tf_op jit(solution)/shard_map/ppermute | solution.py:47
  (88 shorter events, 18.5 us)
Async XLA Ops:
  1.6 7.4 %collective-permute-start.2 = (bf16[1,2,8,1152]{3,2,1,0:T(8,128)(2,1)S(1)}, bf16[1,2,8,1152]{3,2,1,0:T(8,128)(2,1)S(1)}, u32[]{:S(2)}, u32[]{:S(2)}) collective-permute-start(bf16[1,2,8,1152]{3,2,1,0:T(8,128)(2,1)S(1)} %get-tuple-element.67), channel_id=1, source_target_pairs={{0,24},{1,25},{2,26},{3,27},{4,28},{5,29},{6,30},{7,31},{8,16},{9,... | collective-permute-start | bytes 110600 | tf_op jit(solution)/shard_map/ppermute | solution.py:47
  6.7 4.9 %collective-permute-start.1 = (bf16[1,2,8,1152]{3,2,1,0:T(8,128)(2,1)S(1)}, bf16[1,2,8,1152]{3,2,1,0:T(8,128)(2,1)S(1)}, u32[]{:S(2)}, u32[]{:S(2)}) collective-permute-start(bf16[1,2,8,1152]{3,2,1,0:T(8,128)(2,1)S(1)} %get-tuple-element.67), channel_id=1, source_target_pairs={{0,16},{1,17},{2,18},{3,19},{4,20},{5,21},{6,22},{7,23},{8,24},{9,... | collective-permute-start | bytes 110600 | tf_op jit(solution)/shard_map/ppermute | solution.py:47
  6.7 4.9 %collective-permute-start = (bf16[1,2,8,1152]{3,2,1,0:T(8,128)(2,1)S(1)}, bf16[1,2,8,1152]{3,2,1,0:T(8,128)(2,1)S(1)}, u32[]{:S(2)}, u32[]{:S(2)}) collective-permute-start(bf16[1,2,8,1152]{3,2,1,0:T(8,128)(2,1)S(1)} %get-tuple-element.67), channel_id=1, source_target_pairs={{0,8},{1,9},{2,10},{3,11},{4,12},{5,13},{6,14},{7,15},{8,0},{9,1},... | collective-permute-start | bytes 110600 | tf_op jit(solution)/shard_map/ppermute | solution.py:47
  7.3 9.4 %collective-permute-start.4 = (f32[16,32]{1,0:T(8,128)}, f32[16,32]{1,0:T(8,128)S(1)}, u32[]{:S(2)}, u32[]{:S(2)}) collective-permute-start(f32[16,32]{1,0:T(8,128)} %param.10), channel_id=1, source_target_pairs={{0,1},{1,0},{2,3},{3,2},{4,5},{5,4},{6,7},{7,6},{8,9},{9,8},{10,11... | collective-permute-start | bytes 6152 | tf_op jit(solution)/shard_map/ppermute | solution.py:47
  7.3 12.1 %collective-permute-start.8 = (bf16[2,32,4096]{2,1,0:T(8,128)(2,1)}, bf16[2,32,4096]{2,1,0:T(8,128)(2,1)S(1)}, u32[]{:S(2)}, u32[]{:S(2)}) collective-permute-start(bf16[2,32,4096]{2,1,0:T(8,128)(2,1)} %own_ref.7), channel_id=1, source_target_pairs={{0,1},{1,0},{2,3},{3,2},{4,5},{5,4},{6,7},{7,6},{8,9},{9,8},{10,11... | collective-permute-start | bytes 1572872 | tf_op jit(solution)/shard_map/ppermute | solution.py:47
  12.0 5.6 %collective-permute-start.5 = (bf16[2,8,1024]{2,1,0:T(8,128)(2,1)S(1)}, bf16[2,8,1024]{2,1,0:T(8,128)(2,1)S(1)}, u32[]{:S(2)}, u32[]{:S(2)}) collective-permute-start(bf16[2,8,1024]{2,1,0:T(8,128)(2,1)S(1)} %slice.144), channel_id=1, source_target_pairs={{0,1},{1,0},{2,3},{3,2},{4,5},{5,4},{6,7},{7,6},{8,9},{9,8},{10,11... | collective-permute-start | bytes 98312 | tf_op jit(solution)/shard_map/ppermute | solution.py:47
  12.1 5.6 %collective-permute-start.6 = (bf16[2,8,1024]{2,1,0:T(8,128)(2,1)S(1)}, bf16[2,8,1024]{2,1,0:T(8,128)(2,1)S(1)}, u32[]{:S(2)}, u32[]{:S(2)}) collective-permute-start(bf16[2,8,1024]{2,1,0:T(8,128)(2,1)S(1)} %slice.143), channel_id=1, source_target_pairs={{0,5},{1,4},{2,7},{3,6},{4,1},{5,0},{6,3},{7,2},{8,13},{9,12},{10,... | collective-permute-start | bytes 98312 | tf_op jit(solution)/shard_map/ppermute | solution.py:47
  17.7 5.0 %collective-permute-start.7 = (bf16[2,8,2048]{2,1,0:T(8,128)(2,1)S(1)}, bf16[2,8,2048]{2,1,0:T(8,128)(2,1)S(1)}, u32[]{:S(2)}, u32[]{:S(2)}) collective-permute-start(bf16[2,8,2048]{2,1,0:T(8,128)(2,1)S(1)} %pad_maximum_fusion.5.occ_ref), channel_id=1, source_target_pairs={{0,2},{1,3},{2,0},{3,1},{4,6},{5,7},{6,4},{7,5},{8,10},{9,11},{10,... | collective-permute-start | bytes 196616 | tf_op jit(solution)/shard_map/ppermute | solution.py:47
  25.7 4.4 %collective-permute-start.9 = (bf16[272,128]{1,0:T(8,128)(2,1)S(1)}, bf16[272,128]{1,0:T(8,128)(2,1)S(1)}, u32[]{:S(2)}, u32[]{:S(2)}) collective-permute-start(bf16[272,128]{1,0:T(8,128)(2,1)S(1)} %get-tuple-element.56), channel_id=1, source_target_pairs={{0,2},{1,3},{2,0},{3,1},{4,6},{5,7},{6,4},{7,5},{8,10},{9,11},{10,... | collective-permute-start | bytes 208904 | tf_op jit(solution)/shard_map/ppermute | solution.py:47
  26.6 5.2 %collective-permute-start.11 = (bf16[272,128]{1,0:T(8,128)(2,1)S(1)}, bf16[272,128]{1,0:T(8,128)(2,1)S(1)}, u32[]{:S(2)}, u32[]{:S(2)}) collective-permute-start(bf16[272,128]{1,0:T(8,128)(2,1)S(1)} %get-tuple-element.57), channel_id=1, source_target_pairs={{0,6},{1,7},{2,4},{3,5},{4,2},{5,3},{6,0},{7,1},{8,14},{9,15},{10,... | collective-permute-start | bytes 208904 | tf_op jit(solution)/shard_map/ppermute | solution.py:47
  28.0 4.3 %collective-permute-start.10 = (bf16[272,128]{1,0:T(8,128)(2,1)S(1)}, bf16[272,128]{1,0:T(8,128)(2,1)S(1)}, u32[]{:S(2)}, u32[]{:S(2)}) collective-permute-start(bf16[272,128]{1,0:T(8,128)(2,1)S(1)} %get-tuple-element.58), channel_id=1, source_target_pairs={{0,4},{1,5},{2,6},{3,7},{4,0},{5,1},{6,2},{7,3},{8,12},{9,13},{10,... | collective-permute-start | bytes 208904 | tf_op jit(solution)/shard_map/ppermute | solution.py:47
  32.4 6.2 %collective-permute-start.14 = (bf16[272,128]{1,0:T(8,128)(2,1)S(1)}, bf16[272,128]{1,0:T(8,128)(2,1)S(1)}, u32[]{:S(2)}, u32[]{:S(2)}) collective-permute-start(bf16[272,128]{1,0:T(8,128)(2,1)S(1)} %fusion.2), channel_id=1, source_target_pairs={{0,24},{1,25},{2,26},{3,27},{4,28},{5,29},{6,30},{7,31},{8,16},{9,... | collective-permute-start | bytes 208904 | tf_op jit(solution)/shard_map/ppermute | solution.py:47
  33.9 6.1 %collective-permute-start.13 = (bf16[272,128]{1,0:T(8,128)(2,1)S(1)}, bf16[272,128]{1,0:T(8,128)(2,1)S(1)}, u32[]{:S(2)}, u32[]{:S(2)}) collective-permute-start(bf16[272,128]{1,0:T(8,128)(2,1)S(1)} %fusion.2), channel_id=1, source_target_pairs={{0,16},{1,17},{2,18},{3,19},{4,20},{5,21},{6,22},{7,23},{8,24},{9,... | collective-permute-start | bytes 208904 | tf_op jit(solution)/shard_map/ppermute | solution.py:47
  34.5 5.5 %collective-permute-start.12 = (bf16[272,128]{1,0:T(8,128)(2,1)S(1)}, bf16[272,128]{1,0:T(8,128)(2,1)S(1)}, u32[]{:S(2)}, u32[]{:S(2)}) collective-permute-start(bf16[272,128]{1,0:T(8,128)(2,1)S(1)} %fusion.2), channel_id=1, source_target_pairs={{0,8},{1,9},{2,10},{3,11},{4,12},{5,13},{6,14},{7,15},{8,0},{9,1},... | collective-permute-start | bytes 208904 | tf_op jit(solution)/shard_map/ppermute | solution.py:47
  40.1 5.3 %collective-permute-start.17 = (bf16[272,128]{1,0:T(8,128)(2,1)S(1)}, bf16[272,128]{1,0:T(8,128)(2,1)S(1)}, u32[]{:S(2)}, u32[]{:S(2)}) collective-permute-start(bf16[272,128]{1,0:T(8,128)(2,1)S(1)} %add_convert_fusion.2), channel_id=1, source_target_pairs={{0,6},{1,7},{2,4},{3,5},{4,2},{5,3},{6,0},{7,1},{8,14},{9,15},{10,... | collective-permute-start | bytes 208904 | tf_op jit(solution)/shard_map/ppermute | solution.py:47
  42.5 4.3 %collective-permute-start.15 = (bf16[272,128]{1,0:T(8,128)(2,1)S(1)}, bf16[272,128]{1,0:T(8,128)(2,1)S(1)}, u32[]{:S(2)}, u32[]{:S(2)}) collective-permute-start(bf16[272,128]{1,0:T(8,128)(2,1)S(1)} %add_convert_fusion.2), channel_id=1, source_target_pairs={{0,2},{1,3},{2,0},{3,1},{4,6},{5,7},{6,4},{7,5},{8,10},{9,11},{10,... | collective-permute-start | bytes 208904 | tf_op jit(solution)/shard_map/ppermute | solution.py:47
  51.1 4.3 %collective-permute-start.18 = (bf16[2,8,2048]{2,1,0:T(8,128)(2,1)S(1)}, bf16[2,8,2048]{2,1,0:T(8,128)(2,1)S(1)}, u32[]{:S(2)}, u32[]{:S(2)}) collective-permute-start(bf16[2,8,2048]{2,1,0:T(8,128)(2,1)S(1)} %get-tuple-element.37), channel_id=1, source_target_pairs={{0,2},{1,3},{2,0},{3,1},{4,6},{5,7},{6,4},{7,5},{8,10},{9,11},{10,... | collective-permute-start | bytes 196616 | tf_op jit(solution)/shard_map/ppermute | solution.py:47
  55.4 5.3 %collective-permute-start.21 = (bf16[2,8,1024]{2,1,0:T(8,128)(2,1)S(1)}, bf16[2,8,1024]{2,1,0:T(8,128)(2,1)S(1)}, u32[]{:S(2)}, u32[]{:S(2)}) collective-permute-start(bf16[2,8,1024]{2,1,0:T(8,128)(2,1)S(1)} %get-tuple-element.65), channel_id=1, source_target_pairs={{0,5},{1,4},{2,7},{3,6},{4,1},{5,0},{6,3},{7,2},{8,13},{9,12},{10,... | collective-permute-start | bytes 98312 | tf_op jit(solution)/shard_map/ppermute | solution.py:47
  55.5 5.3 %collective-permute-start.19 = (bf16[2,8,1024]{2,1,0:T(8,128)(2,1)S(1)}, bf16[2,8,1024]{2,1,0:T(8,128)(2,1)S(1)}, u32[]{:S(2)}, u32[]{:S(2)}) collective-permute-start(bf16[2,8,1024]{2,1,0:T(8,128)(2,1)S(1)} %get-tuple-element.65), channel_id=1, source_target_pairs={{0,1},{1,0},{2,3},{3,2},{4,5},{5,4},{6,7},{7,6},{8,9},{9,8},{10,11... | collective-permute-start | bytes 98312 | tf_op jit(solution)/shard_map/ppermute | solution.py:47
  57.7 6.9 %collective-permute-start.25 = (bf16[2,32,2048]{2,1,0:T(8,128)(2,1)S(1)}, bf16[2,32,2048]{2,1,0:T(8,128)(2,1)S(1)}, u32[]{:S(2)}, u32[]{:S(2)}) collective-permute-start(bf16[2,32,2048]{2,1,0:T(8,128)(2,1)S(1)} %get-tuple-element.39), channel_id=1, source_target_pairs={{0,1},{1,0},{2,3},{3,2},{4,5},{5,4},{6,7},{7,6},{8,9},{9,8},{10,11... | collective-permute-start | bytes 786440 | tf_op jit(solution)/shard_map/ppermute | solution.py:47
  57.8 6.9 %collective-permute-start.26 = (bf16[2,32,2048]{2,1,0:T(8,128)(2,1)S(1)}, bf16[2,32,2048]{2,1,0:T(8,128)(2,1)S(1)}, u32[]{:S(2)}, u32[]{:S(2)}) collective-permute-start(bf16[2,32,2048]{2,1,0:T(8,128)(2,1)S(1)} %get-tuple-element.41), channel_id=1, source_target_pairs={{0,1},{1,0},{2,3},{3,2},{4,5},{5,4},{6,7},{7,6},{8,9},{9,8},{10,11... | collective-permute-start | bytes 786440 | tf_op jit(solution)/shard_map/ppermute | solution.py:47
  61.1 6.9 %collective-permute-start.22 = (bf16[1,2,8,1024]{3,2,1,0:T(8,128)(2,1)S(1)}, bf16[1,2,8,1024]{3,2,1,0:T(8,128)(2,1)S(1)}, u32[]{:S(2)}, u32[]{:S(2)}) collective-permute-start(bf16[1,2,8,1024]{3,2,1,0:T(8,128)(2,1)S(1)} %get-tuple-element.59), channel_id=1, source_target_pairs={{0,8},{1,9},{2,10},{3,11},{4,12},{5,13},{6,14},{7,15},{8,0},{9,1},... | collective-permute-start | bytes 98312 | tf_op jit(solution)/shard_map/ppermute | solution.py:47
  62.3 5.7 %collective-permute-start.24 = (bf16[1,2,8,1024]{3,2,1,0:T(8,128)(2,1)S(1)}, bf16[1,2,8,1024]{3,2,1,0:T(8,128)(2,1)S(1)}, u32[]{:S(2)}, u32[]{:S(2)}) collective-permute-start(bf16[1,2,8,1024]{3,2,1,0:T(8,128)(2,1)S(1)} %get-tuple-element.60), channel_id=1, source_target_pairs={{0,24},{1,25},{2,26},{3,27},{4,28},{5,29},{6,30},{7,31},{8,16},{9,... | collective-permute-start | bytes 98312 | tf_op jit(solution)/shard_map/ppermute | solution.py:47
  63.7 4.8 %collective-permute-start.23 = (bf16[1,2,8,1024]{3,2,1,0:T(8,128)(2,1)S(1)}, bf16[1,2,8,1024]{3,2,1,0:T(8,128)(2,1)S(1)}, u32[]{:S(2)}, u32[]{:S(2)}) collective-permute-start(bf16[1,2,8,1024]{3,2,1,0:T(8,128)(2,1)S(1)} %get-tuple-element.61), channel_id=1, source_target_pairs={{0,16},{1,17},{2,18},{3,19},{4,20},{5,21},{6,22},{7,23},{8,24},{9,... | collective-permute-start | bytes 98312 | tf_op jit(solution)/shard_map/ppermute | solution.py:47
  (5 other events, 31.9 us)
